TPU v7x, 512 devices: a whole 4x8x8 slice. The times are simulated.
512 devices in a mesh: prow: 32 (over x, z), pcol: 16 (over y, core).
Axes of the slice: x: 4, y: 8, z: 8, core: 2. Of those that a mesh axis runs over, the one named last changes fastest.
Arguments:
- matrix: float32 [8192, 12288], P('prow', 'pcol'), may hold values from -6 to 6
- pivots: int32 [512], replicated, may hold values from 128 to 8191, as said below
- lower_inverse: float32 [4, 128, 128], replicated, may hold values from -1 to 1, as said below
- upper_inverse: float32 [4, 128, 128], replicated, may hold values from -1 to 1, as said below
Outputs:
- factored: float32 [8192, 12288], P('prow', 'pcol')
Inputs may be any that keep to these rules, and one draw needn't show every extreme that they name: For a column j of panel k (k * 128 <= j < (k + 1) * 128), pivots[j] lies in [(k + 1) * 128, 8192); the 128 pivots of one panel are distinct and include (k + 1) * 128 and 8191. Each lower_inverse[k] is unit lower triangular. Each upper_inverse[k] is upper triangular with a positive diagonal.
All inputs are finite; a program needn't handle non-finite values.
Results may differ from a plain program's by a relative error of at most 0.0003.
Values sent between devices are 32-bit elements; how exact they have to be, the bound alone decides.
No kernel may reach another device: no remote copies, remote signals or barrier semaphores. Data moves between devices by JAX's collectives and lax.ppermute only.
A program may use at most 64 MiB of HBM per device.

v0:
```python
import jax
import jax.numpy as jnp
from jax import lax
from jax.sharding import PartitionSpec as P


def from_root(value, axis, source):
    kept = jnp.where(lax.axis_index(axis) == source, value, 0).astype(value.dtype)
    return lax.psum(kept, axis)


def hdot(left, right):
    return jnp.dot(left, right, precision=lax.Precision.HIGHEST, preferred_element_type=jnp.float32)


def refresh(current, pending):
    if pending is None:
        return current
    return current - hdot(pending[0], pending[1])


def per_device(matrix, pivots, lower_inverse, upper_inverse):
    rows_dev, cols_dev = matrix.shape
    width = lower_inverse.shape[1]
    prow_count = lax.axis_size("prow")
    pcol_count = lax.axis_size("pcol")
    prow_index = lax.axis_index("prow")
    pcol_index = lax.axis_index("pcol")
    local_rows = jnp.arange(rows_dev, dtype=jnp.int32)
    local_cols = jnp.arange(cols_dev, dtype=jnp.int32)
    global_rows = (local_rows // width * prow_count + prow_index) * width + local_rows % width
    global_cols = (local_cols // width * pcol_count + pcol_index) * width + local_cols % width
    current = matrix
    pending = None
    for panel_index in range(lower_inverse.shape[0]):
        first_row = panel_index * width
        past_end = first_row + width
        row_owner = panel_index % prow_count
        row_slot = panel_index // prow_count * width
        past_slot = row_slot + width
        col_owner = panel_index % pcol_count
        col_slot = panel_index // pcol_count * width
        targets = pivots[first_row:past_end]
        owner_mask = targets // width % prow_count == prow_index
        local_slots = targets // (width * prow_count) * width + targets % width
        safe_slots = jnp.where(owner_mask, local_slots, 0)
        current = refresh(current, pending)
        source = jnp.take(current, safe_slots, axis=0)
        panel_before = current[row_slot:past_slot]
        source = jnp.where(owner_mask[:, None], source, 0.0)
        at_root = prow_index == row_owner
        incoming = lax.psum(source, "prow")
        initial = from_root(panel_before, "prow", row_owner)
        current = current.at[jnp.where(owner_mask, local_slots, rows_dev)].set(initial, mode="drop")
        kept_rows = current[row_slot:past_slot]
        current = current.at[row_slot:past_slot].set(jnp.where(at_root, incoming, kept_rows))
        below_rows = global_rows >= past_end
        right_cols = global_cols >= past_end
        column = current[:, col_slot : col_slot + width]
        solved = jnp.where(below_rows[:, None], hdot(column, upper_inverse[panel_index]), 0.0)
        multipliers = from_root(solved, "pcol", col_owner)
        upper_rows = jnp.where(right_cols[None, :], hdot(lower_inverse[panel_index], incoming), 0.0)
        kept_rows = current[row_slot:past_slot]
        current = current.at[row_slot:past_slot].set(
            jnp.where(at_root & right_cols[None, :], upper_rows, kept_rows)
        )
        at_column = pcol_index == col_owner
        kept_column = current[:, col_slot : col_slot + width]
        current = current.at[:, col_slot : col_slot + width].set(
            jnp.where(at_column & below_rows[:, None], multipliers, kept_column)
        )
        pending = (multipliers, upper_rows)
    return refresh(current, pending)


def solution(mesh):
    in_specs = (P("prow", "pcol"), P(), P(), P())
    out_specs = P("prow", "pcol")
    return jax.shard_map(
        per_device, mesh=mesh, in_specs=in_specs, out_specs=out_specs, check_vma=False
    )
```

profile of v0, /device:TPU:1, one launch (start us, length us, event | category | flops | bytes accessed | tf_op | source)
XLA Modules:
  0.0 1161.3 jit_solution(9643864148377500224)
XLA Ops:
  6.5 1.1 copy.95
  12.4 161.8 %all-reduce.27.cloned.1.call-done = (f32[128,768]{0,1:T(8,128)}, f32[128,768]{0,1:T(8,128)}) async-done(((f32[128,768]{0,1:T(8,128)}, f32[128,768]{0,1:T(8,128)}), (f32[128,768]{0,1:T(8,128)}, f32[128,768]{0,1:T(8,128)})) %all-reduce.27.cloned.1.call-update) | async-done | bytes 786448 | tf_op jit(solution)/shard_map/psum | solution.py:9
  174.2 1.2 copy.26
  175.3 1.4 scatter_fusion
  180.5 115.9 %all-reduce.13.cloned.1.call-done = f32[256,128]{0,1:T(8,128)} async-done(((f32[256,128]{0,1:T(8,128)}), f32[256,128]{0,1:T(8,128)}) %all-reduce.13.cloned.1.call-update) | async-done | bytes 131088 | tf_op jit(solution)/shard_map/psum | solution.py:9
  296.4 1.6 fusion.12
  301.8 158.0 %all-reduce.25.cloned.1.call-done = (f32[128,768]{0,1:T(8,128)}, f32[128,768]{0,1:T(8,128)}) async-done(((f32[128,768]{0,1:T(8,128)}, f32[128,768]{0,1:T(8,128)}), (f32[128,768]{0,1:T(8,128)}, f32[128,768]{0,1:T(8,128)})) %all-reduce.25.cloned.1.call-update) | async-done | bytes 786448 | tf_op jit(solution)/shard_map/psum | solution.py:9
  459.8 1.2 copy.33
  461.0 1.4 scatter_fusion.1
  463.7 1.0 fusion.2
  465.3 115.9 %all-reduce.15.cloned.1.call-done = f32[256,128]{0,1:T(8,128)} async-done(((f32[256,128]{0,1:T(8,128)}), f32[256,128]{0,1:T(8,128)}) %all-reduce.15.cloned.1.call-update) | async-done | bytes 131088 | tf_op jit(solution)/shard_map/psum | solution.py:9
  581.1 1.6 fusion.13
  586.6 158.0 %all-reduce.23.cloned.1.call-done = (f32[128,768]{0,1:T(8,128)}, f32[128,768]{0,1:T(8,128)}) async-done(((f32[128,768]{0,1:T(8,128)}, f32[128,768]{0,1:T(8,128)}), (f32[128,768]{0,1:T(8,128)}, f32[128,768]{0,1:T(8,128)})) %all-reduce.23.cloned.1.call-update) | async-done | bytes 786448 | tf_op jit(solution)/shard_map/psum | solution.py:9
  744.6 1.2 copy.41
  745.8 1.4 scatter_fusion.2
  750.1 115.9 %all-reduce.17.cloned.1.call-done = f32[256,128]{0,1:T(8,128)} async-done(((f32[256,128]{0,1:T(8,128)}), f32[256,128]{0,1:T(8,128)}) %all-reduce.17.cloned.1.call-update) | async-done | bytes 131088 | tf_op jit(solution)/shard_map/psum | solution.py:9
  865.9 1.7 fusion.14
  871.4 158.0 %all-reduce.21.cloned.1.call-done = (f32[128,768]{0,1:T(8,128)}, f32[128,768]{0,1:T(8,128)}) async-done(((f32[128,768]{0,1:T(8,128)}, f32[128,768]{0,1:T(8,128)}), (f32[128,768]{0,1:T(8,128)}, f32[128,768]{0,1:T(8,128)})) %all-reduce.21.cloned.1.call-update) | async-done | bytes 786448 | tf_op jit(solution)/shard_map/psum | solution.py:9
  1029.4 1.2 copy.49
  1030.5 1.6 scatter_fusion.3
  1033.4 1.0 fusion
  1034.9 115.9 %all-reduce.19.cloned.1.call-done = f32[256,128]{0,1:T(8,128)} async-done(((f32[256,128]{0,1:T(8,128)}), f32[256,128]{0,1:T(8,128)}) %all-reduce.19.cloned.1.call-update) | async-done | bytes 131088 | tf_op jit(solution)/shard_map/psum | solution.py:9
  1150.9 1.7 fusion.15
  1153.3 1.1 copy.56
  (110 shorter events, 26.8 us)
Async XLA Ops:
  6.5 167.6 %all-reduce.27.cloned.1.call-start = ((), (), s32[]{:S(2)}) async-start(), calls=%async_computation.7 | async-start | bytes 1572864 | tf_op jit(solution)/shard_map/psum | solution.py:9
  7.7 0.9 copy-start
  7.7 0.7 copy-start.12
  9.4 1.0 slice-start
  11.5 163.8 %copy-start.1 = (f32[256,768]{1,0:T(8,128)S(1)}, f32[256,768]{1,0:T(8,128)}, u32[]{:S(2)}) copy-start(f32[256,768]{1,0:T(8,128)} %copy-done) | copy-start | bytes 2359300
  11.5 284.8 %all-reduce.13.cloned.1.call-start = ((), (), s32[]{:S(2)}) async-start(), calls=%async_computation | async-start | bytes 262144 | tf_op jit(solution)/shard_map/psum | solution.py:9
  177.0 1.0 copy-start.2
  178.0 0.9 copy-start.10
  178.9 1.1 copy-start.11
  179.9 279.9 %all-reduce.25.cloned.1.call-start = ((), (), s32[]{:S(2)}) async-start(), calls=%async_computation.6 | async-start | bytes 1572864 | tf_op jit(solution)/shard_map/psum | solution.py:9
  296.4 1.7 copy-start.6
  301.7 279.5 %all-reduce.15.cloned.1.call-start = ((), (), s32[]{:S(2)}) async-start(), calls=%async_computation.1 | async-start | bytes 262144 | tf_op jit(solution)/shard_map/psum | solution.py:9
  462.6 1.0 copy-start.3
  464.7 279.9 %all-reduce.23.cloned.1.call-start = ((), (), s32[]{:S(2)}) async-start(), calls=%async_computation.5 | async-start | bytes 1572864 | tf_op jit(solution)/shard_map/psum | solution.py:9
  581.1 1.7 copy-start.7
  586.4 279.5 %all-reduce.17.cloned.1.call-start = ((), (), s32[]{:S(2)}) async-start(), calls=%async_computation.2 | async-start | bytes 262144 | tf_op jit(solution)/shard_map/psum | solution.py:9
  747.4 1.0 copy-start.4
  749.5 279.9 %all-reduce.21.cloned.1.call-start = ((), (), s32[]{:S(2)}) async-start(), calls=%async_computation.4 | async-start | bytes 1572864 | tf_op jit(solution)/shard_map/psum | solution.py:9
  865.9 1.7 copy-start.8
  871.2 279.6 %all-reduce.19.cloned.1.call-start = ((), (), s32[]{:S(2)}) async-start(), calls=%async_computation.3 | async-start | bytes 262144 | tf_op jit(solution)/shard_map/psum | solution.py:9
  1032.4 1.0 copy-start.5
  1150.9 1.7 copy-start.9
Sparse Core Ops, SparseCore 0:
  11.7 162.4 all-reduce.26
  180.1 116.2 all-reduce.12
  301.8 157.9 all-reduce.24
  464.8 116.2 all-reduce.14
  586.5 158.0 all-reduce.22
  749.6 116.2 all-reduce.16
  871.4 157.9 all-reduce.20
  1034.6 116.2 all-reduce.18
where the time goes:
time: 1160 us
  waiting for transfers between devices  1100 us (95%)
  local copies, waits for them, and re-layouts  24.9 us (2%)
  between operations  14 us (1%)
  other arithmetic  13.6 us (1%)
    psum x8, waiting for transfers between devices, from_root(): return lax.psum(kept, axis)  1100 us
  transfers between devices with their start and end apart: 8, of which 8 were waited for; matrix products, arithmetic and copies ran while one was open for 0% of the time, Pallas kernels for 0%

commit v1 on v0

v1 whole, which is shorter than its diff:
```python
import jax
import jax.numpy as jnp
from jax import lax
from jax.experimental import pallas as pl
from jax.experimental.pallas import tpu as pltpu
from jax.sharding import PartitionSpec as P

NB = 128
PANELS = 4
TOP = NB * PANELS
PROW = 32
PCOL = 16
ROWS = 256
COLS = 768
REST = COLS - NB
BF = jnp.bfloat16
F32 = jnp.float32
X_GROUPS = [[x * 8 + z for x in range(4)] for z in range(8)]
Z_GROUPS = [[x * 8 + z for z in range(8)] for x in range(4)]
VMEM = pl.BlockSpec(memory_space=pltpu.VMEM)
SMEM = pl.BlockSpec(memory_space=pltpu.SMEM)


def mm(left, right):
    return lax.dot_general(left, right, (((1,), (0,)), ((), ())), preferred_element_type=F32)


def split2(value):
    high = value.astype(BF)
    low = (value - high.astype(F32)).astype(BF)
    return high, low


def select_rows(onehot, value):
    first = value.astype(BF)
    rest = value - first.astype(F32)
    second = rest.astype(BF)
    third = (rest - second.astype(F32)).astype(BF)
    return mm(onehot, first) + mm(onehot, second) + mm(onehot, third)


def dot3(left, right):
    lh, ll = split2(left)
    rh, rl = split2(right)
    return mm(jnp.concatenate([lh, ll, lh], axis=1), jnp.concatenate([rh, rh, rl], axis=0))


def chase(rows, piv_row_ref, panels):
    lanes = lax.broadcasted_iota(jnp.int32, (rows.shape[0], NB), 1).astype(F32)
    for m in panels:
        equal = rows == piv_row_ref[m : m + 1, :]
        hit = jnp.sum(jnp.where(equal, lanes + float(m * NB + 1), 0.0), axis=1, keepdims=True)
        hit = hit.astype(jnp.int32)
        rows = jnp.where(hit > 0, hit - 1, rows)
    return rows


def pick_kernel(place_ref, piv_row_ref, piv_col_ref, a_ref, first_ref, rest_ref, origin_ref):
    prow = place_ref[0]
    lane = lax.broadcasted_iota(jnp.int32, (NB, ROWS), 1)
    for k in range(PANELS):
        rows = chase(piv_col_ref[k * NB : (k + 1) * NB, :], piv_row_ref, range(k - 1, -1, -1))
        owner = (rows >> 7) & 31
        slot = ((rows >> 12) << 7) | (rows & 127)
        slot = jnp.where(owner == prow, slot, -1)
        onehot = jnp.where(lane == slot, 1.0, 0.0).astype(BF)
        first_ref[k * NB : (k + 1) * NB, :] = select_rows(onehot, a_ref[:, :NB])
        rest_ref[k * NB : (k + 1) * NB, :] = select_rows(onehot, a_ref[:, NB:])
    local = lax.broadcasted_iota(jnp.int32, (ROWS, 1), 0)
    rows = ((local >> 7) * PROW + prow) * NB + (local & 127)
    rows = chase(rows, piv_row_ref, range(PANELS - 1, -1, -1))
    origin_ref[...] = jnp.broadcast_to(rows, (ROWS, NB))


def place_of(origin):
    unit = (origin >> 2) & 31
    return (unit << 5) + 16 + ((origin >> 7) << 2) + (origin & 3)


def moved_rows(origin, gathered, kept):
    lane = lax.broadcasted_iota(jnp.int32, (ROWS, 1024), 1)
    onehot = jnp.where(lane == jnp.where(origin < TOP, place_of(origin), -1), 1.0, 0.0).astype(BF)
    return jnp.where(origin < TOP, select_rows(onehot, gathered), kept)


def column_kernel(origin_ref, gathered_ref, a_ref, out_ref):
    origin = origin_ref[:, :1]
    for unit in range(PROW):
        out_ref[unit * 16 : unit * 16 + 16, :] = gathered_ref[unit * 32 : unit * 32 + 16, :]
    out_ref[TOP:, :] = moved_rows(origin, gathered_ref[...], a_ref[:, :NB])


def factor_kernel(
    place_ref, origin_ref, gathered_ref, a_ref, own_ref, near_ref, across_ref, pair_ref,
    lower_ref, upper_ref, out_ref, z_ref,
):
    prow = place_ref[0]
    pcol = place_ref[1]
    kind = pcol & 3

    def put(index, value):
        z_ref[:, pl.ds(pl.multiple_of(index * NB, NB), NB)] = value

    put(kind, near_ref[...])
    put(kind ^ 2, across_ref[...])
    put(kind ^ 1, pair_ref[:, :NB])
    put(kind ^ 3, pair_ref[:, NB:])
    z_ref[:, TOP : TOP + NB] = own_ref[...]
    for unit in range(PROW):
        z_ref[unit * 16 : unit * 16 + 16, TOP + NB :] = gathered_ref[unit * 32 : unit * 32 + 16, :]
    origin = origin_ref[:, :1]

    @pl.loop(0, REST // NB)
    def _(c):
        cols = pl.ds(pl.multiple_of(c * NB, NB), NB)
        shifted = pl.ds(pl.multiple_of(c * NB + NB, NB), NB)
        target = pl.ds(pl.multiple_of(c * NB + TOP + NB, NB), NB)
        z_ref[TOP:, target] = moved_rows(origin, gathered_ref[:, cols], a_ref[:, shifted])

    for k in range(PANELS):
        s = k * NB
        e = s + NB
        multipliers = dot3(z_ref[e:, s:e], upper_ref[k])
        z_ref[e:, s:e] = multipliers
        mh, ml = split2(multipliers)
        m3 = jnp.concatenate([mh, ml, mh], axis=1)
        lh, ll = split2(lower_ref[k])
        l3 = jnp.concatenate([lh, ll, lh], axis=1)

        @pl.loop(0, (TOP + COLS - e) // NB)
        def _(c):
            cols = pl.ds(pl.multiple_of(c * NB + e, NB), NB)
            bh, bl = split2(z_ref[s:e, cols])
            upper_rows = mm(l3, jnp.concatenate([bh, bh, bl], axis=0))
            z_ref[s:e, cols] = upper_rows
            uh, ul = split2(upper_rows)
            z_ref[e:, cols] = z_ref[e:, cols] - mm(m3, jnp.concatenate([uh, uh, ul], axis=0))

    out_ref[...] = z_ref[TOP:, TOP:]
    panel_cols = pl.ds(pl.multiple_of(kind * NB, NB), NB)
    top_rows = pl.ds(pl.multiple_of((prow & 3) * NB, NB), NB)

    @pl.when(pcol < PANELS)
    def _():
        out_ref[:, :NB] = z_ref[TOP:, panel_cols]

    @pl.when(prow < PANELS)
    def _():
        out_ref[:NB, :] = z_ref[top_rows, TOP:]

    @pl.when((prow < PANELS) & (pcol < PANELS))
    def _():
        out_ref[:NB, :NB] = z_ref[top_rows, panel_cols]


def exchange_first(picked, top):
    sent = jnp.concatenate([picked.reshape(PROW, 16, NB), top.reshape(PROW, 4, NB)], axis=1)
    got = lax.all_to_all(sent, "prow", 0, 0)
    chunk = jnp.concatenate([jnp.sum(got[:, :16], axis=0), got[:4, 16:].reshape(16, NB)], axis=0)
    sent = jnp.broadcast_to(chunk[None], (PROW, 32, NB))
    return lax.all_to_all(sent, "prow", 0, 0).reshape(PROW * 32, NB)


def exchange_rest(picked, top):
    sent = jnp.concatenate([picked.reshape(4, NB, REST), top.reshape(4, 32, REST)], axis=1)
    got = lax.all_to_all(sent, "prow", 0, 0, axis_index_groups=X_GROUPS)
    sent = jnp.concatenate(
        [jnp.sum(got[:, :NB], axis=0).reshape(8, 16, REST), got[0, NB:].reshape(8, 4, REST)], axis=1
    )
    got = lax.all_to_all(sent, "prow", 0, 0, axis_index_groups=Z_GROUPS)
    chunk = jnp.concatenate([jnp.sum(got[:, :16], axis=0), got[:4, 16:].reshape(16, REST)], axis=0)
    got = lax.all_to_all(
        jnp.broadcast_to(chunk[None], (8, 32, REST)), "prow", 0, 0, axis_index_groups=Z_GROUPS
    )
    got = got.reshape(256, REST)
    got = lax.all_to_all(
        jnp.broadcast_to(got[None], (4, 256, REST)), "prow", 0, 0, axis_index_groups=X_GROUPS
    )
    return got.reshape(PROW * 32, REST)


def spread_columns(own, pcol):
    up = lax.ppermute(own, "pcol", [(q, q + 4) for q in range(4)])
    down = lax.ppermute(own, "pcol", [(q, q + 12) for q in range(4)])
    near = jnp.where(pcol < 4, own, jnp.where(pcol < 8, up, down))
    half = near.shape[0] // 2
    left = lax.ppermute(near[:half], "pcol", [(q + 4, q + 8) for q in range(4)])
    right = lax.ppermute(near[half:], "pcol", [(q + 12, q + 8) for q in range(4)])
    far = (pcol >= 8) & (pcol < 12)
    near = jnp.where(far, jnp.concatenate([left, right], axis=0), near)
    across = lax.ppermute(near, "pcol", [(q, q ^ 2) for q in range(PCOL)])
    both = jnp.concatenate([near, across], axis=1)
    pair = lax.ppermute(both, "pcol", [(q, q ^ 1) for q in range(PCOL)])
    return near, across, pair


def per_device(matrix, pivots, lower_inverse, upper_inverse):
    prow = lax.axis_index("prow")
    pcol = lax.axis_index("pcol")
    place = jnp.stack([prow, pcol]).astype(jnp.int32)
    picked_first, picked_rest, origin = pl.pallas_call(
        pick_kernel,
        in_specs=[SMEM, VMEM, VMEM, VMEM],
        out_specs=[VMEM] * 3,
        out_shape=[
            jax.ShapeDtypeStruct((TOP, NB), F32),
            jax.ShapeDtypeStruct((TOP, REST), F32),
            jax.ShapeDtypeStruct((ROWS, NB), jnp.int32),
        ],
    )(place, pivots.reshape(PANELS, NB), pivots.reshape(TOP, 1), matrix)
    gathered_first = exchange_first(picked_first, matrix[:NB, :NB])
    own = pl.pallas_call(
        column_kernel,
        in_specs=[VMEM] * 3,
        out_specs=VMEM,
        out_shape=jax.ShapeDtypeStruct((TOP + ROWS, NB), F32),
    )(origin, gathered_first, matrix)
    near, across, pair = spread_columns(own, pcol)
    gathered_rest = exchange_rest(picked_rest, matrix[:NB, NB:])
    return pl.pallas_call(
        factor_kernel,
        in_specs=[SMEM] + [VMEM] * 9,
        out_specs=VMEM,
        out_shape=jax.ShapeDtypeStruct((ROWS, COLS), F32),
        scratch_shapes=[pltpu.VMEM((TOP + ROWS, TOP + COLS), F32)],
    )(place, origin, gathered_rest, matrix, own, near, across, pair, lower_inverse, upper_inverse)


def solution(mesh):
    in_specs = (P("prow", "pcol"), P(), P(), P())
    out_specs = P("prow", "pcol")
    return jax.shard_map(
        per_device, mesh=mesh, in_specs=in_specs, out_specs=out_specs, check_vma=False
    )
```

time: 1160 us -> 190 us (0.16)
  waiting for transfers between devices: 1100 us -> 89.5 us
  starting transfers between devices: 0.3 us -> 55.9 us
  Pallas kernels: 0 us -> 27.5 us
  local copies, waits for them, and re-layouts: 24.9 us -> 8.4 us
  between operations: 14 us -> 0.19 us
    psum x8 -> x0, waiting for transfers between devices: 1100 us -> none  [from_root(): return lax.psum(kept, axis)]
    all_to_all x0 -> x6, waiting for transfers between devices: none -> 60 us  [the longest x1 14 us: exchange_rest(): got = lax.all_to_all(sent, 'prow', 0, 0, axis_index_groups=X_GROUPS)]
    all_to_all x0 -> x6, starting transfers between devices: none -> 41.4 us  [the longest x1 15.9 us: exchange_first(): got = lax.all_to_all(sent, 'prow', 0, 0)]
    ppermute x0 -> x6, waiting for transfers between devices: none -> 29.5 us  [the longest x1 14.7 us: spread_columns(): down = lax.ppermute(own, 'pcol', [(q, q + 12) for q in range(4)])]
    pallas_call x0 -> x3, Pallas kernels: none -> 27.5 us  [the longest x1 20.8 us: per_device(): pl.pallas_call(factor_kernel, in_specs=[SMEM] + [VMEM] * 9, out_specs=VME...]
    ppermute x0 -> x6, starting transfers between devices: none -> 14.6 us  [the longest x1 4.23 us: spread_columns(): up = lax.ppermute(own, 'pcol', [(q, q + 4) for q in range(4)])]
  transfers between devices with their start and end apart: 8 -> 12, of which waited for: 8 -> 9; matrix products, arithmetic and copies ran while one was open for 0% -> 3% of each run, Pallas kernels for 0% -> 1%
where the time goes in v1:
time: 190 us; the launch traced here: 189 us
  waiting for transfers between devices  89.5 us (47%)
  starting transfers between devices  55.9 us (29%)
  Pallas kernels  27.5 us (14%)
  local copies, waits for them, and re-layouts  8.4 us (4%)
  other arithmetic  7.17 us (4%)
    pallas_call x1, Pallas kernels, per_device(): pl.pallas_call(factor_kernel, in_specs=[SMEM] + [VMEM] * 9, out_specs=VME...  20.8 us
    all_to_all x1, starting transfers between devices, exchange_first(): got = lax.all_to_all(sent, 'prow', 0, 0)  15.9 us
    ppermute x1, waiting for transfers between devices, spread_columns(): down = lax.ppermute(own, 'pcol', [(q, q + 12) for q in range(4)])  14.7 us
    all_to_all x1, waiting for transfers between devices, exchange_rest(): got = lax.all_to_all(sent, 'prow', 0, 0, axis_index_groups=X_GROUPS)  14 us
    all_to_all x1, waiting for transfers between devices, exchange_rest(): got = lax.all_to_all(sent, 'prow', 0, 0, axis_index_groups=Z_GROUPS)  13.7 us
    all_to_all x1, waiting for transfers between devices, exchange_first(): return lax.all_to_all(sent, 'prow', 0, 0).reshape(PROW * 32, NB)  12.5 us
    all_to_all x1, waiting for transfers between devices, exchange_rest(): lax.all_to_all(jnp.broadcast_to(got[None], (4, 256, REST)), 'prow', 0, 0,...  10.2 us
    ppermute x1, waiting for transfers between devices, spread_columns(): across = lax.ppermute(near, 'pcol', [(q, q ^ 2) for q in range(PCOL)])  10 us
  transfers between devices with their start and end apart: 12, of which 9 were waited for; matrix products, arithmetic and copies ran while one was open for 3% of the time, Pallas kernels for 1%

profile of v1, /device:TPU:1, one launch (start us, length us, event | category | flops | bytes accessed | tf_op | source)
XLA Modules:
  0.0 188.8 jit_solution(18116544740534316437)
XLA Ops:
  3.2 4.0 %shard_map.46 = (f32[512,128]{1,0:T(8,128)}, f32[512,640]{1,0:T(8,128)}, s32[256,128]{1,0:T(8,128)}) custom-call(s32[2]{0:T(128)} %pad_add_fusion.place_ref, s32[4,128]{1,0:T(4,128)} %bitcast.23, s32[512,1]{1,0:T(8,128)} %copy.5.piv_col_ref, f32[256,768]{1,0:T(8,128)} %a_ref.5), custom_call_target="tpu_custom_call" | custom-call | tf_op jit(solution)/shard_map/pallas_call | solution.py:201
  7.2 2.6 %pad_maximum_fusion = f32[4,160,640]{2,1,0:T(8,128)} fusion(f32[4,32,640]{2,1,0:T(8,128)S(1)} %bitcast.17, f32[4,128,640]{2,1,0:T(8,128)} %bitcast.16), kind=kLoop, calls=%fused_computation | loop fusion | flops 409600 | bytes 3276800 | tf_op jit(solution)/shard_map/concatenate | solution.py:165
  9.8 5.0 %all-to-all-start = ((f32[4,160,640]{2,1,0:T(8,128)}), f32[4,160,640]{2,1,0:T(8,128)S(1)}, u32[]{:S(2)}, u32[]{:S(2)}) async-start(f32[4,160,640]{2,1,0:T(8,128)} %pad_maximum_fusion), calls=%async_computation | async-start | bytes 3276800 | tf_op jit(solution)/shard_map/all_to_all | solution.py:166
  16.4 14.0 %all-to-all-done = f32[4,160,640]{2,1,0:T(8,128)S(1)} async-done(((f32[4,160,640]{2,1,0:T(8,128)}), f32[4,160,640]{2,1,0:T(8,128)S(1)}, u32[]{:S(2)}, u32[]{:S(2)}) %all-to-all-start) | async-done | bytes 1638432 | tf_op jit(solution)/shard_map/all_to_all | solution.py:166
  30.4 15.9 %all-to-all-start.4 = ((f32[32,20,128]{2,1,0:T(8,128)}), f32[32,20,128]{2,1,0:T(8,128)S(1)}, u32[]{:S(2)}, u32[]{:S(2)}) async-start(f32[32,20,128]{2,1,0:T(8,128)} %pad_maximum_fusion.3), calls=%async_computation.4 | async-start | bytes 786432 | tf_op jit(solution)/shard_map/all_to_all | solution.py:158
  47.3 9.6 %all-to-all-done.4 = f32[32,20,128]{2,1,0:T(8,128)S(1)} async-done(((f32[32,20,128]{2,1,0:T(8,128)}), f32[32,20,128]{2,1,0:T(8,128)S(1)}, u32[]{:S(2)}, u32[]{:S(2)}) %all-to-all-start.4) | async-done | bytes 327712 | tf_op jit(solution)/shard_map/all_to_all | solution.py:158
  56.9 6.0 %all-to-all-start.1 = ((f32[8,20,640]{2,1,0:T(8,128)}), f32[8,20,640]{2,1,0:T(8,128)S(1)}, u32[]{:S(2)}, u32[]{:S(2)}) async-start(f32[8,20,640]{2,1,0:T(8,128)} %pad_maximum_fusion.2), calls=%async_computation.1 | async-start | bytes 983040 | tf_op jit(solution)/shard_map/all_to_all | solution.py:170
  63.0 13.7 %all-to-all-done.1 = f32[8,20,640]{2,1,0:T(8,128)S(1)} async-done(((f32[8,20,640]{2,1,0:T(8,128)}), f32[8,20,640]{2,1,0:T(8,128)S(1)}, u32[]{:S(2)}, u32[]{:S(2)}) %all-to-all-start.1) | async-done | bytes 409632 | tf_op jit(solution)/shard_map/all_to_all | solution.py:170
  77.5 5.1 %all-to-all-start.5 = ((f32[32,32,128]{2,1,0:T(8,128)}), f32[32,32,128]{2,1,0:T(8,128)S(1)}, u32[]{:S(2)}, u32[]{:S(2)}) async-start(f32[32,32,128]{2,1,0:T(8,128)} %broadcast_in_dim.22), calls=%async_computation.5 | async-start | bytes 1048576 | tf_op jit(solution)/shard_map/all_to_all | solution.py:161
  82.8 12.5 %all-to-all-done.5 = f32[32,32,128]{2,1,0:T(8,128)S(1)} async-done(((f32[32,32,128]{2,1,0:T(8,128)}), f32[32,32,128]{2,1,0:T(8,128)S(1)}, u32[]{:S(2)}, u32[]{:S(2)}) %all-to-all-start.5) | async-done | bytes 524320 | tf_op jit(solution)/shard_map/all_to_all | solution.py:161
  96.2 5.7 %all-to-all-start.2 = ((f32[8,32,640]{2,1,0:T(8,128)}), f32[8,32,640]{2,1,0:T(8,128)S(1)}, u32[]{:S(2)}, u32[]{:S(2)}) async-start(f32[8,32,640]{2,1,0:T(8,128)} %broadcast_in_dim.8), calls=%async_computation.2 | async-start | bytes 1310720 | tf_op jit(solution)/shard_map/all_to_all | solution.py:172
  101.9 2.7 %shard_map.47.own_ref = f32[768,128]{1,0:T(8,128)} custom-call(s32[256,128]{1,0:T(8,128)} %get-tuple-element.8.origin_ref, f32[1024,128]{1,0:T(8,128)} %bitcast.15, f32[256,768]{1,0:T(8,128)} %a_ref.5), custom_call_target="tpu_custom_call" | custom-call | tf_op jit(solution)/shard_map/pallas_call | solution.py:212
  104.6 4.2 %collective-permute-start = (f32[768,128]{1,0:T(8,128)}, f32[768,128]{1,0:T(8,128)S(1)}, u32[]{:S(2)}, u32[]{:S(2)}) collective-permute-start(f32[768,128]{1,0:T(8,128)} %shard_map.47.own_ref), channel_id=1, source_target_pairs={{0,4},{1,5},{2,6},{3,7},{16,20},{17,21},{18,22},{19,23},{32,36},{3... | collective-permute-start | bytes 1179656 | tf_op jit(solution)/shard_map/ppermute | solution.py:183
  108.9 2.4 %collective-permute-start.1 = (f32[768,128]{1,0:T(8,128)}, f32[768,128]{1,0:T(8,128)S(1)}, u32[]{:S(2)}, u32[]{:S(2)}) collective-permute-start(f32[768,128]{1,0:T(8,128)} %shard_map.47.own_ref), channel_id=1, source_target_pairs={{0,12},{1,13},{2,14},{3,15},{16,28},{17,29},{18,30},{19,31},{32,44... | collective-permute-start | bytes 1179656 | tf_op jit(solution)/shard_map/ppermute | solution.py:184
  111.2 2.7 %collective-permute-done = f32[768,128]{1,0:T(8,128)S(1)} collective-permute-done((f32[768,128]{1,0:T(8,128)}, f32[768,128]{1,0:T(8,128)S(1)}, u32[]{:S(2)}, u32[]{:S(2)}) %collective-permute-start) | collective-permute-done | bytes 393248 | tf_op jit(solution)/shard_map/ppermute | solution.py:183
  113.9 14.7 %collective-permute-done.1 = f32[768,128]{1,0:T(8,128)S(1)} collective-permute-done((f32[768,128]{1,0:T(8,128)}, f32[768,128]{1,0:T(8,128)S(1)}, u32[]{:S(2)}, u32[]{:S(2)}) %collective-permute-start.1) | collective-permute-done | bytes 393248 | tf_op jit(solution)/shard_map/ppermute | solution.py:184
  129.7 1.7 broadcast_in_dim.10
  131.4 3.7 %all-to-all-start.3 = ((f32[4,256,640]{2,1,0:T(8,128)}), f32[4,256,640]{2,1,0:T(8,128)S(1)}, u32[]{:S(2)}, u32[]{:S(2)}) async-start(f32[4,256,640]{2,1,0:T(8,128)} %broadcast_in_dim.10), calls=%async_computation.3 | async-start | bytes 5242880 | tf_op jit(solution)/shard_map/all_to_all | solution.py:176
  138.8 1.9 %collective-permute-start.4 = (f32[768,128]{1,0:T(8,128)S(1)}, f32[768,128]{1,0:T(8,128)S(1)}, u32[]{:S(2)}, u32[]{:S(2)}) collective-permute-start(f32[768,128]{1,0:T(8,128)S(1)} %maximum_select_fusion.near_ref), channel_id=1, source_target_pairs={{0,2},{1,3},{2,0},{3,1},{4,6},{5,7},{6,4},{7,5},{8,10},{9,11},{10,... | collective-permute-start | bytes 1179656 | tf_op jit(solution)/shard_map/ppermute | solution.py:191
  140.8 10.0 %collective-permute-done.4.across_ref = f32[768,128]{1,0:T(8,128)S(1)} collective-permute-done((f32[768,128]{1,0:T(8,128)S(1)}, f32[768,128]{1,0:T(8,128)S(1)}, u32[]{:S(2)}, u32[]{:S(2)}) %collective-permute-start.4) | collective-permute-done | bytes 393248 | tf_op jit(solution)/shard_map/ppermute | solution.py:191
  150.8 3.4 %collective-permute-start.5 = (f32[768,256]{1,0:T(8,128)S(1)}, f32[768,256]{1,0:T(8,128)}, u32[]{:S(2)}, u32[]{:S(2)}) collective-permute-start(f32[768,256]{1,0:T(8,128)S(1)} %pad_maximum_fusion.1), channel_id=1, source_target_pairs={{0,1},{1,0},{2,3},{3,2},{4,5},{5,4},{6,7},{7,6},{8,9},{9,8},{10,11... | collective-permute-start | bytes 2359304 | tf_op jit(solution)/shard_map/ppermute | solution.py:193
  154.2 2.0 %collective-permute-done.5.pair_ref = f32[768,256]{1,0:T(8,128)} collective-permute-done((f32[768,256]{1,0:T(8,128)S(1)}, f32[768,256]{1,0:T(8,128)}, u32[]{:S(2)}, u32[]{:S(2)}) %collective-permute-start.5) | collective-permute-done | bytes 786464 | tf_op jit(solution)/shard_map/ppermute | solution.py:193
  156.3 10.2 %all-to-all-done.3 = f32[4,256,640]{2,1,0:T(8,128)S(1)} async-done(((f32[4,256,640]{2,1,0:T(8,128)}), f32[4,256,640]{2,1,0:T(8,128)S(1)}, u32[]{:S(2)}, u32[]{:S(2)}) %all-to-all-start.3) | async-done | bytes 2621472 | tf_op jit(solution)/shard_map/all_to_all | solution.py:176
  167.9 20.8 %shard_map.48 = f32[256,768]{1,0:T(8,128)} custom-call(s32[2]{0:T(128)} %pad_add_fusion.place_ref, s32[256,128]{1,0:T(8,128)} %get-tuple-element.8.origin_ref, f32[1024,640]{1,0:T(8,128)} %bitcast.13, f32[256,768]{1,0:T(8,128)} %a_ref.5, f32[768,128]{1,0:T(8,128)} %shard_map.47.own_ref, f32[768,128]{1,0:T(8,128)} %copy-done.1, f32[768,128]{1,0:T(8,128)} %copy-done.3, ...), custom_call_target="tpu_custom_call" | custom-call | tf_op jit(solution)/shard_map/pallas_call | solution.py:220
  (37 shorter events, 14.0 us)
Async XLA Ops:
  9.8 5.8 %copy-start.4 = (f32[512,128]{1,0:T(8,128)S(1)}, f32[512,128]{1,0:T(8,128)}, u32[]{:S(2)}) copy-start(f32[512,128]{1,0:T(8,128)} %get-tuple-element.10) | copy-start | bytes 786436
  9.8 20.6 %all-to-all-start = ((f32[4,160,640]{2,1,0:T(8,128)}), f32[4,160,640]{2,1,0:T(8,128)S(1)}, u32[]{:S(2)}, u32[]{:S(2)}) async-start(f32[4,160,640]{2,1,0:T(8,128)} %pad_maximum_fusion), calls=%async_computation | async-start | bytes 3276800 | tf_op jit(solution)/shard_map/all_to_all | solution.py:166
  30.4 26.5 %all-to-all-start.4 = ((f32[32,20,128]{2,1,0:T(8,128)}), f32[32,20,128]{2,1,0:T(8,128)S(1)}, u32[]{:S(2)}, u32[]{:S(2)}) async-start(f32[32,20,128]{2,1,0:T(8,128)} %pad_maximum_fusion.3), calls=%async_computation.4 | async-start | bytes 786432 | tf_op jit(solution)/shard_map/all_to_all | solution.py:158
  56.9 19.8 %all-to-all-start.1 = ((f32[8,20,640]{2,1,0:T(8,128)}), f32[8,20,640]{2,1,0:T(8,128)S(1)}, u32[]{:S(2)}, u32[]{:S(2)}) async-start(f32[8,20,640]{2,1,0:T(8,128)} %pad_maximum_fusion.2), calls=%async_computation.1 | async-start | bytes 983040 | tf_op jit(solution)/shard_map/all_to_all | solution.py:170
  77.5 17.8 %all-to-all-start.5 = ((f32[32,32,128]{2,1,0:T(8,128)}), f32[32,32,128]{2,1,0:T(8,128)S(1)}, u32[]{:S(2)}, u32[]{:S(2)}) async-start(f32[32,32,128]{2,1,0:T(8,128)} %broadcast_in_dim.22), calls=%async_computation.5 | async-start | bytes 1048576 | tf_op jit(solution)/shard_map/all_to_all | solution.py:161
  95.3 6.6 %copy-start.2 = (f32[32,32,128]{2,1,0:T(8,128)}, f32[32,32,128]{2,1,0:T(8,128)S(1)}, u32[]{:S(2)}) copy-start(f32[32,32,128]{2,1,0:T(8,128)S(1)} %all-to-all-done.5) | copy-start | bytes 1572868
  96.2 33.5 %all-to-all-start.2 = ((f32[8,32,640]{2,1,0:T(8,128)}), f32[8,32,640]{2,1,0:T(8,128)S(1)}, u32[]{:S(2)}, u32[]{:S(2)}) async-start(f32[8,32,640]{2,1,0:T(8,128)} %broadcast_in_dim.8), calls=%async_computation.2 | async-start | bytes 1310720 | tf_op jit(solution)/shard_map/all_to_all | solution.py:172
  104.6 9.3 %collective-permute-start = (f32[768,128]{1,0:T(8,128)}, f32[768,128]{1,0:T(8,128)S(1)}, u32[]{:S(2)}, u32[]{:S(2)}) collective-permute-start(f32[768,128]{1,0:T(8,128)} %shard_map.47.own_ref), channel_id=1, source_target_pairs={{0,4},{1,5},{2,6},{3,7},{16,20},{17,21},{18,22},{19,23},{32,36},{3... | collective-permute-start | bytes 1179656 | tf_op jit(solution)/shard_map/ppermute | solution.py:183
  108.9 19.8 %collective-permute-start.1 = (f32[768,128]{1,0:T(8,128)}, f32[768,128]{1,0:T(8,128)S(1)}, u32[]{:S(2)}, u32[]{:S(2)}) collective-permute-start(f32[768,128]{1,0:T(8,128)} %shard_map.47.own_ref), channel_id=1, source_target_pairs={{0,12},{1,13},{2,14},{3,15},{16,28},{17,29},{18,30},{19,31},{32,44... | collective-permute-start | bytes 1179656 | tf_op jit(solution)/shard_map/ppermute | solution.py:184
  131.4 35.1 %all-to-all-start.3 = ((f32[4,256,640]{2,1,0:T(8,128)}), f32[4,256,640]{2,1,0:T(8,128)S(1)}, u32[]{:S(2)}, u32[]{:S(2)}) async-start(f32[4,256,640]{2,1,0:T(8,128)} %broadcast_in_dim.10), calls=%async_computation.3 | async-start | bytes 5242880 | tf_op jit(solution)/shard_map/all_to_all | solution.py:176
  135.1 2.7 %collective-permute-start.3 = (f32[384,128]{1,0:T(8,128)S(1)}, f32[384,128]{1,0:T(8,128)}, u32[]{:S(2)}, u32[]{:S(2)}) collective-permute-start(f32[384,128]{1,0:T(8,128)S(1)} %get-tuple-element.12), channel_id=1, source_target_pairs={{12,8},{13,9},{14,10},{15,11},{28,24},{29,25},{30,26},{31,27},{44,... | collective-permute-start | bytes 589832 | tf_op jit(solution)/shard_map/ppermute | solution.py:188
  136.4 1.3 collective-permute-start.2
  138.8 27.6 %copy-start.1 = (f32[768,128]{1,0:T(8,128)}, f32[768,128]{1,0:T(8,128)S(1)}, u32[]{:S(2)}) copy-start(f32[768,128]{1,0:T(8,128)S(1)} %maximum_select_fusion.near_ref) | copy-start | bytes 1179652
  138.8 12.0 %collective-permute-start.4 = (f32[768,128]{1,0:T(8,128)S(1)}, f32[768,128]{1,0:T(8,128)S(1)}, u32[]{:S(2)}, u32[]{:S(2)}) collective-permute-start(f32[768,128]{1,0:T(8,128)S(1)} %maximum_select_fusion.near_ref), channel_id=1, source_target_pairs={{0,2},{1,3},{2,0},{3,1},{4,6},{5,7},{6,4},{7,5},{8,10},{9,11},{10,... | collective-permute-start | bytes 1179656 | tf_op jit(solution)/shard_map/ppermute | solution.py:191
  150.8 15.6 %copy-start.3 = (f32[768,128]{1,0:T(8,128)}, f32[768,128]{1,0:T(8,128)S(1)}, u32[]{:S(2)}) copy-start(f32[768,128]{1,0:T(8,128)S(1)} %collective-permute-done.4.across_ref) | copy-start | bytes 1179652
  150.8 5.4 %collective-permute-start.5 = (f32[768,256]{1,0:T(8,128)S(1)}, f32[768,256]{1,0:T(8,128)}, u32[]{:S(2)}, u32[]{:S(2)}) collective-permute-start(f32[768,256]{1,0:T(8,128)S(1)} %pad_maximum_fusion.1), channel_id=1, source_target_pairs={{0,1},{1,0},{2,3},{3,2},{4,5},{5,4},{6,7},{7,6},{8,9},{9,8},{10,11... | collective-permute-start | bytes 2359304 | tf_op jit(solution)/shard_map/ppermute | solution.py:193
  166.4 1.5 copy-start

commit v2 on v1

--- a/solution.py
+++ b/solution.py
@@ -90,69 +90,6 @@
     out_ref[TOP:, :] = moved_rows(origin, gathered_ref[...], a_ref[:, :NB])
 
 
-def factor_kernel(
-    place_ref, origin_ref, gathered_ref, a_ref, own_ref, near_ref, across_ref, pair_ref,
-    lower_ref, upper_ref, out_ref, z_ref,
-):
-    prow = place_ref[0]
-    pcol = place_ref[1]
-    kind = pcol & 3
-
-    def put(index, value):
-        z_ref[:, pl.ds(pl.multiple_of(index * NB, NB), NB)] = value
-
-    put(kind, near_ref[...])
-    put(kind ^ 2, across_ref[...])
-    put(kind ^ 1, pair_ref[:, :NB])
-    put(kind ^ 3, pair_ref[:, NB:])
-    z_ref[:, TOP : TOP + NB] = own_ref[...]
-    for unit in range(PROW):
-        z_ref[unit * 16 : unit * 16 + 16, TOP + NB :] = gathered_ref[unit * 32 : unit * 32 + 16, :]
-    origin = origin_ref[:, :1]
-
-    @pl.loop(0, REST // NB)
-    def _(c):
-        cols = pl.ds(pl.multiple_of(c * NB, NB), NB)
-        shifted = pl.ds(pl.multiple_of(c * NB + NB, NB), NB)
-        target = pl.ds(pl.multiple_of(c * NB + TOP + NB, NB), NB)
-        z_ref[TOP:, target] = moved_rows(origin, gathered_ref[:, cols], a_ref[:, shifted])
-
-    for k in range(PANELS):
-        s = k * NB
-        e = s + NB
-        multipliers = dot3(z_ref[e:, s:e], upper_ref[k])
-        z_ref[e:, s:e] = multipliers
-        mh, ml = split2(multipliers)
-        m3 = jnp.concatenate([mh, ml, mh], axis=1)
-        lh, ll = split2(lower_ref[k])
-        l3 = jnp.concatenate([lh, ll, lh], axis=1)
-
-        @pl.loop(0, (TOP + COLS - e) // NB)
-        def _(c):
-            cols = pl.ds(pl.multiple_of(c * NB + e, NB), NB)
-            bh, bl = split2(z_ref[s:e, cols])
-            upper_rows = mm(l3, jnp.concatenate([bh, bh, bl], axis=0))
-            z_ref[s:e, cols] = upper_rows
-            uh, ul = split2(upper_rows)
-            z_ref[e:, cols] = z_ref[e:, cols] - mm(m3, jnp.concatenate([uh, uh, ul], axis=0))
-
-    out_ref[...] = z_ref[TOP:, TOP:]
-    panel_cols = pl.ds(pl.multiple_of(kind * NB, NB), NB)
-    top_rows = pl.ds(pl.multiple_of((prow & 3) * NB, NB), NB)
-
-    @pl.when(pcol < PANELS)
-    def _():
-        out_ref[:, :NB] = z_ref[TOP:, panel_cols]
-
-    @pl.when(prow < PANELS)
-    def _():
-        out_ref[:NB, :] = z_ref[top_rows, TOP:]
-
-    @pl.when((prow < PANELS) & (pcol < PANELS))
-    def _():
-        out_ref[:NB, :NB] = z_ref[top_rows, panel_cols]
-
-
 def exchange_first(picked, top):
     sent = jnp.concatenate([picked.reshape(PROW, 16, NB), top.reshape(PROW, 4, NB)], axis=1)
     got = lax.all_to_all(sent, "prow", 0, 0)
@@ -179,9 +116,17 @@
     return got.reshape(PROW * 32, REST)
 
 
-def spread_columns(own, pcol):
+def spread_start(own):
     up = lax.ppermute(own, "pcol", [(q, q + 4) for q in range(4)])
     down = lax.ppermute(own, "pcol", [(q, q + 12) for q in range(4)])
+    return up, down
+
+
+def spread_columns(own, pcol):
+    return spread_rest(own, *spread_start(own), pcol)
+
+
+def spread_rest(own, up, down, pcol):
     near = jnp.where(pcol < 4, own, jnp.where(pcol < 8, up, down))
     half = near.shape[0] // 2
     left = lax.ppermute(near[:half], "pcol", [(q + 4, q + 8) for q in range(4)])
@@ -194,7 +139,326 @@
     return near, across, pair
 
 
-def per_device(matrix, pivots, lower_inverse, upper_inverse):
+def lane_sum(mask, value):
+    return jnp.sum(jnp.where(mask, value, 0.0), axis=1, keepdims=True)
+
+
+def sub_sum(mask, value):
+    return jnp.sum(jnp.where(mask, value, 0.0), axis=0, keepdims=True).astype(jnp.int32)
+
+
+def iota(shape, axis):
+    return lax.broadcasted_iota(jnp.int32, shape, axis)
+
+
+def ranks(masks):
+    count = len(masks)
+    padded = -(-count // 8) * 8
+    rows = [jnp.where(mask, 1.0, 0.0) for mask in masks]
+    rows = rows + [jnp.zeros((1, NB), F32)] * (padded - count)
+    before = jnp.where(iota((NB, NB), 0) < iota((NB, NB), 1), 1.0, 0.0).astype(BF)
+    found = mm(jnp.concatenate(rows, axis=0).astype(BF), before)
+    return [found[n : n + 1, :] for n in range(count)]
+
+
+def slots(mask, rank, value, capacity):
+    row = iota((capacity, NB), 0).astype(F32)
+    return lane_sum(mask & (rank == row), value + 1.0).astype(jnp.int32) - 1
+
+
+def onehot_of(column, width):
+    return jnp.where(iota((column.shape[0], width), 1) == column, 1.0, 0.0).astype(BF)
+
+
+def plan_kernel(pivots_ref, a_ref, send_ref, plan_ref, over_ref, source_ref, target_ref):
+    prow = lax.axis_index("prow")
+    x = prow >> 3
+    z = prow & 7
+    sub = iota((NB, NB), 0)
+    lane = iota((NB, NB), 1)
+    subf = sub.astype(F32)
+    lane_row = iota((1, NB), 1)
+    piv_row = [pivots_ref[m : m + 1, :] for m in range(PANELS)]
+    piv_col = []
+    for m in range(PANELS):
+        piv_col.append(lane_sum(sub == lane, piv_row[m].astype(F32)).astype(jnp.int32))
+
+    def met(m, rows):
+        return sub_sum(piv_col[m] == rows, subf + float(m * NB + 1))
+
+    source = []
+    target = []
+    for k in range(PANELS):
+        rows = piv_row[k]
+        for m in range(k - 1, -1, -1):
+            hit = met(m, rows)
+            rows = jnp.where(hit > 0, hit - 1, rows)
+        source.append(rows)
+        source_ref[k : k + 1, :] = rows
+        rows = lane_row + k * NB
+        for m in range(PANELS):
+            if m == k:
+                rows = jnp.where(rows == lane_row + k * NB, piv_row[k], rows)
+                continue
+            hit = met(m, rows)
+            moved = jnp.where(hit > 0, hit - 1, rows)
+            if m > k:
+                look = sub_sum(sub + m * NB == rows, piv_col[m].astype(F32))
+                moved = jnp.where(look > 0, look, moved)
+            rows = moved
+        target.append(rows)
+        target_ref[k : k + 1, :] = rows
+
+    def local_of(rows):
+        return ((rows >> 12) << 7) | (rows & 127)
+
+    def owner_of(rows):
+        return (rows >> 7) & 31
+
+    masks = [owner_of(source[k]) == prow for k in range(PANELS)]
+    order = ranks(masks)
+    pieces = [
+        slots(masks[k], order[k], local_of(source[k]).astype(F32), 16) for k in range(PANELS)
+    ]
+    mine = target_ref[pl.ds(prow & 3, 1), :]
+    leaves = (mine >= TOP) & (prow < PANELS)
+    masks = [leaves & (((mine >> 10) & 3) == n) for n in range(4)]
+    order = ranks(masks)
+    lanef = lane_row.astype(F32)
+    chosen = []
+    for n in range(4):
+        chosen.append(pieces[n])
+        chosen.append(slots(masks[n], order[n], lanef, 48))
+    send_ref[...] = select_rows(onehot_of(jnp.concatenate(chosen, axis=0), ROWS), a_ref[...])
+
+    panel = source_ref[pl.ds(x, 1), :]
+    panel_z = (panel >> 7) & 7
+    panel_x = (panel >> 10) & 3
+    here = panel_z == z
+    masks = [here & (panel_x == n) for n in range(4)] + [here]
+    order = ranks(masks)
+    spot = jnp.zeros((1, NB), F32)
+    for n in range(4):
+        spot = spot + jnp.where(masks[n], order[n] + 64.0 * n, 0.0)
+    wide = lambda column: jnp.broadcast_to(column, (column.shape[0], NB))
+    plan_ref[0:32, :] = wide(slots(here, order[4], spot, 32))
+    other = target_ref[pl.ds(z & 3, 1), :]
+    along = (other >= TOP) & (z < PANELS) & (((other >> 10) & 3) == x)
+    masks = [along & (((other >> 7) & 7) == n) for n in range(8)] + [along]
+    order = ranks(masks)
+    for n in range(8):
+        plan_ref[32 + 16 * n : 48 + 16 * n, :] = wide(slots(masks[n], order[n], order[8], 16))
+    zf = panel_z.astype(F32)
+    zcol = lane_sum(sub == lane, zf)
+    ahead = lane_sum((zf == zcol) & (lane < sub), 1.0)
+    plan_ref[160:288, :] = wide((zcol * 32.0 + ahead).astype(jnp.int32))
+    masks = [(target[k] >= TOP) & (owner_of(target[k]) == prow) for k in range(PANELS)]
+    order = ranks(masks)
+    row = iota((ROWS, NB), 0)
+    total = jnp.zeros((ROWS, 1), F32)
+    for k in range(PANELS):
+        total = total + lane_sum(masks[k] & (local_of(target[k]) == row), order[k] + (16.0 * k + 1.0))
+    plan_ref[288:544, :] = wide(total.astype(jnp.int32) - 1)
+    unit = iota((PROW, NB), 0)
+    over = jnp.zeros((PROW, 1), F32)
+    for k in range(PANELS):
+        leaves = target[k] >= TOP
+        for mask, cap in (
+            (owner_of(source[k]) == unit, 16.0),
+            (((source[k] >> 7) & 7) == unit, 32.0),
+            (leaves & (((target[k] >> 10) & 3) == unit), 48.0),
+            (leaves & (owner_of(target[k]) == unit), 16.0),
+        ):
+            over = jnp.maximum(over, lane_sum(mask, 1.0) - cap)
+    over = jnp.max(over, axis=0, keepdims=True)
+    over_ref[...] = jnp.broadcast_to(over, (8, NB)).astype(jnp.int32)
+
+
+def turn_kernel(plan_ref, got_ref, send_ref):
+    got = got_ref[...].reshape(256, COLS)
+    rows = select_rows(onehot_of(plan_ref[0:32, :1], 256), got)
+    moved = plan_ref[32:160, :1]
+    moved = jnp.where(moved < 0, -1, moved + 16)
+    sent = select_rows(onehot_of(moved, 64), got[:64])
+    for n in range(8):
+        send_ref[n, 0:32, :] = rows
+        send_ref[n, 32:48, :] = sent[n * 16 : n * 16 + 16]
+
+
+def panel_kernel(plan_ref, got_ref, send_ref, lead_ref):
+    got = jnp.concatenate([got_ref[n, 0:32, :] for n in range(8)], axis=0)
+    rows = select_rows(onehot_of(plan_ref[160:288, :1], 256), got)
+    for n in range(4):
+        send_ref[n] = rows
+        lead_ref[NB + n * 16 : NB + n * 16 + 16, :] = got_ref[n, 32:48, :NB]
+    lead_ref[0:NB, :] = rows[:, :NB]
+
+
+def put_columns(near_ref, across_ref, pair_ref, rows, store):
+    kind = lax.axis_index("pcol") & 3
+    store(kind, near_ref[rows, :])
+    store(kind ^ 2, across_ref[rows, :])
+    store(kind ^ 1, pair_ref[rows, :NB])
+    store(kind ^ 3, pair_ref[rows, NB:])
+
+
+def lane_block(index):
+    return pl.ds(pl.multiple_of(index * NB, NB), NB)
+
+
+def corner_kernel(near_ref, across_ref, pair_ref, send_ref, moved_ref):
+    def store_send(index, value):
+        for n in range(4):
+            send_ref[n, :, lane_block(index)] = value
+
+    def store_moved(index, value):
+        moved_ref[:, lane_block(index)] = value
+
+    put_columns(near_ref, across_ref, pair_ref, slice(0, NB), store_send)
+    put_columns(near_ref, across_ref, pair_ref, slice(NB, NB + 64), store_moved)
+
+
+def rows_kernel(plan_ref, got_ref, moved_ref, a_ref, near_ref, across_ref, pair_ref, out_ref):
+    slot = plan_ref[288:544, :1]
+    onehot = onehot_of(slot, 64)
+
+    def store(index, value):
+        out_ref[:, lane_block(index)] = value
+
+    put_columns(near_ref, across_ref, pair_ref, slice(0, ROWS), store)
+    out_ref[:, TOP:] = a_ref[...]
+    moved = jnp.concatenate([got_ref[n, 32:48, :] for n in range(4)], axis=0)
+    moved = jnp.concatenate([moved_ref[...], moved], axis=1)
+    out_ref[...] = jnp.where(slot >= 0, select_rows(onehot, moved), out_ref[...])
+
+
+def factor_kernel(corner_ref, own_ref, rows_ref, lower_ref, upper_ref, out_ref, z_ref, y_ref, m_ref, u_ref):
+    prow = lax.axis_index("prow")
+    pcol = lax.axis_index("pcol")
+    z_ref[:TOP, :] = corner_ref[...]
+    z_ref[TOP:, :] = rows_ref[:, :TOP]
+    for k in range(PANELS):
+        s = k * NB
+        e = s + NB
+        before = own_ref if k == 0 else y_ref
+        multipliers = dot3(z_ref[e:, s:e], upper_ref[k])
+        z_ref[e:, s:e] = multipliers
+        mh, ml = split2(multipliers)
+        m3 = jnp.concatenate([mh, ml, mh], axis=1)
+        m_ref[:, 3 * s : 3 * e] = m3[TOP - e :]
+        lh, ll = split2(lower_ref[k])
+        l3 = jnp.concatenate([lh, ll, lh], axis=1)
+        if e < TOP:
+            bh, bl = split2(z_ref[s:e, e:])
+            corner = mm(l3, jnp.concatenate([bh, bh, bl], axis=0))
+            z_ref[s:e, e:] = corner
+            uh, ul = split2(corner)
+            z_ref[e:, e:] = z_ref[e:, e:] - mm(m3, jnp.concatenate([uh, uh, ul], axis=0))
+        bh, bl = split2(before[s:e, :])
+        upper_rows = mm(l3, jnp.concatenate([bh, bh, bl], axis=0))
+        y_ref[s:e, :] = upper_rows
+        uh, ul = split2(upper_rows)
+        u3 = jnp.concatenate([uh, uh, ul], axis=0)
+        u_ref[3 * s : 3 * e, :] = u3
+        if e < TOP:
+            y_ref[e:TOP, :] = before[e:TOP, :] - mm(m3[: TOP - e], u3)
+    out_ref[...] = rows_ref[:, TOP:] - mm(m_ref[...], u_ref[...])
+    panel_cols = lane_block(pcol & 3)
+    top_rows = pl.ds(pl.multiple_of((prow & 3) * NB, NB), NB)
+
+    @pl.when(pcol < PANELS)
+    def _():
+        out_ref[:, :NB] = z_ref[TOP:, panel_cols]
+
+    @pl.when(prow < PANELS)
+    def _():
+        out_ref[:NB, :] = y_ref[top_rows, :]
+
+    @pl.when((prow < PANELS) & (pcol < PANELS))
+    def _():
+        out_ref[:NB, :NB] = z_ref[top_rows, panel_cols]
+
+
+def kernel_call(body, shapes, scratch=()):
+    def call(*args):
+        return pl.pallas_call(
+            body,
+            in_specs=[VMEM] * len(args),
+            out_specs=[VMEM] * len(shapes),
+            out_shape=[jax.ShapeDtypeStruct(shape, kind) for shape, kind in shapes],
+            scratch_shapes=list(scratch),
+        )(*args)
+
+    return call
+
+
+def factor(corner, own, rows, lower_inverse, upper_inverse):
+    return pl.pallas_call(
+        factor_kernel,
+        in_specs=[VMEM] * 5,
+        out_specs=VMEM,
+        out_shape=jax.ShapeDtypeStruct((ROWS, COLS), F32),
+        scratch_shapes=[
+            pltpu.VMEM((TOP + ROWS, TOP), F32),
+            pltpu.VMEM((TOP, COLS), F32),
+            pltpu.VMEM((ROWS, 3 * TOP), BF),
+            pltpu.VMEM((3 * TOP, COLS), BF),
+        ],
+    )(corner, own, rows, lower_inverse, upper_inverse)
+
+
+def along(value, groups):
+    return lax.all_to_all(value, "prow", 0, 0, axis_index_groups=groups)
+
+
+def slotted(send, plan, matrix, lower_inverse, upper_inverse):
+    pcol = lax.axis_index("pcol")
+    block = matrix[:, :NB]
+    ends = spread_start(block)
+    got = along(send.reshape(4, 64, COLS), X_GROUPS)
+    got, ends = lax.optimization_barrier((got, ends))
+    (send,) = kernel_call(turn_kernel, [((8, 48, COLS), F32)])(plan, got)
+    raw = spread_rest(block, *ends, pcol)
+    got = along(send, Z_GROUPS)
+    got, raw = lax.optimization_barrier((got, raw))
+    send, lead = kernel_call(panel_kernel, [((4, NB, COLS), F32), ((NB + 64, NB), F32)])(plan, got)
+    own = along(send, X_GROUPS).reshape(TOP, COLS)
+    near, across, pair = spread_columns(lead, pcol)
+    send, moved = kernel_call(corner_kernel, [((4, NB, TOP), F32), ((64, TOP), F32)])(
+        near, across, pair
+    )
+    corner = along(send, X_GROUPS).reshape(TOP, TOP)
+    (rows,) = kernel_call(rows_kernel, [((ROWS, TOP + COLS), F32)])(
+        plan, got, moved, matrix, *raw
+    )
+    return factor(corner, own, rows, lower_inverse, upper_inverse)
+
+
+def dense_rows_kernel(
+    origin_ref, gathered_ref, a_ref, own_ref, near_ref, across_ref, pair_ref, corner_ref, top_ref, out_ref
+):
+    def store_corner(index, value):
+        corner_ref[:, lane_block(index)] = value
+
+    def store_rows(index, value):
+        out_ref[:, lane_block(index)] = value
+
+    put_columns(near_ref, across_ref, pair_ref, slice(0, TOP), store_corner)
+    put_columns(near_ref, across_ref, pair_ref, slice(TOP, TOP + ROWS), store_rows)
+    top_ref[:, :NB] = own_ref[:TOP, :]
+    out_ref[:, TOP : TOP + NB] = own_ref[TOP:, :]
+    for unit in range(PROW):
+        top_ref[unit * 16 : unit * 16 + 16, NB:] = gathered_ref[unit * 32 : unit * 32 + 16, :]
+    origin = origin_ref[:, :1]
+
+    @pl.loop(0, REST // NB)
+    def _(c):
+        out_ref[:, lane_block(c + PANELS + 1)] = moved_rows(
+            origin, gathered_ref[:, lane_block(c)], a_ref[:, lane_block(c + 1)]
+        )
+
+
+def dense(pivots, matrix, lower_inverse, upper_inverse):
     prow = lax.axis_index("prow")
     pcol = lax.axis_index("pcol")
     place = jnp.stack([prow, pcol]).astype(jnp.int32)
@@ -209,21 +473,27 @@
         ],
     )(place, pivots.reshape(PANELS, NB), pivots.reshape(TOP, 1), matrix)
     gathered_first = exchange_first(picked_first, matrix[:NB, :NB])
-    own = pl.pallas_call(
-        column_kernel,
-        in_specs=[VMEM] * 3,
-        out_specs=VMEM,
-        out_shape=jax.ShapeDtypeStruct((TOP + ROWS, NB), F32),
-    )(origin, gathered_first, matrix)
+    (own,) = kernel_call(column_kernel, [((TOP + ROWS, NB), F32)])(origin, gathered_first, matrix)
     near, across, pair = spread_columns(own, pcol)
     gathered_rest = exchange_rest(picked_rest, matrix[:NB, NB:])
-    return pl.pallas_call(
-        factor_kernel,
-        in_specs=[SMEM] + [VMEM] * 9,
-        out_specs=VMEM,
-        out_shape=jax.ShapeDtypeStruct((ROWS, COLS), F32),
-        scratch_shapes=[pltpu.VMEM((TOP + ROWS, TOP + COLS), F32)],
-    )(place, origin, gathered_rest, matrix, own, near, across, pair, lower_inverse, upper_inverse)
+    corner, top, rows = kernel_call(
+        dense_rows_kernel,
+        [((TOP, TOP), F32), ((TOP, COLS), F32), ((ROWS, TOP + COLS), F32)],
+    )(origin, gathered_rest, matrix, own, near, across, pair)
+    return factor(corner, top, rows, lower_inverse, upper_inverse)
+
+
+def per_device(matrix, pivots, lower_inverse, upper_inverse):
+    send, plan, over = kernel_call(
+        plan_kernel,
+        [((256, COLS), F32), ((544, NB), jnp.int32), ((8, NB), jnp.int32)],
+        [pltpu.VMEM((8, NB), jnp.int32), pltpu.VMEM((8, NB), jnp.int32)],
+    )(pivots.reshape(PANELS, NB), matrix)
+    return lax.cond(
+        over[0, 0] <= 0,
+        lambda: slotted(send, plan, matrix, lower_inverse, upper_inverse),
+        lambda: dense(pivots, matrix, lower_inverse, upper_inverse),
+    )
 
 
 def solution(mesh):

time: 190 us -> 129 us (0.68)
  waiting for transfers between devices: 89.5 us -> 47.1 us
  other arithmetic: 7.17 us -> 0.1 us
  Pallas kernels: 27.5 us -> 20.5 us
  local copies, waits for them, and re-layouts: 8.4 us -> 5.68 us
  starting transfers between devices: 55.9 us -> 53.5 us
    all_to_all x6 -> x4, waiting for transfers between devices: 60 us -> 33.5 us  [along(): return lax.all_to_all(value, 'prow', 0, 0, axis_index_groups=groups)]
    all_to_all x6 -> x4, starting transfers between devices: 41.4 us -> 22.9 us  [along(): return lax.all_to_all(value, 'prow', 0, 0, axis_index_groups=groups)]
    ppermute x6 -> x12, starting transfers between devices: 14.6 us -> 30.7 us  [the longest x2 12.1 us: spread_start(): down = lax.ppermute(own, 'pcol', [(q, q + 12) for q in range(4)])]
    ppermute x6 -> x12, waiting for transfers between devices: 29.5 us -> 13.6 us  [the longest x2 6.8 us: spread_rest(): across = lax.ppermute(near, 'pcol', [(q, q ^ 2) for q in range(PCOL)])]
    pallas_call x3 -> x6, Pallas kernels: 27.5 us -> 20.5 us  [the longest x5 14.5 us: call(): pl.pallas_call(body, in_specs=[VMEM] * len(args), out_specs=[VMEM] * len(...]
    concatenate x6 -> x2, other arithmetic: 4.29 us -> 0.03 us  [spread_rest(): both = jnp.concatenate([near, across], axis=1)]
    cond x0 -> x26, local copies, waits for them, and re-layouts: none -> 3.59 us
    broadcast_in_dim x3 -> x0, local copies, waits for them, and re-layouts: 3.44 us -> none  [the longest x1 1.66 us: exchange_rest(): jnp.broadcast_to(got[None], (4, 256, REST))]
  transfers between devices with their start and end apart: 12 -> 16, of which waited for: 9 -> 8; matrix products, arithmetic and copies ran while one was open for 3% -> 0% of each run, Pallas kernels for 1% -> 4%
where the time goes in v2:
time: 129 us; the launch traced here: 128 us
  starting transfers between devices  53.5 us (41%)
  waiting for transfers between devices  47.1 us (37%)
  Pallas kernels  20.5 us (16%)
  local copies, waits for them, and re-layouts  5.68 us (4%)
    all_to_all x4, waiting for transfers between devices, along(): return lax.all_to_all(value, 'prow', 0, 0, axis_index_groups=groups)  33.5 us
    all_to_all x4, starting transfers between devices, along(): return lax.all_to_all(value, 'prow', 0, 0, axis_index_groups=groups)  22.9 us
    pallas_call x5, Pallas kernels, call(): pl.pallas_call(body, in_specs=[VMEM] * len(args), out_specs=[VMEM] * len(...  14.5 us
    ppermute x2, starting transfers between devices, spread_start(): down = lax.ppermute(own, 'pcol', [(q, q + 12) for q in range(4)])  12.1 us
    ppermute x2, starting transfers between devices, spread_rest(): pair = lax.ppermute(both, 'pcol', [(q, q ^ 1) for q in range(PCOL)])  8.29 us
    ppermute x2, waiting for transfers between devices, spread_rest(): across = lax.ppermute(near, 'pcol', [(q, q ^ 2) for q in range(PCOL)])  6.8 us
    pallas_call x1, Pallas kernels, factor(): pl.pallas_call(factor_kernel, in_specs=[VMEM] * 5, out_specs=VMEM, out_sh...  6.08 us
    ppermute x2, starting transfers between devices, spread_rest(): across = lax.ppermute(near, 'pcol', [(q, q ^ 2) for q in range(PCOL)])  4.85 us
  transfers between devices with their start and end apart: 16, of which 8 were waited for; matrix products, arithmetic and copies ran while one was open for 0% of the time, Pallas kernels for 4%

profile of v2, /device:TPU:1, one launch (start us, length us, event | category | flops | bytes accessed | tf_op | source)
XLA Modules:
  0.0 128.0 jit_solution(7705299579762687608)
XLA Ops:
  0.0 3.3 %shard_map.48 = (f32[256,768]{1,0:T(8,128)}, s32[544,128]{1,0:T(8,128)}, s32[8,128]{1,0:T(8,128)}) custom-call(s32[4,128]{1,0:T(4,128)} %bitcast.30, f32[256,768]{1,0:T(8,128)} %a_ref.1), custom_call_target="tpu_custom_call" | custom-call | tf_op jit(solution)/shard_map/pallas_call | solution.py:384
  5.1 122.1 %conditional.1 = (f32[256,768]{1,0:T(8,128)S(1)}) conditional(s32[]{:T(128)} %bitcast.17, (s32[512]{0:T(512)}, f32[256,768]{1,0:T(8,128)}, f32[4,128,128]{2,1,0:T(8,128)}, f32[4,128,128]{2,1,0:T(8,128)}) %tuple.13, (f32[256,768]{1,0:T(8,128)}, f32[256,768]{1,0:T(8,128)}, s32[544,128]{1,0:T(8,128)}, f32[4,128,128]{2,1,0:T(8,128)}, ...), branch_computations={%region_0.4_spmd, %region_4.5_spmd} | conditional | flops 1589260 | bytes 66376396 | solution.py:492
  5.1 5.0 %all-to-all-start.6 = ((f32[4,64,768]{2,1,0:T(8,128)}), f32[4,64,768]{2,1,0:T(8,128)S(1)}, u32[]{:S(2)}, u32[]{:S(2)}) async-start(f32[4,64,768]{2,1,0:T(8,128)} %bitcast.26), calls=%async_computation.6 | async-start | bytes 1572864 | tf_op jit(solution)/shard_map/cond/branch_1_fun/all_to_all | solution.py:411
  10.1 5.9 %collective-permute-start.7 = (f32[256,128]{1,0:T(8,128)S(1)}, f32[256,128]{1,0:T(8,128)S(1)}, u32[]{:S(2)}, u32[]{:S(2)}) collective-permute-start(f32[256,128]{1,0:T(8,128)S(1)} %slice.42), channel_id=1, source_target_pairs={{0,12},{1,13},{2,14},{3,15},{16,28},{17,29},{18,30},{19,31},{32,44... | collective-permute-start | bytes 393224 | tf_op jit(solution)/shard_map/cond/branch_1_fun/ppermute | solution.py:121
  16.0 1.3 %collective-permute-start.6 = (f32[256,128]{1,0:T(8,128)S(1)}, f32[256,128]{1,0:T(8,128)S(1)}, u32[]{:S(2)}, u32[]{:S(2)}) collective-permute-start(f32[256,128]{1,0:T(8,128)S(1)} %slice.42), channel_id=1, source_target_pairs={{0,4},{1,5},{2,6},{3,7},{16,20},{17,21},{18,22},{19,23},{32,36},{3... | collective-permute-start | bytes 393224 | tf_op jit(solution)/shard_map/cond/branch_1_fun/ppermute | solution.py:120
  17.3 4.6 %collective-permute-done.7 = f32[256,128]{1,0:T(8,128)S(1)} collective-permute-done((f32[256,128]{1,0:T(8,128)S(1)}, f32[256,128]{1,0:T(8,128)S(1)}, u32[]{:S(2)}, u32[]{:S(2)}) %collective-permute-start.7) | collective-permute-done | bytes 131104 | tf_op jit(solution)/shard_map/cond/branch_1_fun/ppermute | solution.py:121
  22.8 2.7 %branch_1_fun.5 = f32[8,48,768]{2,1,0:T(8,128)} custom-call(s32[544,128]{1,0:T(8,128)S(1)} %copy-done.8, f32[4,64,768]{2,1,0:T(8,128)} %copy-done.7), custom_call_target="tpu_custom_call" | custom-call | tf_op jit(solution)/shard_map/cond/branch_1_fun/pallas_call | solution.py:384
  25.5 10.0 %all-to-all-start.7 = ((f32[8,48,768]{2,1,0:T(8,128)}), f32[8,48,768]{2,1,0:T(8,128)S(1)}, u32[]{:S(2)}, u32[]{:S(2)}) async-start(f32[8,48,768]{2,1,0:T(8,128)} %branch_1_fun.5), calls=%async_computation.7 | async-start | bytes 2359296 | tf_op jit(solution)/shard_map/cond/branch_1_fun/all_to_all | solution.py:411
  37.2 2.9 %collective-permute-start.10 = (f32[256,128]{1,0:T(8,128)S(1)}, f32[256,128]{1,0:T(8,128)S(1)}, u32[]{:S(2)}, u32[]{:S(2)}) collective-permute-start(f32[256,128]{1,0:T(8,128)S(1)} %maximum_select_fusion.1.near_ref), channel_id=1, source_target_pairs={{0,2},{1,3},{2,0},{3,1},{4,6},{5,7},{6,4},{7,5},{8,10},{9,11},{10,... | collective-permute-start | bytes 393224 | tf_op jit(solution)/shard_map/cond/branch_1_fun/ppermute | solution.py:136
  40.1 3.1 %collective-permute-done.10.across_ref = f32[256,128]{1,0:T(8,128)S(1)} collective-permute-done((f32[256,128]{1,0:T(8,128)S(1)}, f32[256,128]{1,0:T(8,128)S(1)}, u32[]{:S(2)}, u32[]{:S(2)}) %collective-permute-start.10) | collective-permute-done | bytes 131104 | tf_op jit(solution)/shard_map/cond/branch_1_fun/ppermute | solution.py:136
  43.2 4.5 %collective-permute-start.11 = (f32[256,256]{1,0:T(8,128)S(1)}, f32[256,256]{1,0:T(8,128)S(1)}, u32[]{:S(2)}, u32[]{:S(2)}) collective-permute-start(f32[256,256]{1,0:T(8,128)S(1)} %pad_maximum_fusion.6), channel_id=1, source_target_pairs={{0,1},{1,0},{2,3},{3,2},{4,5},{5,4},{6,7},{7,6},{8,9},{9,8},{10,11... | collective-permute-start | bytes 786440 | tf_op jit(solution)/shard_map/cond/branch_1_fun/ppermute | solution.py:138
  48.8 18.7 %all-to-all-done.7.got_ref = f32[8,48,768]{2,1,0:T(8,128)S(1)} async-done(((f32[8,48,768]{2,1,0:T(8,128)}), f32[8,48,768]{2,1,0:T(8,128)S(1)}, u32[]{:S(2)}, u32[]{:S(2)}) %all-to-all-start.7) | async-done | bytes 1179680 | tf_op jit(solution)/shard_map/cond/branch_1_fun/all_to_all | solution.py:411
  68.6 2.9 %branch_1_fun.6 = (f32[4,128,768]{2,1,0:T(8,128)}, f32[192,128]{1,0:T(8,128)}) custom-call(s32[544,128]{1,0:T(8,128)S(1)} %copy-done.8, f32[8,48,768]{2,1,0:T(8,128)} %copy-done.2), custom_call_target="tpu_custom_call" | custom-call | tf_op jit(solution)/shard_map/cond/branch_1_fun/pallas_call | solution.py:384
  71.4 6.2 %collective-permute-start.13 = (f32[192,128]{1,0:T(8,128)}, f32[192,128]{1,0:T(8,128)S(1)}, u32[]{:S(2)}, u32[]{:S(2)}) collective-permute-start(f32[192,128]{1,0:T(8,128)} %get-tuple-element.43), channel_id=1, source_target_pairs={{0,12},{1,13},{2,14},{3,15},{16,28},{17,29},{18,30},{19,31},{32,44... | collective-permute-start | bytes 294920 | tf_op jit(solution)/shard_map/cond/branch_1_fun/ppermute | solution.py:121
  79.0 4.3 %all-to-all-start.9 = ((f32[4,128,768]{2,1,0:T(8,128)}), f32[4,128,768]{2,1,0:T(8,128)S(1)}, u32[]{:S(2)}, u32[]{:S(2)}) async-start(f32[4,128,768]{2,1,0:T(8,128)} %get-tuple-element.45), calls=%async_computation.9 | async-start | bytes 3145728 | tf_op jit(solution)/shard_map/cond/branch_1_fun/all_to_all | solution.py:411
  84.8 1.9 %collective-permute-start.16 = (f32[192,128]{1,0:T(8,128)S(1)}, f32[192,128]{1,0:T(8,128)S(1)}, u32[]{:S(2)}, u32[]{:S(2)}) collective-permute-start(f32[192,128]{1,0:T(8,128)S(1)} %maximum_select_fusion.2.near_ref), channel_id=1, source_target_pairs={{0,2},{1,3},{2,0},{3,1},{4,6},{5,7},{6,4},{7,5},{8,10},{9,11},{10,... | collective-permute-start | bytes 294920 | tf_op jit(solution)/shard_map/cond/branch_1_fun/ppermute | solution.py:136
  86.7 3.7 %collective-permute-done.16.across_ref = f32[192,128]{1,0:T(8,128)S(1)} collective-permute-done((f32[192,128]{1,0:T(8,128)S(1)}, f32[192,128]{1,0:T(8,128)S(1)}, u32[]{:S(2)}, u32[]{:S(2)}) %collective-permute-start.16) | collective-permute-done | bytes 98336 | tf_op jit(solution)/shard_map/cond/branch_1_fun/ppermute | solution.py:136
  90.5 3.8 %collective-permute-start.17 = (f32[192,256]{1,0:T(8,128)S(1)}, f32[192,256]{1,0:T(8,128)S(1)}, u32[]{:S(2)}, u32[]{:S(2)}) collective-permute-start(f32[192,256]{1,0:T(8,128)S(1)} %pad_maximum_fusion.7), channel_id=1, source_target_pairs={{0,1},{1,0},{2,3},{3,2},{4,5},{5,4},{6,7},{7,6},{8,9},{9,8},{10,11... | collective-permute-start | bytes 589832 | tf_op jit(solution)/shard_map/cond/branch_1_fun/ppermute | solution.py:138
  96.0 2.2 %branch_1_fun.7 = (f32[4,128,512]{2,1,0:T(8,128)}, f32[64,512]{1,0:T(8,128)}) custom-call(f32[192,128]{1,0:T(8,128)} %copy-done.12, f32[192,128]{1,0:T(8,128)} %copy-done.15, f32[192,256]{1,0:T(8,128)} %copy-done.18), custom_call_target="tpu_custom_call" | custom-call | tf_op jit(solution)/shard_map/cond/branch_1_fun/pallas_call | solution.py:384
  98.2 4.8 %all-to-all-done.9 = f32[4,128,768]{2,1,0:T(8,128)S(1)} async-done(((f32[4,128,768]{2,1,0:T(8,128)}), f32[4,128,768]{2,1,0:T(8,128)S(1)}, u32[]{:S(2)}, u32[]{:S(2)}) %all-to-all-start.9) | async-done | bytes 1572896 | tf_op jit(solution)/shard_map/cond/branch_1_fun/all_to_all | solution.py:411
  103.1 3.5 %all-to-all-start.8 = ((f32[4,128,512]{2,1,0:T(8,128)}), f32[4,128,512]{2,1,0:T(8,128)S(1)}, u32[]{:S(2)}, u32[]{:S(2)}) async-start(f32[4,128,512]{2,1,0:T(8,128)} %get-tuple-element.44), calls=%async_computation.8 | async-start | bytes 2097152 | tf_op jit(solution)/shard_map/cond/branch_1_fun/all_to_all | solution.py:411
  106.6 3.3 %branch_1_fun.8.rows_ref = f32[256,1280]{1,0:T(8,128)} custom-call(s32[544,128]{1,0:T(8,128)} %get-tuple-element.36.plan_ref, f32[8,48,768]{2,1,0:T(8,128)} %copy-done.2, f32[64,512]{1,0:T(8,128)} %get-tuple-element.46.moved_ref, f32[256,768]{1,0:T(8,128)S(1)} %copy-done.1, f32[256,128]{1,0:T(8,128)} %copy-done.11, f32[256,128]{1,0:T(8,128)} %copy-done.14, ...), custom_call_target="tpu_custom_call" | custom-call | tf_op jit(solution)/shard_map/cond/branch_1_fun/pallas_call | solution.py:384
  109.9 9.9 %all-to-all-done.8 = f32[4,128,512]{2,1,0:T(8,128)S(1)} async-done(((f32[4,128,512]{2,1,0:T(8,128)}), f32[4,128,512]{2,1,0:T(8,128)S(1)}, u32[]{:S(2)}, u32[]{:S(2)}) %all-to-all-start.8) | async-done | bytes 1048608 | tf_op jit(solution)/shard_map/cond/branch_1_fun/all_to_all | solution.py:411
  120.8 6.1 %branch_1_fun.9 = f32[256,768]{1,0:T(8,128)S(1)} custom-call(f32[512,512]{1,0:T(8,128)} %bitcast.20, f32[512,768]{1,0:T(8,128)} %bitcast.19, f32[256,1280]{1,0:T(8,128)} %branch_1_fun.8.rows_ref, f32[4,128,128]{2,1,0:T(8,128)} %get-tuple-element.50.lower_ref, f32[4,128,128]{2,1,0:T(8,128)} %get-tuple-element.51.upper_ref), custom_call_target="tpu_custom_call" | custom-call | tf_op jit(solution)/shard_map/cond/branch_1_fun/pallas_call | solution.py:396
  (53 shorter events, 12.1 us)
Async XLA Ops:
  5.1 5.0 %copy-start.1 = (f32[256,768]{1,0:T(8,128)S(1)}, f32[256,768]{1,0:T(8,128)}, u32[]{:S(2)}) copy-start(f32[256,768]{1,0:T(8,128)} %get-tuple-element.38.a_ref) | copy-start | bytes 2359300 | tf_op jit(solution)/shard_map/cond
  5.1 17.7 %copy-start.8 = (s32[544,128]{1,0:T(8,128)S(1)}, s32[544,128]{1,0:T(8,128)}, u32[]{:S(2)}) copy-start(s32[544,128]{1,0:T(8,128)} %get-tuple-element.36.plan_ref) | copy-start | bytes 835588 | tf_op jit(solution)/shard_map/cond
  5.1 16.8 %all-to-all-start.6 = ((f32[4,64,768]{2,1,0:T(8,128)}), f32[4,64,768]{2,1,0:T(8,128)S(1)}, u32[]{:S(2)}, u32[]{:S(2)}) async-start(f32[4,64,768]{2,1,0:T(8,128)} %bitcast.26), calls=%async_computation.6 | async-start | bytes 1572864 | tf_op jit(solution)/shard_map/cond/branch_1_fun/all_to_all | solution.py:411
  10.1 11.8 %collective-permute-start.7 = (f32[256,128]{1,0:T(8,128)S(1)}, f32[256,128]{1,0:T(8,128)S(1)}, u32[]{:S(2)}, u32[]{:S(2)}) collective-permute-start(f32[256,128]{1,0:T(8,128)S(1)} %slice.42), channel_id=1, source_target_pairs={{0,12},{1,13},{2,14},{3,15},{16,28},{17,29},{18,30},{19,31},{32,44... | collective-permute-start | bytes 393224 | tf_op jit(solution)/shard_map/cond/branch_1_fun/ppermute | solution.py:121
  16.0 5.9 %collective-permute-start.6 = (f32[256,128]{1,0:T(8,128)S(1)}, f32[256,128]{1,0:T(8,128)S(1)}, u32[]{:S(2)}, u32[]{:S(2)}) collective-permute-start(f32[256,128]{1,0:T(8,128)S(1)} %slice.42), channel_id=1, source_target_pairs={{0,4},{1,5},{2,6},{3,7},{16,20},{17,21},{18,22},{19,23},{32,36},{3... | collective-permute-start | bytes 393224 | tf_op jit(solution)/shard_map/cond/branch_1_fun/ppermute | solution.py:120
  25.5 42.0 %all-to-all-start.7 = ((f32[8,48,768]{2,1,0:T(8,128)}), f32[8,48,768]{2,1,0:T(8,128)S(1)}, u32[]{:S(2)}, u32[]{:S(2)}) async-start(f32[8,48,768]{2,1,0:T(8,128)} %branch_1_fun.5), calls=%async_computation.7 | async-start | bytes 2359296 | tf_op jit(solution)/shard_map/cond/branch_1_fun/all_to_all | solution.py:411
  35.6 1.5 %collective-permute-start.8 = (f32[128,128]{1,0:T(8,128)S(1)}, f32[128,128]{1,0:T(8,128)S(1)}, u32[]{:S(2)}, u32[]{:S(2)}) collective-permute-start(f32[128,128]{1,0:T(8,128)S(1)} %get-tuple-element.61), channel_id=1, source_target_pairs={{4,8},{5,9},{6,10},{7,11},{20,24},{21,25},{22,26},{23,27},{36,40},... | collective-permute-start | bytes 196616 | tf_op jit(solution)/shard_map/cond/branch_1_fun/ppermute | solution.py:132
  36.2 0.9 collective-permute-start.9
  37.2 41.8 %copy-start.11 = (f32[256,128]{1,0:T(8,128)}, f32[256,128]{1,0:T(8,128)S(1)}, u32[]{:S(2)}) copy-start(f32[256,128]{1,0:T(8,128)S(1)} %maximum_select_fusion.1.near_ref) | copy-start | bytes 393220 | tf_op jit(solution)/shard_map/cond
  37.2 6.0 %collective-permute-start.10 = (f32[256,128]{1,0:T(8,128)S(1)}, f32[256,128]{1,0:T(8,128)S(1)}, u32[]{:S(2)}, u32[]{:S(2)}) collective-permute-start(f32[256,128]{1,0:T(8,128)S(1)} %maximum_select_fusion.1.near_ref), channel_id=1, source_target_pairs={{0,2},{1,3},{2,0},{3,1},{4,6},{5,7},{6,4},{7,5},{8,10},{9,11},{10,... | collective-permute-start | bytes 393224 | tf_op jit(solution)/shard_map/cond/branch_1_fun/ppermute | solution.py:136
  43.2 35.8 %copy-start.14 = (f32[256,128]{1,0:T(8,128)}, f32[256,128]{1,0:T(8,128)S(1)}, u32[]{:S(2)}) copy-start(f32[256,128]{1,0:T(8,128)S(1)} %collective-permute-done.10.across_ref) | copy-start | bytes 393220 | tf_op jit(solution)/shard_map/cond
  43.2 5.6 %collective-permute-start.11 = (f32[256,256]{1,0:T(8,128)S(1)}, f32[256,256]{1,0:T(8,128)S(1)}, u32[]{:S(2)}, u32[]{:S(2)}) collective-permute-start(f32[256,256]{1,0:T(8,128)S(1)} %pad_maximum_fusion.6), channel_id=1, source_target_pairs={{0,1},{1,0},{2,3},{3,2},{4,5},{5,4},{6,7},{7,6},{8,9},{9,8},{10,11... | collective-permute-start | bytes 786440 | tf_op jit(solution)/shard_map/cond/branch_1_fun/ppermute | solution.py:138
  48.8 35.9 %copy-start.16 = (f32[256,256]{1,0:T(8,128)}, f32[256,256]{1,0:T(8,128)S(1)}, u32[]{:S(2)}) copy-start(f32[256,256]{1,0:T(8,128)S(1)} %collective-permute-done.11.pair_ref) | copy-start | bytes 786436 | tf_op jit(solution)/shard_map/cond
  71.4 11.9 %collective-permute-start.13 = (f32[192,128]{1,0:T(8,128)}, f32[192,128]{1,0:T(8,128)S(1)}, u32[]{:S(2)}, u32[]{:S(2)}) collective-permute-start(f32[192,128]{1,0:T(8,128)} %get-tuple-element.43), channel_id=1, source_target_pairs={{0,12},{1,13},{2,14},{3,15},{16,28},{17,29},{18,30},{19,31},{32,44... | collective-permute-start | bytes 294920 | tf_op jit(solution)/shard_map/cond/branch_1_fun/ppermute | solution.py:121
  77.7 5.7 %collective-permute-start.12 = (f32[192,128]{1,0:T(8,128)}, f32[192,128]{1,0:T(8,128)S(1)}, u32[]{:S(2)}, u32[]{:S(2)}) collective-permute-start(f32[192,128]{1,0:T(8,128)} %get-tuple-element.43), channel_id=1, source_target_pairs={{0,4},{1,5},{2,6},{3,7},{16,20},{17,21},{18,22},{19,23},{32,36},{3... | collective-permute-start | bytes 294920 | tf_op jit(solution)/shard_map/cond/branch_1_fun/ppermute | solution.py:120
  79.0 24.1 %all-to-all-start.9 = ((f32[4,128,768]{2,1,0:T(8,128)}), f32[4,128,768]{2,1,0:T(8,128)S(1)}, u32[]{:S(2)}, u32[]{:S(2)}) async-start(f32[4,128,768]{2,1,0:T(8,128)} %get-tuple-element.45), calls=%async_computation.9 | async-start | bytes 3145728 | tf_op jit(solution)/shard_map/cond/branch_1_fun/all_to_all | solution.py:411
  83.4 1.3 %collective-permute-start.14 = (f32[96,128]{1,0:T(8,128)S(1)}, f32[96,128]{1,0:T(8,128)S(1)}, u32[]{:S(2)}, u32[]{:S(2)}) collective-permute-start(f32[96,128]{1,0:T(8,128)S(1)} %get-tuple-element.63), channel_id=1, source_target_pairs={{4,8},{5,9},{6,10},{7,11},{20,24},{21,25},{22,26},{23,27},{36,40},... | collective-permute-start | bytes 147464 | tf_op jit(solution)/shard_map/cond/branch_1_fun/ppermute | solution.py:132
  84.1 0.7 collective-permute-start.15
  84.8 10.6 %copy-start.12 = (f32[192,128]{1,0:T(8,128)}, f32[192,128]{1,0:T(8,128)S(1)}, u32[]{:S(2)}) copy-start(f32[192,128]{1,0:T(8,128)S(1)} %maximum_select_fusion.2.near_ref) | copy-start | bytes 294916 | tf_op jit(solution)/shard_map/cond
  84.8 5.7 %collective-permute-start.16 = (f32[192,128]{1,0:T(8,128)S(1)}, f32[192,128]{1,0:T(8,128)S(1)}, u32[]{:S(2)}, u32[]{:S(2)}) collective-permute-start(f32[192,128]{1,0:T(8,128)S(1)} %maximum_select_fusion.2.near_ref), channel_id=1, source_target_pairs={{0,2},{1,3},{2,0},{3,1},{4,6},{5,7},{6,4},{7,5},{8,10},{9,11},{10,... | collective-permute-start | bytes 294920 | tf_op jit(solution)/shard_map/cond/branch_1_fun/ppermute | solution.py:136
  90.5 4.9 %copy-start.15 = (f32[192,128]{1,0:T(8,128)}, f32[192,128]{1,0:T(8,128)S(1)}, u32[]{:S(2)}) copy-start(f32[192,128]{1,0:T(8,128)S(1)} %collective-permute-done.16.across_ref) | copy-start | bytes 294916 | tf_op jit(solution)/shard_map/cond
  90.5 4.9 %collective-permute-start.17 = (f32[192,256]{1,0:T(8,128)S(1)}, f32[192,256]{1,0:T(8,128)S(1)}, u32[]{:S(2)}, u32[]{:S(2)}) collective-permute-start(f32[192,256]{1,0:T(8,128)S(1)} %pad_maximum_fusion.7), channel_id=1, source_target_pairs={{0,1},{1,0},{2,3},{3,2},{4,5},{5,4},{6,7},{7,6},{8,9},{9,8},{10,11... | collective-permute-start | bytes 589832 | tf_op jit(solution)/shard_map/cond/branch_1_fun/ppermute | solution.py:138
  103.1 6.8 %copy-start.4 = (f32[4,128,768]{2,1,0:T(8,128)}, f32[4,128,768]{2,1,0:T(8,128)S(1)}, u32[]{:S(2)}) copy-start(f32[4,128,768]{2,1,0:T(8,128)S(1)} %all-to-all-done.9) | copy-start | bytes 4718596 | tf_op jit(solution)/shard_map/cond
  103.1 16.8 %all-to-all-start.8 = ((f32[4,128,512]{2,1,0:T(8,128)}), f32[4,128,512]{2,1,0:T(8,128)S(1)}, u32[]{:S(2)}, u32[]{:S(2)}) async-start(f32[4,128,512]{2,1,0:T(8,128)} %get-tuple-element.44), calls=%async_computation.8 | async-start | bytes 2097152 | tf_op jit(solution)/shard_map/cond/branch_1_fun/all_to_all | solution.py:411
  (6 other events, 8.8 us)

commit v3 on v2

--- a/solution.py
+++ b/solution.py
@@ -13,6 +13,9 @@
 ROWS = 256
 COLS = 768
 REST = COLS - NB
+WIDE = TOP + COLS
+KERNEL_VMEM = 20 << 20
+FACTOR_VMEM = 28 << 20
 BF = jnp.bfloat16
 F32 = jnp.float32
 X_GROUPS = [[x * 8 + z for x in range(4)] for z in range(8)]
@@ -217,19 +220,18 @@
 
     masks = [owner_of(source[k]) == prow for k in range(PANELS)]
     order = ranks(masks)
-    pieces = [
+    chosen = [
         slots(masks[k], order[k], local_of(source[k]).astype(F32), 16) for k in range(PANELS)
     ]
+    send_ref[...] = select_rows(onehot_of(jnp.concatenate(chosen, axis=0), ROWS), a_ref[...])
+    wide = lambda column: jnp.broadcast_to(column, (column.shape[0], NB))
     mine = target_ref[pl.ds(prow & 3, 1), :]
     leaves = (mine >= TOP) & (prow < PANELS)
     masks = [leaves & (((mine >> 10) & 3) == n) for n in range(4)]
     order = ranks(masks)
     lanef = lane_row.astype(F32)
-    chosen = []
     for n in range(4):
-        chosen.append(pieces[n])
-        chosen.append(slots(masks[n], order[n], lanef, 48))
-    send_ref[...] = select_rows(onehot_of(jnp.concatenate(chosen, axis=0), ROWS), a_ref[...])
+        plan_ref[544 + 48 * n : 592 + 48 * n, :] = wide(slots(masks[n], order[n], lanef, 48))
 
     panel = source_ref[pl.ds(x, 1), :]
     panel_z = (panel >> 7) & 7
@@ -239,8 +241,7 @@
     order = ranks(masks)
     spot = jnp.zeros((1, NB), F32)
     for n in range(4):
-        spot = spot + jnp.where(masks[n], order[n] + 64.0 * n, 0.0)
-    wide = lambda column: jnp.broadcast_to(column, (column.shape[0], NB))
+        spot = spot + jnp.where(masks[n], order[n] + 16.0 * n, 0.0)
     plan_ref[0:32, :] = wide(slots(here, order[4], spot, 32))
     other = target_ref[pl.ds(z & 3, 1), :]
     along = (other >= TOP) & (z < PANELS) & (((other >> 10) & 3) == x)
@@ -275,23 +276,16 @@
 
 
 def turn_kernel(plan_ref, got_ref, send_ref):
-    got = got_ref[...].reshape(256, COLS)
-    rows = select_rows(onehot_of(plan_ref[0:32, :1], 256), got)
-    moved = plan_ref[32:160, :1]
-    moved = jnp.where(moved < 0, -1, moved + 16)
-    sent = select_rows(onehot_of(moved, 64), got[:64])
+    rows = select_rows(onehot_of(plan_ref[0:32, :1], 64), got_ref[...])
     for n in range(8):
-        send_ref[n, 0:32, :] = rows
-        send_ref[n, 32:48, :] = sent[n * 16 : n * 16 + 16]
+        send_ref[n] = rows
 
 
 def panel_kernel(plan_ref, got_ref, send_ref, lead_ref):
-    got = jnp.concatenate([got_ref[n, 0:32, :] for n in range(8)], axis=0)
-    rows = select_rows(onehot_of(plan_ref[160:288, :1], 256), got)
+    rows = select_rows(onehot_of(plan_ref[160:288, :1], 256), got_ref[...])
     for n in range(4):
         send_ref[n] = rows
-        lead_ref[NB + n * 16 : NB + n * 16 + 16, :] = got_ref[n, 32:48, :NB]
-    lead_ref[0:NB, :] = rows[:, :NB]
+    lead_ref[...] = rows[:, :NB]
 
 
 def put_columns(near_ref, across_ref, pair_ref, rows, store):
@@ -306,19 +300,47 @@
     return pl.ds(pl.multiple_of(index * NB, NB), NB)
 
 
-def corner_kernel(near_ref, across_ref, pair_ref, send_ref, moved_ref):
-    def store_send(index, value):
-        for n in range(4):
-            send_ref[n, :, lane_block(index)] = value
-
-    def store_moved(index, value):
-        moved_ref[:, lane_block(index)] = value
-
-    put_columns(near_ref, across_ref, pair_ref, slice(0, NB), store_send)
-    put_columns(near_ref, across_ref, pair_ref, slice(NB, NB + 64), store_moved)
-
-
-def rows_kernel(plan_ref, got_ref, moved_ref, a_ref, near_ref, across_ref, pair_ref, out_ref):
+def corner_kernel(near_ref, across_ref, pair_ref, send_ref):
+    panel = lax.axis_index("prow") >> 3
+
+    def store(index, value):
+        @pl.when(index != panel)
+        def _():
+            spot = lane_block(jnp.where(index < panel, index, index - 1))
+            for n in range(4):
+                send_ref[n, :, spot] = value
+
+    put_columns(near_ref, across_ref, pair_ref, slice(0, NB), store)
+
+
+def leave_kernel(plan_ref, a_ref, near_ref, across_ref, pair_ref, *refs):
+    out_refs, full_ref = refs[:4], refs[4]
+
+    def store(index, value):
+        full_ref[:, lane_block(index)] = value
+
+    put_columns(near_ref, across_ref, pair_ref, slice(0, NB), store)
+    full_ref[:, TOP:] = a_ref[:NB, :]
+    rows = select_rows(onehot_of(plan_ref[544:736, :1], NB), full_ref[...])
+    for n in range(4):
+        out_refs[n][...] = rows[48 * n : 48 * n + 48]
+
+
+def spread_kernel(plan_ref, lead_ref, home_ref, one_ref, two_ref, three_ref, lead_out_ref, *out_refs):
+    prow = lax.axis_index("prow")
+    z = prow & 7
+    lead_out_ref[...] = lead_ref[...]
+    held = one_ref[...] + two_ref[...] + three_ref[...]
+    held = jnp.where(prow < 8, home_ref[...], held)
+    spots = [plan_ref[pl.ds(pl.multiple_of(32 + 16 * ((z + n) & 7), 8), 16), :1] for n in range(8)]
+    rows = select_rows(onehot_of(jnp.concatenate(spots, axis=0), 48), held)
+    for n in range(8):
+        out_refs[n][...] = rows[16 * n : 16 * n + 16]
+
+
+def rows_kernel(plan_ref, a_ref, near_ref, across_ref, pair_ref, *refs):
+    moved_refs, out_ref, moved_ref = refs[:8], refs[8], refs[9]
+    z = lax.axis_index("prow") & 7
     slot = plan_ref[288:544, :1]
     onehot = onehot_of(slot, 64)
 
@@ -327,15 +349,22 @@
 
     put_columns(near_ref, across_ref, pair_ref, slice(0, ROWS), store)
     out_ref[:, TOP:] = a_ref[...]
-    moved = jnp.concatenate([got_ref[n, 32:48, :] for n in range(4)], axis=0)
-    moved = jnp.concatenate([moved_ref[...], moved], axis=1)
+    for n in range(8):
+        moved_ref[(z - n) & 7] = moved_refs[n][...]
+    moved = moved_ref[0:4].reshape(64, TOP + COLS)
     out_ref[...] = jnp.where(slot >= 0, select_rows(onehot, moved), out_ref[...])
 
 
-def factor_kernel(corner_ref, own_ref, rows_ref, lower_ref, upper_ref, out_ref, z_ref, y_ref, m_ref, u_ref):
+def factor_kernel(corner_ref, own_ref, rows_ref, lower_ref, upper_ref, out_ref, z_ref, y_ref, m_ref, u_ref, d_ref):
     prow = lax.axis_index("prow")
     pcol = lax.axis_index("pcol")
-    z_ref[:TOP, :] = corner_ref[...]
+    for k in range(PANELS):
+        for j in range(PANELS):
+            if j != k:
+                spot = j if j < k else j - 1
+                z_ref[k * NB : k * NB + NB, j * NB : j * NB + NB] = corner_ref[
+                    k * NB : k * NB + NB, spot * NB : spot * NB + NB
+                ]
     z_ref[TOP:, :] = rows_ref[:, :TOP]
     for k in range(PANELS):
         s = k * NB
@@ -354,6 +383,7 @@
             z_ref[s:e, e:] = corner
             uh, ul = split2(corner)
             z_ref[e:, e:] = z_ref[e:, e:] - mm(m3, jnp.concatenate([uh, uh, ul], axis=0))
+        d_ref[s:e, :] = before[s:e, :NB]
         bh, bl = split2(before[s:e, :])
         upper_rows = mm(l3, jnp.concatenate([bh, bh, bl], axis=0))
         y_ref[s:e, :] = upper_rows
@@ -376,7 +406,9 @@
 
     @pl.when((prow < PANELS) & (pcol < PANELS))
     def _():
-        out_ref[:NB, :NB] = z_ref[top_rows, panel_cols]
+        out_ref[:NB, :NB] = jnp.where(
+            prow == pcol, d_ref[top_rows, :], z_ref[top_rows, panel_cols]
+        )
 
 
 def kernel_call(body, shapes, scratch=()):
@@ -387,6 +419,7 @@
             out_specs=[VMEM] * len(shapes),
             out_shape=[jax.ShapeDtypeStruct(shape, kind) for shape, kind in shapes],
             scratch_shapes=list(scratch),
+            compiler_params=pltpu.CompilerParams(vmem_limit_bytes=KERNEL_VMEM),
         )(*args)
 
     return call
@@ -403,34 +436,52 @@
             pltpu.VMEM((TOP, COLS), F32),
             pltpu.VMEM((ROWS, 3 * TOP), BF),
             pltpu.VMEM((3 * TOP, COLS), BF),
+            pltpu.VMEM((TOP, NB), F32),
         ],
+        compiler_params=pltpu.CompilerParams(vmem_limit_bytes=FACTOR_VMEM),
     )(corner, own, rows, lower_inverse, upper_inverse)
 
 
 def along(value, groups):
     return lax.all_to_all(value, "prow", 0, 0, axis_index_groups=groups)
+
+
+def hop(value, pairs):
+    return lax.ppermute(value, "prow", pairs)
 
 
 def slotted(send, plan, matrix, lower_inverse, upper_inverse):
     pcol = lax.axis_index("pcol")
     block = matrix[:, :NB]
     ends = spread_start(block)
-    got = along(send.reshape(4, 64, COLS), X_GROUPS)
+    got = along(send.reshape(4, 16, COLS), X_GROUPS)
     got, ends = lax.optimization_barrier((got, ends))
-    (send,) = kernel_call(turn_kernel, [((8, 48, COLS), F32)])(plan, got)
+    (send,) = kernel_call(turn_kernel, [((8, 32, COLS), F32)])(plan, got.reshape(64, COLS))
     raw = spread_rest(block, *ends, pcol)
     got = along(send, Z_GROUPS)
-    got, raw = lax.optimization_barrier((got, raw))
-    send, lead = kernel_call(panel_kernel, [((4, NB, COLS), F32), ((NB + 64, NB), F32)])(plan, got)
+    leaving = kernel_call(leave_kernel, [((48, WIDE), F32)] * 4, [pltpu.VMEM((NB, WIDE), F32)])(
+        plan, matrix, *raw
+    )
+    held = [hop(leaving[n], [(k, 8 * n + k) for k in range(PANELS)]) for n in range(1, 4)]
+    got, raw, held = lax.optimization_barrier((got, raw, held))
+    send, lead = kernel_call(panel_kernel, [((4, NB, COLS), F32), ((NB, NB), F32)])(
+        plan, got.reshape(256, COLS)
+    )
     own = along(send, X_GROUPS).reshape(TOP, COLS)
+    lead, *parts = kernel_call(spread_kernel, [((NB, NB), F32)] + [((16, WIDE), F32)] * 8)(
+        plan, lead, leaving[0], *held
+    )
     near, across, pair = spread_columns(lead, pcol)
-    send, moved = kernel_call(corner_kernel, [((4, NB, TOP), F32), ((64, TOP), F32)])(
-        near, across, pair
-    )
-    corner = along(send, X_GROUPS).reshape(TOP, TOP)
-    (rows,) = kernel_call(rows_kernel, [((ROWS, TOP + COLS), F32)])(
-        plan, got, moved, matrix, *raw
-    )
+    moved = [parts[0]]
+    for n in range(1, 8):
+        pairs = [(8 * x + k, 8 * x + (k + n) % 8) for x in range(4) for k in range(PANELS)]
+        moved.append(hop(parts[n], pairs))
+    (send,) = kernel_call(corner_kernel, [((4, NB, TOP - NB), F32)])(near, across, pair)
+    send, own, moved = lax.optimization_barrier((send, own, moved))
+    corner = along(send, X_GROUPS).reshape(TOP, TOP - NB)
+    (rows,) = kernel_call(
+        rows_kernel, [((ROWS, WIDE), F32)], [pltpu.VMEM((8, 16, WIDE), F32)]
+    )(plan, matrix, *raw, *moved)
     return factor(corner, own, rows, lower_inverse, upper_inverse)
 
 
@@ -438,7 +489,12 @@
     origin_ref, gathered_ref, a_ref, own_ref, near_ref, across_ref, pair_ref, corner_ref, top_ref, out_ref
 ):
     def store_corner(index, value):
-        corner_ref[:, lane_block(index)] = value
+        for k in range(PANELS):
+
+            @pl.when(index != k)
+            def _():
+                spot = lane_block(jnp.where(index < k, index, index - 1))
+                corner_ref[k * NB : k * NB + NB, spot] = value[k * NB : k * NB + NB]
 
     def store_rows(index, value):
         out_ref[:, lane_block(index)] = value
@@ -478,7 +534,7 @@
     gathered_rest = exchange_rest(picked_rest, matrix[:NB, NB:])
     corner, top, rows = kernel_call(
         dense_rows_kernel,
-        [((TOP, TOP), F32), ((TOP, COLS), F32), ((ROWS, TOP + COLS), F32)],
+        [((TOP, TOP - NB), F32), ((TOP, COLS), F32), ((ROWS, WIDE), F32)],
     )(origin, gathered_rest, matrix, own, near, across, pair)
     return factor(corner, top, rows, lower_inverse, upper_inverse)
 
@@ -486,7 +542,7 @@
 def per_device(matrix, pivots, lower_inverse, upper_inverse):
     send, plan, over = kernel_call(
         plan_kernel,
-        [((256, COLS), F32), ((544, NB), jnp.int32), ((8, NB), jnp.int32)],
+        [((64, COLS), F32), ((736, NB), jnp.int32), ((8, NB), jnp.int32)],
         [pltpu.VMEM((8, NB), jnp.int32), pltpu.VMEM((8, NB), jnp.int32)],
     )(pivots.reshape(PANELS, NB), matrix)
     return lax.cond(

time: 129 us -> 147 us (1.14)
  the two profiles are of different devices: /device:TPU:1 before, /device:TPU:32 now
where the time goes in v3:
time: 147 us; the launch traced here: 145 us
  starting transfers between devices  66 us (45%)
  waiting for transfers between devices  49 us (33%)
  Pallas kernels  19.1 us (13%)
  local copies, waits for them, and re-layouts  9.82 us (7%)
    all_to_all x4, starting transfers between devices, along(): return lax.all_to_all(value, 'prow', 0, 0, axis_index_groups=groups)  25 us
    ppermute x10, starting transfers between devices, hop(): return lax.ppermute(value, 'prow', pairs)  23.8 us
    ppermute x2, waiting for transfers between devices, spread_rest(): left = lax.ppermute(near[:half], 'pcol', [(q + 4, q + 8) for q in range(4)])  15.2 us
    ppermute x10, waiting for transfers between devices, hop(): return lax.ppermute(value, 'prow', pairs)  14.9 us
    pallas_call x7, Pallas kernels, call(): pl.pallas_call(body, in_specs=[VMEM] * len(args), out_specs=[VMEM] * len(...  14 us
    all_to_all x4, waiting for transfers between devices, along(): return lax.all_to_all(value, 'prow', 0, 0, axis_index_groups=groups)  7.85 us
    ppermute x2, waiting for transfers between devices, spread_rest(): across = lax.ppermute(near, 'pcol', [(q, q ^ 2) for q in range(PCOL)])  7.67 us
    cond x30, local copies, waits for them, and re-layouts  7.43 us
  transfers between devices with their start and end apart: 26, of which 13 were waited for; matrix products, arithmetic and copies ran while one was open for 1% of the time, Pallas kernels for 4%

profile of v3, /device:TPU:32, one launch (start us, length us, event | category | flops | bytes accessed | tf_op | source)
XLA Modules:
  0.0 145.3 jit_solution(3657774860144436841)
XLA Ops:
  0.0 3.1 %shard_map.48 = (f32[64,768]{1,0:T(8,128)}, s32[736,128]{1,0:T(8,128)}, s32[8,128]{1,0:T(8,128)S(1)}) custom-call(s32[4,128]{1,0:T(4,128)} %bitcast.33, f32[256,768]{1,0:T(8,128)} %a_ref.1), custom_call_target="tpu_custom_call" | custom-call | tf_op jit(solution)/shard_map/pallas_call | solution.py:416
  4.3 140.1 %conditional.1 = (f32[256,768]{1,0:T(8,128)S(1)}) conditional(s32[]{:T(128)} %bitcast.19, (s32[512]{0:T(512)}, f32[256,768]{1,0:T(8,128)}, f32[4,128,128]{2,1,0:T(8,128)}, f32[4,128,128]{2,1,0:T(8,128)}) %tuple.14, (f32[64,768]{1,0:T(8,128)}, f32[256,768]{1,0:T(8,128)}, s32[736,128]{1,0:T(8,128)}, f32[4,128,128]{2,1,0:T(8,128)}, ...), branch_computations={%region_0.4_spmd, %region_4.5_spmd} | conditional | flops 1589260 | bytes 65065812 | solution.py:548
  4.3 4.3 %all-to-all-start.6 = ((f32[4,16,768]{2,1,0:T(8,128)}), f32[4,16,768]{2,1,0:T(8,128)S(1)}, u32[]{:S(2)}, u32[]{:S(2)}) async-start(f32[4,16,768]{2,1,0:T(8,128)} %bitcast.31), calls=%async_computation.6 | async-start | bytes 393216 | tf_op jit(solution)/shard_map/cond/branch_1_fun/all_to_all | solution.py:446
  11.0 4.0 %all-to-all-done.6 = f32[4,16,768]{2,1,0:T(8,128)S(1)} async-done(((f32[4,16,768]{2,1,0:T(8,128)}), f32[4,16,768]{2,1,0:T(8,128)S(1)}, u32[]{:S(2)}, u32[]{:S(2)}) %all-to-all-start.6) | async-done | bytes 196640 | tf_op jit(solution)/shard_map/cond/branch_1_fun/all_to_all | solution.py:446
  14.9 2.2 %branch_1_fun.7 = f32[8,32,768]{2,1,0:T(8,128)} custom-call(s32[736,128]{1,0:T(8,128)} %get-tuple-element.36.plan_ref, f32[64,768]{1,0:T(8,128)S(1)} %bitcast.24), custom_call_target="tpu_custom_call" | custom-call | tf_op jit(solution)/shard_map/cond/branch_1_fun/pallas_call | solution.py:416
  17.1 10.3 %all-to-all-start.7 = ((f32[8,32,768]{2,1,0:T(8,128)}), f32[8,32,768]{2,1,0:T(8,128)S(1)}, u32[]{:S(2)}, u32[]{:S(2)}) async-start(f32[8,32,768]{2,1,0:T(8,128)} %branch_1_fun.7), calls=%async_computation.7 | async-start | bytes 1572864 | tf_op jit(solution)/shard_map/cond/branch_1_fun/all_to_all | solution.py:446
  30.1 6.8 %collective-permute-done.8 = f32[128,128]{1,0:T(8,128)S(1)} collective-permute-done((f32[128,128]{1,0:T(8,128)S(1)}, f32[128,128]{1,0:T(8,128)S(1)}, u32[]{:S(2)}, u32[]{:S(2)}) %collective-permute-start.8) | collective-permute-done | bytes 65568 | tf_op jit(solution)/shard_map/cond/branch_1_fun/ppermute | solution.py:135
  38.9 3.2 %collective-permute-start.10 = (f32[256,128]{1,0:T(8,128)S(1)}, f32[256,128]{1,0:T(8,128)S(1)}, u32[]{:S(2)}, u32[]{:S(2)}) collective-permute-start(f32[256,128]{1,0:T(8,128)S(1)} %maximum_select_fusion.1.near_ref), channel_id=1, source_target_pairs={{0,2},{1,3},{2,0},{3,1},{4,6},{5,7},{6,4},{7,5},{8,10},{9,11},{10,... | collective-permute-start | bytes 393224 | tf_op jit(solution)/shard_map/cond/branch_1_fun/ppermute | solution.py:139
  42.1 3.6 %collective-permute-done.10.across_ref = f32[256,128]{1,0:T(8,128)S(1)} collective-permute-done((f32[256,128]{1,0:T(8,128)S(1)}, f32[256,128]{1,0:T(8,128)S(1)}, u32[]{:S(2)}, u32[]{:S(2)}) %collective-permute-start.10) | collective-permute-done | bytes 131104 | tf_op jit(solution)/shard_map/cond/branch_1_fun/ppermute | solution.py:139
  50.8 3.7 %collective-permute-start.12 = (f32[48,1280]{1,0:T(8,128)S(1)}, f32[48,1280]{1,0:T(8,128)S(1)}, u32[]{:S(2)}, u32[]{:S(2)}) collective-permute-start(f32[48,1280]{1,0:T(8,128)S(1)} %get-tuple-element.42), channel_id=1, source_target_pairs={{0,128},{16,144},{32,160},{48,176},{1,129},{17,145},{33,161},{49,1... | collective-permute-start | bytes 737288 | tf_op jit(solution)/shard_map/cond/branch_1_fun/ppermute | solution.py:450
  54.5 2.2 %collective-permute-start.13 = (f32[48,1280]{1,0:T(8,128)S(1)}, f32[48,1280]{1,0:T(8,128)S(1)}, u32[]{:S(2)}, u32[]{:S(2)}) collective-permute-start(f32[48,1280]{1,0:T(8,128)S(1)} %get-tuple-element.43), channel_id=1, source_target_pairs={{0,256},{16,272},{32,288},{48,304},{1,257},{17,273},{33,289},{49,3... | collective-permute-start | bytes 737288 | tf_op jit(solution)/shard_map/cond/branch_1_fun/ppermute | solution.py:450
  58.0 2.8 %collective-permute-done.12.one_ref = f32[48,1280]{1,0:T(8,128)S(1)} collective-permute-done((f32[48,1280]{1,0:T(8,128)S(1)}, f32[48,1280]{1,0:T(8,128)S(1)}, u32[]{:S(2)}, u32[]{:S(2)}) %collective-permute-start.12) | collective-permute-done | bytes 245792 | tf_op jit(solution)/shard_map/cond/branch_1_fun/ppermute | solution.py:450
  60.8 4.4 %collective-permute-done.13.two_ref = f32[48,1280]{1,0:T(8,128)S(1)} collective-permute-done((f32[48,1280]{1,0:T(8,128)S(1)}, f32[48,1280]{1,0:T(8,128)S(1)}, u32[]{:S(2)}, u32[]{:S(2)}) %collective-permute-start.13) | collective-permute-done | bytes 245792 | tf_op jit(solution)/shard_map/cond/branch_1_fun/ppermute | solution.py:450
  65.2 2.6 %branch_1_fun.9 = (f32[4,128,768]{2,1,0:T(8,128)}, f32[128,128]{1,0:T(8,128)S(1)}) custom-call(s32[736,128]{1,0:T(8,128)} %get-tuple-element.36.plan_ref, f32[256,768]{1,0:T(8,128)S(1)} %bitcast.22), custom_call_target="tpu_custom_call" | custom-call | tf_op jit(solution)/shard_map/cond/branch_1_fun/pallas_call | solution.py:416
  67.8 5.3 %all-to-all-start.8 = ((f32[4,128,768]{2,1,0:T(8,128)}), f32[4,128,768]{2,1,0:T(8,128)S(1)}, u32[]{:S(2)}, u32[]{:S(2)}) async-start(f32[4,128,768]{2,1,0:T(8,128)} %get-tuple-element.52), calls=%async_computation.8 | async-start | bytes 3145728 | tf_op jit(solution)/shard_map/cond/branch_1_fun/all_to_all | solution.py:446
  78.5 8.4 %collective-permute-done.17 = f32[64,128]{1,0:T(8,128)S(1)} collective-permute-done((f32[64,128]{1,0:T(8,128)S(1)}, f32[64,128]{1,0:T(8,128)S(1)}, u32[]{:S(2)}, u32[]{:S(2)}) %collective-permute-start.17) | collective-permute-done | bytes 32800 | tf_op jit(solution)/shard_map/cond/branch_1_fun/ppermute | solution.py:135
  89.1 4.0 %collective-permute-done.19.across_ref = f32[128,128]{1,0:T(8,128)S(1)} collective-permute-done((f32[128,128]{1,0:T(8,128)S(1)}, f32[128,128]{1,0:T(8,128)S(1)}, u32[]{:S(2)}, u32[]{:S(2)}) %collective-permute-start.19) | collective-permute-done | bytes 65568 | tf_op jit(solution)/shard_map/cond/branch_1_fun/ppermute | solution.py:139
  95.1 3.9 %collective-permute-start.21 = (f32[16,1280]{1,0:T(8,128)S(1)}, f32[16,1280]{1,0:T(8,128)S(1)}, u32[]{:S(2)}, u32[]{:S(2)}) collective-permute-start(f32[16,1280]{1,0:T(8,128)S(1)} %get-tuple-element.54), channel_id=1, source_target_pairs={{0,16},{16,32},{32,48},{48,64},{128,144},{144,160},{160,176},{176,... | collective-permute-start | bytes 245768 | tf_op jit(solution)/shard_map/cond/branch_1_fun/ppermute | solution.py:450
  99.0 4.3 %collective-permute-start.22 = (f32[16,1280]{1,0:T(8,128)S(1)}, f32[16,1280]{1,0:T(8,128)S(1)}, u32[]{:S(2)}, u32[]{:S(2)}) collective-permute-start(f32[16,1280]{1,0:T(8,128)S(1)} %get-tuple-element.55), channel_id=1, source_target_pairs={{0,32},{16,48},{32,64},{48,80},{128,160},{144,176},{160,192},{176,... | collective-permute-start | bytes 245768 | tf_op jit(solution)/shard_map/cond/branch_1_fun/ppermute | solution.py:450
  114.4 2.6 %collective-permute-done.26.refs_6_ = f32[16,1280]{1,0:T(8,128)S(1)} collective-permute-done((f32[16,1280]{1,0:T(8,128)S(1)}, f32[16,1280]{1,0:T(8,128)S(1)}, u32[]{:S(2)}, u32[]{:S(2)}) %collective-permute-start.26) | collective-permute-done | bytes 81952 | tf_op jit(solution)/shard_map/cond/branch_1_fun/ppermute | solution.py:450
  117.0 4.0 %collective-permute-done.27.refs_7_ = f32[16,1280]{1,0:T(8,128)S(1)} collective-permute-done((f32[16,1280]{1,0:T(8,128)S(1)}, f32[16,1280]{1,0:T(8,128)S(1)}, u32[]{:S(2)}, u32[]{:S(2)}) %collective-permute-start.27) | collective-permute-done | bytes 81952 | tf_op jit(solution)/shard_map/cond/branch_1_fun/ppermute | solution.py:450
  121.7 5.1 %all-to-all-start.9 = ((f32[4,128,384]{2,1,0:T(8,128)}), f32[4,128,384]{2,1,0:T(8,128)}, u32[]{:S(2)}, u32[]{:S(2)}) async-start(f32[4,128,384]{2,1,0:T(8,128)} %branch_1_fun.11), calls=%async_computation.9 | async-start | bytes 1572864 | tf_op jit(solution)/shard_map/cond/branch_1_fun/all_to_all | solution.py:446
  135.1 3.9 %all-to-all-done.9 = f32[4,128,384]{2,1,0:T(8,128)} async-done(((f32[4,128,384]{2,1,0:T(8,128)}), f32[4,128,384]{2,1,0:T(8,128)}, u32[]{:S(2)}, u32[]{:S(2)}) %all-to-all-start.9) | async-done | bytes 786464 | tf_op jit(solution)/shard_map/cond/branch_1_fun/all_to_all | solution.py:446
  139.0 5.1 %branch_1_fun.13 = f32[256,768]{1,0:T(8,128)S(1)} custom-call(f32[512,384]{1,0:T(8,128)} %bitcast.17.corner_ref, f32[512,768]{1,0:T(8,128)S(1)} %bitcast.21, f32[256,1280]{1,0:T(8,128)S(1)} %branch_1_fun.12.rows_ref, f32[4,128,128]{2,1,0:T(8,128)} %get-tuple-element.74.lower_ref, f32[4,128,128]{2,1,0:T(8,128)} %get-tuple-element.75.upper_ref), custom_call_target="tpu_custom_call" | custom-call | tf_op jit(solution)/shard_map/cond/branch_1_fun/pallas_call | solution.py:429
  (79 shorter events, 44.1 us)
Async XLA Ops:
  4.3 10.6 %all-to-all-start.6 = ((f32[4,16,768]{2,1,0:T(8,128)}), f32[4,16,768]{2,1,0:T(8,128)S(1)}, u32[]{:S(2)}, u32[]{:S(2)}) async-start(f32[4,16,768]{2,1,0:T(8,128)} %bitcast.31), calls=%async_computation.6 | async-start | bytes 393216 | tf_op jit(solution)/shard_map/cond/branch_1_fun/all_to_all | solution.py:446
  9.6 1.4 collective-permute-start.7
  17.1 48.2 %all-to-all-start.7 = ((f32[8,32,768]{2,1,0:T(8,128)}), f32[8,32,768]{2,1,0:T(8,128)S(1)}, u32[]{:S(2)}, u32[]{:S(2)}) async-start(f32[8,32,768]{2,1,0:T(8,128)} %branch_1_fun.7), calls=%async_computation.7 | async-start | bytes 1572864 | tf_op jit(solution)/shard_map/cond/branch_1_fun/all_to_all | solution.py:446
  27.5 9.4 %collective-permute-start.8 = (f32[128,128]{1,0:T(8,128)S(1)}, f32[128,128]{1,0:T(8,128)S(1)}, u32[]{:S(2)}, u32[]{:S(2)}) collective-permute-start(f32[128,128]{1,0:T(8,128)S(1)} %get-tuple-element.85), channel_id=1, source_target_pairs={{4,8},{5,9},{6,10},{7,11},{20,24},{21,25},{22,26},{23,27},{36,40},... | collective-permute-start | bytes 196616 | tf_op jit(solution)/shard_map/cond/branch_1_fun/ppermute | solution.py:135
  28.8 10.1 %collective-permute-start.9 = (f32[128,128]{1,0:T(8,128)S(1)}, f32[128,128]{1,0:T(8,128)S(1)}, u32[]{:S(2)}, u32[]{:S(2)}) collective-permute-start(f32[128,128]{1,0:T(8,128)S(1)} %get-tuple-element.86), channel_id=1, source_target_pairs={{12,8},{13,9},{14,10},{15,11},{28,24},{29,25},{30,26},{31,27},{44,... | collective-permute-start | bytes 196616 | tf_op jit(solution)/shard_map/cond/branch_1_fun/ppermute | solution.py:136
  38.9 6.9 %collective-permute-start.10 = (f32[256,128]{1,0:T(8,128)S(1)}, f32[256,128]{1,0:T(8,128)S(1)}, u32[]{:S(2)}, u32[]{:S(2)}) collective-permute-start(f32[256,128]{1,0:T(8,128)S(1)} %maximum_select_fusion.1.near_ref), channel_id=1, source_target_pairs={{0,2},{1,3},{2,0},{3,1},{4,6},{5,7},{6,4},{7,5},{8,10},{9,11},{10,... | collective-permute-start | bytes 393224 | tf_op jit(solution)/shard_map/cond/branch_1_fun/ppermute | solution.py:139
  45.8 3.4 %collective-permute-start.11 = (f32[256,256]{1,0:T(8,128)S(1)}, f32[256,256]{1,0:T(8,128)S(1)}, u32[]{:S(2)}, u32[]{:S(2)}) collective-permute-start(f32[256,256]{1,0:T(8,128)S(1)} %pad_maximum_fusion.6), channel_id=1, source_target_pairs={{0,1},{1,0},{2,3},{3,2},{4,5},{5,4},{6,7},{7,6},{8,9},{9,8},{10,11... | collective-permute-start | bytes 786440 | tf_op jit(solution)/shard_map/cond/branch_1_fun/ppermute | solution.py:141
  50.8 10.0 %collective-permute-start.12 = (f32[48,1280]{1,0:T(8,128)S(1)}, f32[48,1280]{1,0:T(8,128)S(1)}, u32[]{:S(2)}, u32[]{:S(2)}) collective-permute-start(f32[48,1280]{1,0:T(8,128)S(1)} %get-tuple-element.42), channel_id=1, source_target_pairs={{0,128},{16,144},{32,160},{48,176},{1,129},{17,145},{33,161},{49,1... | collective-permute-start | bytes 737288 | tf_op jit(solution)/shard_map/cond/branch_1_fun/ppermute | solution.py:450
  54.5 10.7 %collective-permute-start.13 = (f32[48,1280]{1,0:T(8,128)S(1)}, f32[48,1280]{1,0:T(8,128)S(1)}, u32[]{:S(2)}, u32[]{:S(2)}) collective-permute-start(f32[48,1280]{1,0:T(8,128)S(1)} %get-tuple-element.43), channel_id=1, source_target_pairs={{0,256},{16,272},{32,288},{48,304},{1,257},{17,273},{33,289},{49,3... | collective-permute-start | bytes 737288 | tf_op jit(solution)/shard_map/cond/branch_1_fun/ppermute | solution.py:450
  56.7 8.6 %collective-permute-start.14 = (f32[48,1280]{1,0:T(8,128)S(1)}, f32[48,1280]{1,0:T(8,128)S(1)}, u32[]{:S(2)}, u32[]{:S(2)}) collective-permute-start(f32[48,1280]{1,0:T(8,128)S(1)} %get-tuple-element.44), channel_id=1, source_target_pairs={{0,384},{16,400},{32,416},{48,432},{1,385},{17,401},{33,417},{49,4... | collective-permute-start | bytes 737288 | tf_op jit(solution)/shard_map/cond/branch_1_fun/ppermute | solution.py:450
  67.8 53.2 %all-to-all-start.8 = ((f32[4,128,768]{2,1,0:T(8,128)}), f32[4,128,768]{2,1,0:T(8,128)S(1)}, u32[]{:S(2)}, u32[]{:S(2)}) async-start(f32[4,128,768]{2,1,0:T(8,128)} %get-tuple-element.52), calls=%async_computation.8 | async-start | bytes 3145728 | tf_op jit(solution)/shard_map/cond/branch_1_fun/all_to_all | solution.py:446
  74.5 1.3 collective-permute-start.16
  75.9 11.0 %collective-permute-start.17 = (f32[64,128]{1,0:T(8,128)S(1)}, f32[64,128]{1,0:T(8,128)S(1)}, u32[]{:S(2)}, u32[]{:S(2)}) collective-permute-start(f32[64,128]{1,0:T(8,128)S(1)} %get-tuple-element.87), channel_id=1, source_target_pairs={{4,8},{5,9},{6,10},{7,11},{20,24},{21,25},{22,26},{23,27},{36,40},... | collective-permute-start | bytes 98312 | tf_op jit(solution)/shard_map/cond/branch_1_fun/ppermute | solution.py:135
  77.2 9.7 %collective-permute-start.18 = (f32[64,128]{1,0:T(8,128)S(1)}, f32[64,128]{1,0:T(8,128)S(1)}, u32[]{:S(2)}, u32[]{:S(2)}) collective-permute-start(f32[64,128]{1,0:T(8,128)S(1)} %get-tuple-element.88), channel_id=1, source_target_pairs={{12,8},{13,9},{14,10},{15,11},{28,24},{29,25},{30,26},{31,27},{44,... | collective-permute-start | bytes 98312 | tf_op jit(solution)/shard_map/cond/branch_1_fun/ppermute | solution.py:136
  87.0 6.2 %collective-permute-start.19 = (f32[128,128]{1,0:T(8,128)S(1)}, f32[128,128]{1,0:T(8,128)S(1)}, u32[]{:S(2)}, u32[]{:S(2)}) collective-permute-start(f32[128,128]{1,0:T(8,128)S(1)} %maximum_select_fusion.2.near_ref), channel_id=1, source_target_pairs={{0,2},{1,3},{2,0},{3,1},{4,6},{5,7},{6,4},{7,5},{8,10},{9,11},{10,... | collective-permute-start | bytes 196616 | tf_op jit(solution)/shard_map/cond/branch_1_fun/ppermute | solution.py:139
  93.2 16.7 %collective-permute-start.20 = (f32[128,256]{1,0:T(8,128)S(1)}, f32[128,256]{1,0:T(8,128)S(1)}, u32[]{:S(2)}, u32[]{:S(2)}) collective-permute-start(f32[128,256]{1,0:T(8,128)S(1)} %pad_maximum_fusion.7), channel_id=1, source_target_pairs={{0,1},{1,0},{2,3},{3,2},{4,5},{5,4},{6,7},{7,6},{8,9},{9,8},{10,11... | collective-permute-start | bytes 393224 | tf_op jit(solution)/shard_map/cond/branch_1_fun/ppermute | solution.py:141
  95.1 10.9 %collective-permute-start.21 = (f32[16,1280]{1,0:T(8,128)S(1)}, f32[16,1280]{1,0:T(8,128)S(1)}, u32[]{:S(2)}, u32[]{:S(2)}) collective-permute-start(f32[16,1280]{1,0:T(8,128)S(1)} %get-tuple-element.54), channel_id=1, source_target_pairs={{0,16},{16,32},{32,48},{48,64},{128,144},{144,160},{160,176},{176,... | collective-permute-start | bytes 245768 | tf_op jit(solution)/shard_map/cond/branch_1_fun/ppermute | solution.py:450
  99.0 8.9 %collective-permute-start.22 = (f32[16,1280]{1,0:T(8,128)S(1)}, f32[16,1280]{1,0:T(8,128)S(1)}, u32[]{:S(2)}, u32[]{:S(2)}) collective-permute-start(f32[16,1280]{1,0:T(8,128)S(1)} %get-tuple-element.55), channel_id=1, source_target_pairs={{0,32},{16,48},{32,64},{48,80},{128,160},{144,176},{160,192},{176,... | collective-permute-start | bytes 245768 | tf_op jit(solution)/shard_map/cond/branch_1_fun/ppermute | solution.py:450
  103.3 9.5 %collective-permute-start.23 = (f32[16,1280]{1,0:T(8,128)S(1)}, f32[16,1280]{1,0:T(8,128)S(1)}, u32[]{:S(2)}, u32[]{:S(2)}) collective-permute-start(f32[16,1280]{1,0:T(8,128)S(1)} %get-tuple-element.56), channel_id=1, source_target_pairs={{0,48},{16,64},{32,80},{48,96},{128,176},{144,192},{160,208},{176,... | collective-permute-start | bytes 245768 | tf_op jit(solution)/shard_map/cond/branch_1_fun/ppermute | solution.py:450
  104.7 8.7 %collective-permute-start.24 = (f32[16,1280]{1,0:T(8,128)S(1)}, f32[16,1280]{1,0:T(8,128)S(1)}, u32[]{:S(2)}, u32[]{:S(2)}) collective-permute-start(f32[16,1280]{1,0:T(8,128)S(1)} %get-tuple-element.57), channel_id=1, source_target_pairs={{0,64},{16,80},{32,96},{48,112},{128,192},{144,208},{160,224},{176... | collective-permute-start | bytes 245768 | tf_op jit(solution)/shard_map/cond/branch_1_fun/ppermute | solution.py:450
  106.0 8.4 %collective-permute-start.25 = (f32[16,1280]{1,0:T(8,128)S(1)}, f32[16,1280]{1,0:T(8,128)S(1)}, u32[]{:S(2)}, u32[]{:S(2)}) collective-permute-start(f32[16,1280]{1,0:T(8,128)S(1)} %get-tuple-element.58), channel_id=1, source_target_pairs={{0,80},{16,96},{32,112},{48,0},{128,208},{144,224},{160,240},{176,... | collective-permute-start | bytes 245768 | tf_op jit(solution)/shard_map/cond/branch_1_fun/ppermute | solution.py:450
  107.9 9.1 %collective-permute-start.26 = (f32[16,1280]{1,0:T(8,128)S(1)}, f32[16,1280]{1,0:T(8,128)S(1)}, u32[]{:S(2)}, u32[]{:S(2)}) collective-permute-start(f32[16,1280]{1,0:T(8,128)S(1)} %get-tuple-element.59), channel_id=1, source_target_pairs={{0,96},{16,112},{32,0},{48,16},{128,224},{144,240},{160,128},{176,... | collective-permute-start | bytes 245768 | tf_op jit(solution)/shard_map/cond/branch_1_fun/ppermute | solution.py:450
  109.9 11.2 %collective-permute-start.27 = (f32[16,1280]{1,0:T(8,128)S(1)}, f32[16,1280]{1,0:T(8,128)S(1)}, u32[]{:S(2)}, u32[]{:S(2)}) collective-permute-start(f32[16,1280]{1,0:T(8,128)S(1)} %get-tuple-element.60), channel_id=1, source_target_pairs={{0,112},{16,0},{32,16},{48,32},{128,240},{144,128},{160,144},{176,... | collective-permute-start | bytes 245768 | tf_op jit(solution)/shard_map/cond/branch_1_fun/ppermute | solution.py:450
  121.7 17.4 %all-to-all-start.9 = ((f32[4,128,384]{2,1,0:T(8,128)}), f32[4,128,384]{2,1,0:T(8,128)}, u32[]{:S(2)}, u32[]{:S(2)}) async-start(f32[4,128,384]{2,1,0:T(8,128)} %branch_1_fun.11), calls=%async_computation.9 | async-start | bytes 1572864 | tf_op jit(solution)/shard_map/cond/branch_1_fun/all_to_all | solution.py:446
  (18 other events, 75.1 us)

commit v4 on v2

--- a/solution.py
+++ b/solution.py
@@ -13,6 +13,8 @@
 ROWS = 256
 COLS = 768
 REST = COLS - NB
+KERNEL_VMEM = 20 << 20
+FACTOR_VMEM = 28 << 20
 BF = jnp.bfloat16
 F32 = jnp.float32
 X_GROUPS = [[x * 8 + z for x in range(4)] for z in range(8)]
@@ -307,9 +309,12 @@
 
 
 def corner_kernel(near_ref, across_ref, pair_ref, send_ref, moved_ref):
+    panel = lax.axis_index("prow") >> 3
+
     def store_send(index, value):
-        for n in range(4):
-            send_ref[n, :, lane_block(index)] = value
+        @pl.when(index != panel)
+        def _():
+            send_ref[:, lane_block(jnp.where(index < panel, index, index - 1))] = value
 
     def store_moved(index, value):
         moved_ref[:, lane_block(index)] = value
@@ -318,25 +323,36 @@
     put_columns(near_ref, across_ref, pair_ref, slice(NB, NB + 64), store_moved)
 
 
-def rows_kernel(plan_ref, got_ref, moved_ref, a_ref, near_ref, across_ref, pair_ref, out_ref):
+def own_rows_kernel(plan_ref, got_ref, a_ref, out_ref):
     slot = plan_ref[288:544, :1]
-    onehot = onehot_of(slot, 64)
+    moved = jnp.concatenate([got_ref[n, 32:48, :] for n in range(4)], axis=0)
+    out_ref[...] = jnp.where(slot >= 0, select_rows(onehot_of(slot, 64), moved), a_ref[...])
+
+
+def panel_rows_kernel(plan_ref, moved_ref, near_ref, across_ref, pair_ref, out_ref):
+    slot = plan_ref[288:544, :1]
 
     def store(index, value):
         out_ref[:, lane_block(index)] = value
 
     put_columns(near_ref, across_ref, pair_ref, slice(0, ROWS), store)
-    out_ref[:, TOP:] = a_ref[...]
-    moved = jnp.concatenate([got_ref[n, 32:48, :] for n in range(4)], axis=0)
-    moved = jnp.concatenate([moved_ref[...], moved], axis=1)
-    out_ref[...] = jnp.where(slot >= 0, select_rows(onehot, moved), out_ref[...])
-
-
-def factor_kernel(corner_ref, own_ref, rows_ref, lower_ref, upper_ref, out_ref, z_ref, y_ref, m_ref, u_ref):
+    moved = select_rows(onehot_of(slot, 64), moved_ref[...])
+    out_ref[...] = jnp.where(slot >= 0, moved, out_ref[...])
+
+
+def factor_kernel(
+    home_ref, one_ref, two_ref, three_ref, own_ref, left_ref, right_ref, lower_ref, upper_ref,
+    out_ref, z_ref, y_ref, m_ref, u_ref, d_ref,
+):
     prow = lax.axis_index("prow")
     pcol = lax.axis_index("pcol")
-    z_ref[:TOP, :] = corner_ref[...]
-    z_ref[TOP:, :] = rows_ref[:, :TOP]
+    for n, ref in enumerate((home_ref, one_ref, two_ref, three_ref)):
+        panel = ((prow >> 3) - n) & 3
+        rows = pl.ds(pl.multiple_of(panel * NB, NB), NB)
+        for spot in range(PANELS - 1):
+            block = jnp.where(spot < panel, spot, spot + 1)
+            z_ref[rows, lane_block(block)] = ref[:, spot * NB : spot * NB + NB]
+    z_ref[TOP:, :] = left_ref[...]
     for k in range(PANELS):
         s = k * NB
         e = s + NB
@@ -354,6 +370,7 @@
             z_ref[s:e, e:] = corner
             uh, ul = split2(corner)
             z_ref[e:, e:] = z_ref[e:, e:] - mm(m3, jnp.concatenate([uh, uh, ul], axis=0))
+        d_ref[s:e, :] = before[s:e, :NB]
         bh, bl = split2(before[s:e, :])
         upper_rows = mm(l3, jnp.concatenate([bh, bh, bl], axis=0))
         y_ref[s:e, :] = upper_rows
@@ -362,7 +379,7 @@
         u_ref[3 * s : 3 * e, :] = u3
         if e < TOP:
             y_ref[e:TOP, :] = before[e:TOP, :] - mm(m3[: TOP - e], u3)
-    out_ref[...] = rows_ref[:, TOP:] - mm(m_ref[...], u_ref[...])
+    out_ref[...] = right_ref[...] - mm(m_ref[...], u_ref[...])
     panel_cols = lane_block(pcol & 3)
     top_rows = pl.ds(pl.multiple_of((prow & 3) * NB, NB), NB)
 
@@ -376,7 +393,9 @@
 
     @pl.when((prow < PANELS) & (pcol < PANELS))
     def _():
-        out_ref[:NB, :NB] = z_ref[top_rows, panel_cols]
+        out_ref[:NB, :NB] = jnp.where(
+            prow == pcol, d_ref[top_rows, :], z_ref[top_rows, panel_cols]
+        )
 
 
 def kernel_call(body, shapes, scratch=()):
@@ -387,15 +406,16 @@
             out_specs=[VMEM] * len(shapes),
             out_shape=[jax.ShapeDtypeStruct(shape, kind) for shape, kind in shapes],
             scratch_shapes=list(scratch),
+            compiler_params=pltpu.CompilerParams(vmem_limit_bytes=KERNEL_VMEM),
         )(*args)
 
     return call
 
 
-def factor(corner, own, rows, lower_inverse, upper_inverse):
+def factor(*args):
     return pl.pallas_call(
         factor_kernel,
-        in_specs=[VMEM] * 5,
+        in_specs=[VMEM] * len(args),
         out_specs=VMEM,
         out_shape=jax.ShapeDtypeStruct((ROWS, COLS), F32),
         scratch_shapes=[
@@ -403,8 +423,10 @@
             pltpu.VMEM((TOP, COLS), F32),
             pltpu.VMEM((ROWS, 3 * TOP), BF),
             pltpu.VMEM((3 * TOP, COLS), BF),
+            pltpu.VMEM((TOP, NB), F32),
         ],
-    )(corner, own, rows, lower_inverse, upper_inverse)
+        compiler_params=pltpu.CompilerParams(vmem_limit_bytes=FACTOR_VMEM),
+    )(*args)
 
 
 def along(value, groups):
@@ -423,37 +445,53 @@
     got, raw = lax.optimization_barrier((got, raw))
     send, lead = kernel_call(panel_kernel, [((4, NB, COLS), F32), ((NB + 64, NB), F32)])(plan, got)
     own = along(send, X_GROUPS).reshape(TOP, COLS)
-    near, across, pair = spread_columns(lead, pcol)
-    send, moved = kernel_call(corner_kernel, [((4, NB, TOP), F32), ((64, TOP), F32)])(
+    ends = spread_start(lead)
+    near, across, pair = spread_rest(lead, *ends, pcol)
+    (right,) = kernel_call(own_rows_kernel, [((ROWS, COLS), F32)])(plan, got, matrix)
+    home, moved = kernel_call(corner_kernel, [((NB, TOP - NB), F32), ((64, TOP), F32)])(
         near, across, pair
     )
-    corner = along(send, X_GROUPS).reshape(TOP, TOP)
-    (rows,) = kernel_call(rows_kernel, [((ROWS, TOP + COLS), F32)])(
-        plan, got, moved, matrix, *raw
-    )
-    return factor(corner, own, rows, lower_inverse, upper_inverse)
+    others = [
+        lax.ppermute(home, "prow", [(p, (p + 8 * n) % PROW) for p in range(PROW)])
+        for n in range(1, 4)
+    ]
+    (left,) = kernel_call(panel_rows_kernel, [((ROWS, TOP), F32)])(plan, moved, *raw)
+    return factor(home, *others, own, left, right, lower_inverse, upper_inverse)
 
 
 def dense_rows_kernel(
-    origin_ref, gathered_ref, a_ref, own_ref, near_ref, across_ref, pair_ref, corner_ref, top_ref, out_ref
+    origin_ref, gathered_ref, a_ref, own_ref, near_ref, across_ref, pair_ref,
+    home_ref, one_ref, two_ref, three_ref, top_ref, left_ref, right_ref,
 ):
+    x = lax.axis_index("prow") >> 3
+
     def store_corner(index, value):
-        corner_ref[:, lane_block(index)] = value
-
-    def store_rows(index, value):
-        out_ref[:, lane_block(index)] = value
+        for n, ref in enumerate((home_ref, one_ref, two_ref, three_ref)):
+            panel = (x - n) & 3
+
+            @pl.when(index != panel)
+            def _():
+                spot = lane_block(jnp.where(index < panel, index, index - 1))
+                for k in range(PANELS):
+
+                    @pl.when(panel == k)
+                    def _():
+                        ref[:, spot] = value[k * NB : k * NB + NB]
+
+    def store_left(index, value):
+        left_ref[:, lane_block(index)] = value
 
     put_columns(near_ref, across_ref, pair_ref, slice(0, TOP), store_corner)
-    put_columns(near_ref, across_ref, pair_ref, slice(TOP, TOP + ROWS), store_rows)
+    put_columns(near_ref, across_ref, pair_ref, slice(TOP, TOP + ROWS), store_left)
     top_ref[:, :NB] = own_ref[:TOP, :]
-    out_ref[:, TOP : TOP + NB] = own_ref[TOP:, :]
+    right_ref[:, :NB] = own_ref[TOP:, :]
     for unit in range(PROW):
         top_ref[unit * 16 : unit * 16 + 16, NB:] = gathered_ref[unit * 32 : unit * 32 + 16, :]
     origin = origin_ref[:, :1]
 
     @pl.loop(0, REST // NB)
     def _(c):
-        out_ref[:, lane_block(c + PANELS + 1)] = moved_rows(
+        right_ref[:, lane_block(c + 1)] = moved_rows(
             origin, gathered_ref[:, lane_block(c)], a_ref[:, lane_block(c + 1)]
         )
 
@@ -476,11 +514,11 @@
     (own,) = kernel_call(column_kernel, [((TOP + ROWS, NB), F32)])(origin, gathered_first, matrix)
     near, across, pair = spread_columns(own, pcol)
     gathered_rest = exchange_rest(picked_rest, matrix[:NB, NB:])
-    corner, top, rows = kernel_call(
+    *corners, top, left, right = kernel_call(
         dense_rows_kernel,
-        [((TOP, TOP), F32), ((TOP, COLS), F32), ((ROWS, TOP + COLS), F32)],
+        [((NB, TOP - NB), F32)] * 4 + [((TOP, COLS), F32), ((ROWS, TOP), F32), ((ROWS, COLS), F32)],
     )(origin, gathered_rest, matrix, own, near, across, pair)
-    return factor(corner, top, rows, lower_inverse, upper_inverse)
+    return factor(*corners, top, left, right, lower_inverse, upper_inverse)
 
 
 def per_device(matrix, pivots, lower_inverse, upper_inverse):

time: 129 us -> 123 us (0.953)
  Pallas kernels: 20.5 us -> 11.3 us
  waiting for transfers between devices: 47.1 us -> 38.4 us
  starting transfers between devices: 53.5 us -> 59.1 us
  local copies, waits for them, and re-layouts: 5.68 us -> 10.1 us
    all_to_all x4 -> x3, waiting for transfers between devices: 33.5 us -> 18.1 us  [along(): return lax.all_to_all(value, 'prow', 0, 0, axis_index_groups=groups)]
    ppermute x0 -> x3, starting transfers between devices: none -> 9.83 us  [slotted(): lax.ppermute(home, 'prow', [(p, (p + 8 * n) % PROW) for p in range(PROW)])]
    pallas_call x5 -> x6, Pallas kernels: 14.5 us -> 6.35 us  [call(): pl.pallas_call(body, in_specs=[VMEM] * len(args), out_specs=[VMEM] * len(...]
    ppermute x0 -> x3, waiting for transfers between devices: none -> 6.91 us  [slotted(): lax.ppermute(home, 'prow', [(p, (p + 8 * n) % PROW) for p in range(PROW)])]
    cond x26 -> x36, local copies, waits for them, and re-layouts: 3.59 us -> 7.67 us
    all_to_all x4 -> x3, starting transfers between devices: 22.9 us -> 19.2 us  [along(): return lax.all_to_all(value, 'prow', 0, 0, axis_index_groups=groups)]
  transfers between devices with their start and end apart: 16 -> 18, of which waited for: 8 -> 9; matrix products, arithmetic and copies ran while one was open for 0% -> 2% of each run, Pallas kernels for 4% -> 1%
where the time goes in v4:
time: 123 us; the launch traced here: 121 us
  starting transfers between devices  59.1 us (48%)
  waiting for transfers between devices  38.4 us (31%)
  Pallas kernels  11.3 us (9%)
  local copies, waits for them, and re-layouts  10.1 us (8%)
    all_to_all x3, starting transfers between devices, along(): return lax.all_to_all(value, 'prow', 0, 0, axis_index_groups=groups)  19.2 us
    all_to_all x3, waiting for transfers between devices, along(): return lax.all_to_all(value, 'prow', 0, 0, axis_index_groups=groups)  18.1 us
    ppermute x2, starting transfers between devices, spread_start(): down = lax.ppermute(own, 'pcol', [(q, q + 12) for q in range(4)])  12.1 us
    ppermute x3, starting transfers between devices, slotted(): lax.ppermute(home, 'prow', [(p, (p + 8 * n) % PROW) for p in range(PROW)])  9.83 us
    cond x36, local copies, waits for them, and re-layouts  7.67 us
    ppermute x2, starting transfers between devices, spread_rest(): pair = lax.ppermute(both, 'pcol', [(q, q ^ 1) for q in range(PCOL)])  7.6 us
    ppermute x3, waiting for transfers between devices, slotted(): lax.ppermute(home, 'prow', [(p, (p + 8 * n) % PROW) for p in range(PROW)])  6.91 us
    ppermute x2, waiting for transfers between devices, spread_rest(): across = lax.ppermute(near, 'pcol', [(q, q ^ 2) for q in range(PCOL)])  6.85 us
  transfers between devices with their start and end apart: 18, of which 9 were waited for; matrix products, arithmetic and copies ran while one was open for 2% of the time, Pallas kernels for 1%

profile of v4, /device:TPU:1, one launch (start us, length us, event | category | flops | bytes accessed | tf_op | source)
XLA Modules:
  0.0 121.3 jit_solution(714377083521932824)
XLA Ops:
  0.0 3.4 %shard_map.48 = (f32[256,768]{1,0:T(8,128)}, s32[544,128]{1,0:T(8,128)}, s32[8,128]{1,0:T(8,128)S(1)}) custom-call(s32[4,128]{1,0:T(4,128)} %bitcast.28, f32[256,768]{1,0:T(8,128)} %a_ref.1), custom_call_target="tpu_custom_call" | custom-call | tf_op jit(solution)/shard_map/pallas_call | solution.py:403
  4.6 115.8 %conditional.1 = (f32[256,768]{1,0:T(8,128)S(1)}) conditional(s32[]{:T(128)} %bitcast.16, (s32[512]{0:T(512)}, f32[256,768]{1,0:T(8,128)}, f32[4,128,128]{2,1,0:T(8,128)}, f32[4,128,128]{2,1,0:T(8,128)}) %tuple.13, (f32[256,768]{1,0:T(8,128)}, f32[256,768]{1,0:T(8,128)}, s32[544,128]{1,0:T(8,128)}, f32[4,128,128]{2,1,0:T(8,128)}, ...), branch_computations={%region_0.4_spmd, %region_4.5_spmd} | conditional | flops 1589260 | bytes 65065812 | solution.py:530
  4.6 5.0 %all-to-all-start.6 = ((f32[4,64,768]{2,1,0:T(8,128)}), f32[4,64,768]{2,1,0:T(8,128)S(1)}, u32[]{:S(2)}, u32[]{:S(2)}) async-start(f32[4,64,768]{2,1,0:T(8,128)} %bitcast.24), calls=%async_computation.6 | async-start | bytes 1572864 | tf_op jit(solution)/shard_map/cond/branch_1_fun/all_to_all | solution.py:433
  10.5 5.9 %collective-permute-start.7 = (f32[256,128]{1,0:T(8,128)S(1)}, f32[256,128]{1,0:T(8,128)S(1)}, u32[]{:S(2)}, u32[]{:S(2)}) collective-permute-start(f32[256,128]{1,0:T(8,128)S(1)} %slice.42), channel_id=1, source_target_pairs={{0,12},{1,13},{2,14},{3,15},{16,28},{17,29},{18,30},{19,31},{32,44... | collective-permute-start | bytes 393224 | tf_op jit(solution)/shard_map/cond/branch_1_fun/ppermute | solution.py:123
  16.4 1.5 %collective-permute-start.6 = (f32[256,128]{1,0:T(8,128)S(1)}, f32[256,128]{1,0:T(8,128)S(1)}, u32[]{:S(2)}, u32[]{:S(2)}) collective-permute-start(f32[256,128]{1,0:T(8,128)S(1)} %slice.42), channel_id=1, source_target_pairs={{0,4},{1,5},{2,6},{3,7},{16,20},{17,21},{18,22},{19,23},{32,36},{3... | collective-permute-start | bytes 393224 | tf_op jit(solution)/shard_map/cond/branch_1_fun/ppermute | solution.py:122
  17.9 4.4 %collective-permute-done.7 = f32[256,128]{1,0:T(8,128)S(1)} collective-permute-done((f32[256,128]{1,0:T(8,128)S(1)}, f32[256,128]{1,0:T(8,128)S(1)}, u32[]{:S(2)}, u32[]{:S(2)}) %collective-permute-start.7) | collective-permute-done | bytes 131104 | tf_op jit(solution)/shard_map/cond/branch_1_fun/ppermute | solution.py:123
  22.3 1.6 %branch_1_fun.6 = f32[8,48,768]{2,1,0:T(8,128)} custom-call(s32[544,128]{1,0:T(8,128)S(1)} %copy-done.22, f32[4,64,768]{2,1,0:T(8,128)S(1)} %all-to-all-done.6.got_ref), custom_call_target="tpu_custom_call" | custom-call | tf_op jit(solution)/shard_map/cond/branch_1_fun/pallas_call | solution.py:403
  23.8 10.0 %all-to-all-start.7 = ((f32[8,48,768]{2,1,0:T(8,128)}), f32[8,48,768]{2,1,0:T(8,128)S(1)}, u32[]{:S(2)}, u32[]{:S(2)}) async-start(f32[8,48,768]{2,1,0:T(8,128)} %branch_1_fun.6), calls=%async_computation.7 | async-start | bytes 2359296 | tf_op jit(solution)/shard_map/cond/branch_1_fun/all_to_all | solution.py:433
  36.2 2.9 %collective-permute-start.10 = (f32[256,128]{1,0:T(8,128)S(1)}, f32[256,128]{1,0:T(8,128)S(1)}, u32[]{:S(2)}, u32[]{:S(2)}) collective-permute-start(f32[256,128]{1,0:T(8,128)S(1)} %maximum_select_fusion.1.near_ref), channel_id=1, source_target_pairs={{0,2},{1,3},{2,0},{3,1},{4,6},{5,7},{6,4},{7,5},{8,10},{9,11},{10,... | collective-permute-start | bytes 393224 | tf_op jit(solution)/shard_map/cond/branch_1_fun/ppermute | solution.py:138
  39.2 3.1 %collective-permute-done.10.across_ref = f32[256,128]{1,0:T(8,128)S(1)} collective-permute-done((f32[256,128]{1,0:T(8,128)S(1)}, f32[256,128]{1,0:T(8,128)S(1)}, u32[]{:S(2)}, u32[]{:S(2)}) %collective-permute-start.10) | collective-permute-done | bytes 131104 | tf_op jit(solution)/shard_map/cond/branch_1_fun/ppermute | solution.py:138
  42.3 3.7 %collective-permute-start.11 = (f32[256,256]{1,0:T(8,128)S(1)}, f32[256,256]{1,0:T(8,128)S(1)}, u32[]{:S(2)}, u32[]{:S(2)}) collective-permute-start(f32[256,256]{1,0:T(8,128)S(1)} %pad_maximum_fusion.6), channel_id=1, source_target_pairs={{0,1},{1,0},{2,3},{3,2},{4,5},{5,4},{6,7},{7,6},{8,9},{9,8},{10,11... | collective-permute-start | bytes 786440 | tf_op jit(solution)/shard_map/cond/branch_1_fun/ppermute | solution.py:140
  47.8 18.1 %all-to-all-done.7.got_ref = f32[8,48,768]{2,1,0:T(8,128)S(1)} async-done(((f32[8,48,768]{2,1,0:T(8,128)}), f32[8,48,768]{2,1,0:T(8,128)S(1)}, u32[]{:S(2)}, u32[]{:S(2)}) %all-to-all-start.7) | async-done | bytes 1179680 | tf_op jit(solution)/shard_map/cond/branch_1_fun/all_to_all | solution.py:433
  67.6 6.2 %collective-permute-start.13 = (f32[192,128]{1,0:T(8,128)S(1)}, f32[192,128]{1,0:T(8,128)S(1)}, u32[]{:S(2)}, u32[]{:S(2)}) collective-permute-start(f32[192,128]{1,0:T(8,128)S(1)} %get-tuple-element.47), channel_id=1, source_target_pairs={{0,12},{1,13},{2,14},{3,15},{16,28},{17,29},{18,30},{19,31},{32,44... | collective-permute-start | bytes 294920 | tf_op jit(solution)/shard_map/cond/branch_1_fun/ppermute | solution.py:123
  73.8 1.3 %collective-permute-start.12 = (f32[192,128]{1,0:T(8,128)S(1)}, f32[192,128]{1,0:T(8,128)S(1)}, u32[]{:S(2)}, u32[]{:S(2)}) collective-permute-start(f32[192,128]{1,0:T(8,128)S(1)} %get-tuple-element.47), channel_id=1, source_target_pairs={{0,4},{1,5},{2,6},{3,7},{16,20},{17,21},{18,22},{19,23},{32,36},{3... | collective-permute-start | bytes 294920 | tf_op jit(solution)/shard_map/cond/branch_1_fun/ppermute | solution.py:122
  75.1 4.2 %all-to-all-start.8 = ((f32[4,128,768]{2,1,0:T(8,128)}), f32[4,128,768]{2,1,0:T(8,128)S(1)}, u32[]{:S(2)}, u32[]{:S(2)}) async-start(f32[4,128,768]{2,1,0:T(8,128)} %copy-done), calls=%async_computation.8 | async-start | bytes 3145728 | tf_op jit(solution)/shard_map/cond/branch_1_fun/all_to_all | solution.py:433
  80.8 1.9 %collective-permute-start.16 = (f32[192,128]{1,0:T(8,128)S(1)}, f32[192,128]{1,0:T(8,128)S(1)}, u32[]{:S(2)}, u32[]{:S(2)}) collective-permute-start(f32[192,128]{1,0:T(8,128)S(1)} %maximum_select_fusion.2.near_ref), channel_id=1, source_target_pairs={{0,2},{1,3},{2,0},{3,1},{4,6},{5,7},{6,4},{7,5},{8,10},{9,11},{10,... | collective-permute-start | bytes 294920 | tf_op jit(solution)/shard_map/cond/branch_1_fun/ppermute | solution.py:138
  82.8 3.7 %collective-permute-done.16.across_ref = f32[192,128]{1,0:T(8,128)S(1)} collective-permute-done((f32[192,128]{1,0:T(8,128)S(1)}, f32[192,128]{1,0:T(8,128)S(1)}, u32[]{:S(2)}, u32[]{:S(2)}) %collective-permute-start.16) | collective-permute-done | bytes 98336 | tf_op jit(solution)/shard_map/cond/branch_1_fun/ppermute | solution.py:138
  86.5 4.0 %collective-permute-start.17 = (f32[192,256]{1,0:T(8,128)S(1)}, f32[192,256]{1,0:T(8,128)S(1)}, u32[]{:S(2)}, u32[]{:S(2)}) collective-permute-start(f32[192,256]{1,0:T(8,128)S(1)} %pad_maximum_fusion.7), channel_id=1, source_target_pairs={{0,1},{1,0},{2,3},{3,2},{4,5},{5,4},{6,7},{7,6},{8,9},{9,8},{10,11... | collective-permute-start | bytes 589832 | tf_op jit(solution)/shard_map/cond/branch_1_fun/ppermute | solution.py:140
  91.6 4.9 %collective-permute-start.20 = (f32[128,384]{1,0:T(8,128)S(1)}, f32[128,384]{1,0:T(8,128)S(1)}, u32[]{:S(2)}, u32[]{:S(2)}) collective-permute-start(f32[128,384]{1,0:T(8,128)S(1)} %get-tuple-element.48.home_ref), channel_id=1, source_target_pairs={{0,384},{16,400},{32,416},{48,432},{64,448},{80,464},{96,480},{112... | collective-permute-start | bytes 589832 | tf_op jit(solution)/shard_map/cond/branch_1_fun/ppermute | solution.py:455
  96.5 2.5 %collective-permute-start.19 = (f32[128,384]{1,0:T(8,128)S(1)}, f32[128,384]{1,0:T(8,128)S(1)}, u32[]{:S(2)}, u32[]{:S(2)}) collective-permute-start(f32[128,384]{1,0:T(8,128)S(1)} %get-tuple-element.48.home_ref), channel_id=1, source_target_pairs={{0,256},{16,272},{32,288},{48,304},{64,320},{80,336},{96,352},{112... | collective-permute-start | bytes 589832 | tf_op jit(solution)/shard_map/cond/branch_1_fun/ppermute | solution.py:455
  99.0 2.5 %collective-permute-start.18 = (f32[128,384]{1,0:T(8,128)S(1)}, f32[128,384]{1,0:T(8,128)S(1)}, u32[]{:S(2)}, u32[]{:S(2)}) collective-permute-start(f32[128,384]{1,0:T(8,128)S(1)} %get-tuple-element.48.home_ref), channel_id=1, source_target_pairs={{0,128},{16,144},{32,160},{48,176},{64,192},{80,208},{96,224},{112... | collective-permute-start | bytes 589832 | tf_op jit(solution)/shard_map/cond/branch_1_fun/ppermute | solution.py:455
  103.6 2.1 %collective-permute-done.19.two_ref = f32[128,384]{1,0:T(8,128)S(1)} collective-permute-done((f32[128,384]{1,0:T(8,128)S(1)}, f32[128,384]{1,0:T(8,128)S(1)}, u32[]{:S(2)}, u32[]{:S(2)}) %collective-permute-start.19) | collective-permute-done | bytes 196640 | tf_op jit(solution)/shard_map/cond/branch_1_fun/ppermute | solution.py:455
  106.4 4.4 %collective-permute-done.18.one_ref = f32[128,384]{1,0:T(8,128)S(1)} collective-permute-done((f32[128,384]{1,0:T(8,128)S(1)}, f32[128,384]{1,0:T(8,128)S(1)}, u32[]{:S(2)}, u32[]{:S(2)}) %collective-permute-start.18) | collective-permute-done | bytes 196640 | tf_op jit(solution)/shard_map/cond/branch_1_fun/ppermute | solution.py:455
  115.1 5.0 %branch_1_fun.11 = f32[256,768]{1,0:T(8,128)S(1)} custom-call(f32[128,384]{1,0:T(8,128)S(1)} %copy-done.13, f32[128,384]{1,0:T(8,128)S(1)} %copy-done.19, f32[128,384]{1,0:T(8,128)S(1)} %copy-done.17, f32[128,384]{1,0:T(8,128)S(1)} %copy-done.15, f32[512,768]{1,0:T(8,128)S(1)} %bitcast.18, f32[256,512]{1,0:T(8,128)S(1)} %branch_1_fun.9.left_ref, ...), custom_call_target="tpu_custom_call" | custom-call | tf_op jit(solution)/shard_map/cond/branch_1_fun/pallas_call | solution.py:416
  (68 shorter events, 17.9 us)
Async XLA Ops:
  4.6 17.7 %copy-start.22 = (s32[544,128]{1,0:T(8,128)S(1)}, s32[544,128]{1,0:T(8,128)}, u32[]{:S(2)}) copy-start(s32[544,128]{1,0:T(8,128)} %get-tuple-element.40.plan_ref) | copy-start | bytes 835588 | tf_op jit(solution)/shard_map/cond
  4.6 17.7 %all-to-all-start.6 = ((f32[4,64,768]{2,1,0:T(8,128)}), f32[4,64,768]{2,1,0:T(8,128)S(1)}, u32[]{:S(2)}, u32[]{:S(2)}) async-start(f32[4,64,768]{2,1,0:T(8,128)} %bitcast.24), calls=%async_computation.6 | async-start | bytes 1572864 | tf_op jit(solution)/shard_map/cond/branch_1_fun/all_to_all | solution.py:433
  10.5 11.8 %collective-permute-start.7 = (f32[256,128]{1,0:T(8,128)S(1)}, f32[256,128]{1,0:T(8,128)S(1)}, u32[]{:S(2)}, u32[]{:S(2)}) collective-permute-start(f32[256,128]{1,0:T(8,128)S(1)} %slice.42), channel_id=1, source_target_pairs={{0,12},{1,13},{2,14},{3,15},{16,28},{17,29},{18,30},{19,31},{32,44... | collective-permute-start | bytes 393224 | tf_op jit(solution)/shard_map/cond/branch_1_fun/ppermute | solution.py:123
  16.4 5.9 %collective-permute-start.6 = (f32[256,128]{1,0:T(8,128)S(1)}, f32[256,128]{1,0:T(8,128)S(1)}, u32[]{:S(2)}, u32[]{:S(2)}) collective-permute-start(f32[256,128]{1,0:T(8,128)S(1)} %slice.42), channel_id=1, source_target_pairs={{0,4},{1,5},{2,6},{3,7},{16,20},{17,21},{18,22},{19,23},{32,36},{3... | collective-permute-start | bytes 393224 | tf_op jit(solution)/shard_map/cond/branch_1_fun/ppermute | solution.py:122
  23.8 42.1 %all-to-all-start.7 = ((f32[8,48,768]{2,1,0:T(8,128)}), f32[8,48,768]{2,1,0:T(8,128)S(1)}, u32[]{:S(2)}, u32[]{:S(2)}) async-start(f32[8,48,768]{2,1,0:T(8,128)} %branch_1_fun.6), calls=%async_computation.7 | async-start | bytes 2359296 | tf_op jit(solution)/shard_map/cond/branch_1_fun/all_to_all | solution.py:433
  34.8 1.4 %collective-permute-start.8 = (f32[128,128]{1,0:T(8,128)S(1)}, f32[128,128]{1,0:T(8,128)S(1)}, u32[]{:S(2)}, u32[]{:S(2)}) collective-permute-start(f32[128,128]{1,0:T(8,128)S(1)} %get-tuple-element.65), channel_id=1, source_target_pairs={{4,8},{5,9},{6,10},{7,11},{20,24},{21,25},{22,26},{23,27},{36,40},... | collective-permute-start | bytes 196616 | tf_op jit(solution)/shard_map/cond/branch_1_fun/ppermute | solution.py:134
  35.5 0.7 collective-permute-start.9
  36.2 6.1 %collective-permute-start.10 = (f32[256,128]{1,0:T(8,128)S(1)}, f32[256,128]{1,0:T(8,128)S(1)}, u32[]{:S(2)}, u32[]{:S(2)}) collective-permute-start(f32[256,128]{1,0:T(8,128)S(1)} %maximum_select_fusion.1.near_ref), channel_id=1, source_target_pairs={{0,2},{1,3},{2,0},{3,1},{4,6},{5,7},{6,4},{7,5},{8,10},{9,11},{10,... | collective-permute-start | bytes 393224 | tf_op jit(solution)/shard_map/cond/branch_1_fun/ppermute | solution.py:138
  42.3 4.8 %collective-permute-start.11 = (f32[256,256]{1,0:T(8,128)S(1)}, f32[256,256]{1,0:T(8,128)S(1)}, u32[]{:S(2)}, u32[]{:S(2)}) collective-permute-start(f32[256,256]{1,0:T(8,128)S(1)} %pad_maximum_fusion.6), channel_id=1, source_target_pairs={{0,1},{1,0},{2,3},{3,2},{4,5},{5,4},{6,7},{7,6},{8,9},{9,8},{10,11... | collective-permute-start | bytes 786440 | tf_op jit(solution)/shard_map/cond/branch_1_fun/ppermute | solution.py:140
  67.6 11.7 %collective-permute-start.13 = (f32[192,128]{1,0:T(8,128)S(1)}, f32[192,128]{1,0:T(8,128)S(1)}, u32[]{:S(2)}, u32[]{:S(2)}) collective-permute-start(f32[192,128]{1,0:T(8,128)S(1)} %get-tuple-element.47), channel_id=1, source_target_pairs={{0,12},{1,13},{2,14},{3,15},{16,28},{17,29},{18,30},{19,31},{32,44... | collective-permute-start | bytes 294920 | tf_op jit(solution)/shard_map/cond/branch_1_fun/ppermute | solution.py:123
  73.8 5.5 %collective-permute-start.12 = (f32[192,128]{1,0:T(8,128)S(1)}, f32[192,128]{1,0:T(8,128)S(1)}, u32[]{:S(2)}, u32[]{:S(2)}) collective-permute-start(f32[192,128]{1,0:T(8,128)S(1)} %get-tuple-element.47), channel_id=1, source_target_pairs={{0,4},{1,5},{2,6},{3,7},{16,20},{17,21},{18,22},{19,23},{32,36},{3... | collective-permute-start | bytes 294920 | tf_op jit(solution)/shard_map/cond/branch_1_fun/ppermute | solution.py:122
  75.1 36.4 %all-to-all-start.8 = ((f32[4,128,768]{2,1,0:T(8,128)}), f32[4,128,768]{2,1,0:T(8,128)S(1)}, u32[]{:S(2)}, u32[]{:S(2)}) async-start(f32[4,128,768]{2,1,0:T(8,128)} %copy-done), calls=%async_computation.8 | async-start | bytes 3145728 | tf_op jit(solution)/shard_map/cond/branch_1_fun/all_to_all | solution.py:433
  79.2 22.2 %copy-start.21 = (f32[256,768]{1,0:T(8,128)S(1)}, f32[256,768]{1,0:T(8,128)}, u32[]{:S(2)}) copy-start(f32[256,768]{1,0:T(8,128)} %get-tuple-element.42.a_ref) | copy-start | bytes 2359300 | tf_op jit(solution)/shard_map/cond
  79.2 22.2 %copy-start.23 = (s32[544,128]{1,0:T(8,128)S(1)}, s32[544,128]{1,0:T(8,128)}, u32[]{:S(2)}) copy-start(s32[544,128]{1,0:T(8,128)} %get-tuple-element.40.plan_ref) | copy-start | bytes 835588 | tf_op jit(solution)/shard_map/cond
  79.3 1.5 %collective-permute-start.14 = (f32[96,128]{1,0:T(8,128)S(1)}, f32[96,128]{1,0:T(8,128)S(1)}, u32[]{:S(2)}, u32[]{:S(2)}) collective-permute-start(f32[96,128]{1,0:T(8,128)S(1)} %get-tuple-element.67), channel_id=1, source_target_pairs={{4,8},{5,9},{6,10},{7,11},{20,24},{21,25},{22,26},{23,27},{36,40},... | collective-permute-start | bytes 147464 | tf_op jit(solution)/shard_map/cond/branch_1_fun/ppermute | solution.py:134
  80.1 0.7 collective-permute-start.15
  80.8 5.7 %collective-permute-start.16 = (f32[192,128]{1,0:T(8,128)S(1)}, f32[192,128]{1,0:T(8,128)S(1)}, u32[]{:S(2)}, u32[]{:S(2)}) collective-permute-start(f32[192,128]{1,0:T(8,128)S(1)} %maximum_select_fusion.2.near_ref), channel_id=1, source_target_pairs={{0,2},{1,3},{2,0},{3,1},{4,6},{5,7},{6,4},{7,5},{8,10},{9,11},{10,... | collective-permute-start | bytes 294920 | tf_op jit(solution)/shard_map/cond/branch_1_fun/ppermute | solution.py:138
  86.5 15.5 %copy-start.4 = (f32[256,128]{1,0:T(8,128)S(1)}, f32[256,128]{1,0:T(8,128)}, u32[]{:S(2)}) copy-start(f32[256,128]{1,0:T(8,128)} %copy-done.3) | copy-start | bytes 393220 | tf_op jit(solution)/shard_map/cond
  86.5 15.5 %copy-start.9 = (f32[256,128]{1,0:T(8,128)S(1)}, f32[256,128]{1,0:T(8,128)}, u32[]{:S(2)}) copy-start(f32[256,128]{1,0:T(8,128)} %copy-done.8) | copy-start | bytes 393220 | tf_op jit(solution)/shard_map/cond
  86.5 15.5 %copy-start.11 = (f32[256,256]{1,0:T(8,128)S(1)}, f32[256,256]{1,0:T(8,128)}, u32[]{:S(2)}) copy-start(f32[256,256]{1,0:T(8,128)} %copy-done.10) | copy-start | bytes 786436 | tf_op jit(solution)/shard_map/cond
  86.5 5.0 %collective-permute-start.17 = (f32[192,256]{1,0:T(8,128)S(1)}, f32[192,256]{1,0:T(8,128)S(1)}, u32[]{:S(2)}, u32[]{:S(2)}) collective-permute-start(f32[192,256]{1,0:T(8,128)S(1)} %pad_maximum_fusion.7), channel_id=1, source_target_pairs={{0,1},{1,0},{2,3},{3,2},{4,5},{5,4},{6,7},{7,6},{8,9},{9,8},{10,11... | collective-permute-start | bytes 589832 | tf_op jit(solution)/shard_map/cond/branch_1_fun/ppermute | solution.py:140
  91.6 11.3 %collective-permute-start.20 = (f32[128,384]{1,0:T(8,128)S(1)}, f32[128,384]{1,0:T(8,128)S(1)}, u32[]{:S(2)}, u32[]{:S(2)}) collective-permute-start(f32[128,384]{1,0:T(8,128)S(1)} %get-tuple-element.48.home_ref), channel_id=1, source_target_pairs={{0,384},{16,400},{32,416},{48,432},{64,448},{80,464},{96,480},{112... | collective-permute-start | bytes 589832 | tf_op jit(solution)/shard_map/cond/branch_1_fun/ppermute | solution.py:455
  96.5 9.2 %collective-permute-start.19 = (f32[128,384]{1,0:T(8,128)S(1)}, f32[128,384]{1,0:T(8,128)S(1)}, u32[]{:S(2)}, u32[]{:S(2)}) collective-permute-start(f32[128,384]{1,0:T(8,128)S(1)} %get-tuple-element.48.home_ref), channel_id=1, source_target_pairs={{0,256},{16,272},{32,288},{48,304},{64,320},{80,336},{96,352},{112... | collective-permute-start | bytes 589832 | tf_op jit(solution)/shard_map/cond/branch_1_fun/ppermute | solution.py:455
  99.0 11.8 %collective-permute-start.18 = (f32[128,384]{1,0:T(8,128)S(1)}, f32[128,384]{1,0:T(8,128)S(1)}, u32[]{:S(2)}, u32[]{:S(2)}) collective-permute-start(f32[128,384]{1,0:T(8,128)S(1)} %get-tuple-element.48.home_ref), channel_id=1, source_target_pairs={{0,128},{16,144},{32,160},{48,176},{64,192},{80,208},{96,224},{112... | collective-permute-start | bytes 589832 | tf_op jit(solution)/shard_map/cond/branch_1_fun/ppermute | solution.py:455
  (13 other events, 32.9 us)

commit v5 on v4

--- a/solution.py
+++ b/solution.py
@@ -13,6 +13,7 @@
 ROWS = 256
 COLS = 768
 REST = COLS - NB
+WIDE = TOP + COLS
 KERNEL_VMEM = 20 << 20
 FACTOR_VMEM = 28 << 20
 BF = jnp.bfloat16
@@ -276,24 +277,46 @@
     over_ref[...] = jnp.broadcast_to(over, (8, NB)).astype(jnp.int32)
 
 
-def turn_kernel(plan_ref, got_ref, send_ref):
+def turn_kernel(plan_ref, got_ref, first_ref, rest_ref):
     got = got_ref[...].reshape(256, COLS)
     rows = select_rows(onehot_of(plan_ref[0:32, :1], 256), got)
     moved = plan_ref[32:160, :1]
     moved = jnp.where(moved < 0, -1, moved + 16)
     sent = select_rows(onehot_of(moved, 64), got[:64])
     for n in range(8):
-        send_ref[n, 0:32, :] = rows
-        send_ref[n, 32:48, :] = sent[n * 16 : n * 16 + 16]
-
-
-def panel_kernel(plan_ref, got_ref, send_ref, lead_ref):
+        first_ref[n, 0:32, :] = rows[:, :NB]
+        rest_ref[n, 0:32, :] = rows[:, NB:]
+        first_ref[n, 32:48, :] = sent[n * 16 : n * 16 + 16, :NB]
+        rest_ref[n, 32:48, :] = sent[n * 16 : n * 16 + 16, NB:]
+
+
+def lead_kernel(plan_ref, got_ref, lead_ref):
+    got = jnp.concatenate([got_ref[n, 0:32, :] for n in range(8)], axis=0)
+    lead_ref[0:NB, :] = select_rows(onehot_of(plan_ref[160:288, :1], 256), got)
+    for n in range(4):
+        lead_ref[NB + n * 16 : NB + n * 16 + 16, :] = got_ref[n, 32:48, :]
+
+
+def panel_kernel(plan_ref, lead_ref, got_ref, near_ref, across_ref, pair_ref, send_ref, moved_ref):
+    panel = lax.axis_index("prow") >> 3
     got = jnp.concatenate([got_ref[n, 0:32, :] for n in range(8)], axis=0)
     rows = select_rows(onehot_of(plan_ref[160:288, :1], 256), got)
     for n in range(4):
-        send_ref[n] = rows
-        lead_ref[NB + n * 16 : NB + n * 16 + 16, :] = got_ref[n, 32:48, :NB]
-    lead_ref[0:NB, :] = rows[:, :NB]
+        send_ref[n, :, :NB] = lead_ref[0:NB, :]
+        send_ref[n, :, NB:COLS] = rows
+
+    def store_send(index, value):
+        @pl.when(index != panel)
+        def _():
+            spot = lane_block(COLS // NB + jnp.where(index < panel, index, index - 1))
+            for n in range(4):
+                send_ref[n, :, spot] = value
+
+    def store_moved(index, value):
+        moved_ref[:, lane_block(index)] = value
+
+    put_columns(near_ref, across_ref, pair_ref, slice(0, NB), store_send)
+    put_columns(near_ref, across_ref, pair_ref, slice(NB, NB + 64), store_moved)
 
 
 def put_columns(near_ref, across_ref, pair_ref, rows, store):
@@ -308,24 +331,10 @@
     return pl.ds(pl.multiple_of(index * NB, NB), NB)
 
 
-def corner_kernel(near_ref, across_ref, pair_ref, send_ref, moved_ref):
-    panel = lax.axis_index("prow") >> 3
-
-    def store_send(index, value):
-        @pl.when(index != panel)
-        def _():
-            send_ref[:, lane_block(jnp.where(index < panel, index, index - 1))] = value
-
-    def store_moved(index, value):
-        moved_ref[:, lane_block(index)] = value
-
-    put_columns(near_ref, across_ref, pair_ref, slice(0, NB), store_send)
-    put_columns(near_ref, across_ref, pair_ref, slice(NB, NB + 64), store_moved)
-
-
-def own_rows_kernel(plan_ref, got_ref, a_ref, out_ref):
+def own_rows_kernel(plan_ref, lead_ref, got_ref, a_ref, out_ref):
     slot = plan_ref[288:544, :1]
-    moved = jnp.concatenate([got_ref[n, 32:48, :] for n in range(4)], axis=0)
+    rest = jnp.concatenate([got_ref[n, 32:48, :] for n in range(4)], axis=0)
+    moved = jnp.concatenate([lead_ref[NB : NB + 64, :], rest], axis=1)
     out_ref[...] = jnp.where(slot >= 0, select_rows(onehot_of(slot, 64), moved), a_ref[...])
 
 
@@ -341,22 +350,22 @@
 
 
 def factor_kernel(
-    home_ref, one_ref, two_ref, three_ref, own_ref, left_ref, right_ref, lower_ref, upper_ref,
-    out_ref, z_ref, y_ref, m_ref, u_ref, d_ref,
+    top_ref, left_ref, right_ref, lower_ref, upper_ref, out_ref, z_ref, y_ref, m_ref, u_ref, d_ref
 ):
     prow = lax.axis_index("prow")
     pcol = lax.axis_index("pcol")
-    for n, ref in enumerate((home_ref, one_ref, two_ref, three_ref)):
-        panel = ((prow >> 3) - n) & 3
-        rows = pl.ds(pl.multiple_of(panel * NB, NB), NB)
+    for k in range(PANELS):
+        rows = slice(k * NB, k * NB + NB)
         for spot in range(PANELS - 1):
-            block = jnp.where(spot < panel, spot, spot + 1)
-            z_ref[rows, lane_block(block)] = ref[:, spot * NB : spot * NB + NB]
+            block = spot if spot < k else spot + 1
+            z_ref[rows, block * NB : block * NB + NB] = top_ref[
+                rows, COLS + spot * NB : COLS + spot * NB + NB
+            ]
     z_ref[TOP:, :] = left_ref[...]
     for k in range(PANELS):
         s = k * NB
         e = s + NB
-        before = own_ref if k == 0 else y_ref
+        before = top_ref if k == 0 else y_ref
         multipliers = dot3(z_ref[e:, s:e], upper_ref[k])
         z_ref[e:, s:e] = multipliers
         mh, ml = split2(multipliers)
@@ -371,14 +380,14 @@
             uh, ul = split2(corner)
             z_ref[e:, e:] = z_ref[e:, e:] - mm(m3, jnp.concatenate([uh, uh, ul], axis=0))
         d_ref[s:e, :] = before[s:e, :NB]
-        bh, bl = split2(before[s:e, :])
+        bh, bl = split2(before[s:e, :COLS])
         upper_rows = mm(l3, jnp.concatenate([bh, bh, bl], axis=0))
         y_ref[s:e, :] = upper_rows
         uh, ul = split2(upper_rows)
         u3 = jnp.concatenate([uh, uh, ul], axis=0)
         u_ref[3 * s : 3 * e, :] = u3
         if e < TOP:
-            y_ref[e:TOP, :] = before[e:TOP, :] - mm(m3[: TOP - e], u3)
+            y_ref[e:TOP, :] = before[e:TOP, :COLS] - mm(m3[: TOP - e], u3)
     out_ref[...] = right_ref[...] - mm(m_ref[...], u_ref[...])
     panel_cols = lane_block(pcol & 3)
     top_rows = pl.ds(pl.multiple_of((prow & 3) * NB, NB), NB)
@@ -435,48 +444,35 @@
 
 def slotted(send, plan, matrix, lower_inverse, upper_inverse):
     pcol = lax.axis_index("pcol")
+    got = along(send.reshape(4, 64, COLS), X_GROUPS)
+    first, rest = kernel_call(turn_kernel, [((8, 48, NB), F32), ((8, 48, REST), F32)])(plan, got)
+    first = along(first, Z_GROUPS)
+    rest = along(rest, Z_GROUPS)
+    (lead,) = kernel_call(lead_kernel, [((NB + 64, NB), F32)])(plan, first)
+    ends = spread_start(lead)
+    late = spread_rest(lead, *ends, pcol)
+    send, moved = kernel_call(
+        panel_kernel, [((4, NB, WIDE - NB), F32), ((64, TOP), F32)]
+    )(plan, lead, rest, *late)
+    top = along(send, X_GROUPS).reshape(TOP, WIDE - NB)
     block = matrix[:, :NB]
     ends = spread_start(block)
-    got = along(send.reshape(4, 64, COLS), X_GROUPS)
-    got, ends = lax.optimization_barrier((got, ends))
-    (send,) = kernel_call(turn_kernel, [((8, 48, COLS), F32)])(plan, got)
     raw = spread_rest(block, *ends, pcol)
-    got = along(send, Z_GROUPS)
-    got, raw = lax.optimization_barrier((got, raw))
-    send, lead = kernel_call(panel_kernel, [((4, NB, COLS), F32), ((NB + 64, NB), F32)])(plan, got)
-    own = along(send, X_GROUPS).reshape(TOP, COLS)
-    ends = spread_start(lead)
-    near, across, pair = spread_rest(lead, *ends, pcol)
-    (right,) = kernel_call(own_rows_kernel, [((ROWS, COLS), F32)])(plan, got, matrix)
-    home, moved = kernel_call(corner_kernel, [((NB, TOP - NB), F32), ((64, TOP), F32)])(
-        near, across, pair
-    )
-    others = [
-        lax.ppermute(home, "prow", [(p, (p + 8 * n) % PROW) for p in range(PROW)])
-        for n in range(1, 4)
-    ]
+    (right,) = kernel_call(own_rows_kernel, [((ROWS, COLS), F32)])(plan, lead, rest, matrix)
     (left,) = kernel_call(panel_rows_kernel, [((ROWS, TOP), F32)])(plan, moved, *raw)
-    return factor(home, *others, own, left, right, lower_inverse, upper_inverse)
+    return factor(top, left, right, lower_inverse, upper_inverse)
 
 
 def dense_rows_kernel(
-    origin_ref, gathered_ref, a_ref, own_ref, near_ref, across_ref, pair_ref,
-    home_ref, one_ref, two_ref, three_ref, top_ref, left_ref, right_ref,
+    origin_ref, gathered_ref, a_ref, own_ref, near_ref, across_ref, pair_ref, top_ref, left_ref, right_ref
 ):
-    x = lax.axis_index("prow") >> 3
-
     def store_corner(index, value):
-        for n, ref in enumerate((home_ref, one_ref, two_ref, three_ref)):
-            panel = (x - n) & 3
-
-            @pl.when(index != panel)
+        for k in range(PANELS):
+
+            @pl.when(index != k)
             def _():
-                spot = lane_block(jnp.where(index < panel, index, index - 1))
-                for k in range(PANELS):
-
-                    @pl.when(panel == k)
-                    def _():
-                        ref[:, spot] = value[k * NB : k * NB + NB]
+                spot = lane_block(COLS // NB + jnp.where(index < k, index, index - 1))
+                top_ref[k * NB : k * NB + NB, spot] = value[k * NB : k * NB + NB]
 
     def store_left(index, value):
         left_ref[:, lane_block(index)] = value
@@ -486,7 +482,7 @@
     top_ref[:, :NB] = own_ref[:TOP, :]
     right_ref[:, :NB] = own_ref[TOP:, :]
     for unit in range(PROW):
-        top_ref[unit * 16 : unit * 16 + 16, NB:] = gathered_ref[unit * 32 : unit * 32 + 16, :]
+        top_ref[unit * 16 : unit * 16 + 16, NB:COLS] = gathered_ref[unit * 32 : unit * 32 + 16, :]
     origin = origin_ref[:, :1]
 
     @pl.loop(0, REST // NB)
@@ -514,11 +510,11 @@
     (own,) = kernel_call(column_kernel, [((TOP + ROWS, NB), F32)])(origin, gathered_first, matrix)
     near, across, pair = spread_columns(own, pcol)
     gathered_rest = exchange_rest(picked_rest, matrix[:NB, NB:])
-    *corners, top, left, right = kernel_call(
+    top, left, right = kernel_call(
         dense_rows_kernel,
-        [((NB, TOP - NB), F32)] * 4 + [((TOP, COLS), F32), ((ROWS, TOP), F32), ((ROWS, COLS), F32)],
+        [((TOP, WIDE - NB), F32), ((ROWS, TOP), F32), ((ROWS, COLS), F32)],
     )(origin, gathered_rest, matrix, own, near, across, pair)
-    return factor(*corners, top, left, right, lower_inverse, upper_inverse)
+    return factor(top, left, right, lower_inverse, upper_inverse)
 
 
 def per_device(matrix, pivots, lower_inverse, upper_inverse):

time: 123 us -> 116 us (0.943)
  the two profiles are of different devices: /device:TPU:1 before, /device:TPU:43 now
where the time goes in v5:
time: 116 us
  starting transfers between devices  37.9 us (33%)
  blocking collectives  33.1 us (29%)
  waiting for transfers between devices  23.8 us (21%)
  Pallas kernels  11.4 us (10%)
  local copies, waits for them, and re-layouts  7.2 us (6%)
    all_to_all x2, blocking collectives, along(): return lax.all_to_all(value, 'prow', 0, 0, axis_index_groups=groups)  33.1 us
    ppermute x2, waiting for transfers between devices, spread_rest(): left = lax.ppermute(near[:half], 'pcol', [(q + 4, q + 8) for q in range(4)])  15.9 us
    ppermute x2, starting transfers between devices, spread_rest(): pair = lax.ppermute(both, 'pcol', [(q, q ^ 1) for q in range(PCOL)])  15.6 us
    all_to_all x2, starting transfers between devices, along(): return lax.all_to_all(value, 'prow', 0, 0, axis_index_groups=groups)  8.51 us
    ppermute x2, waiting for transfers between devices, spread_rest(): across = lax.ppermute(near, 'pcol', [(q, q ^ 2) for q in range(PCOL)])  6.85 us
    pallas_call x6, Pallas kernels, call(): pl.pallas_call(body, in_specs=[VMEM] * len(args), out_specs=[VMEM] * len(...  6.51 us
    ppermute x2, starting transfers between devices, spread_rest(): across = lax.ppermute(near, 'pcol', [(q, q ^ 2) for q in range(PCOL)])  5.91 us
    pallas_call x1, Pallas kernels, factor(): pl.pallas_call(factor_kernel, in_specs=[VMEM] * len(args), out_specs=VMEM...  4.88 us
  transfers between devices with their start and end apart: 14, of which 5 were waited for; matrix products, arithmetic and copies ran while one was open for 2% of the time, Pallas kernels for 1%

profile of v5, /device:TPU:43, one launch (start us, length us, event | category | flops | bytes accessed | tf_op | source)
XLA Modules:
  0.0 115.7 jit_solution(5289726087104725169)
XLA Ops:
  0.0 3.4 %shard_map.48 = (f32[256,768]{1,0:T(8,128)}, s32[544,128]{1,0:T(8,128)}, s32[8,128]{1,0:T(8,128)S(1)}) custom-call(s32[4,128]{1,0:T(4,128)} %bitcast.28, f32[256,768]{1,0:T(8,128)} %a_ref.1), custom_call_target="tpu_custom_call" | custom-call | tf_op jit(solution)/shard_map/pallas_call | solution.py:412
  4.5 110.3 %conditional.1 = (f32[256,768]{1,0:T(8,128)S(1)}) conditional(s32[]{:T(128)} %bitcast.16, (s32[512]{0:T(512)}, f32[256,768]{1,0:T(8,128)}, f32[4,128,128]{2,1,0:T(8,128)}, f32[4,128,128]{2,1,0:T(8,128)}) %tuple.11, (f32[256,768]{1,0:T(8,128)}, s32[544,128]{1,0:T(8,128)}, f32[256,768]{1,0:T(8,128)}, f32[4,128,128]{2,1,0:T(8,128)}, ...), branch_computations={%region_0.4_spmd, %region_4.5_spmd} | conditional | flops 1589260 | bytes 65065812 | solution.py:526
  4.6 14.7 %all_to_all.40.got_ref = f32[4,64,768]{2,1,0:T(8,128)S(1)} all-to-all(f32[4,64,768]{2,1,0:T(8,128)} %bitcast.24), channel_id=1, replica_groups={{0,128,256,384},{16,144,272,400},{32,160,288,416},{48,176,304,432},{64,..., dimensions={0} | all-to-all | bytes 1572864 | tf_op jit(solution)/shard_map/cond/branch_1_fun/all_to_all | solution.py:442
  19.2 1.5 %branch_1_fun.6 = (f32[8,48,128]{2,1,0:T(8,128)S(1)}, f32[8,48,640]{2,1,0:T(8,128)}) custom-call(s32[544,128]{1,0:T(8,128)S(1)} %copy-done.14, f32[4,64,768]{2,1,0:T(8,128)S(1)} %all_to_all.40.got_ref), custom_call_target="tpu_custom_call" | custom-call | tf_op jit(solution)/shard_map/cond/branch_1_fun/pallas_call | solution.py:412
  20.7 18.5 %all_to_all.41.got_ref = f32[8,48,128]{2,1,0:T(8,128)S(1)} all-to-all(f32[8,48,128]{2,1,0:T(8,128)S(1)} %get-tuple-element.38), channel_id=1, replica_groups={{0,16,32,48,64,80,96,112},{128,144,160,176,192,208,224,240},{256,272,28..., dimensions={0} | all-to-all | bytes 393216 | tf_op jit(solution)/shard_map/cond/branch_1_fun/all_to_all | solution.py:442
  39.2 3.7 %all-to-all-start.8 = ((f32[8,48,640]{2,1,0:T(8,128)}), f32[8,48,640]{2,1,0:T(8,128)S(1)}, u32[]{:S(2)}, u32[]{:S(2)}) async-start(f32[8,48,640]{2,1,0:T(8,128)} %get-tuple-element.39), calls=%async_computation.8 | async-start | bytes 1966080 | tf_op jit(solution)/shard_map/cond/branch_1_fun/all_to_all | solution.py:442
  44.6 1.3 %collective-permute-start.8 = (f32[96,128]{1,0:T(8,128)S(1)}, f32[96,128]{1,0:T(8,128)S(1)}, u32[]{:S(2)}, u32[]{:S(2)}) collective-permute-start(f32[96,128]{1,0:T(8,128)S(1)} %get-tuple-element.56), channel_id=1, source_target_pairs={{4,8},{5,9},{6,10},{7,11},{20,24},{21,25},{22,26},{23,27},{36,40},... | collective-permute-start | bytes 147464 | tf_op jit(solution)/shard_map/cond/branch_1_fun/ppermute | solution.py:135
  45.9 1.3 %collective-permute-start.9 = (f32[96,128]{1,0:T(8,128)S(1)}, f32[96,128]{1,0:T(8,128)S(1)}, u32[]{:S(2)}, u32[]{:S(2)}) collective-permute-start(f32[96,128]{1,0:T(8,128)S(1)} %get-tuple-element.57), channel_id=1, source_target_pairs={{12,8},{13,9},{14,10},{15,11},{28,24},{29,25},{30,26},{31,27},{44,... | collective-permute-start | bytes 147464 | tf_op jit(solution)/shard_map/cond/branch_1_fun/ppermute | solution.py:136
  47.2 10.0 %collective-permute-done.8 = f32[96,128]{1,0:T(8,128)S(1)} collective-permute-done((f32[96,128]{1,0:T(8,128)S(1)}, f32[96,128]{1,0:T(8,128)S(1)}, u32[]{:S(2)}, u32[]{:S(2)}) %collective-permute-start.8) | collective-permute-done | bytes 49184 | tf_op jit(solution)/shard_map/cond/branch_1_fun/ppermute | solution.py:135
  57.3 1.9 %collective-permute-start.10 = (f32[192,128]{1,0:T(8,128)S(1)}, f32[192,128]{1,0:T(8,128)S(1)}, u32[]{:S(2)}, u32[]{:S(2)}) collective-permute-start(f32[192,128]{1,0:T(8,128)S(1)} %maximum_select_fusion.2.near_ref), channel_id=1, source_target_pairs={{0,2},{1,3},{2,0},{3,1},{4,6},{5,7},{6,4},{7,5},{8,10},{9,11},{10,... | collective-permute-start | bytes 294920 | tf_op jit(solution)/shard_map/cond/branch_1_fun/ppermute | solution.py:139
  59.2 3.7 %collective-permute-done.10.across_ref = f32[192,128]{1,0:T(8,128)S(1)} collective-permute-done((f32[192,128]{1,0:T(8,128)S(1)}, f32[192,128]{1,0:T(8,128)S(1)}, u32[]{:S(2)}, u32[]{:S(2)}) %collective-permute-start.10) | collective-permute-done | bytes 98336 | tf_op jit(solution)/shard_map/cond/branch_1_fun/ppermute | solution.py:139
  62.9 7.5 %collective-permute-start.11 = (f32[192,256]{1,0:T(8,128)S(1)}, f32[192,256]{1,0:T(8,128)S(1)}, u32[]{:S(2)}, u32[]{:S(2)}) collective-permute-start(f32[192,256]{1,0:T(8,128)S(1)} %pad_maximum_fusion.7), channel_id=1, source_target_pairs={{0,1},{1,0},{2,3},{3,2},{4,5},{5,4},{6,7},{7,6},{8,9},{9,8},{10,11... | collective-permute-start | bytes 589832 | tf_op jit(solution)/shard_map/cond/branch_1_fun/ppermute | solution.py:141
  70.4 1.0 collective-permute-done.11.pair_ref
  71.9 1.4 %copy-done.2 = f32[4,128,1152]{2,1,0:T(8,128)} copy-done((f32[4,128,1152]{2,1,0:T(8,128)}, f32[4,128,1152]{2,1,0:T(8,128)S(1)}, u32[]{:S(2)}) %copy-start.2) | copy-done | bytes 2359320 | tf_op jit(solution)/shard_map/cond
  74.0 4.8 %all-to-all-start.9 = ((f32[4,128,1152]{2,1,0:T(8,128)}), f32[4,128,1152]{2,1,0:T(8,128)S(1)}, u32[]{:S(2)}, u32[]{:S(2)}) async-start(f32[4,128,1152]{2,1,0:T(8,128)} %copy-done.2), calls=%async_computation.9 | async-start | bytes 4718592 | tf_op jit(solution)/shard_map/cond/branch_1_fun/all_to_all | solution.py:442
  78.8 1.0 slice.44
  82.1 1.3 %collective-permute-start.14 = (f32[128,128]{1,0:T(8,128)S(1)}, f32[128,128]{1,0:T(8,128)S(1)}, u32[]{:S(2)}, u32[]{:S(2)}) collective-permute-start(f32[128,128]{1,0:T(8,128)S(1)} %get-tuple-element.54), channel_id=1, source_target_pairs={{4,8},{5,9},{6,10},{7,11},{20,24},{21,25},{22,26},{23,27},{36,40},... | collective-permute-start | bytes 196616 | tf_op jit(solution)/shard_map/cond/branch_1_fun/ppermute | solution.py:135
  83.4 1.3 %collective-permute-start.15 = (f32[128,128]{1,0:T(8,128)S(1)}, f32[128,128]{1,0:T(8,128)S(1)}, u32[]{:S(2)}, u32[]{:S(2)}) collective-permute-start(f32[128,128]{1,0:T(8,128)S(1)} %get-tuple-element.55), channel_id=1, source_target_pairs={{12,8},{13,9},{14,10},{15,11},{28,24},{29,25},{30,26},{31,27},{44,... | collective-permute-start | bytes 196616 | tf_op jit(solution)/shard_map/cond/branch_1_fun/ppermute | solution.py:136
  84.7 5.9 %collective-permute-done.14 = f32[128,128]{1,0:T(8,128)S(1)} collective-permute-done((f32[128,128]{1,0:T(8,128)S(1)}, f32[128,128]{1,0:T(8,128)S(1)}, u32[]{:S(2)}, u32[]{:S(2)}) %collective-permute-start.14) | collective-permute-done | bytes 65568 | tf_op jit(solution)/shard_map/cond/branch_1_fun/ppermute | solution.py:135
  90.7 4.0 %collective-permute-start.16 = (f32[256,128]{1,0:T(8,128)S(1)}, f32[256,128]{1,0:T(8,128)S(1)}, u32[]{:S(2)}, u32[]{:S(2)}) collective-permute-start(f32[256,128]{1,0:T(8,128)S(1)} %maximum_select_fusion.1.near_ref), channel_id=1, source_target_pairs={{0,2},{1,3},{2,0},{3,1},{4,6},{5,7},{6,4},{7,5},{8,10},{9,11},{10,... | collective-permute-start | bytes 393224 | tf_op jit(solution)/shard_map/cond/branch_1_fun/ppermute | solution.py:139
  94.7 3.1 %collective-permute-done.16.across_ref = f32[256,128]{1,0:T(8,128)S(1)} collective-permute-done((f32[256,128]{1,0:T(8,128)S(1)}, f32[256,128]{1,0:T(8,128)S(1)}, u32[]{:S(2)}, u32[]{:S(2)}) %collective-permute-start.16) | collective-permute-done | bytes 131104 | tf_op jit(solution)/shard_map/cond/branch_1_fun/ppermute | solution.py:139
  97.8 8.2 %collective-permute-start.17 = (f32[256,256]{1,0:T(8,128)S(1)}, f32[256,256]{1,0:T(8,128)S(1)}, u32[]{:S(2)}, u32[]{:S(2)}) collective-permute-start(f32[256,256]{1,0:T(8,128)S(1)} %pad_maximum_fusion.6), channel_id=1, source_target_pairs={{0,1},{1,0},{2,3},{3,2},{4,5},{5,4},{6,7},{7,6},{8,9},{9,8},{10,11... | collective-permute-start | bytes 786440 | tf_op jit(solution)/shard_map/cond/branch_1_fun/ppermute | solution.py:141
  108.7 1.0 copy-done.4
  109.7 4.9 %branch_1_fun.11 = f32[256,768]{1,0:T(8,128)S(1)} custom-call(f32[512,1152]{1,0:T(8,128)S(1)} %bitcast.18, f32[256,512]{1,0:T(8,128)S(1)} %copy-done.4, f32[256,768]{1,0:T(8,128)S(1)} %copy-done.1, f32[4,128,128]{2,1,0:T(8,128)} %get-tuple-element.43.lower_ref, f32[4,128,128]{2,1,0:T(8,128)} %get-tuple-element.44.upper_ref), custom_call_target="tpu_custom_call" | custom-call | tf_op jit(solution)/shard_map/cond/branch_1_fun/pallas_call | solution.py:425
  (46 shorter events, 9.1 us)
Async XLA Ops:
  4.6 14.7 %copy-start.14 = (s32[544,128]{1,0:T(8,128)S(1)}, s32[544,128]{1,0:T(8,128)}, u32[]{:S(2)}) copy-start(s32[544,128]{1,0:T(8,128)} %get-tuple-element.36.plan_ref) | copy-start | bytes 835588 | tf_op jit(solution)/shard_map/cond
  39.2 32.2 %all-to-all-start.8 = ((f32[8,48,640]{2,1,0:T(8,128)}), f32[8,48,640]{2,1,0:T(8,128)S(1)}, u32[]{:S(2)}, u32[]{:S(2)}) async-start(f32[8,48,640]{2,1,0:T(8,128)} %get-tuple-element.39), calls=%async_computation.8 | async-start | bytes 1966080 | tf_op jit(solution)/shard_map/cond/branch_1_fun/all_to_all | solution.py:442
  43.2 1.4 %collective-permute-start.7 = (f32[192,128]{1,0:T(8,128)S(1)}, f32[192,128]{1,0:T(8,128)S(1)}, u32[]{:S(2)}, u32[]{:S(2)}) collective-permute-start(f32[192,128]{1,0:T(8,128)S(1)} %branch_1_fun.7.lead_ref), channel_id=1, source_target_pairs={{0,12},{1,13},{2,14},{3,15},{16,28},{17,29},{18,30},{19,31},{32,44... | collective-permute-start | bytes 294920 | tf_op jit(solution)/shard_map/cond/branch_1_fun/ppermute | solution.py:124
  43.9 0.7 collective-permute-start.6
  44.6 12.6 %collective-permute-start.8 = (f32[96,128]{1,0:T(8,128)S(1)}, f32[96,128]{1,0:T(8,128)S(1)}, u32[]{:S(2)}, u32[]{:S(2)}) collective-permute-start(f32[96,128]{1,0:T(8,128)S(1)} %get-tuple-element.56), channel_id=1, source_target_pairs={{4,8},{5,9},{6,10},{7,11},{20,24},{21,25},{22,26},{23,27},{36,40},... | collective-permute-start | bytes 147464 | tf_op jit(solution)/shard_map/cond/branch_1_fun/ppermute | solution.py:135
  45.9 11.3 %collective-permute-start.9 = (f32[96,128]{1,0:T(8,128)S(1)}, f32[96,128]{1,0:T(8,128)S(1)}, u32[]{:S(2)}, u32[]{:S(2)}) collective-permute-start(f32[96,128]{1,0:T(8,128)S(1)} %get-tuple-element.57), channel_id=1, source_target_pairs={{12,8},{13,9},{14,10},{15,11},{28,24},{29,25},{30,26},{31,27},{44,... | collective-permute-start | bytes 147464 | tf_op jit(solution)/shard_map/cond/branch_1_fun/ppermute | solution.py:136
  57.3 5.7 %collective-permute-start.10 = (f32[192,128]{1,0:T(8,128)S(1)}, f32[192,128]{1,0:T(8,128)S(1)}, u32[]{:S(2)}, u32[]{:S(2)}) collective-permute-start(f32[192,128]{1,0:T(8,128)S(1)} %maximum_select_fusion.2.near_ref), channel_id=1, source_target_pairs={{0,2},{1,3},{2,0},{3,1},{4,6},{5,7},{6,4},{7,5},{8,10},{9,11},{10,... | collective-permute-start | bytes 294920 | tf_op jit(solution)/shard_map/cond/branch_1_fun/ppermute | solution.py:139
  62.9 8.5 %collective-permute-start.11 = (f32[192,256]{1,0:T(8,128)S(1)}, f32[192,256]{1,0:T(8,128)S(1)}, u32[]{:S(2)}, u32[]{:S(2)}) collective-permute-start(f32[192,256]{1,0:T(8,128)S(1)} %pad_maximum_fusion.7), channel_id=1, source_target_pairs={{0,1},{1,0},{2,3},{3,2},{4,5},{5,4},{6,7},{7,6},{8,9},{9,8},{10,11... | collective-permute-start | bytes 589832 | tf_op jit(solution)/shard_map/cond/branch_1_fun/ppermute | solution.py:141
  71.9 1.4 %copy-start.2 = (f32[4,128,1152]{2,1,0:T(8,128)}, f32[4,128,1152]{2,1,0:T(8,128)S(1)}, u32[]{:S(2)}) copy-start(f32[4,128,1152]{2,1,0:T(8,128)S(1)} %get-tuple-element.40) | copy-start | bytes 7077892 | tf_op jit(solution)/shard_map/cond
  74.0 34.7 %all-to-all-start.9 = ((f32[4,128,1152]{2,1,0:T(8,128)}), f32[4,128,1152]{2,1,0:T(8,128)S(1)}, u32[]{:S(2)}, u32[]{:S(2)}) async-start(f32[4,128,1152]{2,1,0:T(8,128)} %copy-done.2), calls=%async_computation.9 | async-start | bytes 4718592 | tf_op jit(solution)/shard_map/cond/branch_1_fun/all_to_all | solution.py:442
  78.8 27.2 %copy-start.13 = (f32[256,768]{1,0:T(8,128)S(1)}, f32[256,768]{1,0:T(8,128)}, u32[]{:S(2)}) copy-start(f32[256,768]{1,0:T(8,128)} %get-tuple-element.42.a_ref) | copy-start | bytes 2359300 | tf_op jit(solution)/shard_map/cond
  78.8 27.3 %copy-start.15 = (s32[544,128]{1,0:T(8,128)S(1)}, s32[544,128]{1,0:T(8,128)}, u32[]{:S(2)}) copy-start(s32[544,128]{1,0:T(8,128)} %get-tuple-element.36.plan_ref) | copy-start | bytes 835588 | tf_op jit(solution)/shard_map/cond
  79.8 1.4 %collective-permute-start.13 = (f32[256,128]{1,0:T(8,128)S(1)}, f32[256,128]{1,0:T(8,128)S(1)}, u32[]{:S(2)}, u32[]{:S(2)}) collective-permute-start(f32[256,128]{1,0:T(8,128)S(1)} %slice.44), channel_id=1, source_target_pairs={{0,12},{1,13},{2,14},{3,15},{16,28},{17,29},{18,30},{19,31},{32,44... | collective-permute-start | bytes 393224 | tf_op jit(solution)/shard_map/cond/branch_1_fun/ppermute | solution.py:124
  80.5 0.7 collective-permute-start.12
  82.1 8.5 %collective-permute-start.14 = (f32[128,128]{1,0:T(8,128)S(1)}, f32[128,128]{1,0:T(8,128)S(1)}, u32[]{:S(2)}, u32[]{:S(2)}) collective-permute-start(f32[128,128]{1,0:T(8,128)S(1)} %get-tuple-element.54), channel_id=1, source_target_pairs={{4,8},{5,9},{6,10},{7,11},{20,24},{21,25},{22,26},{23,27},{36,40},... | collective-permute-start | bytes 196616 | tf_op jit(solution)/shard_map/cond/branch_1_fun/ppermute | solution.py:135
  83.4 7.2 %collective-permute-start.15 = (f32[128,128]{1,0:T(8,128)S(1)}, f32[128,128]{1,0:T(8,128)S(1)}, u32[]{:S(2)}, u32[]{:S(2)}) collective-permute-start(f32[128,128]{1,0:T(8,128)S(1)} %get-tuple-element.55), channel_id=1, source_target_pairs={{12,8},{13,9},{14,10},{15,11},{28,24},{29,25},{30,26},{31,27},{44,... | collective-permute-start | bytes 196616 | tf_op jit(solution)/shard_map/cond/branch_1_fun/ppermute | solution.py:136
  90.7 16.8 %copy-start.11 = (f32[64,512]{1,0:T(8,128)S(1)}, f32[64,512]{1,0:T(8,128)}, u32[]{:S(2)}) copy-start(f32[64,512]{1,0:T(8,128)} %copy-done.10) | copy-start | bytes 393220 | tf_op jit(solution)/shard_map/cond
  90.7 7.1 %collective-permute-start.16 = (f32[256,128]{1,0:T(8,128)S(1)}, f32[256,128]{1,0:T(8,128)S(1)}, u32[]{:S(2)}, u32[]{:S(2)}) collective-permute-start(f32[256,128]{1,0:T(8,128)S(1)} %maximum_select_fusion.1.near_ref), channel_id=1, source_target_pairs={{0,2},{1,3},{2,0},{3,1},{4,6},{5,7},{6,4},{7,5},{8,10},{9,11},{10,... | collective-permute-start | bytes 393224 | tf_op jit(solution)/shard_map/cond/branch_1_fun/ppermute | solution.py:139
  97.8 9.6 %collective-permute-start.17 = (f32[256,256]{1,0:T(8,128)S(1)}, f32[256,256]{1,0:T(8,128)S(1)}, u32[]{:S(2)}, u32[]{:S(2)}) collective-permute-start(f32[256,256]{1,0:T(8,128)S(1)} %pad_maximum_fusion.6), channel_id=1, source_target_pairs={{0,1},{1,0},{2,3},{3,2},{4,5},{5,4},{6,7},{7,6},{8,9},{9,8},{10,11... | collective-permute-start | bytes 786440 | tf_op jit(solution)/shard_map/cond/branch_1_fun/ppermute | solution.py:141
  106.5 0.9 copy-start
  107.4 1.2 %copy-start.1 = (f32[256,768]{1,0:T(8,128)S(1)}, f32[256,768]{1,0:T(8,128)}, u32[]{:S(2)}) copy-start(f32[256,768]{1,0:T(8,128)} %copy-done) | copy-start | bytes 2359300 | tf_op jit(solution)/shard_map/cond
  107.9 0.8 copy-start.3
  108.7 1.0 copy-start.4
  114.8 0.9 copy-start.19
  (1 other events, 0.7 us)

commit v6 on v5

--- a/solution.py
+++ b/solution.py
@@ -22,6 +22,7 @@
 Z_GROUPS = [[x * 8 + z for z in range(8)] for x in range(4)]
 VMEM = pl.BlockSpec(memory_space=pltpu.VMEM)
 SMEM = pl.BlockSpec(memory_space=pltpu.SMEM)
+HBM = pl.BlockSpec(memory_space=pltpu.HBM)
 
 
 def mm(left, right):
@@ -136,10 +137,7 @@
     right = lax.ppermute(near[half:], "pcol", [(q + 12, q + 8) for q in range(4)])
     far = (pcol >= 8) & (pcol < 12)
     near = jnp.where(far, jnp.concatenate([left, right], axis=0), near)
-    across = lax.ppermute(near, "pcol", [(q, q ^ 2) for q in range(PCOL)])
-    both = jnp.concatenate([near, across], axis=1)
-    pair = lax.ppermute(both, "pcol", [(q, q ^ 1) for q in range(PCOL)])
-    return near, across, pair
+    return [near] + [lax.ppermute(near, "pcol", [(q, q ^ n) for q in range(PCOL)]) for n in (1, 2, 3)]
 
 
 def lane_sum(mask, value):
@@ -290,70 +288,69 @@
         rest_ref[n, 32:48, :] = sent[n * 16 : n * 16 + 16, NB:]
 
 
-def lead_kernel(plan_ref, got_ref, lead_ref):
+def lead_kernel(plan_ref, got_ref, a_ref, lead_ref, rows_ref):
     got = jnp.concatenate([got_ref[n, 0:32, :] for n in range(8)], axis=0)
-    lead_ref[0:NB, :] = select_rows(onehot_of(plan_ref[160:288, :1], 256), got)
-    for n in range(4):
-        lead_ref[NB + n * 16 : NB + n * 16 + 16, :] = got_ref[n, 32:48, :]
-
-
-def panel_kernel(plan_ref, lead_ref, got_ref, near_ref, across_ref, pair_ref, send_ref, moved_ref):
+    lead_ref[...] = select_rows(onehot_of(plan_ref[160:288, :1], 256), got)
+    moved = jnp.concatenate([got_ref[n, 32:48, :] for n in range(4)], axis=0)
+    slot = plan_ref[288:544, :1]
+    moved = select_rows(onehot_of(slot, 64), moved)
+    rows_ref[...] = jnp.where(slot >= 0, moved, a_ref[:, :NB])
+
+
+def panel_kernel(plan_ref, lead_ref, got_ref, *refs):
+    blocks, send_ref, full_ref, sems = refs[:4], refs[4], refs[5], refs[6]
     panel = lax.axis_index("prow") >> 3
     got = jnp.concatenate([got_ref[n, 0:32, :] for n in range(8)], axis=0)
-    rows = select_rows(onehot_of(plan_ref[160:288, :1], 256), got)
-    for n in range(4):
-        send_ref[n, :, :NB] = lead_ref[0:NB, :]
-        send_ref[n, :, NB:COLS] = rows
-
-    def store_send(index, value):
+    full_ref[:, :NB] = lead_ref[...]
+    full_ref[:, NB:COLS] = select_rows(onehot_of(plan_ref[160:288, :1], 256), got)
+
+    def store(index, value):
         @pl.when(index != panel)
         def _():
-            spot = lane_block(COLS // NB + jnp.where(index < panel, index, index - 1))
-            for n in range(4):
-                send_ref[n, :, spot] = value
-
-    def store_moved(index, value):
-        moved_ref[:, lane_block(index)] = value
-
-    put_columns(near_ref, across_ref, pair_ref, slice(0, NB), store_send)
-    put_columns(near_ref, across_ref, pair_ref, slice(NB, NB + 64), store_moved)
-
-
-def put_columns(near_ref, across_ref, pair_ref, rows, store):
+            spot = COLS // NB + jnp.where(index < panel, index, index - 1)
+            full_ref[:, lane_block(spot)] = value
+
+    put_columns(blocks, slice(0, NB), store)
+    copies = [
+        pltpu.make_async_copy(full_ref, send_ref.at[n], sems.at[n]) for n in range(4)
+    ]
+    for copy in copies:
+        copy.start()
+    for copy in copies:
+        copy.wait()
+
+
+def put_columns(block_refs, rows, store):
     kind = lax.axis_index("pcol") & 3
-    store(kind, near_ref[rows, :])
-    store(kind ^ 2, across_ref[rows, :])
-    store(kind ^ 1, pair_ref[rows, :NB])
-    store(kind ^ 3, pair_ref[rows, NB:])
+    for n, ref in enumerate(block_refs):
+        store(kind ^ n, ref[rows, :])
 
 
 def lane_block(index):
     return pl.ds(pl.multiple_of(index * NB, NB), NB)
 
 
-def own_rows_kernel(plan_ref, lead_ref, got_ref, a_ref, out_ref):
+def own_rows_kernel(plan_ref, rows_ref, got_ref, a_ref, out_ref):
     slot = plan_ref[288:544, :1]
-    rest = jnp.concatenate([got_ref[n, 32:48, :] for n in range(4)], axis=0)
-    moved = jnp.concatenate([lead_ref[NB : NB + 64, :], rest], axis=1)
-    out_ref[...] = jnp.where(slot >= 0, select_rows(onehot_of(slot, 64), moved), a_ref[...])
-
-
-def panel_rows_kernel(plan_ref, moved_ref, near_ref, across_ref, pair_ref, out_ref):
-    slot = plan_ref[288:544, :1]
-
-    def store(index, value):
-        out_ref[:, lane_block(index)] = value
-
-    put_columns(near_ref, across_ref, pair_ref, slice(0, ROWS), store)
-    moved = select_rows(onehot_of(slot, 64), moved_ref[...])
-    out_ref[...] = jnp.where(slot >= 0, moved, out_ref[...])
+    moved = jnp.concatenate([got_ref[n, 32:48, :] for n in range(4)], axis=0)
+    moved = select_rows(onehot_of(slot, 64), moved)
+    out_ref[:, :NB] = rows_ref[...]
+    out_ref[:, NB:] = jnp.where(slot >= 0, moved, a_ref[:, NB:])
 
 
 def factor_kernel(
-    top_ref, left_ref, right_ref, lower_ref, upper_ref, out_ref, z_ref, y_ref, m_ref, u_ref, d_ref
+    top_ref, right_ref, lower_ref, upper_ref, left0_ref, left1_ref, left2_ref, left3_ref,
+    result_ref, z_ref, y_ref, m_ref, u_ref, d_ref, out_ref, sems,
 ):
     prow = lax.axis_index("prow")
     pcol = lax.axis_index("pcol")
+    fetches = []
+    for n, ref in enumerate((left0_ref, left1_ref, left2_ref, left3_ref)):
+        target = z_ref.at[TOP : TOP + ROWS, lane_block((pcol & 3) ^ n)]
+        fetches.append(pltpu.make_async_copy(ref, target, sems.at[n]))
+    fetches.append(pltpu.make_async_copy(right_ref, out_ref, sems.at[4]))
+    for fetch in fetches:
+        fetch.start()
     for k in range(PANELS):
         rows = slice(k * NB, k * NB + NB)
         for spot in range(PANELS - 1):
@@ -361,7 +358,8 @@
             z_ref[rows, block * NB : block * NB + NB] = top_ref[
                 rows, COLS + spot * NB : COLS + spot * NB + NB
             ]
-    z_ref[TOP:, :] = left_ref[...]
+    for fetch in fetches[:4]:
+        fetch.wait()
     for k in range(PANELS):
         s = k * NB
         e = s + NB
@@ -388,7 +386,8 @@
         u_ref[3 * s : 3 * e, :] = u3
         if e < TOP:
             y_ref[e:TOP, :] = before[e:TOP, :COLS] - mm(m3[: TOP - e], u3)
-    out_ref[...] = right_ref[...] - mm(m_ref[...], u_ref[...])
+    fetches[4].wait()
+    out_ref[...] = out_ref[...] - mm(m_ref[...], u_ref[...])
     panel_cols = lane_block(pcol & 3)
     top_rows = pl.ds(pl.multiple_of((prow & 3) * NB, NB), NB)
 
@@ -406,13 +405,17 @@
             prow == pcol, d_ref[top_rows, :], z_ref[top_rows, panel_cols]
         )
 
-
-def kernel_call(body, shapes, scratch=()):
+    copy = pltpu.make_async_copy(out_ref, result_ref, sems.at[5])
+    copy.start()
+    copy.wait()
+
+
+def kernel_call(body, shapes, scratch=(), out=VMEM):
     def call(*args):
         return pl.pallas_call(
             body,
             in_specs=[VMEM] * len(args),
-            out_specs=[VMEM] * len(shapes),
+            out_specs=[out] * len(shapes),
             out_shape=[jax.ShapeDtypeStruct(shape, kind) for shape, kind in shapes],
             scratch_shapes=list(scratch),
             compiler_params=pltpu.CompilerParams(vmem_limit_bytes=KERNEL_VMEM),
@@ -421,11 +424,15 @@
     return call
 
 
-def factor(*args):
-    return pl.pallas_call(
+def factor(top, right, lower_inverse, upper_inverse, *left):
+    right, *left = [
+        pltpu.with_memory_space_constraint(value, pltpu.HBM) for value in (right, *left)
+    ]
+    args = (top, right, lower_inverse, upper_inverse, *left)
+    result = pl.pallas_call(
         factor_kernel,
-        in_specs=[VMEM] * len(args),
-        out_specs=VMEM,
+        in_specs=[VMEM, HBM, VMEM, VMEM] + [HBM] * 4,
+        out_specs=HBM,
         out_shape=jax.ShapeDtypeStruct((ROWS, COLS), F32),
         scratch_shapes=[
             pltpu.VMEM((TOP + ROWS, TOP), F32),
@@ -433,9 +440,12 @@
             pltpu.VMEM((ROWS, 3 * TOP), BF),
             pltpu.VMEM((3 * TOP, COLS), BF),
             pltpu.VMEM((TOP, NB), F32),
+            pltpu.VMEM((ROWS, COLS), F32),
+            pltpu.SemaphoreType.DMA((6,)),
         ],
         compiler_params=pltpu.CompilerParams(vmem_limit_bytes=FACTOR_VMEM),
     )(*args)
+    return pltpu.with_memory_space_constraint(result, pltpu.HBM)
 
 
 def along(value, groups):
@@ -448,23 +458,27 @@
     first, rest = kernel_call(turn_kernel, [((8, 48, NB), F32), ((8, 48, REST), F32)])(plan, got)
     first = along(first, Z_GROUPS)
     rest = along(rest, Z_GROUPS)
-    (lead,) = kernel_call(lead_kernel, [((NB + 64, NB), F32)])(plan, first)
+    lead, rows = kernel_call(lead_kernel, [((NB, NB), F32), ((ROWS, NB), F32)])(
+        plan, first, matrix
+    )
     ends = spread_start(lead)
     late = spread_rest(lead, *ends, pcol)
-    send, moved = kernel_call(
-        panel_kernel, [((4, NB, WIDE - NB), F32), ((64, TOP), F32)]
+    (send,) = kernel_call(
+        panel_kernel,
+        [((4, NB, WIDE - NB), F32)],
+        [pltpu.VMEM((NB, WIDE - NB), F32), pltpu.SemaphoreType.DMA((4,))],
+        HBM,
     )(plan, lead, rest, *late)
     top = along(send, X_GROUPS).reshape(TOP, WIDE - NB)
-    block = matrix[:, :NB]
-    ends = spread_start(block)
-    raw = spread_rest(block, *ends, pcol)
-    (right,) = kernel_call(own_rows_kernel, [((ROWS, COLS), F32)])(plan, lead, rest, matrix)
-    (left,) = kernel_call(panel_rows_kernel, [((ROWS, TOP), F32)])(plan, moved, *raw)
-    return factor(top, left, right, lower_inverse, upper_inverse)
+    ends = spread_start(rows)
+    left = spread_rest(rows, *ends, pcol)
+    (right,) = kernel_call(own_rows_kernel, [((ROWS, COLS), F32)])(plan, rows, rest, matrix)
+    return factor(top, right, lower_inverse, upper_inverse, *left)
 
 
 def dense_rows_kernel(
-    origin_ref, gathered_ref, a_ref, own_ref, near_ref, across_ref, pair_ref, top_ref, left_ref, right_ref
+    origin_ref, gathered_ref, a_ref, own_ref, block0_ref, block1_ref, block2_ref, block3_ref,
+    top_ref, right_ref,
 ):
     def store_corner(index, value):
         for k in range(PANELS):
@@ -474,11 +488,7 @@
                 spot = lane_block(COLS // NB + jnp.where(index < k, index, index - 1))
                 top_ref[k * NB : k * NB + NB, spot] = value[k * NB : k * NB + NB]
 
-    def store_left(index, value):
-        left_ref[:, lane_block(index)] = value
-
-    put_columns(near_ref, across_ref, pair_ref, slice(0, TOP), store_corner)
-    put_columns(near_ref, across_ref, pair_ref, slice(TOP, TOP + ROWS), store_left)
+    put_columns((block0_ref, block1_ref, block2_ref, block3_ref), slice(0, TOP), store_corner)
     top_ref[:, :NB] = own_ref[:TOP, :]
     right_ref[:, :NB] = own_ref[TOP:, :]
     for unit in range(PROW):
@@ -508,13 +518,13 @@
     )(place, pivots.reshape(PANELS, NB), pivots.reshape(TOP, 1), matrix)
     gathered_first = exchange_first(picked_first, matrix[:NB, :NB])
     (own,) = kernel_call(column_kernel, [((TOP + ROWS, NB), F32)])(origin, gathered_first, matrix)
-    near, across, pair = spread_columns(own, pcol)
+    blocks = spread_columns(own, pcol)
     gathered_rest = exchange_rest(picked_rest, matrix[:NB, NB:])
-    top, left, right = kernel_call(
-        dense_rows_kernel,
-        [((TOP, WIDE - NB), F32), ((ROWS, TOP), F32), ((ROWS, COLS), F32)],
-    )(origin, gathered_rest, matrix, own, near, across, pair)
-    return factor(top, left, right, lower_inverse, upper_inverse)
+    top, right = kernel_call(
+        dense_rows_kernel, [((TOP, WIDE - NB), F32), ((ROWS, COLS), F32)]
+    )(origin, gathered_rest, matrix, own, *blocks)
+    left = [block[TOP:] for block in blocks]
+    return factor(top, right, lower_inverse, upper_inverse, *left)
 
 
 def per_device(matrix, pivots, lower_inverse, upper_inverse):

time: 116 us -> 115 us (level)
  the two profiles are of different devices: /device:TPU:43 before, /device:TPU:40 now
where the time goes in v6:
time: 115 us; the launch traced here: 114 us
  blocking collectives  36.6 us (32%)
  starting transfers between devices  31.6 us (27%)
  waiting for transfers between devices  26.1 us (23%)
  Pallas kernels  14.7 us (13%)
  local copies, waits for them, and re-layouts  3.6 us (3%)
    all_to_all x2, blocking collectives, along(): return lax.all_to_all(value, 'prow', 0, 0, axis_index_groups=groups)  36.6 us
    ppermute x6, starting transfers between devices, spread_rest(): lax.ppermute(near, 'pcol', [(q, q ^ n) for q in range(PCOL)])  16.5 us
    ppermute x2, waiting for transfers between devices, spread_rest(): left = lax.ppermute(near[:half], 'pcol', [(q + 4, q + 8) for q in range(4)])  9.9 us
    ppermute x2, waiting for transfers between devices, spread_rest(): lax.ppermute(near[half:], 'pcol', [(q + 12, q + 8) for q in range(4)])  9.74 us
    pallas_call x5, Pallas kernels, call(): pl.pallas_call(body, in_specs=[VMEM] * len(args), out_specs=[out] * len(s...  8.4 us
    all_to_all x2, starting transfers between devices, along(): return lax.all_to_all(value, 'prow', 0, 0, axis_index_groups=groups)  7.2 us
    pallas_call x1, Pallas kernels, factor(): pl.pallas_call(factor_kernel, in_specs=[VMEM, HBM, VMEM, VMEM] + [HBM] *...  6.29 us
    ppermute x6, waiting for transfers between devices, spread_rest(): lax.ppermute(near, 'pcol', [(q, q ^ n) for q in range(PCOL)])  5.61 us
  transfers between devices with their start and end apart: 16, of which 7 were waited for; matrix products, arithmetic and copies ran while one was open for 0% of the time, Pallas kernels for 2%

profile of v6, /device:TPU:40, one launch (start us, length us, event | category | flops | bytes accessed | tf_op | source)
XLA Modules:
  0.0 114.0 jit_solution(16758093107117342947)
XLA Ops:
  0.0 3.4 %shard_map.48 = (f32[256,768]{1,0:T(8,128)}, s32[544,128]{1,0:T(8,128)}, s32[8,128]{1,0:T(8,128)S(1)}) custom-call(s32[4,128]{1,0:T(4,128)} %bitcast.28, f32[256,768]{1,0:T(8,128)} %a_ref.1), custom_call_target="tpu_custom_call" | custom-call | tf_op jit(solution)/shard_map/pallas_call | solution.py:415
  4.5 108.5 %conditional.1 = (f32[256,768]{1,0:T(8,128)S(1)}) conditional(s32[]{:T(128)} %bitcast.16, (s32[512]{0:T(512)}, f32[256,768]{1,0:T(8,128)}, f32[4,128,128]{2,1,0:T(8,128)}, f32[4,128,128]{2,1,0:T(8,128)}) %tuple.11, (f32[256,768]{1,0:T(8,128)}, s32[544,128]{1,0:T(8,128)}, f32[256,768]{1,0:T(8,128)}, f32[4,128,128]{2,1,0:T(8,128)}, ...), branch_computations={%region_0.4_spmd, %region_4.5_spmd} | conditional | flops 1392652 | bytes 63624084 | solution.py:536
  4.6 16.7 %all_to_all.41.got_ref = f32[4,64,768]{2,1,0:T(8,128)S(1)} all-to-all(f32[4,64,768]{2,1,0:T(8,128)} %bitcast.24), channel_id=1, replica_groups={{0,128,256,384},{16,144,272,400},{32,160,288,416},{48,176,304,432},{64,..., dimensions={0} | all-to-all | bytes 1572864 | tf_op jit(solution)/shard_map/cond/branch_1_fun/all_to_all | solution.py:452
  21.3 1.5 %branch_1_fun.5 = (f32[8,48,128]{2,1,0:T(8,128)S(1)}, f32[8,48,640]{2,1,0:T(8,128)}) custom-call(s32[544,128]{1,0:T(8,128)S(1)} %copy-done.12, f32[4,64,768]{2,1,0:T(8,128)S(1)} %all_to_all.41.got_ref), custom_call_target="tpu_custom_call" | custom-call | tf_op jit(solution)/shard_map/cond/branch_1_fun/pallas_call | solution.py:415
  22.8 19.9 %all_to_all.42.got_ref = f32[8,48,128]{2,1,0:T(8,128)S(1)} all-to-all(f32[8,48,128]{2,1,0:T(8,128)S(1)} %get-tuple-element.37), channel_id=1, replica_groups={{0,16,32,48,64,80,96,112},{128,144,160,176,192,208,224,240},{256,272,28..., dimensions={0} | all-to-all | bytes 393216 | tf_op jit(solution)/shard_map/cond/branch_1_fun/all_to_all | solution.py:452
  42.7 3.6 %all-to-all-start.8 = ((f32[8,48,640]{2,1,0:T(8,128)}), f32[8,48,640]{2,1,0:T(8,128)S(1)}, u32[]{:S(2)}, u32[]{:S(2)}) async-start(f32[8,48,640]{2,1,0:T(8,128)} %get-tuple-element.40), calls=%async_computation.8 | async-start | bytes 1966080 | tf_op jit(solution)/shard_map/cond/branch_1_fun/all_to_all | solution.py:452
  48.0 1.3 %collective-permute-start.10 = (f32[64,128]{1,0:T(8,128)S(1)}, f32[64,128]{1,0:T(8,128)S(1)}, u32[]{:S(2)}, u32[]{:S(2)}) collective-permute-start(f32[64,128]{1,0:T(8,128)S(1)} %get-tuple-element.56), channel_id=1, source_target_pairs={{12,8},{13,9},{14,10},{15,11},{28,24},{29,25},{30,26},{31,27},{44,... | collective-permute-start | bytes 98312 | tf_op jit(solution)/shard_map/cond/branch_1_fun/ppermute | solution.py:137
  49.3 1.3 %collective-permute-start.9 = (f32[64,128]{1,0:T(8,128)S(1)}, f32[64,128]{1,0:T(8,128)S(1)}, u32[]{:S(2)}, u32[]{:S(2)}) collective-permute-start(f32[64,128]{1,0:T(8,128)S(1)} %get-tuple-element.55), channel_id=1, source_target_pairs={{4,8},{5,9},{6,10},{7,11},{20,24},{21,25},{22,26},{23,27},{36,40},... | collective-permute-start | bytes 98312 | tf_op jit(solution)/shard_map/cond/branch_1_fun/ppermute | solution.py:136
  50.6 9.0 %collective-permute-done.10 = f32[64,128]{1,0:T(8,128)S(1)} collective-permute-done((f32[64,128]{1,0:T(8,128)S(1)}, f32[64,128]{1,0:T(8,128)S(1)}, u32[]{:S(2)}, u32[]{:S(2)}) %collective-permute-start.10) | collective-permute-done | bytes 32800 | tf_op jit(solution)/shard_map/cond/branch_1_fun/ppermute | solution.py:137
  59.6 1.9 %collective-permute-start.11 = (f32[128,128]{1,0:T(8,128)S(1)}, f32[128,128]{1,0:T(8,128)S(1)}, u32[]{:S(2)}, u32[]{:S(2)}) collective-permute-start(f32[128,128]{1,0:T(8,128)S(1)} %maximum_select_fusion.2.refs_0_), channel_id=1, source_target_pairs={{0,1},{1,0},{2,3},{3,2},{4,5},{5,4},{6,7},{7,6},{8,9},{9,8},{10,11... | collective-permute-start | bytes 196616 | tf_op jit(solution)/shard_map/cond/branch_1_fun/ppermute | solution.py:140
  61.5 3.9 %collective-permute-start.12 = (f32[128,128]{1,0:T(8,128)S(1)}, f32[128,128]{1,0:T(8,128)S(1)}, u32[]{:S(2)}, u32[]{:S(2)}) collective-permute-start(f32[128,128]{1,0:T(8,128)S(1)} %maximum_select_fusion.2.refs_0_), channel_id=1, source_target_pairs={{0,2},{1,3},{2,0},{3,1},{4,6},{5,7},{6,4},{7,5},{8,10},{9,11},{10,... | collective-permute-start | bytes 196616 | tf_op jit(solution)/shard_map/cond/branch_1_fun/ppermute | solution.py:140
  65.4 2.0 %collective-permute-start.13 = (f32[128,128]{1,0:T(8,128)S(1)}, f32[128,128]{1,0:T(8,128)S(1)}, u32[]{:S(2)}, u32[]{:S(2)}) collective-permute-start(f32[128,128]{1,0:T(8,128)S(1)} %maximum_select_fusion.2.refs_0_), channel_id=1, source_target_pairs={{0,3},{1,2},{2,1},{3,0},{4,7},{5,6},{6,5},{7,4},{8,11},{9,10},{10,... | collective-permute-start | bytes 196616 | tf_op jit(solution)/shard_map/cond/branch_1_fun/ppermute | solution.py:140
  68.1 3.1 %collective-permute-done.13.refs_3_ = f32[128,128]{1,0:T(8,128)S(1)} collective-permute-done((f32[128,128]{1,0:T(8,128)S(1)}, f32[128,128]{1,0:T(8,128)S(1)}, u32[]{:S(2)}, u32[]{:S(2)}) %collective-permute-start.13) | collective-permute-done | bytes 65568 | tf_op jit(solution)/shard_map/cond/branch_1_fun/ppermute | solution.py:140
  71.3 1.8 %branch_1_fun.7 = f32[4,128,1152]{2,1,0:T(8,128)} custom-call(s32[544,128]{1,0:T(8,128)S(1)} %copy-done.12, f32[128,128]{1,0:T(8,128)S(1)} %get-tuple-element.39.lead_ref, f32[8,48,640]{2,1,0:T(8,128)S(1)} %all-to-all-done.8.got_ref, f32[128,128]{1,0:T(8,128)S(1)} %maximum_select_fusion.2.refs_0_, f32[128,128]{1,0:T(8,128)S(1)} %collective-permute-done.11.refs_1_, ...), custom_call_target="tpu_custom_call" | custom-call | tf_op jit(solution)/shard_map/cond/branch_1_fun/pallas_call | solution.py:415
  73.1 3.6 %all-to-all-start.9 = ((f32[4,128,1152]{2,1,0:T(8,128)}), f32[4,128,1152]{2,1,0:T(8,128)S(1)}, u32[]{:S(2)}, u32[]{:S(2)}) async-start(f32[4,128,1152]{2,1,0:T(8,128)} %branch_1_fun.7), calls=%async_computation.9 | async-start | bytes 4718592 | tf_op jit(solution)/shard_map/cond/branch_1_fun/all_to_all | solution.py:452
  78.4 1.3 %collective-permute-start.16 = (f32[128,128]{1,0:T(8,128)S(1)}, f32[128,128]{1,0:T(8,128)S(1)}, u32[]{:S(2)}, u32[]{:S(2)}) collective-permute-start(f32[128,128]{1,0:T(8,128)S(1)} %get-tuple-element.53), channel_id=1, source_target_pairs={{4,8},{5,9},{6,10},{7,11},{20,24},{21,25},{22,26},{23,27},{36,40},... | collective-permute-start | bytes 196616 | tf_op jit(solution)/shard_map/cond/branch_1_fun/ppermute | solution.py:136
  79.7 1.3 %collective-permute-start.17 = (f32[128,128]{1,0:T(8,128)S(1)}, f32[128,128]{1,0:T(8,128)S(1)}, u32[]{:S(2)}, u32[]{:S(2)}) collective-permute-start(f32[128,128]{1,0:T(8,128)S(1)} %get-tuple-element.54), channel_id=1, source_target_pairs={{12,8},{13,9},{14,10},{15,11},{28,24},{29,25},{30,26},{31,27},{44,... | collective-permute-start | bytes 196616 | tf_op jit(solution)/shard_map/cond/branch_1_fun/ppermute | solution.py:137
  81.0 9.9 %collective-permute-done.16 = f32[128,128]{1,0:T(8,128)S(1)} collective-permute-done((f32[128,128]{1,0:T(8,128)S(1)}, f32[128,128]{1,0:T(8,128)S(1)}, u32[]{:S(2)}, u32[]{:S(2)}) %collective-permute-start.16) | collective-permute-done | bytes 65568 | tf_op jit(solution)/shard_map/cond/branch_1_fun/ppermute | solution.py:136
  91.6 1.9 %collective-permute-start.18 = (f32[256,128]{1,0:T(8,128)S(1)}, f32[256,128]{1,0:T(8,128)S(1)}, u32[]{:S(2)}, u32[]{:S(2)}) collective-permute-start(f32[256,128]{1,0:T(8,128)S(1)} %maximum_select_fusion.1.left0_ref), channel_id=1, source_target_pairs={{0,1},{1,0},{2,3},{3,2},{4,5},{5,4},{6,7},{7,6},{8,9},{9,8},{10,11... | collective-permute-start | bytes 393224 | tf_op jit(solution)/shard_map/cond/branch_1_fun/ppermute | solution.py:140
  93.5 4.7 %collective-permute-start.19 = (f32[256,128]{1,0:T(8,128)S(1)}, f32[256,128]{1,0:T(8,128)S(1)}, u32[]{:S(2)}, u32[]{:S(2)}) collective-permute-start(f32[256,128]{1,0:T(8,128)S(1)} %maximum_select_fusion.1.left0_ref), channel_id=1, source_target_pairs={{0,2},{1,3},{2,0},{3,1},{4,6},{5,7},{6,4},{7,5},{8,10},{9,11},{10,... | collective-permute-start | bytes 393224 | tf_op jit(solution)/shard_map/cond/branch_1_fun/ppermute | solution.py:140
  98.3 2.0 %collective-permute-start.20 = (f32[256,128]{1,0:T(8,128)S(1)}, f32[256,128]{1,0:T(8,128)}, u32[]{:S(2)}, u32[]{:S(2)}) collective-permute-start(f32[256,128]{1,0:T(8,128)S(1)} %maximum_select_fusion.1.left0_ref), channel_id=1, source_target_pairs={{0,3},{1,2},{2,1},{3,0},{4,7},{5,6},{6,5},{7,4},{8,11},{9,10},{10,... | collective-permute-start | bytes 393224 | tf_op jit(solution)/shard_map/cond/branch_1_fun/ppermute | solution.py:140
  100.3 1.4 %branch_1_fun.8.right_ref = f32[256,768]{1,0:T(8,128)S(1)} custom-call(s32[544,128]{1,0:T(8,128)} %get-tuple-element.35.plan_ref, f32[256,128]{1,0:T(8,128)S(1)} %get-tuple-element.41.rows_ref, f32[8,48,640]{2,1,0:T(8,128)S(1)} %all-to-all-done.8.got_ref, f32[256,768]{1,0:T(8,128)S(1)} %copy-done.11), custom_call_target="tpu_custom_call" | custom-call | tf_op jit(solution)/shard_map/cond/branch_1_fun/pallas_call | solution.py:415
  103.9 1.8 %collective-permute-done.20.left3_ref = f32[256,128]{1,0:T(8,128)} collective-permute-done((f32[256,128]{1,0:T(8,128)S(1)}, f32[256,128]{1,0:T(8,128)}, u32[]{:S(2)}, u32[]{:S(2)}) %collective-permute-start.20) | collective-permute-done | bytes 131104 | tf_op jit(solution)/shard_map/cond/branch_1_fun/ppermute | solution.py:140
  106.6 6.3 %branch_1_fun.9 = f32[256,768]{1,0:T(8,128)S(1)} custom-call(f32[512,1152]{1,0:T(8,128)S(1)} %bitcast.18, f32[256,768]{1,0:T(8,128)} %copy-done, f32[4,128,128]{2,1,0:T(8,128)} %get-tuple-element.42.lower_ref, f32[4,128,128]{2,1,0:T(8,128)} %get-tuple-element.43.upper_ref, f32[256,128]{1,0:T(8,128)} %copy-done.17, f32[256,128]{1,0:T(8,128)} %copy-done.19, ...), custom_call_target="tpu_custom_call" | custom-call | tf_op jit(solution)/shard_map/cond/branch_1_fun/pallas_call | solution.py:432
  (40 shorter events, 9.1 us)
Async XLA Ops:
  4.6 16.7 %copy-start.12 = (s32[544,128]{1,0:T(8,128)S(1)}, s32[544,128]{1,0:T(8,128)}, u32[]{:S(2)}) copy-start(s32[544,128]{1,0:T(8,128)} %get-tuple-element.35.plan_ref) | copy-start | bytes 835588 | tf_op jit(solution)/shard_map/cond
  21.3 24.9 %copy-start.10 = (f32[256,768]{1,0:T(8,128)S(1)}, f32[256,768]{1,0:T(8,128)}, u32[]{:S(2)}) copy-start(f32[256,768]{1,0:T(8,128)} %get-tuple-element.38.a_ref) | copy-start | bytes 2359300 | tf_op jit(solution)/shard_map/cond
  42.7 28.6 %all-to-all-start.8 = ((f32[8,48,640]{2,1,0:T(8,128)}), f32[8,48,640]{2,1,0:T(8,128)S(1)}, u32[]{:S(2)}, u32[]{:S(2)}) async-start(f32[8,48,640]{2,1,0:T(8,128)} %get-tuple-element.40), calls=%async_computation.8 | async-start | bytes 1966080 | tf_op jit(solution)/shard_map/cond/branch_1_fun/all_to_all | solution.py:452
  46.6 1.4 %collective-permute-start.7 = (f32[128,128]{1,0:T(8,128)S(1)}, f32[128,128]{1,0:T(8,128)S(1)}, u32[]{:S(2)}, u32[]{:S(2)}) collective-permute-start(f32[128,128]{1,0:T(8,128)S(1)} %get-tuple-element.39.lead_ref), channel_id=1, source_target_pairs={{0,4},{1,5},{2,6},{3,7},{16,20},{17,21},{18,22},{19,23},{32,36},{3... | collective-permute-start | bytes 196616 | tf_op jit(solution)/shard_map/cond/branch_1_fun/ppermute | solution.py:124
  47.2 0.7 collective-permute-start.8
  48.0 11.6 %collective-permute-start.10 = (f32[64,128]{1,0:T(8,128)S(1)}, f32[64,128]{1,0:T(8,128)S(1)}, u32[]{:S(2)}, u32[]{:S(2)}) collective-permute-start(f32[64,128]{1,0:T(8,128)S(1)} %get-tuple-element.56), channel_id=1, source_target_pairs={{12,8},{13,9},{14,10},{15,11},{28,24},{29,25},{30,26},{31,27},{44,... | collective-permute-start | bytes 98312 | tf_op jit(solution)/shard_map/cond/branch_1_fun/ppermute | solution.py:137
  49.3 10.3 %collective-permute-start.9 = (f32[64,128]{1,0:T(8,128)S(1)}, f32[64,128]{1,0:T(8,128)S(1)}, u32[]{:S(2)}, u32[]{:S(2)}) collective-permute-start(f32[64,128]{1,0:T(8,128)S(1)} %get-tuple-element.55), channel_id=1, source_target_pairs={{4,8},{5,9},{6,10},{7,11},{20,24},{21,25},{22,26},{23,27},{36,40},... | collective-permute-start | bytes 98312 | tf_op jit(solution)/shard_map/cond/branch_1_fun/ppermute | solution.py:136
  59.6 7.8 %collective-permute-start.11 = (f32[128,128]{1,0:T(8,128)S(1)}, f32[128,128]{1,0:T(8,128)S(1)}, u32[]{:S(2)}, u32[]{:S(2)}) collective-permute-start(f32[128,128]{1,0:T(8,128)S(1)} %maximum_select_fusion.2.refs_0_), channel_id=1, source_target_pairs={{0,1},{1,0},{2,3},{3,2},{4,5},{5,4},{6,7},{7,6},{8,9},{9,8},{10,11... | collective-permute-start | bytes 196616 | tf_op jit(solution)/shard_map/cond/branch_1_fun/ppermute | solution.py:140
  61.5 6.6 %collective-permute-start.12 = (f32[128,128]{1,0:T(8,128)S(1)}, f32[128,128]{1,0:T(8,128)S(1)}, u32[]{:S(2)}, u32[]{:S(2)}) collective-permute-start(f32[128,128]{1,0:T(8,128)S(1)} %maximum_select_fusion.2.refs_0_), channel_id=1, source_target_pairs={{0,2},{1,3},{2,0},{3,1},{4,6},{5,7},{6,4},{7,5},{8,10},{9,11},{10,... | collective-permute-start | bytes 196616 | tf_op jit(solution)/shard_map/cond/branch_1_fun/ppermute | solution.py:140
  65.4 5.9 %collective-permute-start.13 = (f32[128,128]{1,0:T(8,128)S(1)}, f32[128,128]{1,0:T(8,128)S(1)}, u32[]{:S(2)}, u32[]{:S(2)}) collective-permute-start(f32[128,128]{1,0:T(8,128)S(1)} %maximum_select_fusion.2.refs_0_), channel_id=1, source_target_pairs={{0,3},{1,2},{2,1},{3,0},{4,7},{5,6},{6,5},{7,4},{8,11},{9,10},{10,... | collective-permute-start | bytes 196616 | tf_op jit(solution)/shard_map/cond/branch_1_fun/ppermute | solution.py:140
  73.1 33.4 %all-to-all-start.9 = ((f32[4,128,1152]{2,1,0:T(8,128)}), f32[4,128,1152]{2,1,0:T(8,128)S(1)}, u32[]{:S(2)}, u32[]{:S(2)}) async-start(f32[4,128,1152]{2,1,0:T(8,128)} %branch_1_fun.7), calls=%async_computation.9 | async-start | bytes 4718592 | tf_op jit(solution)/shard_map/cond/branch_1_fun/all_to_all | solution.py:452
  76.8 23.5 %copy-start.11 = (f32[256,768]{1,0:T(8,128)S(1)}, f32[256,768]{1,0:T(8,128)}, u32[]{:S(2)}) copy-start(f32[256,768]{1,0:T(8,128)} %get-tuple-element.38.a_ref) | copy-start | bytes 2359300 | tf_op jit(solution)/shard_map/cond
  76.8 1.5 %collective-permute-start.14 = (f32[256,128]{1,0:T(8,128)S(1)}, f32[256,128]{1,0:T(8,128)S(1)}, u32[]{:S(2)}, u32[]{:S(2)}) collective-permute-start(f32[256,128]{1,0:T(8,128)S(1)} %get-tuple-element.41.rows_ref), channel_id=1, source_target_pairs={{0,4},{1,5},{2,6},{3,7},{16,20},{17,21},{18,22},{19,23},{32,36},{3... | collective-permute-start | bytes 393224 | tf_op jit(solution)/shard_map/cond/branch_1_fun/ppermute | solution.py:124
  77.6 0.7 collective-permute-start.15
  78.4 12.5 %collective-permute-start.16 = (f32[128,128]{1,0:T(8,128)S(1)}, f32[128,128]{1,0:T(8,128)S(1)}, u32[]{:S(2)}, u32[]{:S(2)}) collective-permute-start(f32[128,128]{1,0:T(8,128)S(1)} %get-tuple-element.53), channel_id=1, source_target_pairs={{4,8},{5,9},{6,10},{7,11},{20,24},{21,25},{22,26},{23,27},{36,40},... | collective-permute-start | bytes 196616 | tf_op jit(solution)/shard_map/cond/branch_1_fun/ppermute | solution.py:136
  79.7 11.9 %collective-permute-start.17 = (f32[128,128]{1,0:T(8,128)S(1)}, f32[128,128]{1,0:T(8,128)S(1)}, u32[]{:S(2)}, u32[]{:S(2)}) collective-permute-start(f32[128,128]{1,0:T(8,128)S(1)} %get-tuple-element.54), channel_id=1, source_target_pairs={{12,8},{13,9},{14,10},{15,11},{28,24},{29,25},{30,26},{31,27},{44,... | collective-permute-start | bytes 196616 | tf_op jit(solution)/shard_map/cond/branch_1_fun/ppermute | solution.py:137
  91.6 11.0 %copy-start.17 = (f32[256,128]{1,0:T(8,128)}, f32[256,128]{1,0:T(8,128)S(1)}, u32[]{:S(2)}) copy-start(f32[256,128]{1,0:T(8,128)S(1)} %maximum_select_fusion.1.left0_ref) | copy-start | bytes 393220 | tf_op jit(solution)/shard_map/cond
  91.6 11.0 %collective-permute-start.18 = (f32[256,128]{1,0:T(8,128)S(1)}, f32[256,128]{1,0:T(8,128)S(1)}, u32[]{:S(2)}, u32[]{:S(2)}) collective-permute-start(f32[256,128]{1,0:T(8,128)S(1)} %maximum_select_fusion.1.left0_ref), channel_id=1, source_target_pairs={{0,1},{1,0},{2,3},{3,2},{4,5},{5,4},{6,7},{7,6},{8,9},{9,8},{10,11... | collective-permute-start | bytes 393224 | tf_op jit(solution)/shard_map/cond/branch_1_fun/ppermute | solution.py:140
  93.5 9.1 %collective-permute-start.19 = (f32[256,128]{1,0:T(8,128)S(1)}, f32[256,128]{1,0:T(8,128)S(1)}, u32[]{:S(2)}, u32[]{:S(2)}) collective-permute-start(f32[256,128]{1,0:T(8,128)S(1)} %maximum_select_fusion.1.left0_ref), channel_id=1, source_target_pairs={{0,2},{1,3},{2,0},{3,1},{4,6},{5,7},{6,4},{7,5},{8,10},{9,11},{10,... | collective-permute-start | bytes 393224 | tf_op jit(solution)/shard_map/cond/branch_1_fun/ppermute | solution.py:140
  98.3 7.4 %collective-permute-start.20 = (f32[256,128]{1,0:T(8,128)S(1)}, f32[256,128]{1,0:T(8,128)}, u32[]{:S(2)}, u32[]{:S(2)}) collective-permute-start(f32[256,128]{1,0:T(8,128)S(1)} %maximum_select_fusion.1.left0_ref), channel_id=1, source_target_pairs={{0,3},{1,2},{2,1},{3,0},{4,7},{5,6},{6,5},{7,4},{8,11},{9,10},{10,... | collective-permute-start | bytes 393224 | tf_op jit(solution)/shard_map/cond/branch_1_fun/ppermute | solution.py:140
  101.7 0.9 copy-start
  102.6 0.6 copy-start.19
  103.3 0.6 copy-start.20
  113.1 0.9 copy-start.16

commit v7 on v6

--- a/solution.py
+++ b/solution.py
@@ -358,17 +358,10 @@
             z_ref[rows, block * NB : block * NB + NB] = top_ref[
                 rows, COLS + spot * NB : COLS + spot * NB + NB
             ]
-    for fetch in fetches[:4]:
-        fetch.wait()
     for k in range(PANELS):
         s = k * NB
         e = s + NB
         before = top_ref if k == 0 else y_ref
-        multipliers = dot3(z_ref[e:, s:e], upper_ref[k])
-        z_ref[e:, s:e] = multipliers
-        mh, ml = split2(multipliers)
-        m3 = jnp.concatenate([mh, ml, mh], axis=1)
-        m_ref[:, 3 * s : 3 * e] = m3[TOP - e :]
         lh, ll = split2(lower_ref[k])
         l3 = jnp.concatenate([lh, ll, lh], axis=1)
         if e < TOP:
@@ -376,7 +369,7 @@
             corner = mm(l3, jnp.concatenate([bh, bh, bl], axis=0))
             z_ref[s:e, e:] = corner
             uh, ul = split2(corner)
-            z_ref[e:, e:] = z_ref[e:, e:] - mm(m3, jnp.concatenate([uh, uh, ul], axis=0))
+            corner3 = jnp.concatenate([uh, uh, ul], axis=0)
         d_ref[s:e, :] = before[s:e, :NB]
         bh, bl = split2(before[s:e, :COLS])
         upper_rows = mm(l3, jnp.concatenate([bh, bh, bl], axis=0))
@@ -384,7 +377,16 @@
         uh, ul = split2(upper_rows)
         u3 = jnp.concatenate([uh, uh, ul], axis=0)
         u_ref[3 * s : 3 * e, :] = u3
+        if k == 0:
+            for fetch in fetches[:4]:
+                fetch.wait()
+        multipliers = dot3(z_ref[e:, s:e], upper_ref[k])
+        z_ref[e:, s:e] = multipliers
+        mh, ml = split2(multipliers)
+        m3 = jnp.concatenate([mh, ml, mh], axis=1)
+        m_ref[:, 3 * s : 3 * e] = m3[TOP - e :]
         if e < TOP:
+            z_ref[e:, e:] = z_ref[e:, e:] - mm(m3, corner3)
             y_ref[e:TOP, :] = before[e:TOP, :COLS] - mm(m3[: TOP - e], u3)
     fetches[4].wait()
     out_ref[...] = out_ref[...] - mm(m_ref[...], u_ref[...])
@@ -452,9 +454,8 @@
     return lax.all_to_all(value, "prow", 0, 0, axis_index_groups=groups)
 
 
-def slotted(send, plan, matrix, lower_inverse, upper_inverse):
+def slotted(got, plan, matrix, lower_inverse, upper_inverse):
     pcol = lax.axis_index("pcol")
-    got = along(send.reshape(4, 64, COLS), X_GROUPS)
     first, rest = kernel_call(turn_kernel, [((8, 48, NB), F32), ((8, 48, REST), F32)])(plan, got)
     first = along(first, Z_GROUPS)
     rest = along(rest, Z_GROUPS)
@@ -533,9 +534,10 @@
         [((256, COLS), F32), ((544, NB), jnp.int32), ((8, NB), jnp.int32)],
         [pltpu.VMEM((8, NB), jnp.int32), pltpu.VMEM((8, NB), jnp.int32)],
     )(pivots.reshape(PANELS, NB), matrix)
+    got = along(send.reshape(4, 64, COLS), X_GROUPS)
     return lax.cond(
         over[0, 0] <= 0,
-        lambda: slotted(send, plan, matrix, lower_inverse, upper_inverse),
+        lambda: slotted(got, plan, matrix, lower_inverse, upper_inverse),
         lambda: dense(pivots, matrix, lower_inverse, upper_inverse),
     )
 

time: 115 us -> 117 us (1.017)
  blocking collectives: 36.6 us -> 19.9 us
  waiting for transfers between devices: 26.1 us -> 36.9 us
  starting transfers between devices: 31.6 us -> 36.3 us
  Pallas kernels: 14.7 us -> 16.9 us
    all_to_all x2 -> x1, blocking collectives: 36.6 us -> 19.9 us  [along(): return lax.all_to_all(value, 'prow', 0, 0, axis_index_groups=groups)]
    all_to_all x2 -> x3, waiting for transfers between devices: 0.89 us -> 11.9 us  [along(): return lax.all_to_all(value, 'prow', 0, 0, axis_index_groups=groups)]
    all_to_all x2 -> x3, starting transfers between devices: 7.2 us -> 11.7 us  [along(): return lax.all_to_all(value, 'prow', 0, 0, axis_index_groups=groups)]
    pallas_call x5, Pallas kernels: 8.4 us -> 10.9 us  [call(): pl.pallas_call(body, in_specs=[VMEM] * len(args), out_specs=[out] * len(s...]
    cond x14 -> x16, local copies, waits for them, and re-layouts: 2.17 us -> 3.05 us
  transfers between devices with their start and end apart: 16 -> 17, of which waited for: 7 -> 8; matrix products, arithmetic and copies ran while one was open for 0% -> 1% of each run, Pallas kernels for 2% -> 2%
where the time goes in v7:
time: 117 us; the launch traced here: 116 us
  waiting for transfers between devices  36.9 us (32%)
  starting transfers between devices  36.3 us (31%)
  blocking collectives  19.9 us (17%)
  Pallas kernels  16.9 us (14%)
  local copies, waits for them, and re-layouts  4.53 us (4%)
    all_to_all x1, blocking collectives, along(): return lax.all_to_all(value, 'prow', 0, 0, axis_index_groups=groups)  19.9 us
    ppermute x6, starting transfers between devices, spread_rest(): lax.ppermute(near, 'pcol', [(q, q ^ n) for q in range(PCOL)])  16.7 us
    all_to_all x3, waiting for transfers between devices, along(): return lax.all_to_all(value, 'prow', 0, 0, axis_index_groups=groups)  11.9 us
    all_to_all x3, starting transfers between devices, along(): return lax.all_to_all(value, 'prow', 0, 0, axis_index_groups=groups)  11.7 us
    pallas_call x5, Pallas kernels, call(): pl.pallas_call(body, in_specs=[VMEM] * len(args), out_specs=[out] * len(s...  10.9 us
    ppermute x2, waiting for transfers between devices, spread_rest(): lax.ppermute(near[half:], 'pcol', [(q + 12, q + 8) for q in range(4)])  10.7 us
    ppermute x2, waiting for transfers between devices, spread_rest(): left = lax.ppermute(near[:half], 'pcol', [(q + 4, q + 8) for q in range(4)])  8.76 us
    pallas_call x1, Pallas kernels, factor(): pl.pallas_call(factor_kernel, in_specs=[VMEM, HBM, VMEM, VMEM] + [HBM] *...  5.96 us
  transfers between devices with their start and end apart: 17, of which 8 were waited for; matrix products, arithmetic and copies ran while one was open for 1% of the time, Pallas kernels for 2%

profile of v7, /device:TPU:40, one launch (start us, length us, event | category | flops | bytes accessed | tf_op | source)
XLA Modules:
  0.0 115.9 jit_solution(6835114685733586385)
XLA Ops:
  0.0 3.4 %shard_map.48 = (f32[256,768]{1,0:T(8,128)}, s32[544,128]{1,0:T(8,128)}, s32[8,128]{1,0:T(8,128)S(1)}) custom-call(s32[4,128]{1,0:T(4,128)} %bitcast.27, f32[256,768]{1,0:T(8,128)} %a_ref.1), custom_call_target="tpu_custom_call" | custom-call | tf_op jit(solution)/shard_map/pallas_call | solution.py:417
  3.5 4.3 %all-to-all-start.9 = ((f32[4,64,768]{2,1,0:T(8,128)}), f32[4,64,768]{2,1,0:T(8,128)S(1)}, u32[]{:S(2)}, u32[]{:S(2)}) async-start(f32[4,64,768]{2,1,0:T(8,128)} %bitcast.16), calls=%async_computation.9 | async-start | bytes 1572864 | tf_op jit(solution)/shard_map/all_to_all | solution.py:454
  9.0 11.0 %all-to-all-done.9 = f32[4,64,768]{2,1,0:T(8,128)S(1)} async-done(((f32[4,64,768]{2,1,0:T(8,128)}), f32[4,64,768]{2,1,0:T(8,128)S(1)}, u32[]{:S(2)}, u32[]{:S(2)}) %all-to-all-start.9) | async-done | bytes 786464 | tf_op jit(solution)/shard_map/all_to_all | solution.py:454
  20.0 94.9 %conditional.1 = (f32[256,768]{1,0:T(8,128)S(1)}) conditional(s32[]{:T(128)} %bitcast.15, (s32[512]{0:T(512)S(1)}, f32[256,768]{1,0:T(8,128)S(1)}, f32[4,128,128]{2,1,0:T(8,128)}, f32[4,128,128]{2,1,0:T(8,128)}) %tuple.23, (s32[544,128]{1,0:T(8,128)}, f32[4,64,768]{2,1,0:T(8,128)S(1)}, f32[256,768]{1,0:T(8,128)S(1)}, f32[4,128,128]{2,1,0:T(8,128)}, ...), branch_computations={%region_0.4_spmd, %region_4.5_spmd} | conditional | flops 1392652 | bytes 65196952 | solution.py:538
  20.9 2.8 %branch_1_fun.5 = (f32[8,48,128]{2,1,0:T(8,128)S(1)}, f32[8,48,640]{2,1,0:T(8,128)}) custom-call(s32[544,128]{1,0:T(8,128)} %get-tuple-element.35.plan_ref, f32[4,64,768]{2,1,0:T(8,128)} %copy-done.15), custom_call_target="tpu_custom_call" | custom-call | tf_op jit(solution)/shard_map/cond/branch_1_fun/pallas_call | solution.py:417
  23.7 19.9 %all_to_all.42.got_ref = f32[8,48,128]{2,1,0:T(8,128)S(1)} all-to-all(f32[8,48,128]{2,1,0:T(8,128)S(1)} %get-tuple-element.37), channel_id=1, replica_groups={{0,16,32,48,64,80,96,112},{128,144,160,176,192,208,224,240},{256,272,28..., dimensions={0} | all-to-all | bytes 393216 | tf_op jit(solution)/shard_map/cond/branch_1_fun/all_to_all | solution.py:454
  43.6 3.7 %all-to-all-start.7 = ((f32[8,48,640]{2,1,0:T(8,128)}), f32[8,48,640]{2,1,0:T(8,128)S(1)}, u32[]{:S(2)}, u32[]{:S(2)}) async-start(f32[8,48,640]{2,1,0:T(8,128)} %get-tuple-element.40), calls=%async_computation.7 | async-start | bytes 1966080 | tf_op jit(solution)/shard_map/cond/branch_1_fun/all_to_all | solution.py:454
  47.3 1.4 %branch_1_fun.6 = (f32[128,128]{1,0:T(8,128)S(1)}, f32[256,128]{1,0:T(8,128)S(1)}) custom-call(s32[544,128]{1,0:T(8,128)S(1)} %copy-done.14, f32[8,48,128]{2,1,0:T(8,128)S(1)} %all_to_all.42.got_ref, f32[256,768]{1,0:T(8,128)} %copy-done.12), custom_call_target="tpu_custom_call" | custom-call | tf_op jit(solution)/shard_map/cond/branch_1_fun/pallas_call | solution.py:417
  50.2 1.3 %collective-permute-start.10 = (f32[64,128]{1,0:T(8,128)S(1)}, f32[64,128]{1,0:T(8,128)S(1)}, u32[]{:S(2)}, u32[]{:S(2)}) collective-permute-start(f32[64,128]{1,0:T(8,128)S(1)} %get-tuple-element.56), channel_id=1, source_target_pairs={{12,8},{13,9},{14,10},{15,11},{28,24},{29,25},{30,26},{31,27},{44,... | collective-permute-start | bytes 98312 | tf_op jit(solution)/shard_map/cond/branch_1_fun/ppermute | solution.py:137
  52.8 9.0 %collective-permute-done.10 = f32[64,128]{1,0:T(8,128)S(1)} collective-permute-done((f32[64,128]{1,0:T(8,128)S(1)}, f32[64,128]{1,0:T(8,128)S(1)}, u32[]{:S(2)}, u32[]{:S(2)}) %collective-permute-start.10) | collective-permute-done | bytes 32800 | tf_op jit(solution)/shard_map/cond/branch_1_fun/ppermute | solution.py:137
  61.8 1.9 %collective-permute-start.11 = (f32[128,128]{1,0:T(8,128)S(1)}, f32[128,128]{1,0:T(8,128)S(1)}, u32[]{:S(2)}, u32[]{:S(2)}) collective-permute-start(f32[128,128]{1,0:T(8,128)S(1)} %maximum_select_fusion.2.refs_0_), channel_id=1, source_target_pairs={{0,1},{1,0},{2,3},{3,2},{4,5},{5,4},{6,7},{7,6},{8,9},{9,8},{10,11... | collective-permute-start | bytes 196616 | tf_op jit(solution)/shard_map/cond/branch_1_fun/ppermute | solution.py:140
  63.8 3.9 %collective-permute-start.12 = (f32[128,128]{1,0:T(8,128)S(1)}, f32[128,128]{1,0:T(8,128)S(1)}, u32[]{:S(2)}, u32[]{:S(2)}) collective-permute-start(f32[128,128]{1,0:T(8,128)S(1)} %maximum_select_fusion.2.refs_0_), channel_id=1, source_target_pairs={{0,2},{1,3},{2,0},{3,1},{4,6},{5,7},{6,4},{7,5},{8,10},{9,11},{10,... | collective-permute-start | bytes 196616 | tf_op jit(solution)/shard_map/cond/branch_1_fun/ppermute | solution.py:140
  67.6 2.0 %collective-permute-start.13 = (f32[128,128]{1,0:T(8,128)S(1)}, f32[128,128]{1,0:T(8,128)S(1)}, u32[]{:S(2)}, u32[]{:S(2)}) collective-permute-start(f32[128,128]{1,0:T(8,128)S(1)} %maximum_select_fusion.2.refs_0_), channel_id=1, source_target_pairs={{0,3},{1,2},{2,1},{3,0},{4,7},{5,6},{6,5},{7,4},{8,11},{9,10},{10,... | collective-permute-start | bytes 196616 | tf_op jit(solution)/shard_map/cond/branch_1_fun/ppermute | solution.py:140
  70.4 3.1 %collective-permute-done.13.refs_3_ = f32[128,128]{1,0:T(8,128)S(1)} collective-permute-done((f32[128,128]{1,0:T(8,128)S(1)}, f32[128,128]{1,0:T(8,128)S(1)}, u32[]{:S(2)}, u32[]{:S(2)}) %collective-permute-start.13) | collective-permute-done | bytes 65568 | tf_op jit(solution)/shard_map/cond/branch_1_fun/ppermute | solution.py:140
  73.5 1.8 %branch_1_fun.7 = f32[4,128,1152]{2,1,0:T(8,128)} custom-call(s32[544,128]{1,0:T(8,128)S(1)} %copy-done.14, f32[128,128]{1,0:T(8,128)S(1)} %get-tuple-element.39.lead_ref, f32[8,48,640]{2,1,0:T(8,128)S(1)} %all-to-all-done.7.got_ref, f32[128,128]{1,0:T(8,128)S(1)} %maximum_select_fusion.2.refs_0_, f32[128,128]{1,0:T(8,128)S(1)} %collective-permute-done.11.refs_1_, ...), custom_call_target="tpu_custom_call" | custom-call | tf_op jit(solution)/shard_map/cond/branch_1_fun/pallas_call | solution.py:417
  75.4 3.6 %all-to-all-start.8 = ((f32[4,128,1152]{2,1,0:T(8,128)}), f32[4,128,1152]{2,1,0:T(8,128)S(1)}, u32[]{:S(2)}, u32[]{:S(2)}) async-start(f32[4,128,1152]{2,1,0:T(8,128)} %branch_1_fun.7), calls=%async_computation.8 | async-start | bytes 4718592 | tf_op jit(solution)/shard_map/cond/branch_1_fun/all_to_all | solution.py:454
  83.2 8.8 %collective-permute-done.16 = f32[128,128]{1,0:T(8,128)S(1)} collective-permute-done((f32[128,128]{1,0:T(8,128)S(1)}, f32[128,128]{1,0:T(8,128)S(1)}, u32[]{:S(2)}, u32[]{:S(2)}) %collective-permute-start.16) | collective-permute-done | bytes 65568 | tf_op jit(solution)/shard_map/cond/branch_1_fun/ppermute | solution.py:136
  91.9 1.7 %collective-permute-done.17 = f32[128,128]{1,0:T(8,128)S(1)} collective-permute-done((f32[128,128]{1,0:T(8,128)S(1)}, f32[128,128]{1,0:T(8,128)S(1)}, u32[]{:S(2)}, u32[]{:S(2)}) %collective-permute-start.17) | collective-permute-done | bytes 65568 | tf_op jit(solution)/shard_map/cond/branch_1_fun/ppermute | solution.py:137
  93.6 1.9 %collective-permute-start.18 = (f32[256,128]{1,0:T(8,128)S(1)}, f32[256,128]{1,0:T(8,128)S(1)}, u32[]{:S(2)}, u32[]{:S(2)}) collective-permute-start(f32[256,128]{1,0:T(8,128)S(1)} %maximum_select_fusion.1.left0_ref), channel_id=1, source_target_pairs={{0,1},{1,0},{2,3},{3,2},{4,5},{5,4},{6,7},{7,6},{8,9},{9,8},{10,11... | collective-permute-start | bytes 393224 | tf_op jit(solution)/shard_map/cond/branch_1_fun/ppermute | solution.py:140
  95.6 4.9 %collective-permute-start.19 = (f32[256,128]{1,0:T(8,128)S(1)}, f32[256,128]{1,0:T(8,128)S(1)}, u32[]{:S(2)}, u32[]{:S(2)}) collective-permute-start(f32[256,128]{1,0:T(8,128)S(1)} %maximum_select_fusion.1.left0_ref), channel_id=1, source_target_pairs={{0,2},{1,3},{2,0},{3,1},{4,6},{5,7},{6,4},{7,5},{8,10},{9,11},{10,... | collective-permute-start | bytes 393224 | tf_op jit(solution)/shard_map/cond/branch_1_fun/ppermute | solution.py:140
  100.5 2.0 %collective-permute-start.20 = (f32[256,128]{1,0:T(8,128)S(1)}, f32[256,128]{1,0:T(8,128)}, u32[]{:S(2)}, u32[]{:S(2)}) collective-permute-start(f32[256,128]{1,0:T(8,128)S(1)} %maximum_select_fusion.1.left0_ref), channel_id=1, source_target_pairs={{0,3},{1,2},{2,1},{3,0},{4,7},{5,6},{6,5},{7,4},{8,11},{9,10},{10,... | collective-permute-start | bytes 393224 | tf_op jit(solution)/shard_map/cond/branch_1_fun/ppermute | solution.py:140
  102.5 1.4 %branch_1_fun.8.right_ref = f32[256,768]{1,0:T(8,128)S(1)} custom-call(s32[544,128]{1,0:T(8,128)} %get-tuple-element.35.plan_ref, f32[256,128]{1,0:T(8,128)S(1)} %get-tuple-element.41.rows_ref, f32[8,48,640]{2,1,0:T(8,128)S(1)} %all-to-all-done.7.got_ref, f32[256,768]{1,0:T(8,128)S(1)} %copy-done.13), custom_call_target="tpu_custom_call" | custom-call | tf_op jit(solution)/shard_map/cond/branch_1_fun/pallas_call | solution.py:417
  106.2 1.7 %collective-permute-done.20.left3_ref = f32[256,128]{1,0:T(8,128)} collective-permute-done((f32[256,128]{1,0:T(8,128)S(1)}, f32[256,128]{1,0:T(8,128)}, u32[]{:S(2)}, u32[]{:S(2)}) %collective-permute-start.20) | collective-permute-done | bytes 131104 | tf_op jit(solution)/shard_map/cond/branch_1_fun/ppermute | solution.py:140
  108.8 6.0 %branch_1_fun.9 = f32[256,768]{1,0:T(8,128)S(1)} custom-call(f32[512,1152]{1,0:T(8,128)S(1)} %bitcast.18, f32[256,768]{1,0:T(8,128)} %copy-done, f32[4,128,128]{2,1,0:T(8,128)} %get-tuple-element.42.lower_ref, f32[4,128,128]{2,1,0:T(8,128)} %get-tuple-element.43.upper_ref, f32[256,128]{1,0:T(8,128)} %copy-done.19, f32[256,128]{1,0:T(8,128)} %copy-done.21, ...), custom_call_target="tpu_custom_call" | custom-call | tf_op jit(solution)/shard_map/cond/branch_1_fun/pallas_call | solution.py:434
  (47 shorter events, 12.9 us)
Async XLA Ops:
  0.0 20.0 %copy-start.23 = (s32[512]{0:T(512)S(1)}, s32[512]{0:T(512)}, u32[]{:S(2)}) copy-start(s32[512]{0:T(512)} %param.7) | copy-start | bytes 6148
  0.0 20.0 %copy-start.10 = (f32[256,768]{1,0:T(8,128)S(1)}, f32[256,768]{1,0:T(8,128)}, u32[]{:S(2)}) copy-start(f32[256,768]{1,0:T(8,128)} %a_ref.1) | copy-start | bytes 2359300
  3.5 16.6 %all-to-all-start.9 = ((f32[4,64,768]{2,1,0:T(8,128)}), f32[4,64,768]{2,1,0:T(8,128)S(1)}, u32[]{:S(2)}, u32[]{:S(2)}) async-start(f32[4,64,768]{2,1,0:T(8,128)} %bitcast.16), calls=%async_computation.9 | async-start | bytes 1572864 | tf_op jit(solution)/shard_map/all_to_all | solution.py:454
  20.0 23.5 %copy-start.12 = (f32[256,768]{1,0:T(8,128)}, f32[256,768]{1,0:T(8,128)S(1)}, u32[]{:S(2)}) copy-start(f32[256,768]{1,0:T(8,128)S(1)} %get-tuple-element.38.a_ref) | copy-start | bytes 2359300 | tf_op jit(solution)/shard_map/cond
  20.9 26.4 %copy-start.14 = (s32[544,128]{1,0:T(8,128)S(1)}, s32[544,128]{1,0:T(8,128)}, u32[]{:S(2)}) copy-start(s32[544,128]{1,0:T(8,128)} %get-tuple-element.35.plan_ref) | copy-start | bytes 835588 | tf_op jit(solution)/shard_map/cond
  43.6 29.9 %all-to-all-start.7 = ((f32[8,48,640]{2,1,0:T(8,128)}), f32[8,48,640]{2,1,0:T(8,128)S(1)}, u32[]{:S(2)}, u32[]{:S(2)}) async-start(f32[8,48,640]{2,1,0:T(8,128)} %get-tuple-element.40), calls=%async_computation.7 | async-start | bytes 1966080 | tf_op jit(solution)/shard_map/cond/branch_1_fun/all_to_all | solution.py:454
  48.8 1.4 %collective-permute-start.7 = (f32[128,128]{1,0:T(8,128)S(1)}, f32[128,128]{1,0:T(8,128)S(1)}, u32[]{:S(2)}, u32[]{:S(2)}) collective-permute-start(f32[128,128]{1,0:T(8,128)S(1)} %get-tuple-element.39.lead_ref), channel_id=1, source_target_pairs={{0,4},{1,5},{2,6},{3,7},{16,20},{17,21},{18,22},{19,23},{32,36},{3... | collective-permute-start | bytes 196616 | tf_op jit(solution)/shard_map/cond/branch_1_fun/ppermute | solution.py:124
  49.5 0.7 collective-permute-start.8
  50.2 11.6 %collective-permute-start.10 = (f32[64,128]{1,0:T(8,128)S(1)}, f32[64,128]{1,0:T(8,128)S(1)}, u32[]{:S(2)}, u32[]{:S(2)}) collective-permute-start(f32[64,128]{1,0:T(8,128)S(1)} %get-tuple-element.56), channel_id=1, source_target_pairs={{12,8},{13,9},{14,10},{15,11},{28,24},{29,25},{30,26},{31,27},{44,... | collective-permute-start | bytes 98312 | tf_op jit(solution)/shard_map/cond/branch_1_fun/ppermute | solution.py:137
  51.5 10.3 %collective-permute-start.9 = (f32[64,128]{1,0:T(8,128)S(1)}, f32[64,128]{1,0:T(8,128)S(1)}, u32[]{:S(2)}, u32[]{:S(2)}) collective-permute-start(f32[64,128]{1,0:T(8,128)S(1)} %get-tuple-element.55), channel_id=1, source_target_pairs={{4,8},{5,9},{6,10},{7,11},{20,24},{21,25},{22,26},{23,27},{36,40},... | collective-permute-start | bytes 98312 | tf_op jit(solution)/shard_map/cond/branch_1_fun/ppermute | solution.py:136
  61.8 7.8 %collective-permute-start.11 = (f32[128,128]{1,0:T(8,128)S(1)}, f32[128,128]{1,0:T(8,128)S(1)}, u32[]{:S(2)}, u32[]{:S(2)}) collective-permute-start(f32[128,128]{1,0:T(8,128)S(1)} %maximum_select_fusion.2.refs_0_), channel_id=1, source_target_pairs={{0,1},{1,0},{2,3},{3,2},{4,5},{5,4},{6,7},{7,6},{8,9},{9,8},{10,11... | collective-permute-start | bytes 196616 | tf_op jit(solution)/shard_map/cond/branch_1_fun/ppermute | solution.py:140
  63.8 6.6 %collective-permute-start.12 = (f32[128,128]{1,0:T(8,128)S(1)}, f32[128,128]{1,0:T(8,128)S(1)}, u32[]{:S(2)}, u32[]{:S(2)}) collective-permute-start(f32[128,128]{1,0:T(8,128)S(1)} %maximum_select_fusion.2.refs_0_), channel_id=1, source_target_pairs={{0,2},{1,3},{2,0},{3,1},{4,6},{5,7},{6,4},{7,5},{8,10},{9,11},{10,... | collective-permute-start | bytes 196616 | tf_op jit(solution)/shard_map/cond/branch_1_fun/ppermute | solution.py:140
  67.6 5.9 %collective-permute-start.13 = (f32[128,128]{1,0:T(8,128)S(1)}, f32[128,128]{1,0:T(8,128)S(1)}, u32[]{:S(2)}, u32[]{:S(2)}) collective-permute-start(f32[128,128]{1,0:T(8,128)S(1)} %maximum_select_fusion.2.refs_0_), channel_id=1, source_target_pairs={{0,3},{1,2},{2,1},{3,0},{4,7},{5,6},{6,5},{7,4},{8,11},{9,10},{10,... | collective-permute-start | bytes 196616 | tf_op jit(solution)/shard_map/cond/branch_1_fun/ppermute | solution.py:140
  75.4 33.4 %all-to-all-start.8 = ((f32[4,128,1152]{2,1,0:T(8,128)}), f32[4,128,1152]{2,1,0:T(8,128)S(1)}, u32[]{:S(2)}, u32[]{:S(2)}) async-start(f32[4,128,1152]{2,1,0:T(8,128)} %branch_1_fun.7), calls=%async_computation.8 | async-start | bytes 4718592 | tf_op jit(solution)/shard_map/cond/branch_1_fun/all_to_all | solution.py:454
  79.0 23.5 %copy-start.13 = (f32[256,768]{1,0:T(8,128)S(1)}, f32[256,768]{1,0:T(8,128)}, u32[]{:S(2)}) copy-start(f32[256,768]{1,0:T(8,128)} %copy-done.12) | copy-start | bytes 2359300 | tf_op jit(solution)/shard_map/cond
  79.0 1.5 %collective-permute-start.14 = (f32[256,128]{1,0:T(8,128)S(1)}, f32[256,128]{1,0:T(8,128)S(1)}, u32[]{:S(2)}, u32[]{:S(2)}) collective-permute-start(f32[256,128]{1,0:T(8,128)S(1)} %get-tuple-element.41.rows_ref), channel_id=1, source_target_pairs={{0,4},{1,5},{2,6},{3,7},{16,20},{17,21},{18,22},{19,23},{32,36},{3... | collective-permute-start | bytes 393224 | tf_op jit(solution)/shard_map/cond/branch_1_fun/ppermute | solution.py:124
  79.8 0.7 collective-permute-start.15
  80.6 11.4 %collective-permute-start.16 = (f32[128,128]{1,0:T(8,128)S(1)}, f32[128,128]{1,0:T(8,128)S(1)}, u32[]{:S(2)}, u32[]{:S(2)}) collective-permute-start(f32[128,128]{1,0:T(8,128)S(1)} %get-tuple-element.53), channel_id=1, source_target_pairs={{4,8},{5,9},{6,10},{7,11},{20,24},{21,25},{22,26},{23,27},{36,40},... | collective-permute-start | bytes 196616 | tf_op jit(solution)/shard_map/cond/branch_1_fun/ppermute | solution.py:136
  81.9 11.7 %collective-permute-start.17 = (f32[128,128]{1,0:T(8,128)S(1)}, f32[128,128]{1,0:T(8,128)S(1)}, u32[]{:S(2)}, u32[]{:S(2)}) collective-permute-start(f32[128,128]{1,0:T(8,128)S(1)} %get-tuple-element.54), channel_id=1, source_target_pairs={{12,8},{13,9},{14,10},{15,11},{28,24},{29,25},{30,26},{31,27},{44,... | collective-permute-start | bytes 196616 | tf_op jit(solution)/shard_map/cond/branch_1_fun/ppermute | solution.py:137
  93.6 11.2 %copy-start.19 = (f32[256,128]{1,0:T(8,128)}, f32[256,128]{1,0:T(8,128)S(1)}, u32[]{:S(2)}) copy-start(f32[256,128]{1,0:T(8,128)S(1)} %maximum_select_fusion.1.left0_ref) | copy-start | bytes 393220 | tf_op jit(solution)/shard_map/cond
  93.6 11.2 %collective-permute-start.18 = (f32[256,128]{1,0:T(8,128)S(1)}, f32[256,128]{1,0:T(8,128)S(1)}, u32[]{:S(2)}, u32[]{:S(2)}) collective-permute-start(f32[256,128]{1,0:T(8,128)S(1)} %maximum_select_fusion.1.left0_ref), channel_id=1, source_target_pairs={{0,1},{1,0},{2,3},{3,2},{4,5},{5,4},{6,7},{7,6},{8,9},{9,8},{10,11... | collective-permute-start | bytes 393224 | tf_op jit(solution)/shard_map/cond/branch_1_fun/ppermute | solution.py:140
  95.6 9.3 %collective-permute-start.19 = (f32[256,128]{1,0:T(8,128)S(1)}, f32[256,128]{1,0:T(8,128)S(1)}, u32[]{:S(2)}, u32[]{:S(2)}) collective-permute-start(f32[256,128]{1,0:T(8,128)S(1)} %maximum_select_fusion.1.left0_ref), channel_id=1, source_target_pairs={{0,2},{1,3},{2,0},{3,1},{4,6},{5,7},{6,4},{7,5},{8,10},{9,11},{10,... | collective-permute-start | bytes 393224 | tf_op jit(solution)/shard_map/cond/branch_1_fun/ppermute | solution.py:140
  100.5 7.4 %collective-permute-start.20 = (f32[256,128]{1,0:T(8,128)S(1)}, f32[256,128]{1,0:T(8,128)}, u32[]{:S(2)}, u32[]{:S(2)}) collective-permute-start(f32[256,128]{1,0:T(8,128)S(1)} %maximum_select_fusion.1.left0_ref), channel_id=1, source_target_pairs={{0,3},{1,2},{2,1},{3,0},{4,7},{5,6},{6,5},{7,4},{8,11},{9,10},{10,... | collective-permute-start | bytes 393224 | tf_op jit(solution)/shard_map/cond/branch_1_fun/ppermute | solution.py:140
  104.0 0.9 copy-start
  (4 other events, 3.1 us)

commit v8 on v7

--- a/solution.py
+++ b/solution.py
@@ -171,7 +171,9 @@
     return jnp.where(iota((column.shape[0], width), 1) == column, 1.0, 0.0).astype(BF)
 
 
-def plan_kernel(pivots_ref, a_ref, send_ref, plan_ref, over_ref, source_ref, target_ref):
+def plan_kernel(
+    pivots_ref, a_ref, first_ref, send_ref, plan_ref, over_ref, source_ref, target_ref
+):
     prow = lax.axis_index("prow")
     x = prow >> 3
     z = prow & 7
@@ -230,7 +232,10 @@
     for n in range(4):
         chosen.append(pieces[n])
         chosen.append(slots(masks[n], order[n], lanef, 48))
-    send_ref[...] = select_rows(onehot_of(jnp.concatenate(chosen, axis=0), ROWS), a_ref[...])
+    picked = select_rows(onehot_of(jnp.concatenate(chosen, axis=0), ROWS), a_ref[...])
+    send_ref[...] = picked
+    for n in range(PROW):
+        first_ref[n] = picked[64 * (n // 8) : 64 * (n // 8) + 16, :NB]
 
     panel = source_ref[pl.ds(x, 1), :]
     panel_z = (panel >> 7) & 7
@@ -253,6 +258,10 @@
     zcol = lane_sum(sub == lane, zf)
     ahead = lane_sum((zf == zcol) & (lane < sub), 1.0)
     plan_ref[160:288, :] = wide((zcol * 32.0 + ahead).astype(jnp.int32))
+    own = owner_of(panel).astype(F32)
+    owncol = lane_sum(sub == lane, own)
+    ahead = lane_sum((own == owncol) & (lane < sub), 1.0)
+    plan_ref[544:672, :] = wide((owncol * 16.0 + ahead).astype(jnp.int32))
     masks = [(target[k] >= TOP) & (owner_of(target[k]) == prow) for k in range(PANELS)]
     order = ranks(masks)
     row = iota((ROWS, NB), 0)
@@ -275,32 +284,37 @@
     over_ref[...] = jnp.broadcast_to(over, (8, NB)).astype(jnp.int32)
 
 
-def turn_kernel(plan_ref, got_ref, first_ref, rest_ref):
+def turn_kernel(plan_ref, got_ref, send_ref):
     got = got_ref[...].reshape(256, COLS)
-    rows = select_rows(onehot_of(plan_ref[0:32, :1], 256), got)
+    rows = select_rows(onehot_of(plan_ref[0:32, :1], 256), got[:, NB:])
     moved = plan_ref[32:160, :1]
     moved = jnp.where(moved < 0, -1, moved + 16)
     sent = select_rows(onehot_of(moved, 64), got[:64])
     for n in range(8):
-        first_ref[n, 0:32, :] = rows[:, :NB]
-        rest_ref[n, 0:32, :] = rows[:, NB:]
-        first_ref[n, 32:48, :] = sent[n * 16 : n * 16 + 16, :NB]
-        rest_ref[n, 32:48, :] = sent[n * 16 : n * 16 + 16, NB:]
-
-
-def lead_kernel(plan_ref, got_ref, a_ref, lead_ref, rows_ref):
-    got = jnp.concatenate([got_ref[n, 0:32, :] for n in range(8)], axis=0)
-    lead_ref[...] = select_rows(onehot_of(plan_ref[160:288, :1], 256), got)
-    moved = jnp.concatenate([got_ref[n, 32:48, :] for n in range(4)], axis=0)
-    slot = plan_ref[288:544, :1]
-    moved = select_rows(onehot_of(slot, 64), moved)
-    rows_ref[...] = jnp.where(slot >= 0, moved, a_ref[:, :NB])
+        for c in range(REST // NB):
+            send_ref[n, 32 * c : 32 * c + 32, :] = rows[:, c * NB : c * NB + NB]
+        for c in range(COLS // NB):
+            spot = 160 + 16 * c
+            send_ref[n, spot : spot + 16, :] = sent[16 * n : 16 * n + 16, c * NB : c * NB + NB]
+
+
+def pivot_part(got_ref, c):
+    return jnp.concatenate([got_ref[n, 32 * c : 32 * c + 32, :] for n in range(8)], axis=0)
+
+
+def moved_part(got_ref, c):
+    spot = 160 + 16 * c
+    return jnp.concatenate([got_ref[n, spot : spot + 16, :] for n in range(4)], axis=0)
+
+
+def lead_kernel(plan_ref, got_ref, lead_ref):
+    lead_ref[...] = select_rows(onehot_of(plan_ref[544:672, :1], PROW * 16), got_ref[...])
 
 
 def panel_kernel(plan_ref, lead_ref, got_ref, *refs):
     blocks, send_ref, full_ref, sems = refs[:4], refs[4], refs[5], refs[6]
     panel = lax.axis_index("prow") >> 3
-    got = jnp.concatenate([got_ref[n, 0:32, :] for n in range(8)], axis=0)
+    got = jnp.concatenate([pivot_part(got_ref, c) for c in range(REST // NB)], axis=1)
     full_ref[:, :NB] = lead_ref[...]
     full_ref[:, NB:COLS] = select_rows(onehot_of(plan_ref[160:288, :1], 256), got)
 
@@ -330,9 +344,15 @@
     return pl.ds(pl.multiple_of(index * NB, NB), NB)
 
 
+def first_rows_kernel(plan_ref, got_ref, a_ref, out_ref):
+    slot = plan_ref[288:544, :1]
+    moved = select_rows(onehot_of(slot, 64), moved_part(got_ref, 0))
+    out_ref[...] = jnp.where(slot >= 0, moved, a_ref[:, :NB])
+
+
 def own_rows_kernel(plan_ref, rows_ref, got_ref, a_ref, out_ref):
     slot = plan_ref[288:544, :1]
-    moved = jnp.concatenate([got_ref[n, 32:48, :] for n in range(4)], axis=0)
+    moved = jnp.concatenate([moved_part(got_ref, c) for c in range(1, COLS // NB)], axis=1)
     moved = select_rows(onehot_of(slot, 64), moved)
     out_ref[:, :NB] = rows_ref[...]
     out_ref[:, NB:] = jnp.where(slot >= 0, moved, a_ref[:, NB:])
@@ -454,15 +474,13 @@
     return lax.all_to_all(value, "prow", 0, 0, axis_index_groups=groups)
 
 
-def slotted(got, plan, matrix, lower_inverse, upper_inverse):
+def slotted(first, send, plan, matrix, lower_inverse, upper_inverse):
     pcol = lax.axis_index("pcol")
-    first, rest = kernel_call(turn_kernel, [((8, 48, NB), F32), ((8, 48, REST), F32)])(plan, got)
-    first = along(first, Z_GROUPS)
+    (lead,) = kernel_call(lead_kernel, [((NB, NB), F32)])(plan, first)
+    got = along(send.reshape(4, 64, COLS), X_GROUPS)
+    ends = spread_start(lead)
+    (rest,) = kernel_call(turn_kernel, [((8, 256, NB), F32)])(plan, got)
     rest = along(rest, Z_GROUPS)
-    lead, rows = kernel_call(lead_kernel, [((NB, NB), F32), ((ROWS, NB), F32)])(
-        plan, first, matrix
-    )
-    ends = spread_start(lead)
     late = spread_rest(lead, *ends, pcol)
     (send,) = kernel_call(
         panel_kernel,
@@ -471,6 +489,7 @@
         HBM,
     )(plan, lead, rest, *late)
     top = along(send, X_GROUPS).reshape(TOP, WIDE - NB)
+    (rows,) = kernel_call(first_rows_kernel, [((ROWS, NB), F32)])(plan, rest, matrix)
     ends = spread_start(rows)
     left = spread_rest(rows, *ends, pcol)
     (right,) = kernel_call(own_rows_kernel, [((ROWS, COLS), F32)])(plan, rows, rest, matrix)
@@ -529,15 +548,20 @@
 
 
 def per_device(matrix, pivots, lower_inverse, upper_inverse):
-    send, plan, over = kernel_call(
+    first, send, plan, over = kernel_call(
         plan_kernel,
-        [((256, COLS), F32), ((544, NB), jnp.int32), ((8, NB), jnp.int32)],
+        [
+            ((PROW, 16, NB), F32),
+            ((256, COLS), F32),
+            ((672, NB), jnp.int32),
+            ((8, NB), jnp.int32),
+        ],
         [pltpu.VMEM((8, NB), jnp.int32), pltpu.VMEM((8, NB), jnp.int32)],
     )(pivots.reshape(PANELS, NB), matrix)
-    got = along(send.reshape(4, 64, COLS), X_GROUPS)
+    first = lax.all_to_all(first, "prow", 0, 0).reshape(PROW * 16, NB)
     return lax.cond(
         over[0, 0] <= 0,
-        lambda: slotted(got, plan, matrix, lower_inverse, upper_inverse),
+        lambda: slotted(first, send, plan, matrix, lower_inverse, upper_inverse),
         lambda: dense(pivots, matrix, lower_inverse, upper_inverse),
     )
 

time: 117 us -> 120 us (1.026)
  the two profiles are of different devices: /device:TPU:40 before, /device:TPU:43 now
where the time goes in v8:
time: 120 us; the launch traced here: 119 us
  starting transfers between devices  56 us (47%)
  waiting for transfers between devices  31 us (26%)
  Pallas kernels  15.9 us (13%)
  blocking collectives  11.9 us (10%)
  local copies, waits for them, and re-layouts  3.07 us (3%)
    ppermute x6, starting transfers between devices, spread_rest(): lax.ppermute(near, 'pcol', [(q, q ^ n) for q in range(PCOL)])  23.7 us
    all_to_all x1, starting transfers between devices, per_device(): first = lax.all_to_all(first, 'prow', 0, 0).reshape(PROW * 16, NB)  12.9 us
    all_to_all x1, blocking collectives, along(): return lax.all_to_all(value, 'prow', 0, 0, axis_index_groups=groups)  11.9 us
    all_to_all x2, starting transfers between devices, along(): return lax.all_to_all(value, 'prow', 0, 0, axis_index_groups=groups)  11.6 us
    ppermute x2, waiting for transfers between devices, spread_rest(): lax.ppermute(near[half:], 'pcol', [(q + 12, q + 8) for q in range(4)])  10 us
    pallas_call x6, Pallas kernels, call(): pl.pallas_call(body, in_specs=[VMEM] * len(args), out_specs=[out] * len(s...  9.98 us
    all_to_all x1, waiting for transfers between devices, per_device(): first = lax.all_to_all(first, 'prow', 0, 0).reshape(PROW * 16, NB)  7.68 us
    ppermute x6, waiting for transfers between devices, spread_rest(): lax.ppermute(near, 'pcol', [(q, q ^ n) for q in range(PCOL)])  7.57 us
  transfers between devices with their start and end apart: 17, of which 8 were waited for; matrix products, arithmetic and copies ran while one was open for 0% of the time, Pallas kernels for 3%

profile of v8, /device:TPU:43, one launch (start us, length us, event | category | flops | bytes accessed | tf_op | source)
XLA Modules:
  0.0 119.1 jit_solution(12480259907320683005)
XLA Ops:
  0.0 3.4 %shard_map.48 = (f32[32,16,128]{2,1,0:T(8,128)}, f32[256,768]{1,0:T(8,128)}, s32[672,128]{1,0:T(8,128)}, s32[8,128]{1,0:T(8,128)S(1)}) custom-call(s32[4,128]{1,0:T(4,128)} %bitcast.30, f32[256,768]{1,0:T(8,128)} %a_ref.1), custom_call_target="tpu_custom_call" | custom-call | tf_op jit(solution)/shard_map/pallas_call | solution.py:437
  3.4 12.9 %all-to-all-start.9 = ((f32[32,16,128]{2,1,0:T(8,128)}), f32[32,16,128]{2,1,0:T(8,128)S(1)}, u32[]{:S(2)}, u32[]{:S(2)}) async-start(f32[32,16,128]{2,1,0:T(8,128)} %get-tuple-element.49), calls=%async_computation.9 | async-start | bytes 524288 | tf_op jit(solution)/shard_map/all_to_all | solution.py:561
  17.4 7.7 %all-to-all-done.9 = f32[32,16,128]{2,1,0:T(8,128)S(1)} async-done(((f32[32,16,128]{2,1,0:T(8,128)}), f32[32,16,128]{2,1,0:T(8,128)S(1)}, u32[]{:S(2)}, u32[]{:S(2)}) %all-to-all-start.9) | async-done | bytes 262176 | tf_op jit(solution)/shard_map/all_to_all | solution.py:561
  25.1 93.2 %conditional.1 = (f32[256,768]{1,0:T(8,128)S(1)}) conditional(s32[]{:T(128)} %bitcast.17, (s32[512]{0:T(512)}, f32[256,768]{1,0:T(8,128)}, f32[4,128,128]{2,1,0:T(8,128)}, f32[4,128,128]{2,1,0:T(8,128)}) %tuple.11, (f32[32,16,128]{2,1,0:T(8,128)S(1)}, s32[672,128]{1,0:T(8,128)}, f32[256,768]{1,0:T(8,128)}, f32[256,768]{1,0:T(8,128)}, ...), branch_computations={%region_0.4_spmd, %region_4.5_spmd} | conditional | flops 1392652 | bytes 63624084 | solution.py:562
  25.1 11.9 %all_to_all.42.got_ref = f32[4,64,768]{2,1,0:T(8,128)S(1)} all-to-all(f32[4,64,768]{2,1,0:T(8,128)} %bitcast.26), channel_id=1, replica_groups={{0,128,256,384},{16,144,272,400},{32,160,288,416},{48,176,304,432},{64,..., dimensions={0} | all-to-all | bytes 1572864 | tf_op jit(solution)/shard_map/cond/branch_1_fun/all_to_all | solution.py:474
  37.0 1.5 %branch_1_fun.7 = f32[8,256,128]{2,1,0:T(8,128)} custom-call(s32[672,128]{1,0:T(8,128)S(1)} %copy-done.11, f32[4,64,768]{2,1,0:T(8,128)S(1)} %all_to_all.42.got_ref), custom_call_target="tpu_custom_call" | custom-call | tf_op jit(solution)/shard_map/cond/branch_1_fun/pallas_call | solution.py:437
  38.5 6.8 %all-to-all-start.7 = ((f32[8,256,128]{2,1,0:T(8,128)}), f32[8,256,128]{2,1,0:T(8,128)S(1)}, u32[]{:S(2)}, u32[]{:S(2)}) async-start(f32[8,256,128]{2,1,0:T(8,128)} %branch_1_fun.7), calls=%async_computation.7 | async-start | bytes 2097152 | tf_op jit(solution)/shard_map/cond/branch_1_fun/all_to_all | solution.py:474
  48.0 1.3 %collective-permute-start.10 = (f32[64,128]{1,0:T(8,128)S(1)}, f32[64,128]{1,0:T(8,128)S(1)}, u32[]{:S(2)}, u32[]{:S(2)}) collective-permute-start(f32[64,128]{1,0:T(8,128)S(1)} %get-tuple-element.58), channel_id=1, source_target_pairs={{12,8},{13,9},{14,10},{15,11},{28,24},{29,25},{30,26},{31,27},{44,... | collective-permute-start | bytes 98312 | tf_op jit(solution)/shard_map/cond/branch_1_fun/ppermute | solution.py:137
  49.3 1.3 %collective-permute-start.9 = (f32[64,128]{1,0:T(8,128)S(1)}, f32[64,128]{1,0:T(8,128)S(1)}, u32[]{:S(2)}, u32[]{:S(2)}) collective-permute-start(f32[64,128]{1,0:T(8,128)S(1)} %get-tuple-element.57), channel_id=1, source_target_pairs={{4,8},{5,9},{6,10},{7,11},{20,24},{21,25},{22,26},{23,27},{36,40},... | collective-permute-start | bytes 98312 | tf_op jit(solution)/shard_map/cond/branch_1_fun/ppermute | solution.py:136
  50.6 7.5 %collective-permute-done.10 = f32[64,128]{1,0:T(8,128)S(1)} collective-permute-done((f32[64,128]{1,0:T(8,128)S(1)}, f32[64,128]{1,0:T(8,128)S(1)}, u32[]{:S(2)}, u32[]{:S(2)}) %collective-permute-start.10) | collective-permute-done | bytes 32800 | tf_op jit(solution)/shard_map/cond/branch_1_fun/ppermute | solution.py:137
  58.1 6.5 %collective-permute-start.11 = (f32[128,128]{1,0:T(8,128)S(1)}, f32[128,128]{1,0:T(8,128)S(1)}, u32[]{:S(2)}, u32[]{:S(2)}) collective-permute-start(f32[128,128]{1,0:T(8,128)S(1)} %maximum_select_fusion.2.refs_0_), channel_id=1, source_target_pairs={{0,1},{1,0},{2,3},{3,2},{4,5},{5,4},{6,7},{7,6},{8,9},{9,8},{10,11... | collective-permute-start | bytes 196616 | tf_op jit(solution)/shard_map/cond/branch_1_fun/ppermute | solution.py:140
  64.6 3.6 %collective-permute-start.12 = (f32[128,128]{1,0:T(8,128)S(1)}, f32[128,128]{1,0:T(8,128)S(1)}, u32[]{:S(2)}, u32[]{:S(2)}) collective-permute-start(f32[128,128]{1,0:T(8,128)S(1)} %maximum_select_fusion.2.refs_0_), channel_id=1, source_target_pairs={{0,2},{1,3},{2,0},{3,1},{4,6},{5,7},{6,4},{7,5},{8,10},{9,11},{10,... | collective-permute-start | bytes 196616 | tf_op jit(solution)/shard_map/cond/branch_1_fun/ppermute | solution.py:140
  68.2 1.9 %collective-permute-start.13 = (f32[128,128]{1,0:T(8,128)S(1)}, f32[128,128]{1,0:T(8,128)S(1)}, u32[]{:S(2)}, u32[]{:S(2)}) collective-permute-start(f32[128,128]{1,0:T(8,128)S(1)} %maximum_select_fusion.2.refs_0_), channel_id=1, source_target_pairs={{0,3},{1,2},{2,1},{3,0},{4,7},{5,6},{6,5},{7,4},{8,11},{9,10},{10,... | collective-permute-start | bytes 196616 | tf_op jit(solution)/shard_map/cond/branch_1_fun/ppermute | solution.py:140
  70.6 3.8 %collective-permute-done.13.refs_3_ = f32[128,128]{1,0:T(8,128)S(1)} collective-permute-done((f32[128,128]{1,0:T(8,128)S(1)}, f32[128,128]{1,0:T(8,128)S(1)}, u32[]{:S(2)}, u32[]{:S(2)}) %collective-permute-start.13) | collective-permute-done | bytes 65568 | tf_op jit(solution)/shard_map/cond/branch_1_fun/ppermute | solution.py:140
  74.4 1.8 %branch_1_fun.8 = f32[4,128,1152]{2,1,0:T(8,128)} custom-call(s32[672,128]{1,0:T(8,128)S(1)} %copy-done.11, f32[128,128]{1,0:T(8,128)S(1)} %branch_1_fun.6.lead_ref, f32[8,256,128]{2,1,0:T(8,128)S(1)} %all-to-all-done.7.got_ref, f32[128,128]{1,0:T(8,128)S(1)} %maximum_select_fusion.2.refs_0_, f32[128,128]{1,0:T(8,128)S(1)} %collective-permute-done.11.refs_1_, ...), custom_call_target="tpu_custom_call" | custom-call | tf_op jit(solution)/shard_map/cond/branch_1_fun/pallas_call | solution.py:437
  76.2 4.8 %all-to-all-start.8 = ((f32[4,128,1152]{2,1,0:T(8,128)}), f32[4,128,1152]{2,1,0:T(8,128)S(1)}, u32[]{:S(2)}, u32[]{:S(2)}) async-start(f32[4,128,1152]{2,1,0:T(8,128)} %branch_1_fun.8), calls=%async_computation.8 | async-start | bytes 4718592 | tf_op jit(solution)/shard_map/cond/branch_1_fun/all_to_all | solution.py:474
  81.0 1.6 %branch_1_fun.9.rows_ref = f32[256,128]{1,0:T(8,128)S(1)} custom-call(s32[672,128]{1,0:T(8,128)} %get-tuple-element.38.plan_ref, f32[8,256,128]{2,1,0:T(8,128)S(1)} %all-to-all-done.7.got_ref, f32[256,768]{1,0:T(8,128)} %get-tuple-element.41.a_ref), custom_call_target="tpu_custom_call" | custom-call | tf_op jit(solution)/shard_map/cond/branch_1_fun/pallas_call | solution.py:437
  86.6 5.7 %collective-permute-done.16 = f32[128,128]{1,0:T(8,128)S(1)} collective-permute-done((f32[128,128]{1,0:T(8,128)S(1)}, f32[128,128]{1,0:T(8,128)S(1)}, u32[]{:S(2)}, u32[]{:S(2)}) %collective-permute-start.16) | collective-permute-done | bytes 65568 | tf_op jit(solution)/shard_map/cond/branch_1_fun/ppermute | solution.py:136
  92.3 2.5 %collective-permute-done.17 = f32[128,128]{1,0:T(8,128)S(1)} collective-permute-done((f32[128,128]{1,0:T(8,128)S(1)}, f32[128,128]{1,0:T(8,128)S(1)}, u32[]{:S(2)}, u32[]{:S(2)}) %collective-permute-start.17) | collective-permute-done | bytes 65568 | tf_op jit(solution)/shard_map/cond/branch_1_fun/ppermute | solution.py:137
  94.9 5.2 %collective-permute-start.18 = (f32[256,128]{1,0:T(8,128)S(1)}, f32[256,128]{1,0:T(8,128)S(1)}, u32[]{:S(2)}, u32[]{:S(2)}) collective-permute-start(f32[256,128]{1,0:T(8,128)S(1)} %maximum_select_fusion.1.left0_ref), channel_id=1, source_target_pairs={{0,1},{1,0},{2,3},{3,2},{4,5},{5,4},{6,7},{7,6},{8,9},{9,8},{10,11... | collective-permute-start | bytes 393224 | tf_op jit(solution)/shard_map/cond/branch_1_fun/ppermute | solution.py:140
  100.1 4.5 %collective-permute-start.19 = (f32[256,128]{1,0:T(8,128)S(1)}, f32[256,128]{1,0:T(8,128)S(1)}, u32[]{:S(2)}, u32[]{:S(2)}) collective-permute-start(f32[256,128]{1,0:T(8,128)S(1)} %maximum_select_fusion.1.left0_ref), channel_id=1, source_target_pairs={{0,2},{1,3},{2,0},{3,1},{4,6},{5,7},{6,4},{7,5},{8,10},{9,11},{10,... | collective-permute-start | bytes 393224 | tf_op jit(solution)/shard_map/cond/branch_1_fun/ppermute | solution.py:140
  104.7 1.9 %collective-permute-start.20 = (f32[256,128]{1,0:T(8,128)S(1)}, f32[256,128]{1,0:T(8,128)}, u32[]{:S(2)}, u32[]{:S(2)}) collective-permute-start(f32[256,128]{1,0:T(8,128)S(1)} %maximum_select_fusion.1.left0_ref), channel_id=1, source_target_pairs={{0,3},{1,2},{2,1},{3,0},{4,7},{5,6},{6,5},{7,4},{8,11},{9,10},{10,... | collective-permute-start | bytes 393224 | tf_op jit(solution)/shard_map/cond/branch_1_fun/ppermute | solution.py:140
  109.3 2.8 %collective-permute-done.20.left3_ref = f32[256,128]{1,0:T(8,128)} collective-permute-done((f32[256,128]{1,0:T(8,128)S(1)}, f32[256,128]{1,0:T(8,128)}, u32[]{:S(2)}, u32[]{:S(2)}) %collective-permute-start.20) | collective-permute-done | bytes 131104 | tf_op jit(solution)/shard_map/cond/branch_1_fun/ppermute | solution.py:140
  112.1 5.9 %branch_1_fun.11 = f32[256,768]{1,0:T(8,128)S(1)} custom-call(f32[512,1152]{1,0:T(8,128)S(1)} %bitcast.19, f32[256,768]{1,0:T(8,128)} %copy-done, f32[4,128,128]{2,1,0:T(8,128)} %get-tuple-element.42.lower_ref, f32[4,128,128]{2,1,0:T(8,128)} %get-tuple-element.43.upper_ref, f32[256,128]{1,0:T(8,128)} %copy-done.18, f32[256,128]{1,0:T(8,128)} %copy-done.20, ...), custom_call_target="tpu_custom_call" | custom-call | tf_op jit(solution)/shard_map/cond/branch_1_fun/pallas_call | solution.py:454
  (44 shorter events, 11.1 us)
Async XLA Ops:
  3.4 21.7 %all-to-all-start.9 = ((f32[32,16,128]{2,1,0:T(8,128)}), f32[32,16,128]{2,1,0:T(8,128)S(1)}, u32[]{:S(2)}, u32[]{:S(2)}) async-start(f32[32,16,128]{2,1,0:T(8,128)} %get-tuple-element.49), calls=%async_computation.9 | async-start | bytes 524288 | tf_op jit(solution)/shard_map/all_to_all | solution.py:561
  25.1 13.4 %copy-start.16 = (f32[32,16,128]{2,1,0:T(8,128)}, f32[32,16,128]{2,1,0:T(8,128)S(1)}, u32[]{:S(2)}) copy-start(f32[32,16,128]{2,1,0:T(8,128)S(1)} %get-tuple-element.39) | copy-start | bytes 786436 | tf_op jit(solution)/shard_map/cond
  25.1 11.9 %copy-start.11 = (s32[672,128]{1,0:T(8,128)S(1)}, s32[672,128]{1,0:T(8,128)}, u32[]{:S(2)}) copy-start(s32[672,128]{1,0:T(8,128)} %get-tuple-element.38.plan_ref) | copy-start | bytes 1032196 | tf_op jit(solution)/shard_map/cond
  38.5 35.9 %all-to-all-start.7 = ((f32[8,256,128]{2,1,0:T(8,128)}), f32[8,256,128]{2,1,0:T(8,128)S(1)}, u32[]{:S(2)}, u32[]{:S(2)}) async-start(f32[8,256,128]{2,1,0:T(8,128)} %branch_1_fun.7), calls=%async_computation.7 | async-start | bytes 2097152 | tf_op jit(solution)/shard_map/cond/branch_1_fun/all_to_all | solution.py:474
  46.6 1.4 %collective-permute-start.7 = (f32[128,128]{1,0:T(8,128)S(1)}, f32[128,128]{1,0:T(8,128)S(1)}, u32[]{:S(2)}, u32[]{:S(2)}) collective-permute-start(f32[128,128]{1,0:T(8,128)S(1)} %branch_1_fun.6.lead_ref), channel_id=1, source_target_pairs={{0,4},{1,5},{2,6},{3,7},{16,20},{17,21},{18,22},{19,23},{32,36},{3... | collective-permute-start | bytes 196616 | tf_op jit(solution)/shard_map/cond/branch_1_fun/ppermute | solution.py:124
  47.2 0.7 collective-permute-start.8
  48.0 10.1 %collective-permute-start.10 = (f32[64,128]{1,0:T(8,128)S(1)}, f32[64,128]{1,0:T(8,128)S(1)}, u32[]{:S(2)}, u32[]{:S(2)}) collective-permute-start(f32[64,128]{1,0:T(8,128)S(1)} %get-tuple-element.58), channel_id=1, source_target_pairs={{12,8},{13,9},{14,10},{15,11},{28,24},{29,25},{30,26},{31,27},{44,... | collective-permute-start | bytes 98312 | tf_op jit(solution)/shard_map/cond/branch_1_fun/ppermute | solution.py:137
  49.3 8.8 %collective-permute-start.9 = (f32[64,128]{1,0:T(8,128)S(1)}, f32[64,128]{1,0:T(8,128)S(1)}, u32[]{:S(2)}, u32[]{:S(2)}) collective-permute-start(f32[64,128]{1,0:T(8,128)S(1)} %get-tuple-element.57), channel_id=1, source_target_pairs={{4,8},{5,9},{6,10},{7,11},{20,24},{21,25},{22,26},{23,27},{36,40},... | collective-permute-start | bytes 98312 | tf_op jit(solution)/shard_map/cond/branch_1_fun/ppermute | solution.py:136
  58.1 12.0 %collective-permute-start.11 = (f32[128,128]{1,0:T(8,128)S(1)}, f32[128,128]{1,0:T(8,128)S(1)}, u32[]{:S(2)}, u32[]{:S(2)}) collective-permute-start(f32[128,128]{1,0:T(8,128)S(1)} %maximum_select_fusion.2.refs_0_), channel_id=1, source_target_pairs={{0,1},{1,0},{2,3},{3,2},{4,5},{5,4},{6,7},{7,6},{8,9},{9,8},{10,11... | collective-permute-start | bytes 196616 | tf_op jit(solution)/shard_map/cond/branch_1_fun/ppermute | solution.py:140
  64.6 6.0 %collective-permute-start.12 = (f32[128,128]{1,0:T(8,128)S(1)}, f32[128,128]{1,0:T(8,128)S(1)}, u32[]{:S(2)}, u32[]{:S(2)}) collective-permute-start(f32[128,128]{1,0:T(8,128)S(1)} %maximum_select_fusion.2.refs_0_), channel_id=1, source_target_pairs={{0,2},{1,3},{2,0},{3,1},{4,6},{5,7},{6,4},{7,5},{8,10},{9,11},{10,... | collective-permute-start | bytes 196616 | tf_op jit(solution)/shard_map/cond/branch_1_fun/ppermute | solution.py:140
  68.2 6.2 %collective-permute-start.13 = (f32[128,128]{1,0:T(8,128)S(1)}, f32[128,128]{1,0:T(8,128)S(1)}, u32[]{:S(2)}, u32[]{:S(2)}) collective-permute-start(f32[128,128]{1,0:T(8,128)S(1)} %maximum_select_fusion.2.refs_0_), channel_id=1, source_target_pairs={{0,3},{1,2},{2,1},{3,0},{4,7},{5,6},{6,5},{7,4},{8,11},{9,10},{10,... | collective-permute-start | bytes 196616 | tf_op jit(solution)/shard_map/cond/branch_1_fun/ppermute | solution.py:140
  76.2 35.9 %all-to-all-start.8 = ((f32[4,128,1152]{2,1,0:T(8,128)}), f32[4,128,1152]{2,1,0:T(8,128)S(1)}, u32[]{:S(2)}, u32[]{:S(2)}) async-start(f32[4,128,1152]{2,1,0:T(8,128)} %branch_1_fun.8), calls=%async_computation.8 | async-start | bytes 4718592 | tf_op jit(solution)/shard_map/cond/branch_1_fun/all_to_all | solution.py:474
  81.0 25.6 %copy-start.10 = (f32[256,768]{1,0:T(8,128)S(1)}, f32[256,768]{1,0:T(8,128)}, u32[]{:S(2)}) copy-start(f32[256,768]{1,0:T(8,128)} %get-tuple-element.41.a_ref) | copy-start | bytes 2359300 | tf_op jit(solution)/shard_map/cond
  81.0 25.6 %copy-start.12 = (s32[672,128]{1,0:T(8,128)S(1)}, s32[672,128]{1,0:T(8,128)}, u32[]{:S(2)}) copy-start(s32[672,128]{1,0:T(8,128)} %get-tuple-element.38.plan_ref) | copy-start | bytes 1032196 | tf_op jit(solution)/shard_map/cond
  82.6 1.4 %collective-permute-start.14 = (f32[256,128]{1,0:T(8,128)S(1)}, f32[256,128]{1,0:T(8,128)S(1)}, u32[]{:S(2)}, u32[]{:S(2)}) collective-permute-start(f32[256,128]{1,0:T(8,128)S(1)} %branch_1_fun.9.rows_ref), channel_id=1, source_target_pairs={{0,4},{1,5},{2,6},{3,7},{16,20},{17,21},{18,22},{19,23},{32,36},{3... | collective-permute-start | bytes 393224 | tf_op jit(solution)/shard_map/cond/branch_1_fun/ppermute | solution.py:124
  83.3 0.7 collective-permute-start.15
  84.0 8.3 %collective-permute-start.16 = (f32[128,128]{1,0:T(8,128)S(1)}, f32[128,128]{1,0:T(8,128)S(1)}, u32[]{:S(2)}, u32[]{:S(2)}) collective-permute-start(f32[128,128]{1,0:T(8,128)S(1)} %get-tuple-element.55), channel_id=1, source_target_pairs={{4,8},{5,9},{6,10},{7,11},{20,24},{21,25},{22,26},{23,27},{36,40},... | collective-permute-start | bytes 196616 | tf_op jit(solution)/shard_map/cond/branch_1_fun/ppermute | solution.py:136
  85.3 9.6 %collective-permute-start.17 = (f32[128,128]{1,0:T(8,128)S(1)}, f32[128,128]{1,0:T(8,128)S(1)}, u32[]{:S(2)}, u32[]{:S(2)}) collective-permute-start(f32[128,128]{1,0:T(8,128)S(1)} %get-tuple-element.56), channel_id=1, source_target_pairs={{12,8},{13,9},{14,10},{15,11},{28,24},{29,25},{30,26},{31,27},{44,... | collective-permute-start | bytes 196616 | tf_op jit(solution)/shard_map/cond/branch_1_fun/ppermute | solution.py:137
  94.9 17.2 %copy-start.18 = (f32[256,128]{1,0:T(8,128)}, f32[256,128]{1,0:T(8,128)S(1)}, u32[]{:S(2)}) copy-start(f32[256,128]{1,0:T(8,128)S(1)} %maximum_select_fusion.1.left0_ref) | copy-start | bytes 393220 | tf_op jit(solution)/shard_map/cond
  94.9 13.1 %collective-permute-start.18 = (f32[256,128]{1,0:T(8,128)S(1)}, f32[256,128]{1,0:T(8,128)S(1)}, u32[]{:S(2)}, u32[]{:S(2)}) collective-permute-start(f32[256,128]{1,0:T(8,128)S(1)} %maximum_select_fusion.1.left0_ref), channel_id=1, source_target_pairs={{0,1},{1,0},{2,3},{3,2},{4,5},{5,4},{6,7},{7,6},{8,9},{9,8},{10,11... | collective-permute-start | bytes 393224 | tf_op jit(solution)/shard_map/cond/branch_1_fun/ppermute | solution.py:140
  100.1 8.4 %collective-permute-start.19 = (f32[256,128]{1,0:T(8,128)S(1)}, f32[256,128]{1,0:T(8,128)S(1)}, u32[]{:S(2)}, u32[]{:S(2)}) collective-permute-start(f32[256,128]{1,0:T(8,128)S(1)} %maximum_select_fusion.1.left0_ref), channel_id=1, source_target_pairs={{0,2},{1,3},{2,0},{3,1},{4,6},{5,7},{6,4},{7,5},{8,10},{9,11},{10,... | collective-permute-start | bytes 393224 | tf_op jit(solution)/shard_map/cond/branch_1_fun/ppermute | solution.py:140
  104.7 7.4 %collective-permute-start.20 = (f32[256,128]{1,0:T(8,128)S(1)}, f32[256,128]{1,0:T(8,128)}, u32[]{:S(2)}, u32[]{:S(2)}) collective-permute-start(f32[256,128]{1,0:T(8,128)S(1)} %maximum_select_fusion.1.left0_ref), channel_id=1, source_target_pairs={{0,3},{1,2},{2,1},{3,0},{4,7},{5,6},{6,5},{7,4},{8,11},{9,10},{10,... | collective-permute-start | bytes 393224 | tf_op jit(solution)/shard_map/cond/branch_1_fun/ppermute | solution.py:140
  107.1 0.9 copy-start
  118.2 0.9 copy-start.17
  (2 other events, 1.3 us)

commit v9 on v8

--- a/solution.py
+++ b/solution.py
@@ -172,7 +172,8 @@
 
 
 def plan_kernel(
-    pivots_ref, a_ref, first_ref, send_ref, plan_ref, over_ref, source_ref, target_ref
+    pivots_ref, a_ref, send_ref, leave0_ref, leave1_ref, leave2_ref, leave3_ref, plan_ref, over_ref,
+    source_ref, target_ref,
 ):
     prow = lax.axis_index("prow")
     x = prow >> 3
@@ -220,22 +221,19 @@
 
     masks = [owner_of(source[k]) == prow for k in range(PANELS)]
     order = ranks(masks)
-    pieces = [
+    chosen = [
         slots(masks[k], order[k], local_of(source[k]).astype(F32), 16) for k in range(PANELS)
     ]
+    send_ref[...] = select_rows(onehot_of(jnp.concatenate(chosen, axis=0), ROWS), a_ref[...])
     mine = target_ref[pl.ds(prow & 3, 1), :]
     leaves = (mine >= TOP) & (prow < PANELS)
     masks = [leaves & (((mine >> 10) & 3) == n) for n in range(4)]
     order = ranks(masks)
     lanef = lane_row.astype(F32)
-    chosen = []
-    for n in range(4):
-        chosen.append(pieces[n])
-        chosen.append(slots(masks[n], order[n], lanef, 48))
-    picked = select_rows(onehot_of(jnp.concatenate(chosen, axis=0), ROWS), a_ref[...])
-    send_ref[...] = picked
-    for n in range(PROW):
-        first_ref[n] = picked[64 * (n // 8) : 64 * (n // 8) + 16, :NB]
+    chosen = [slots(masks[n], order[n], lanef, 48) for n in range(4)]
+    leaving = select_rows(onehot_of(jnp.concatenate(chosen, axis=0), NB), a_ref[:NB, :])
+    for n, ref in enumerate((leave0_ref, leave1_ref, leave2_ref, leave3_ref)):
+        ref[...] = leaving[48 * n : 48 * n + 48]
 
     panel = source_ref[pl.ds(x, 1), :]
     panel_z = (panel >> 7) & 7
@@ -245,7 +243,7 @@
     order = ranks(masks)
     spot = jnp.zeros((1, NB), F32)
     for n in range(4):
-        spot = spot + jnp.where(masks[n], order[n] + 64.0 * n, 0.0)
+        spot = spot + jnp.where(masks[n], order[n] + 16.0 * n, 0.0)
     wide = lambda column: jnp.broadcast_to(column, (column.shape[0], NB))
     plan_ref[0:32, :] = wide(slots(here, order[4], spot, 32))
     other = target_ref[pl.ds(z & 3, 1), :]
@@ -258,10 +256,6 @@
     zcol = lane_sum(sub == lane, zf)
     ahead = lane_sum((zf == zcol) & (lane < sub), 1.0)
     plan_ref[160:288, :] = wide((zcol * 32.0 + ahead).astype(jnp.int32))
-    own = owner_of(panel).astype(F32)
-    owncol = lane_sum(sub == lane, own)
-    ahead = lane_sum((own == owncol) & (lane < sub), 1.0)
-    plan_ref[544:672, :] = wide((owncol * 16.0 + ahead).astype(jnp.int32))
     masks = [(target[k] >= TOP) & (owner_of(target[k]) == prow) for k in range(PANELS)]
     order = ranks(masks)
     row = iota((ROWS, NB), 0)
@@ -284,20 +278,29 @@
     over_ref[...] = jnp.broadcast_to(over, (8, NB)).astype(jnp.int32)
 
 
-def turn_kernel(plan_ref, got_ref, send_ref):
-    got = got_ref[...].reshape(256, COLS)
-    rows = select_rows(onehot_of(plan_ref[0:32, :1], 256), got[:, NB:])
-    moved = plan_ref[32:160, :1]
-    moved = jnp.where(moved < 0, -1, moved + 16)
-    sent = select_rows(onehot_of(moved, 64), got[:64])
+def turn_kernel(plan_ref, got_ref, first_ref, rest_ref):
+    rows = select_rows(onehot_of(plan_ref[0:32, :1], 64), got_ref[...])
+    for n in range(8):
+        first_ref[n] = rows[:, :NB]
+    rest_ref[...] = rows[:, NB:]
+
+
+def join_kernel(plan_ref, rows_ref, leave0_ref, leave1_ref, leave2_ref, leave3_ref, send_ref):
+    held = leave1_ref[...] + leave2_ref[...] + leave3_ref[...]
+    held = jnp.where(lax.axis_index("prow") < 8, leave0_ref[...], held)
+    sent = select_rows(onehot_of(plan_ref[32:160, :1], 48), held)
     for n in range(8):
         for c in range(REST // NB):
-            send_ref[n, 32 * c : 32 * c + 32, :] = rows[:, c * NB : c * NB + NB]
+            send_ref[n, 32 * c : 32 * c + 32, :] = rows_ref[:, c * NB : c * NB + NB]
         for c in range(COLS // NB):
             spot = 160 + 16 * c
             send_ref[n, spot : spot + 16, :] = sent[16 * n : 16 * n + 16, c * NB : c * NB + NB]
 
 
+def lead_kernel(plan_ref, got_ref, lead_ref):
+    lead_ref[...] = select_rows(onehot_of(plan_ref[160:288, :1], 256), got_ref[...])
+
+
 def pivot_part(got_ref, c):
     return jnp.concatenate([got_ref[n, 32 * c : 32 * c + 32, :] for n in range(8)], axis=0)
 
@@ -305,10 +308,6 @@
 def moved_part(got_ref, c):
     spot = 160 + 16 * c
     return jnp.concatenate([got_ref[n, spot : spot + 16, :] for n in range(4)], axis=0)
-
-
-def lead_kernel(plan_ref, got_ref, lead_ref):
-    lead_ref[...] = select_rows(onehot_of(plan_ref[544:672, :1], PROW * 16), got_ref[...])
 
 
 def panel_kernel(plan_ref, lead_ref, got_ref, *refs):
@@ -474,13 +473,21 @@
     return lax.all_to_all(value, "prow", 0, 0, axis_index_groups=groups)
 
 
-def slotted(first, send, plan, matrix, lower_inverse, upper_inverse):
+def slotted(send, leaving, plan, matrix, lower_inverse, upper_inverse):
     pcol = lax.axis_index("pcol")
-    (lead,) = kernel_call(lead_kernel, [((NB, NB), F32)])(plan, first)
-    got = along(send.reshape(4, 64, COLS), X_GROUPS)
+    got = along(send.reshape(4, 16, COLS), X_GROUPS)
+    held = [leaving[0]]
+    for n in range(1, 4):
+        pairs = [(k, 8 * n + k) for k in range(PANELS)]
+        held.append(lax.ppermute(leaving[n], "prow", pairs))
+    first, rest = kernel_call(turn_kernel, [((8, 32, NB), F32), ((32, REST), F32)])(
+        plan, got.reshape(64, COLS)
+    )
+    first = along(first, Z_GROUPS)
+    (rest,) = kernel_call(join_kernel, [((8, 256, NB), F32)])(plan, rest, *held)
+    rest = along(rest, Z_GROUPS)
+    (lead,) = kernel_call(lead_kernel, [((NB, NB), F32)])(plan, first.reshape(256, NB))
     ends = spread_start(lead)
-    (rest,) = kernel_call(turn_kernel, [((8, 256, NB), F32)])(plan, got)
-    rest = along(rest, Z_GROUPS)
     late = spread_rest(lead, *ends, pcol)
     (send,) = kernel_call(
         panel_kernel,
@@ -548,20 +555,16 @@
 
 
 def per_device(matrix, pivots, lower_inverse, upper_inverse):
-    first, send, plan, over = kernel_call(
+    send, *leaving, plan, over = kernel_call(
         plan_kernel,
-        [
-            ((PROW, 16, NB), F32),
-            ((256, COLS), F32),
-            ((672, NB), jnp.int32),
-            ((8, NB), jnp.int32),
-        ],
+        [((64, COLS), F32)]
+        + [((48, COLS), F32)] * 4
+        + [((544, NB), jnp.int32), ((8, NB), jnp.int32)],
         [pltpu.VMEM((8, NB), jnp.int32), pltpu.VMEM((8, NB), jnp.int32)],
     )(pivots.reshape(PANELS, NB), matrix)
-    first = lax.all_to_all(first, "prow", 0, 0).reshape(PROW * 16, NB)
     return lax.cond(
         over[0, 0] <= 0,
-        lambda: slotted(first, send, plan, matrix, lower_inverse, upper_inverse),
+        lambda: slotted(send, leaving, plan, matrix, lower_inverse, upper_inverse),
         lambda: dense(pivots, matrix, lower_inverse, upper_inverse),
     )
 

time: 120 us -> 115 us (0.958)
  waiting for transfers between devices: 31 us -> 27 us
  blocking collectives: 11.9 us -> 8.38 us
  Pallas kernels: 15.9 us -> 17.8 us
    all_to_all x1 -> x0, starting transfers between devices: 12.9 us -> none  [per_device(): first = lax.all_to_all(first, 'prow', 0, 0).reshape(PROW * 16, NB)]
    all_to_all x2 -> x3, starting transfers between devices: 11.6 us -> 21.2 us  [along(): return lax.all_to_all(value, 'prow', 0, 0, axis_index_groups=groups)]
    all_to_all x1 -> x0, waiting for transfers between devices: 7.68 us -> none  [per_device(): first = lax.all_to_all(first, 'prow', 0, 0).reshape(PROW * 16, NB)]
    ppermute x2, waiting for transfers between devices: 5.72 us -> 11.1 us  [spread_rest(): left = lax.ppermute(near[:half], 'pcol', [(q + 4, q + 8) for q in range(4)])]
    ppermute x2, waiting for transfers between devices: 10 us -> 5.12 us  [spread_rest(): lax.ppermute(near[half:], 'pcol', [(q + 12, q + 8) for q in range(4)])]
    all_to_all x1, blocking collectives: 11.9 us -> 8.38 us  [along(): return lax.all_to_all(value, 'prow', 0, 0, axis_index_groups=groups)]
    ppermute x0 -> x3, waiting for transfers between devices: none -> 3.27 us  [slotted(): held.append(lax.ppermute(leaving[n], 'prow', pairs))]
    ppermute x0 -> x3, starting transfers between devices: none -> 2.8 us  [slotted(): held.append(lax.ppermute(leaving[n], 'prow', pairs))]
  transfers between devices with their start and end apart: 17 -> 20, of which waited for: 8 -> 9; matrix products, arithmetic and copies ran while one was open for 0% -> 0% of each run, Pallas kernels for 3% -> 4%
where the time goes in v9:
time: 115 us; the launch traced here: 114 us
  starting transfers between devices  56.3 us (49%)
  waiting for transfers between devices  27 us (23%)
  Pallas kernels  17.8 us (15%)
  blocking collectives  8.38 us (7%)
  local copies, waits for them, and re-layouts  3.05 us (3%)
    ppermute x6, starting transfers between devices, spread_rest(): lax.ppermute(near, 'pcol', [(q, q ^ n) for q in range(PCOL)])  24.5 us
    all_to_all x3, starting transfers between devices, along(): return lax.all_to_all(value, 'prow', 0, 0, axis_index_groups=groups)  21.2 us
    pallas_call x7, Pallas kernels, call(): pl.pallas_call(body, in_specs=[VMEM] * len(args), out_specs=[out] * len(s...  11.8 us
    ppermute x2, waiting for transfers between devices, spread_rest(): left = lax.ppermute(near[:half], 'pcol', [(q + 4, q + 8) for q in range(4)])  11.1 us
    all_to_all x1, blocking collectives, along(): return lax.all_to_all(value, 'prow', 0, 0, axis_index_groups=groups)  8.38 us
    ppermute x6, waiting for transfers between devices, spread_rest(): lax.ppermute(near, 'pcol', [(q, q ^ n) for q in range(PCOL)])  7.42 us
    pallas_call x1, Pallas kernels, factor(): pl.pallas_call(factor_kernel, in_specs=[VMEM, HBM, VMEM, VMEM] + [HBM] *...  5.94 us
    ppermute x2, waiting for transfers between devices, spread_rest(): lax.ppermute(near[half:], 'pcol', [(q + 12, q + 8) for q in range(4)])  5.12 us
  transfers between devices with their start and end apart: 20, of which 9 were waited for; matrix products, arithmetic and copies ran while one was open for 0% of the time, Pallas kernels for 4%

profile of v9, /device:TPU:43, one launch (start us, length us, event | category | flops | bytes accessed | tf_op | source)
XLA Modules:
  0.0 113.7 jit_solution(8663527152985135299)
XLA Ops:
  0.0 3.4 %shard_map.48 = (f32[64,768]{1,0:T(8,128)}, f32[48,768]{1,0:T(8,128)}, f32[48,768]{1,0:T(8,128)}, f32[48,768]{1,0:T(8,128)}, f32[48,768]{1,0:T(8,128)}, /*index=5*/s32[544,128]{1,0:T(8,128)}, s32[8,128]{1,0:T(8,128)S(1)}) custom-call(s32[4,128]{1,0:T(4,128)} %bitcast.32, f32[256,768]{1,0:T(8,128)} %a_ref.1), custom_call_target="tpu_custom_call" | custom-call | tf_op jit(solution)/shard_map/pallas_call | solution.py:436
  4.6 108.2 %conditional.1 = (f32[256,768]{1,0:T(8,128)S(1)}) conditional(s32[]{:T(128)} %bitcast.18, (s32[512]{0:T(512)}, f32[256,768]{1,0:T(8,128)}, f32[4,128,128]{2,1,0:T(8,128)}, f32[4,128,128]{2,1,0:T(8,128)}) %tuple.11, (f32[64,768]{1,0:T(8,128)}, s32[544,128]{1,0:T(8,128)}, f32[48,768]{1,0:T(8,128)}, f32[48,768]{1,0:T(8,128)}, f32[48,768]{1,0:T(8,128)}, ...), branch_computations={%region_0.4_spmd, %region_4.5_spmd} | conditional | flops 1392652 | bytes 63624084 | solution.py:565
  4.6 8.4 %all_to_all.41 = f32[4,16,768]{2,1,0:T(8,128)S(1)} all-to-all(f32[4,16,768]{2,1,0:T(8,128)} %bitcast.30), channel_id=1, replica_groups={{0,128,256,384},{16,144,272,400},{32,160,288,416},{48,176,304,432},{64,..., dimensions={0} | all-to-all | bytes 393216 | tf_op jit(solution)/shard_map/cond/branch_1_fun/all_to_all | solution.py:473
  13.0 1.9 %branch_1_fun.7 = (f32[8,32,128]{2,1,0:T(8,128)}, f32[32,640]{1,0:T(8,128)S(1)}) custom-call(s32[544,128]{1,0:T(8,128)} %get-tuple-element.43.plan_ref, f32[64,768]{1,0:T(8,128)S(1)} %bitcast.22), custom_call_target="tpu_custom_call" | custom-call | tf_op jit(solution)/shard_map/cond/branch_1_fun/pallas_call | solution.py:436
  14.8 10.0 %all-to-all-start.7 = ((f32[8,32,128]{2,1,0:T(8,128)}), f32[8,32,128]{2,1,0:T(8,128)S(1)}, u32[]{:S(2)}, u32[]{:S(2)}) async-start(f32[8,32,128]{2,1,0:T(8,128)} %get-tuple-element.45), calls=%async_computation.7 | async-start | bytes 262144 | tf_op jit(solution)/shard_map/cond/branch_1_fun/all_to_all | solution.py:473
  27.7 3.3 %collective-permute-done.7.leave1_ref = f32[48,768]{1,0:T(8,128)S(1)} collective-permute-done((f32[48,768]{1,0:T(8,128)}, f32[48,768]{1,0:T(8,128)S(1)}, u32[]{:S(2)}, u32[]{:S(2)}) %collective-permute-start.7) | collective-permute-done | bytes 147488 | tf_op jit(solution)/shard_map/cond/branch_1_fun/ppermute | solution.py:482
  31.0 2.4 %branch_1_fun.9 = f32[8,256,128]{2,1,0:T(8,128)} custom-call(s32[544,128]{1,0:T(8,128)} %get-tuple-element.43.plan_ref, f32[32,640]{1,0:T(8,128)S(1)} %get-tuple-element.46.rows_ref, f32[48,768]{1,0:T(8,128)} %get-tuple-element.47.leave0_ref, f32[48,768]{1,0:T(8,128)S(1)} %collective-permute-done.7.leave1_ref, ...), custom_call_target="tpu_custom_call" | custom-call | tf_op jit(solution)/shard_map/cond/branch_1_fun/pallas_call | solution.py:436
  33.4 4.8 %all-to-all-start.8 = ((f32[8,256,128]{2,1,0:T(8,128)}), f32[8,256,128]{2,1,0:T(8,128)S(1)}, u32[]{:S(2)}, u32[]{:S(2)}) async-start(f32[8,256,128]{2,1,0:T(8,128)} %branch_1_fun.9), calls=%async_computation.8 | async-start | bytes 2097152 | tf_op jit(solution)/shard_map/cond/branch_1_fun/all_to_all | solution.py:473
  42.5 6.0 %collective-permute-done.12 = f32[64,128]{1,0:T(8,128)S(1)} collective-permute-done((f32[64,128]{1,0:T(8,128)S(1)}, f32[64,128]{1,0:T(8,128)S(1)}, u32[]{:S(2)}, u32[]{:S(2)}) %collective-permute-start.12) | collective-permute-done | bytes 32800 | tf_op jit(solution)/shard_map/cond/branch_1_fun/ppermute | solution.py:136
  48.6 2.1 %collective-permute-done.13 = f32[64,128]{1,0:T(8,128)S(1)} collective-permute-done((f32[64,128]{1,0:T(8,128)S(1)}, f32[64,128]{1,0:T(8,128)S(1)}, u32[]{:S(2)}, u32[]{:S(2)}) %collective-permute-start.13) | collective-permute-done | bytes 32800 | tf_op jit(solution)/shard_map/cond/branch_1_fun/ppermute | solution.py:137
  50.7 7.3 %collective-permute-start.14 = (f32[128,128]{1,0:T(8,128)S(1)}, f32[128,128]{1,0:T(8,128)S(1)}, u32[]{:S(2)}, u32[]{:S(2)}) collective-permute-start(f32[128,128]{1,0:T(8,128)S(1)} %maximum_select_fusion.2.refs_0_), channel_id=1, source_target_pairs={{0,1},{1,0},{2,3},{3,2},{4,5},{5,4},{6,7},{7,6},{8,9},{9,8},{10,11... | collective-permute-start | bytes 196616 | tf_op jit(solution)/shard_map/cond/branch_1_fun/ppermute | solution.py:140
  58.0 3.6 %collective-permute-start.15 = (f32[128,128]{1,0:T(8,128)S(1)}, f32[128,128]{1,0:T(8,128)S(1)}, u32[]{:S(2)}, u32[]{:S(2)}) collective-permute-start(f32[128,128]{1,0:T(8,128)S(1)} %maximum_select_fusion.2.refs_0_), channel_id=1, source_target_pairs={{0,2},{1,3},{2,0},{3,1},{4,6},{5,7},{6,4},{7,5},{8,10},{9,11},{10,... | collective-permute-start | bytes 196616 | tf_op jit(solution)/shard_map/cond/branch_1_fun/ppermute | solution.py:140
  61.6 1.9 %collective-permute-start.16 = (f32[128,128]{1,0:T(8,128)S(1)}, f32[128,128]{1,0:T(8,128)S(1)}, u32[]{:S(2)}, u32[]{:S(2)}) collective-permute-start(f32[128,128]{1,0:T(8,128)S(1)} %maximum_select_fusion.2.refs_0_), channel_id=1, source_target_pairs={{0,3},{1,2},{2,1},{3,0},{4,7},{5,6},{6,5},{7,4},{8,11},{9,10},{10,... | collective-permute-start | bytes 196616 | tf_op jit(solution)/shard_map/cond/branch_1_fun/ppermute | solution.py:140
  63.9 3.6 %collective-permute-done.16.refs_3_ = f32[128,128]{1,0:T(8,128)S(1)} collective-permute-done((f32[128,128]{1,0:T(8,128)S(1)}, f32[128,128]{1,0:T(8,128)S(1)}, u32[]{:S(2)}, u32[]{:S(2)}) %collective-permute-start.16) | collective-permute-done | bytes 65568 | tf_op jit(solution)/shard_map/cond/branch_1_fun/ppermute | solution.py:140
  67.6 1.8 %branch_1_fun.10 = f32[4,128,1152]{2,1,0:T(8,128)} custom-call(s32[544,128]{1,0:T(8,128)S(1)} %copy-done.11, f32[128,128]{1,0:T(8,128)S(1)} %branch_1_fun.8.lead_ref, f32[8,256,128]{2,1,0:T(8,128)S(1)} %all-to-all-done.8.got_ref, f32[128,128]{1,0:T(8,128)S(1)} %maximum_select_fusion.2.refs_0_, f32[128,128]{1,0:T(8,128)S(1)} %collective-permute-done.14.refs_1_, ...), custom_call_target="tpu_custom_call" | custom-call | tf_op jit(solution)/shard_map/cond/branch_1_fun/pallas_call | solution.py:436
  69.4 6.3 %all-to-all-start.9 = ((f32[4,128,1152]{2,1,0:T(8,128)}), f32[4,128,1152]{2,1,0:T(8,128)S(1)}, u32[]{:S(2)}, u32[]{:S(2)}) async-start(f32[4,128,1152]{2,1,0:T(8,128)} %branch_1_fun.10), calls=%async_computation.9 | async-start | bytes 4718592 | tf_op jit(solution)/shard_map/cond/branch_1_fun/all_to_all | solution.py:473
  75.7 1.6 %branch_1_fun.11.rows_ref = f32[256,128]{1,0:T(8,128)S(1)} custom-call(s32[544,128]{1,0:T(8,128)} %get-tuple-element.43.plan_ref, f32[8,256,128]{2,1,0:T(8,128)S(1)} %all-to-all-done.8.got_ref, f32[256,768]{1,0:T(8,128)} %get-tuple-element.51.a_ref), custom_call_target="tpu_custom_call" | custom-call | tf_op jit(solution)/shard_map/cond/branch_1_fun/pallas_call | solution.py:436
  81.3 5.1 %collective-permute-done.19 = f32[128,128]{1,0:T(8,128)S(1)} collective-permute-done((f32[128,128]{1,0:T(8,128)S(1)}, f32[128,128]{1,0:T(8,128)S(1)}, u32[]{:S(2)}, u32[]{:S(2)}) %collective-permute-start.19) | collective-permute-done | bytes 65568 | tf_op jit(solution)/shard_map/cond/branch_1_fun/ppermute | solution.py:136
  86.4 3.0 %collective-permute-done.20 = f32[128,128]{1,0:T(8,128)S(1)} collective-permute-done((f32[128,128]{1,0:T(8,128)S(1)}, f32[128,128]{1,0:T(8,128)S(1)}, u32[]{:S(2)}, u32[]{:S(2)}) %collective-permute-start.20) | collective-permute-done | bytes 65568 | tf_op jit(solution)/shard_map/cond/branch_1_fun/ppermute | solution.py:137
  89.4 5.4 %collective-permute-start.21 = (f32[256,128]{1,0:T(8,128)S(1)}, f32[256,128]{1,0:T(8,128)S(1)}, u32[]{:S(2)}, u32[]{:S(2)}) collective-permute-start(f32[256,128]{1,0:T(8,128)S(1)} %maximum_select_fusion.1.left0_ref), channel_id=1, source_target_pairs={{0,1},{1,0},{2,3},{3,2},{4,5},{5,4},{6,7},{7,6},{8,9},{9,8},{10,11... | collective-permute-start | bytes 393224 | tf_op jit(solution)/shard_map/cond/branch_1_fun/ppermute | solution.py:140
  94.8 4.4 %collective-permute-start.22 = (f32[256,128]{1,0:T(8,128)S(1)}, f32[256,128]{1,0:T(8,128)S(1)}, u32[]{:S(2)}, u32[]{:S(2)}) collective-permute-start(f32[256,128]{1,0:T(8,128)S(1)} %maximum_select_fusion.1.left0_ref), channel_id=1, source_target_pairs={{0,2},{1,3},{2,0},{3,1},{4,6},{5,7},{6,4},{7,5},{8,10},{9,11},{10,... | collective-permute-start | bytes 393224 | tf_op jit(solution)/shard_map/cond/branch_1_fun/ppermute | solution.py:140
  99.2 1.9 %collective-permute-start.23 = (f32[256,128]{1,0:T(8,128)S(1)}, f32[256,128]{1,0:T(8,128)}, u32[]{:S(2)}, u32[]{:S(2)}) collective-permute-start(f32[256,128]{1,0:T(8,128)S(1)} %maximum_select_fusion.1.left0_ref), channel_id=1, source_target_pairs={{0,3},{1,2},{2,1},{3,0},{4,7},{5,6},{6,5},{7,4},{8,11},{9,10},{10,... | collective-permute-start | bytes 393224 | tf_op jit(solution)/shard_map/cond/branch_1_fun/ppermute | solution.py:140
  103.8 2.8 %collective-permute-done.23.left3_ref = f32[256,128]{1,0:T(8,128)} collective-permute-done((f32[256,128]{1,0:T(8,128)S(1)}, f32[256,128]{1,0:T(8,128)}, u32[]{:S(2)}, u32[]{:S(2)}) %collective-permute-start.23) | collective-permute-done | bytes 131104 | tf_op jit(solution)/shard_map/cond/branch_1_fun/ppermute | solution.py:140
  106.6 5.9 %branch_1_fun.13 = f32[256,768]{1,0:T(8,128)S(1)} custom-call(f32[512,1152]{1,0:T(8,128)S(1)} %bitcast.20, f32[256,768]{1,0:T(8,128)} %copy-done, f32[4,128,128]{2,1,0:T(8,128)} %get-tuple-element.52.lower_ref, f32[4,128,128]{2,1,0:T(8,128)} %get-tuple-element.53.upper_ref, f32[256,128]{1,0:T(8,128)} %copy-done.17, f32[256,128]{1,0:T(8,128)} %copy-done.19, ...), custom_call_target="tpu_custom_call" | custom-call | tf_op jit(solution)/shard_map/cond/branch_1_fun/pallas_call | solution.py:453
  (49 shorter events, 15.5 us)
Async XLA Ops:
  14.8 18.6 %all-to-all-start.7 = ((f32[8,32,128]{2,1,0:T(8,128)}), f32[8,32,128]{2,1,0:T(8,128)S(1)}, u32[]{:S(2)}, u32[]{:S(2)}) async-start(f32[8,32,128]{2,1,0:T(8,128)} %get-tuple-element.45), calls=%async_computation.7 | async-start | bytes 262144 | tf_op jit(solution)/shard_map/cond/branch_1_fun/all_to_all | solution.py:473
  24.9 6.1 %collective-permute-start.7 = (f32[48,768]{1,0:T(8,128)}, f32[48,768]{1,0:T(8,128)S(1)}, u32[]{:S(2)}, u32[]{:S(2)}) collective-permute-start(f32[48,768]{1,0:T(8,128)} %get-tuple-element.48), channel_id=1, source_target_pairs={{0,128},{16,144},{32,160},{48,176},{1,129},{17,145},{33,161},{49,1... | collective-permute-start | bytes 442376 | tf_op jit(solution)/shard_map/cond/branch_1_fun/ppermute | solution.py:482
  26.2 4.8 %collective-permute-start.8 = (f32[48,768]{1,0:T(8,128)}, f32[48,768]{1,0:T(8,128)S(1)}, u32[]{:S(2)}, u32[]{:S(2)}) collective-permute-start(f32[48,768]{1,0:T(8,128)} %get-tuple-element.49), channel_id=1, source_target_pairs={{0,256},{16,272},{32,288},{48,304},{1,257},{17,273},{33,289},{49,3... | collective-permute-start | bytes 442376 | tf_op jit(solution)/shard_map/cond/branch_1_fun/ppermute | solution.py:482
  26.8 4.1 %collective-permute-start.9 = (f32[48,768]{1,0:T(8,128)}, f32[48,768]{1,0:T(8,128)S(1)}, u32[]{:S(2)}, u32[]{:S(2)}) collective-permute-start(f32[48,768]{1,0:T(8,128)} %get-tuple-element.50), channel_id=1, source_target_pairs={{0,384},{16,400},{32,416},{48,432},{1,385},{17,401},{33,417},{49,4... | collective-permute-start | bytes 442376 | tf_op jit(solution)/shard_map/cond/branch_1_fun/ppermute | solution.py:482
  31.0 7.3 %copy-start.11 = (s32[544,128]{1,0:T(8,128)S(1)}, s32[544,128]{1,0:T(8,128)}, u32[]{:S(2)}) copy-start(s32[544,128]{1,0:T(8,128)} %get-tuple-element.43.plan_ref) | copy-start | bytes 835588 | tf_op jit(solution)/shard_map/cond
  33.4 34.2 %all-to-all-start.8 = ((f32[8,256,128]{2,1,0:T(8,128)}), f32[8,256,128]{2,1,0:T(8,128)S(1)}, u32[]{:S(2)}, u32[]{:S(2)}) async-start(f32[8,256,128]{2,1,0:T(8,128)} %branch_1_fun.9), calls=%async_computation.8 | async-start | bytes 2097152 | tf_op jit(solution)/shard_map/cond/branch_1_fun/all_to_all | solution.py:473
  38.5 1.4 %collective-permute-start.10 = (f32[128,128]{1,0:T(8,128)S(1)}, f32[128,128]{1,0:T(8,128)S(1)}, u32[]{:S(2)}, u32[]{:S(2)}) collective-permute-start(f32[128,128]{1,0:T(8,128)S(1)} %branch_1_fun.8.lead_ref), channel_id=1, source_target_pairs={{0,4},{1,5},{2,6},{3,7},{16,20},{17,21},{18,22},{19,23},{32,36},{3... | collective-permute-start | bytes 196616 | tf_op jit(solution)/shard_map/cond/branch_1_fun/ppermute | solution.py:124
  39.2 0.7 collective-permute-start.11
  39.9 8.7 %collective-permute-start.12 = (f32[64,128]{1,0:T(8,128)S(1)}, f32[64,128]{1,0:T(8,128)S(1)}, u32[]{:S(2)}, u32[]{:S(2)}) collective-permute-start(f32[64,128]{1,0:T(8,128)S(1)} %get-tuple-element.73), channel_id=1, source_target_pairs={{4,8},{5,9},{6,10},{7,11},{20,24},{21,25},{22,26},{23,27},{36,40},... | collective-permute-start | bytes 98312 | tf_op jit(solution)/shard_map/cond/branch_1_fun/ppermute | solution.py:136
  41.2 9.5 %collective-permute-start.13 = (f32[64,128]{1,0:T(8,128)S(1)}, f32[64,128]{1,0:T(8,128)S(1)}, u32[]{:S(2)}, u32[]{:S(2)}) collective-permute-start(f32[64,128]{1,0:T(8,128)S(1)} %get-tuple-element.74), channel_id=1, source_target_pairs={{12,8},{13,9},{14,10},{15,11},{28,24},{29,25},{30,26},{31,27},{44,... | collective-permute-start | bytes 98312 | tf_op jit(solution)/shard_map/cond/branch_1_fun/ppermute | solution.py:137
  50.7 12.8 %collective-permute-start.14 = (f32[128,128]{1,0:T(8,128)S(1)}, f32[128,128]{1,0:T(8,128)S(1)}, u32[]{:S(2)}, u32[]{:S(2)}) collective-permute-start(f32[128,128]{1,0:T(8,128)S(1)} %maximum_select_fusion.2.refs_0_), channel_id=1, source_target_pairs={{0,1},{1,0},{2,3},{3,2},{4,5},{5,4},{6,7},{7,6},{8,9},{9,8},{10,11... | collective-permute-start | bytes 196616 | tf_op jit(solution)/shard_map/cond/branch_1_fun/ppermute | solution.py:140
  58.0 6.0 %collective-permute-start.15 = (f32[128,128]{1,0:T(8,128)S(1)}, f32[128,128]{1,0:T(8,128)S(1)}, u32[]{:S(2)}, u32[]{:S(2)}) collective-permute-start(f32[128,128]{1,0:T(8,128)S(1)} %maximum_select_fusion.2.refs_0_), channel_id=1, source_target_pairs={{0,2},{1,3},{2,0},{3,1},{4,6},{5,7},{6,4},{7,5},{8,10},{9,11},{10,... | collective-permute-start | bytes 196616 | tf_op jit(solution)/shard_map/cond/branch_1_fun/ppermute | solution.py:140
  61.6 6.0 %collective-permute-start.16 = (f32[128,128]{1,0:T(8,128)S(1)}, f32[128,128]{1,0:T(8,128)S(1)}, u32[]{:S(2)}, u32[]{:S(2)}) collective-permute-start(f32[128,128]{1,0:T(8,128)S(1)} %maximum_select_fusion.2.refs_0_), channel_id=1, source_target_pairs={{0,3},{1,2},{2,1},{3,0},{4,7},{5,6},{6,5},{7,4},{8,11},{9,10},{10,... | collective-permute-start | bytes 196616 | tf_op jit(solution)/shard_map/cond/branch_1_fun/ppermute | solution.py:140
  69.4 37.2 %all-to-all-start.9 = ((f32[4,128,1152]{2,1,0:T(8,128)}), f32[4,128,1152]{2,1,0:T(8,128)S(1)}, u32[]{:S(2)}, u32[]{:S(2)}) async-start(f32[4,128,1152]{2,1,0:T(8,128)} %branch_1_fun.10), calls=%async_computation.9 | async-start | bytes 4718592 | tf_op jit(solution)/shard_map/cond/branch_1_fun/all_to_all | solution.py:473
  75.7 25.5 %copy-start.10 = (f32[256,768]{1,0:T(8,128)S(1)}, f32[256,768]{1,0:T(8,128)}, u32[]{:S(2)}) copy-start(f32[256,768]{1,0:T(8,128)} %get-tuple-element.51.a_ref) | copy-start | bytes 2359300 | tf_op jit(solution)/shard_map/cond
  75.7 25.5 %copy-start.12 = (s32[544,128]{1,0:T(8,128)S(1)}, s32[544,128]{1,0:T(8,128)}, u32[]{:S(2)}) copy-start(s32[544,128]{1,0:T(8,128)} %get-tuple-element.43.plan_ref) | copy-start | bytes 835588 | tf_op jit(solution)/shard_map/cond
  77.3 1.4 %collective-permute-start.17 = (f32[256,128]{1,0:T(8,128)S(1)}, f32[256,128]{1,0:T(8,128)S(1)}, u32[]{:S(2)}, u32[]{:S(2)}) collective-permute-start(f32[256,128]{1,0:T(8,128)S(1)} %branch_1_fun.11.rows_ref), channel_id=1, source_target_pairs={{0,4},{1,5},{2,6},{3,7},{16,20},{17,21},{18,22},{19,23},{32,36},{3... | collective-permute-start | bytes 393224 | tf_op jit(solution)/shard_map/cond/branch_1_fun/ppermute | solution.py:124
  78.0 0.7 collective-permute-start.18
  78.7 7.7 %collective-permute-start.19 = (f32[128,128]{1,0:T(8,128)S(1)}, f32[128,128]{1,0:T(8,128)S(1)}, u32[]{:S(2)}, u32[]{:S(2)}) collective-permute-start(f32[128,128]{1,0:T(8,128)S(1)} %get-tuple-element.71), channel_id=1, source_target_pairs={{4,8},{5,9},{6,10},{7,11},{20,24},{21,25},{22,26},{23,27},{36,40},... | collective-permute-start | bytes 196616 | tf_op jit(solution)/shard_map/cond/branch_1_fun/ppermute | solution.py:136
  80.0 9.4 %collective-permute-start.20 = (f32[128,128]{1,0:T(8,128)S(1)}, f32[128,128]{1,0:T(8,128)S(1)}, u32[]{:S(2)}, u32[]{:S(2)}) collective-permute-start(f32[128,128]{1,0:T(8,128)S(1)} %get-tuple-element.72), channel_id=1, source_target_pairs={{12,8},{13,9},{14,10},{15,11},{28,24},{29,25},{30,26},{31,27},{44,... | collective-permute-start | bytes 196616 | tf_op jit(solution)/shard_map/cond/branch_1_fun/ppermute | solution.py:137
  89.4 17.2 %copy-start.17 = (f32[256,128]{1,0:T(8,128)}, f32[256,128]{1,0:T(8,128)S(1)}, u32[]{:S(2)}) copy-start(f32[256,128]{1,0:T(8,128)S(1)} %maximum_select_fusion.1.left0_ref) | copy-start | bytes 393220 | tf_op jit(solution)/shard_map/cond
  89.4 13.1 %collective-permute-start.21 = (f32[256,128]{1,0:T(8,128)S(1)}, f32[256,128]{1,0:T(8,128)S(1)}, u32[]{:S(2)}, u32[]{:S(2)}) collective-permute-start(f32[256,128]{1,0:T(8,128)S(1)} %maximum_select_fusion.1.left0_ref), channel_id=1, source_target_pairs={{0,1},{1,0},{2,3},{3,2},{4,5},{5,4},{6,7},{7,6},{8,9},{9,8},{10,11... | collective-permute-start | bytes 393224 | tf_op jit(solution)/shard_map/cond/branch_1_fun/ppermute | solution.py:140
  94.8 8.2 %collective-permute-start.22 = (f32[256,128]{1,0:T(8,128)S(1)}, f32[256,128]{1,0:T(8,128)S(1)}, u32[]{:S(2)}, u32[]{:S(2)}) collective-permute-start(f32[256,128]{1,0:T(8,128)S(1)} %maximum_select_fusion.1.left0_ref), channel_id=1, source_target_pairs={{0,2},{1,3},{2,0},{3,1},{4,6},{5,7},{6,4},{7,5},{8,10},{9,11},{10,... | collective-permute-start | bytes 393224 | tf_op jit(solution)/shard_map/cond/branch_1_fun/ppermute | solution.py:140
  99.2 7.4 %collective-permute-start.23 = (f32[256,128]{1,0:T(8,128)S(1)}, f32[256,128]{1,0:T(8,128)}, u32[]{:S(2)}, u32[]{:S(2)}) collective-permute-start(f32[256,128]{1,0:T(8,128)S(1)} %maximum_select_fusion.1.left0_ref), channel_id=1, source_target_pairs={{0,3},{1,2},{2,1},{3,0},{4,7},{5,6},{6,5},{7,4},{8,11},{9,10},{10,... | collective-permute-start | bytes 393224 | tf_op jit(solution)/shard_map/cond/branch_1_fun/ppermute | solution.py:140
  (4 other events, 3.1 us)

commit v10 on v9

--- a/solution.py
+++ b/solution.py
@@ -172,8 +172,8 @@
 
 
 def plan_kernel(
-    pivots_ref, a_ref, send_ref, leave0_ref, leave1_ref, leave2_ref, leave3_ref, plan_ref, over_ref,
-    source_ref, target_ref,
+    pivots_ref, a_ref, send_ref, leave0_ref, leave1_ref, leave2_ref, leave3_ref, block_ref, plan_ref,
+    over_ref, source_ref, target_ref,
 ):
     prow = lax.axis_index("prow")
     x = prow >> 3
@@ -232,6 +232,7 @@
     lanef = lane_row.astype(F32)
     chosen = [slots(masks[n], order[n], lanef, 48) for n in range(4)]
     leaving = select_rows(onehot_of(jnp.concatenate(chosen, axis=0), NB), a_ref[:NB, :])
+    block_ref[...] = a_ref[:, :NB]
     for n, ref in enumerate((leave0_ref, leave1_ref, leave2_ref, leave3_ref)):
         ref[...] = leaving[48 * n : 48 * n + 48]
 
@@ -310,8 +311,8 @@
     return jnp.concatenate([got_ref[n, spot : spot + 16, :] for n in range(4)], axis=0)
 
 
-def panel_kernel(plan_ref, lead_ref, got_ref, *refs):
-    blocks, send_ref, full_ref, sems = refs[:4], refs[4], refs[5], refs[6]
+def panel_kernel(plan_ref, lead_ref, got_ref, block_ref, *refs):
+    blocks, (send_ref, rows_ref, full_ref, sems) = refs[:4], refs[4:]
     panel = lax.axis_index("prow") >> 3
     got = jnp.concatenate([pivot_part(got_ref, c) for c in range(REST // NB)], axis=1)
     full_ref[:, :NB] = lead_ref[...]
@@ -329,6 +330,9 @@
     ]
     for copy in copies:
         copy.start()
+    slot = plan_ref[288:544, :1]
+    moved = select_rows(onehot_of(slot, 64), moved_part(got_ref, 0))
+    rows_ref[...] = jnp.where(slot >= 0, moved, block_ref[...])
     for copy in copies:
         copy.wait()
 
@@ -341,12 +345,6 @@
 
 def lane_block(index):
     return pl.ds(pl.multiple_of(index * NB, NB), NB)
-
-
-def first_rows_kernel(plan_ref, got_ref, a_ref, out_ref):
-    slot = plan_ref[288:544, :1]
-    moved = select_rows(onehot_of(slot, 64), moved_part(got_ref, 0))
-    out_ref[...] = jnp.where(slot >= 0, moved, a_ref[:, :NB])
 
 
 def own_rows_kernel(plan_ref, rows_ref, got_ref, a_ref, out_ref):
@@ -431,12 +429,12 @@
     copy.wait()
 
 
-def kernel_call(body, shapes, scratch=(), out=VMEM):
+def kernel_call(body, shapes, scratch=(), out=None):
     def call(*args):
         return pl.pallas_call(
             body,
             in_specs=[VMEM] * len(args),
-            out_specs=[out] * len(shapes),
+            out_specs=out or [VMEM] * len(shapes),
             out_shape=[jax.ShapeDtypeStruct(shape, kind) for shape, kind in shapes],
             scratch_shapes=list(scratch),
             compiler_params=pltpu.CompilerParams(vmem_limit_bytes=KERNEL_VMEM),
@@ -473,7 +471,7 @@
     return lax.all_to_all(value, "prow", 0, 0, axis_index_groups=groups)
 
 
-def slotted(send, leaving, plan, matrix, lower_inverse, upper_inverse):
+def slotted(send, leaving, block, plan, matrix, lower_inverse, upper_inverse):
     pcol = lax.axis_index("pcol")
     got = along(send.reshape(4, 16, COLS), X_GROUPS)
     held = [leaving[0]]
@@ -489,14 +487,13 @@
     (lead,) = kernel_call(lead_kernel, [((NB, NB), F32)])(plan, first.reshape(256, NB))
     ends = spread_start(lead)
     late = spread_rest(lead, *ends, pcol)
-    (send,) = kernel_call(
+    send, rows = kernel_call(
         panel_kernel,
-        [((4, NB, WIDE - NB), F32)],
+        [((4, NB, WIDE - NB), F32), ((ROWS, NB), F32)],
         [pltpu.VMEM((NB, WIDE - NB), F32), pltpu.SemaphoreType.DMA((4,))],
-        HBM,
-    )(plan, lead, rest, *late)
+        [HBM, VMEM],
+    )(plan, lead, rest, block, *late)
     top = along(send, X_GROUPS).reshape(TOP, WIDE - NB)
-    (rows,) = kernel_call(first_rows_kernel, [((ROWS, NB), F32)])(plan, rest, matrix)
     ends = spread_start(rows)
     left = spread_rest(rows, *ends, pcol)
     (right,) = kernel_call(own_rows_kernel, [((ROWS, COLS), F32)])(plan, rows, rest, matrix)
@@ -555,16 +552,16 @@
 
 
 def per_device(matrix, pivots, lower_inverse, upper_inverse):
-    send, *leaving, plan, over = kernel_call(
+    send, *leaving, block, plan, over = kernel_call(
         plan_kernel,
         [((64, COLS), F32)]
         + [((48, COLS), F32)] * 4
-        + [((544, NB), jnp.int32), ((8, NB), jnp.int32)],
+        + [((ROWS, NB), F32), ((544, NB), jnp.int32), ((8, NB), jnp.int32)],
         [pltpu.VMEM((8, NB), jnp.int32), pltpu.VMEM((8, NB), jnp.int32)],
     )(pivots.reshape(PANELS, NB), matrix)
     return lax.cond(
         over[0, 0] <= 0,
-        lambda: slotted(send, leaving, plan, matrix, lower_inverse, upper_inverse),
+        lambda: slotted(send, leaving, block, plan, matrix, lower_inverse, upper_inverse),
         lambda: dense(pivots, matrix, lower_inverse, upper_inverse),
     )
 

time: 115 us -> 114 us (level)
  local copies, waits for them, and re-layouts: 3.05 us -> 5 us
  waiting for transfers between devices: 27 us -> 25.5 us
  Pallas kernels: 17.8 us -> 16.6 us
    cond x14 -> x16, local copies, waits for them, and re-layouts: 1.64 us -> 3.6 us
    ppermute x6, waiting for transfers between devices: 7.42 us -> 5.92 us  [spread_rest(): lax.ppermute(near, 'pcol', [(q, q ^ n) for q in range(PCOL)])]
    pallas_call x7 -> x6, Pallas kernels: 11.8 us -> 10.6 us  [call(): pl.pallas_call(body, in_specs=[VMEM] * len(args), out_specs=out or [VMEM]...]
  transfers between devices with their start and end apart: 20 -> 20, of which waited for: 9 -> 8; matrix products, arithmetic and copies ran while one was open for 0% -> 0% of each run, Pallas kernels for 4% -> 4%
where the time goes in v10:
time: 114 us; the launch traced here: 113 us
  starting transfers between devices  56.5 us (50%)
  waiting for transfers between devices  25.5 us (22%)
  Pallas kernels  16.6 us (15%)
  blocking collectives  8.38 us (7%)
  local copies, waits for them, and re-layouts  5 us (4%)
    ppermute x6, starting transfers between devices, spread_rest(): lax.ppermute(near, 'pcol', [(q, q ^ n) for q in range(PCOL)])  24.5 us
    all_to_all x3, starting transfers between devices, along(): return lax.all_to_all(value, 'prow', 0, 0, axis_index_groups=groups)  21.3 us
    ppermute x2, waiting for transfers between devices, spread_rest(): left = lax.ppermute(near[:half], 'pcol', [(q + 4, q + 8) for q in range(4)])  11.1 us
    pallas_call x6, Pallas kernels, call(): pl.pallas_call(body, in_specs=[VMEM] * len(args), out_specs=out or [VMEM]...  10.6 us
    all_to_all x1, blocking collectives, along(): return lax.all_to_all(value, 'prow', 0, 0, axis_index_groups=groups)  8.38 us
    pallas_call x1, Pallas kernels, factor(): pl.pallas_call(factor_kernel, in_specs=[VMEM, HBM, VMEM, VMEM] + [HBM] *...  5.94 us
    ppermute x6, waiting for transfers between devices, spread_rest(): lax.ppermute(near, 'pcol', [(q, q ^ n) for q in range(PCOL)])  5.92 us
    ppermute x2, waiting for transfers between devices, spread_rest(): lax.ppermute(near[half:], 'pcol', [(q + 12, q + 8) for q in range(4)])  5.12 us
  transfers between devices with their start and end apart: 20, of which 8 were waited for; matrix products, arithmetic and copies ran while one was open for 0% of the time, Pallas kernels for 4%

profile of v10, /device:TPU:43, one launch (start us, length us, event | category | flops | bytes accessed | tf_op | source)
XLA Modules:
  0.0 113.2 jit_solution(16692667774090703805)
XLA Ops:
  0.0 3.4 %shard_map.48 = (f32[64,768]{1,0:T(8,128)}, f32[48,768]{1,0:T(8,128)}, f32[48,768]{1,0:T(8,128)}, f32[48,768]{1,0:T(8,128)}, f32[48,768]{1,0:T(8,128)}, /*index=...) custom-call(s32[4,128]{1,0:T(4,128)} %bitcast.32, f32[256,768]{1,0:T(8,128)} %a_ref.1), custom_call_target="tpu_custom_call" | custom-call | tf_op jit(solution)/shard_map/pallas_call | solution.py:434
  4.6 107.7 %conditional.1 = (f32[256,768]{1,0:T(8,128)S(1)}) conditional(s32[]{:T(128)} %bitcast.18, (s32[512]{0:T(512)}, f32[256,768]{1,0:T(8,128)}, f32[4,128,128]{2,1,0:T(8,128)}, f32[4,128,128]{2,1,0:T(8,128)}) %tuple.11, (f32[64,768]{1,0:T(8,128)}, s32[544,128]{1,0:T(8,128)}, f32[48,768]{1,0:T(8,128)}, f32[48,768]{1,0:T(8,128)}, f32[48,768]{1,0:T(8,128)}, ...), branch_computations={%region_0.4_spmd, %region_4.5_spmd} | conditional | flops 1392652 | bytes 63624084 | solution.py:562
  4.6 8.4 %all_to_all.41 = f32[4,16,768]{2,1,0:T(8,128)S(1)} all-to-all(f32[4,16,768]{2,1,0:T(8,128)} %bitcast.30), channel_id=1, replica_groups={{0,128,256,384},{16,144,272,400},{32,160,288,416},{48,176,304,432},{64,..., dimensions={0} | all-to-all | bytes 393216 | tf_op jit(solution)/shard_map/cond/branch_1_fun/all_to_all | solution.py:471
  13.0 1.9 %branch_1_fun.6 = (f32[8,32,128]{2,1,0:T(8,128)}, f32[32,640]{1,0:T(8,128)S(1)}) custom-call(s32[544,128]{1,0:T(8,128)} %get-tuple-element.45.plan_ref, f32[64,768]{1,0:T(8,128)S(1)} %bitcast.22), custom_call_target="tpu_custom_call" | custom-call | tf_op jit(solution)/shard_map/cond/branch_1_fun/pallas_call | solution.py:434
  14.8 10.0 %all-to-all-start.7 = ((f32[8,32,128]{2,1,0:T(8,128)}), f32[8,32,128]{2,1,0:T(8,128)S(1)}, u32[]{:S(2)}, u32[]{:S(2)}) async-start(f32[8,32,128]{2,1,0:T(8,128)} %get-tuple-element.47), calls=%async_computation.7 | async-start | bytes 262144 | tf_op jit(solution)/shard_map/cond/branch_1_fun/all_to_all | solution.py:471
  27.7 3.3 %collective-permute-done.7.leave1_ref = f32[48,768]{1,0:T(8,128)S(1)} collective-permute-done((f32[48,768]{1,0:T(8,128)}, f32[48,768]{1,0:T(8,128)S(1)}, u32[]{:S(2)}, u32[]{:S(2)}) %collective-permute-start.7) | collective-permute-done | bytes 147488 | tf_op jit(solution)/shard_map/cond/branch_1_fun/ppermute | solution.py:480
  31.0 2.4 %branch_1_fun.8 = f32[8,256,128]{2,1,0:T(8,128)} custom-call(s32[544,128]{1,0:T(8,128)} %get-tuple-element.45.plan_ref, f32[32,640]{1,0:T(8,128)S(1)} %get-tuple-element.48.rows_ref, f32[48,768]{1,0:T(8,128)} %get-tuple-element.49.leave0_ref, f32[48,768]{1,0:T(8,128)S(1)} %collective-permute-done.7.leave1_ref, ...), custom_call_target="tpu_custom_call" | custom-call | tf_op jit(solution)/shard_map/cond/branch_1_fun/pallas_call | solution.py:434
  33.4 5.0 %all-to-all-start.8 = ((f32[8,256,128]{2,1,0:T(8,128)}), f32[8,256,128]{2,1,0:T(8,128)S(1)}, u32[]{:S(2)}, u32[]{:S(2)}) async-start(f32[8,256,128]{2,1,0:T(8,128)} %branch_1_fun.8), calls=%async_computation.8 | async-start | bytes 2097152 | tf_op jit(solution)/shard_map/cond/branch_1_fun/all_to_all | solution.py:471
  42.7 6.0 %collective-permute-done.12 = f32[64,128]{1,0:T(8,128)S(1)} collective-permute-done((f32[64,128]{1,0:T(8,128)S(1)}, f32[64,128]{1,0:T(8,128)S(1)}, u32[]{:S(2)}, u32[]{:S(2)}) %collective-permute-start.12) | collective-permute-done | bytes 32800 | tf_op jit(solution)/shard_map/cond/branch_1_fun/ppermute | solution.py:136
  48.7 2.1 %collective-permute-done.13 = f32[64,128]{1,0:T(8,128)S(1)} collective-permute-done((f32[64,128]{1,0:T(8,128)S(1)}, f32[64,128]{1,0:T(8,128)S(1)}, u32[]{:S(2)}, u32[]{:S(2)}) %collective-permute-start.13) | collective-permute-done | bytes 32800 | tf_op jit(solution)/shard_map/cond/branch_1_fun/ppermute | solution.py:137
  50.8 7.3 %collective-permute-start.14 = (f32[128,128]{1,0:T(8,128)S(1)}, f32[128,128]{1,0:T(8,128)S(1)}, u32[]{:S(2)}, u32[]{:S(2)}) collective-permute-start(f32[128,128]{1,0:T(8,128)S(1)} %maximum_select_fusion.2.refs_0_), channel_id=1, source_target_pairs={{0,1},{1,0},{2,3},{3,2},{4,5},{5,4},{6,7},{7,6},{8,9},{9,8},{10,11... | collective-permute-start | bytes 196616 | tf_op jit(solution)/shard_map/cond/branch_1_fun/ppermute | solution.py:140
  58.1 3.6 %collective-permute-start.15 = (f32[128,128]{1,0:T(8,128)S(1)}, f32[128,128]{1,0:T(8,128)S(1)}, u32[]{:S(2)}, u32[]{:S(2)}) collective-permute-start(f32[128,128]{1,0:T(8,128)S(1)} %maximum_select_fusion.2.refs_0_), channel_id=1, source_target_pairs={{0,2},{1,3},{2,0},{3,1},{4,6},{5,7},{6,4},{7,5},{8,10},{9,11},{10,... | collective-permute-start | bytes 196616 | tf_op jit(solution)/shard_map/cond/branch_1_fun/ppermute | solution.py:140
  61.7 1.9 %collective-permute-start.16 = (f32[128,128]{1,0:T(8,128)S(1)}, f32[128,128]{1,0:T(8,128)S(1)}, u32[]{:S(2)}, u32[]{:S(2)}) collective-permute-start(f32[128,128]{1,0:T(8,128)S(1)} %maximum_select_fusion.2.refs_0_), channel_id=1, source_target_pairs={{0,3},{1,2},{2,1},{3,0},{4,7},{5,6},{6,5},{7,4},{8,11},{9,10},{10,... | collective-permute-start | bytes 196616 | tf_op jit(solution)/shard_map/cond/branch_1_fun/ppermute | solution.py:140
  64.1 3.6 %collective-permute-done.16.refs_3_ = f32[128,128]{1,0:T(8,128)S(1)} collective-permute-done((f32[128,128]{1,0:T(8,128)S(1)}, f32[128,128]{1,0:T(8,128)S(1)}, u32[]{:S(2)}, u32[]{:S(2)}) %collective-permute-start.16) | collective-permute-done | bytes 65568 | tf_op jit(solution)/shard_map/cond/branch_1_fun/ppermute | solution.py:140
  69.0 1.4 %copy-done.1 = f32[4,128,1152]{2,1,0:T(8,128)} copy-done((f32[4,128,1152]{2,1,0:T(8,128)}, f32[4,128,1152]{2,1,0:T(8,128)S(1)}, u32[]{:S(2)}) %copy-start.1) | copy-done | bytes 2359320 | tf_op jit(solution)/shard_map/cond
  70.4 6.3 %all-to-all-start.9 = ((f32[4,128,1152]{2,1,0:T(8,128)}), f32[4,128,1152]{2,1,0:T(8,128)S(1)}, u32[]{:S(2)}, u32[]{:S(2)}) async-start(f32[4,128,1152]{2,1,0:T(8,128)} %copy-done.1), calls=%async_computation.9 | async-start | bytes 4718592 | tf_op jit(solution)/shard_map/cond/branch_1_fun/all_to_all | solution.py:471
  80.8 5.1 %collective-permute-done.19 = f32[128,128]{1,0:T(8,128)S(1)} collective-permute-done((f32[128,128]{1,0:T(8,128)S(1)}, f32[128,128]{1,0:T(8,128)S(1)}, u32[]{:S(2)}, u32[]{:S(2)}) %collective-permute-start.19) | collective-permute-done | bytes 65568 | tf_op jit(solution)/shard_map/cond/branch_1_fun/ppermute | solution.py:136
  85.9 3.0 %collective-permute-done.20 = f32[128,128]{1,0:T(8,128)S(1)} collective-permute-done((f32[128,128]{1,0:T(8,128)S(1)}, f32[128,128]{1,0:T(8,128)S(1)}, u32[]{:S(2)}, u32[]{:S(2)}) %collective-permute-start.20) | collective-permute-done | bytes 65568 | tf_op jit(solution)/shard_map/cond/branch_1_fun/ppermute | solution.py:137
  88.9 5.4 %collective-permute-start.21 = (f32[256,128]{1,0:T(8,128)S(1)}, f32[256,128]{1,0:T(8,128)S(1)}, u32[]{:S(2)}, u32[]{:S(2)}) collective-permute-start(f32[256,128]{1,0:T(8,128)S(1)} %maximum_select_fusion.1.left0_ref), channel_id=1, source_target_pairs={{0,1},{1,0},{2,3},{3,2},{4,5},{5,4},{6,7},{7,6},{8,9},{9,8},{10,11... | collective-permute-start | bytes 393224 | tf_op jit(solution)/shard_map/cond/branch_1_fun/ppermute | solution.py:140
  94.3 4.4 %collective-permute-start.22 = (f32[256,128]{1,0:T(8,128)S(1)}, f32[256,128]{1,0:T(8,128)S(1)}, u32[]{:S(2)}, u32[]{:S(2)}) collective-permute-start(f32[256,128]{1,0:T(8,128)S(1)} %maximum_select_fusion.1.left0_ref), channel_id=1, source_target_pairs={{0,2},{1,3},{2,0},{3,1},{4,6},{5,7},{6,4},{7,5},{8,10},{9,11},{10,... | collective-permute-start | bytes 393224 | tf_op jit(solution)/shard_map/cond/branch_1_fun/ppermute | solution.py:140
  98.8 1.9 %collective-permute-start.23 = (f32[256,128]{1,0:T(8,128)S(1)}, f32[256,128]{1,0:T(8,128)}, u32[]{:S(2)}, u32[]{:S(2)}) collective-permute-start(f32[256,128]{1,0:T(8,128)S(1)} %maximum_select_fusion.1.left0_ref), channel_id=1, source_target_pairs={{0,3},{1,2},{2,1},{3,0},{4,7},{5,6},{6,5},{7,4},{8,11},{9,10},{10,... | collective-permute-start | bytes 393224 | tf_op jit(solution)/shard_map/cond/branch_1_fun/ppermute | solution.py:140
  100.7 1.4 %branch_1_fun.10.right_ref = f32[256,768]{1,0:T(8,128)S(1)} custom-call(s32[544,128]{1,0:T(8,128)} %get-tuple-element.45.plan_ref, f32[256,128]{1,0:T(8,128)S(1)} %get-tuple-element.55.rows_ref, f32[8,256,128]{2,1,0:T(8,128)S(1)} %all-to-all-done.8.got_ref, f32[256,768]{1,0:T(8,128)S(1)} %copy-done.11), custom_call_target="tpu_custom_call" | custom-call | tf_op jit(solution)/shard_map/cond/branch_1_fun/pallas_call | solution.py:434
  104.3 1.8 %collective-permute-done.23.left3_ref = f32[256,128]{1,0:T(8,128)} collective-permute-done((f32[256,128]{1,0:T(8,128)S(1)}, f32[256,128]{1,0:T(8,128)}, u32[]{:S(2)}, u32[]{:S(2)}) %collective-permute-start.23) | collective-permute-done | bytes 131104 | tf_op jit(solution)/shard_map/cond/branch_1_fun/ppermute | solution.py:140
  106.2 5.9 %branch_1_fun.11 = f32[256,768]{1,0:T(8,128)S(1)} custom-call(f32[512,1152]{1,0:T(8,128)S(1)} %bitcast.20, f32[256,768]{1,0:T(8,128)} %copy-done, f32[4,128,128]{2,1,0:T(8,128)} %get-tuple-element.57.lower_ref, f32[4,128,128]{2,1,0:T(8,128)} %get-tuple-element.58.upper_ref, f32[256,128]{1,0:T(8,128)} %copy-done.17, f32[256,128]{1,0:T(8,128)} %copy-done.20, ...), custom_call_target="tpu_custom_call" | custom-call | tf_op jit(solution)/shard_map/cond/branch_1_fun/pallas_call | solution.py:451
  (50 shorter events, 16.4 us)
Async XLA Ops:
  14.8 18.6 %all-to-all-start.7 = ((f32[8,32,128]{2,1,0:T(8,128)}), f32[8,32,128]{2,1,0:T(8,128)S(1)}, u32[]{:S(2)}, u32[]{:S(2)}) async-start(f32[8,32,128]{2,1,0:T(8,128)} %get-tuple-element.47), calls=%async_computation.7 | async-start | bytes 262144 | tf_op jit(solution)/shard_map/cond/branch_1_fun/all_to_all | solution.py:471
  24.9 6.1 %collective-permute-start.7 = (f32[48,768]{1,0:T(8,128)}, f32[48,768]{1,0:T(8,128)S(1)}, u32[]{:S(2)}, u32[]{:S(2)}) collective-permute-start(f32[48,768]{1,0:T(8,128)} %get-tuple-element.50), channel_id=1, source_target_pairs={{0,128},{16,144},{32,160},{48,176},{1,129},{17,145},{33,161},{49,1... | collective-permute-start | bytes 442376 | tf_op jit(solution)/shard_map/cond/branch_1_fun/ppermute | solution.py:480
  26.2 4.8 %collective-permute-start.8 = (f32[48,768]{1,0:T(8,128)}, f32[48,768]{1,0:T(8,128)S(1)}, u32[]{:S(2)}, u32[]{:S(2)}) collective-permute-start(f32[48,768]{1,0:T(8,128)} %get-tuple-element.51), channel_id=1, source_target_pairs={{0,256},{16,272},{32,288},{48,304},{1,257},{17,273},{33,289},{49,3... | collective-permute-start | bytes 442376 | tf_op jit(solution)/shard_map/cond/branch_1_fun/ppermute | solution.py:480
  26.8 4.1 %collective-permute-start.9 = (f32[48,768]{1,0:T(8,128)}, f32[48,768]{1,0:T(8,128)S(1)}, u32[]{:S(2)}, u32[]{:S(2)}) collective-permute-start(f32[48,768]{1,0:T(8,128)} %get-tuple-element.52), channel_id=1, source_target_pairs={{0,384},{16,400},{32,416},{48,432},{1,385},{17,401},{33,417},{49,4... | collective-permute-start | bytes 442376 | tf_op jit(solution)/shard_map/cond/branch_1_fun/ppermute | solution.py:480
  31.0 7.4 %copy-start.12 = (s32[544,128]{1,0:T(8,128)S(1)}, s32[544,128]{1,0:T(8,128)}, u32[]{:S(2)}) copy-start(s32[544,128]{1,0:T(8,128)} %get-tuple-element.45.plan_ref) | copy-start | bytes 835588 | tf_op jit(solution)/shard_map/cond
  33.4 34.3 %copy-start.19 = (f32[256,128]{1,0:T(8,128)S(1)}, f32[256,128]{1,0:T(8,128)}, u32[]{:S(2)}) copy-start(f32[256,128]{1,0:T(8,128)} %get-tuple-element.53.block_ref) | copy-start | bytes 393220 | tf_op jit(solution)/shard_map/cond
  33.4 34.3 %all-to-all-start.8 = ((f32[8,256,128]{2,1,0:T(8,128)}), f32[8,256,128]{2,1,0:T(8,128)S(1)}, u32[]{:S(2)}, u32[]{:S(2)}) async-start(f32[8,256,128]{2,1,0:T(8,128)} %branch_1_fun.8), calls=%async_computation.8 | async-start | bytes 2097152 | tf_op jit(solution)/shard_map/cond/branch_1_fun/all_to_all | solution.py:471
  38.6 1.4 %collective-permute-start.10 = (f32[128,128]{1,0:T(8,128)S(1)}, f32[128,128]{1,0:T(8,128)S(1)}, u32[]{:S(2)}, u32[]{:S(2)}) collective-permute-start(f32[128,128]{1,0:T(8,128)S(1)} %branch_1_fun.7.lead_ref), channel_id=1, source_target_pairs={{0,4},{1,5},{2,6},{3,7},{16,20},{17,21},{18,22},{19,23},{32,36},{3... | collective-permute-start | bytes 196616 | tf_op jit(solution)/shard_map/cond/branch_1_fun/ppermute | solution.py:124
  39.3 0.7 collective-permute-start.11
  40.0 8.7 %collective-permute-start.12 = (f32[64,128]{1,0:T(8,128)S(1)}, f32[64,128]{1,0:T(8,128)S(1)}, u32[]{:S(2)}, u32[]{:S(2)}) collective-permute-start(f32[64,128]{1,0:T(8,128)S(1)} %get-tuple-element.80), channel_id=1, source_target_pairs={{4,8},{5,9},{6,10},{7,11},{20,24},{21,25},{22,26},{23,27},{36,40},... | collective-permute-start | bytes 98312 | tf_op jit(solution)/shard_map/cond/branch_1_fun/ppermute | solution.py:136
  41.3 9.5 %collective-permute-start.13 = (f32[64,128]{1,0:T(8,128)S(1)}, f32[64,128]{1,0:T(8,128)S(1)}, u32[]{:S(2)}, u32[]{:S(2)}) collective-permute-start(f32[64,128]{1,0:T(8,128)S(1)} %get-tuple-element.81), channel_id=1, source_target_pairs={{12,8},{13,9},{14,10},{15,11},{28,24},{29,25},{30,26},{31,27},{44,... | collective-permute-start | bytes 98312 | tf_op jit(solution)/shard_map/cond/branch_1_fun/ppermute | solution.py:137
  50.8 12.8 %collective-permute-start.14 = (f32[128,128]{1,0:T(8,128)S(1)}, f32[128,128]{1,0:T(8,128)S(1)}, u32[]{:S(2)}, u32[]{:S(2)}) collective-permute-start(f32[128,128]{1,0:T(8,128)S(1)} %maximum_select_fusion.2.refs_0_), channel_id=1, source_target_pairs={{0,1},{1,0},{2,3},{3,2},{4,5},{5,4},{6,7},{7,6},{8,9},{9,8},{10,11... | collective-permute-start | bytes 196616 | tf_op jit(solution)/shard_map/cond/branch_1_fun/ppermute | solution.py:140
  58.1 6.0 %collective-permute-start.15 = (f32[128,128]{1,0:T(8,128)S(1)}, f32[128,128]{1,0:T(8,128)S(1)}, u32[]{:S(2)}, u32[]{:S(2)}) collective-permute-start(f32[128,128]{1,0:T(8,128)S(1)} %maximum_select_fusion.2.refs_0_), channel_id=1, source_target_pairs={{0,2},{1,3},{2,0},{3,1},{4,6},{5,7},{6,4},{7,5},{8,10},{9,11},{10,... | collective-permute-start | bytes 196616 | tf_op jit(solution)/shard_map/cond/branch_1_fun/ppermute | solution.py:140
  61.7 6.0 %collective-permute-start.16 = (f32[128,128]{1,0:T(8,128)S(1)}, f32[128,128]{1,0:T(8,128)S(1)}, u32[]{:S(2)}, u32[]{:S(2)}) collective-permute-start(f32[128,128]{1,0:T(8,128)S(1)} %maximum_select_fusion.2.refs_0_), channel_id=1, source_target_pairs={{0,3},{1,2},{2,1},{3,0},{4,7},{5,6},{6,5},{7,4},{8,11},{9,10},{10,... | collective-permute-start | bytes 196616 | tf_op jit(solution)/shard_map/cond/branch_1_fun/ppermute | solution.py:140
  70.4 35.7 %all-to-all-start.9 = ((f32[4,128,1152]{2,1,0:T(8,128)}), f32[4,128,1152]{2,1,0:T(8,128)S(1)}, u32[]{:S(2)}, u32[]{:S(2)}) async-start(f32[4,128,1152]{2,1,0:T(8,128)} %copy-done.1), calls=%async_computation.9 | async-start | bytes 4718592 | tf_op jit(solution)/shard_map/cond/branch_1_fun/all_to_all | solution.py:471
  76.7 24.0 %copy-start.11 = (f32[256,768]{1,0:T(8,128)S(1)}, f32[256,768]{1,0:T(8,128)}, u32[]{:S(2)}) copy-start(f32[256,768]{1,0:T(8,128)} %get-tuple-element.56.a_ref) | copy-start | bytes 2359300 | tf_op jit(solution)/shard_map/cond
  76.7 1.5 %collective-permute-start.17 = (f32[256,128]{1,0:T(8,128)S(1)}, f32[256,128]{1,0:T(8,128)S(1)}, u32[]{:S(2)}, u32[]{:S(2)}) collective-permute-start(f32[256,128]{1,0:T(8,128)S(1)} %get-tuple-element.55.rows_ref), channel_id=1, source_target_pairs={{0,4},{1,5},{2,6},{3,7},{16,20},{17,21},{18,22},{19,23},{32,36},{3... | collective-permute-start | bytes 393224 | tf_op jit(solution)/shard_map/cond/branch_1_fun/ppermute | solution.py:124
  77.5 0.7 collective-permute-start.18
  78.2 7.7 %collective-permute-start.19 = (f32[128,128]{1,0:T(8,128)S(1)}, f32[128,128]{1,0:T(8,128)S(1)}, u32[]{:S(2)}, u32[]{:S(2)}) collective-permute-start(f32[128,128]{1,0:T(8,128)S(1)} %get-tuple-element.78), channel_id=1, source_target_pairs={{4,8},{5,9},{6,10},{7,11},{20,24},{21,25},{22,26},{23,27},{36,40},... | collective-permute-start | bytes 196616 | tf_op jit(solution)/shard_map/cond/branch_1_fun/ppermute | solution.py:136
  79.5 9.4 %collective-permute-start.20 = (f32[128,128]{1,0:T(8,128)S(1)}, f32[128,128]{1,0:T(8,128)S(1)}, u32[]{:S(2)}, u32[]{:S(2)}) collective-permute-start(f32[128,128]{1,0:T(8,128)S(1)} %get-tuple-element.79), channel_id=1, source_target_pairs={{12,8},{13,9},{14,10},{15,11},{28,24},{29,25},{30,26},{31,27},{44,... | collective-permute-start | bytes 196616 | tf_op jit(solution)/shard_map/cond/branch_1_fun/ppermute | solution.py:137
  88.9 14.1 %copy-start.17 = (f32[256,128]{1,0:T(8,128)}, f32[256,128]{1,0:T(8,128)S(1)}, u32[]{:S(2)}) copy-start(f32[256,128]{1,0:T(8,128)S(1)} %maximum_select_fusion.1.left0_ref) | copy-start | bytes 393220 | tf_op jit(solution)/shard_map/cond
  88.9 14.1 %collective-permute-start.21 = (f32[256,128]{1,0:T(8,128)S(1)}, f32[256,128]{1,0:T(8,128)S(1)}, u32[]{:S(2)}, u32[]{:S(2)}) collective-permute-start(f32[256,128]{1,0:T(8,128)S(1)} %maximum_select_fusion.1.left0_ref), channel_id=1, source_target_pairs={{0,1},{1,0},{2,3},{3,2},{4,5},{5,4},{6,7},{7,6},{8,9},{9,8},{10,11... | collective-permute-start | bytes 393224 | tf_op jit(solution)/shard_map/cond/branch_1_fun/ppermute | solution.py:140
  94.3 8.7 %collective-permute-start.22 = (f32[256,128]{1,0:T(8,128)S(1)}, f32[256,128]{1,0:T(8,128)S(1)}, u32[]{:S(2)}, u32[]{:S(2)}) collective-permute-start(f32[256,128]{1,0:T(8,128)S(1)} %maximum_select_fusion.1.left0_ref), channel_id=1, source_target_pairs={{0,2},{1,3},{2,0},{3,1},{4,6},{5,7},{6,4},{7,5},{8,10},{9,11},{10,... | collective-permute-start | bytes 393224 | tf_op jit(solution)/shard_map/cond/branch_1_fun/ppermute | solution.py:140
  98.8 7.4 %collective-permute-start.23 = (f32[256,128]{1,0:T(8,128)S(1)}, f32[256,128]{1,0:T(8,128)}, u32[]{:S(2)}, u32[]{:S(2)}) collective-permute-start(f32[256,128]{1,0:T(8,128)S(1)} %maximum_select_fusion.1.left0_ref), channel_id=1, source_target_pairs={{0,3},{1,2},{2,1},{3,0},{4,7},{5,6},{6,5},{7,4},{8,11},{9,10},{10,... | collective-permute-start | bytes 393224 | tf_op jit(solution)/shard_map/cond/branch_1_fun/ppermute | solution.py:140
  (5 other events, 4.5 us)

commit v11 on v10

--- a/solution.py
+++ b/solution.py
@@ -311,8 +311,8 @@
     return jnp.concatenate([got_ref[n, spot : spot + 16, :] for n in range(4)], axis=0)
 
 
-def panel_kernel(plan_ref, lead_ref, got_ref, block_ref, *refs):
-    blocks, (send_ref, rows_ref, full_ref, sems) = refs[:4], refs[4:]
+def panel_kernel(plan_ref, lead_ref, got_ref, *refs):
+    blocks, (send_ref, full_ref, sems) = refs[:4], refs[4:]
     panel = lax.axis_index("prow") >> 3
     got = jnp.concatenate([pivot_part(got_ref, c) for c in range(REST // NB)], axis=1)
     full_ref[:, :NB] = lead_ref[...]
@@ -330,9 +330,6 @@
     ]
     for copy in copies:
         copy.start()
-    slot = plan_ref[288:544, :1]
-    moved = select_rows(onehot_of(slot, 64), moved_part(got_ref, 0))
-    rows_ref[...] = jnp.where(slot >= 0, moved, block_ref[...])
     for copy in copies:
         copy.wait()
 
@@ -345,6 +342,12 @@
 
 def lane_block(index):
     return pl.ds(pl.multiple_of(index * NB, NB), NB)
+
+
+def first_rows_kernel(plan_ref, got_ref, block_ref, out_ref):
+    slot = plan_ref[288:544, :1]
+    moved = select_rows(onehot_of(slot, 64), moved_part(got_ref, 0))
+    out_ref[...] = jnp.where(slot >= 0, moved, block_ref[...])
 
 
 def own_rows_kernel(plan_ref, rows_ref, got_ref, a_ref, out_ref):
@@ -487,13 +490,14 @@
     (lead,) = kernel_call(lead_kernel, [((NB, NB), F32)])(plan, first.reshape(256, NB))
     ends = spread_start(lead)
     late = spread_rest(lead, *ends, pcol)
-    send, rows = kernel_call(
+    (send,) = kernel_call(
         panel_kernel,
-        [((4, NB, WIDE - NB), F32), ((ROWS, NB), F32)],
+        [((4, NB, WIDE - NB), F32)],
         [pltpu.VMEM((NB, WIDE - NB), F32), pltpu.SemaphoreType.DMA((4,))],
-        [HBM, VMEM],
-    )(plan, lead, rest, block, *late)
+        [HBM],
+    )(plan, lead, rest, *late)
     top = along(send, X_GROUPS).reshape(TOP, WIDE - NB)
+    (rows,) = kernel_call(first_rows_kernel, [((ROWS, NB), F32)])(plan, rest, block)
     ends = spread_start(rows)
     left = spread_rest(rows, *ends, pcol)
     (right,) = kernel_call(own_rows_kernel, [((ROWS, COLS), F32)])(plan, rows, rest, matrix)

time: 114 us -> 114 us (level)
  local copies, waits for them, and re-layouts: 5 us -> 3.03 us
  waiting for transfers between devices: 25.5 us -> 27 us
    cond x16, local copies, waits for them, and re-layouts: 3.6 us -> 1.62 us
    ppermute x6, waiting for transfers between devices: 5.92 us -> 7.45 us  [spread_rest(): lax.ppermute(near, 'pcol', [(q, q ^ n) for q in range(PCOL)])]
    pallas_call x6 -> x7, Pallas kernels: 10.6 us -> 11.5 us  [call(): pl.pallas_call(body, in_specs=[VMEM] * len(args), out_specs=out or [VMEM]...]
  transfers between devices with their start and end apart: 20 -> 20, of which waited for: 8 -> 9; matrix products, arithmetic and copies ran while one was open for 0% -> 0% of each run, Pallas kernels for 4% -> 4%
where the time goes in v11:
time: 114 us
  starting transfers between devices  56.4 us (49%)
  waiting for transfers between devices  27 us (24%)
  Pallas kernels  17.5 us (15%)
  blocking collectives  8.38 us (7%)
  local copies, waits for them, and re-layouts  3.03 us (3%)
    ppermute x6, starting transfers between devices, spread_rest(): lax.ppermute(near, 'pcol', [(q, q ^ n) for q in range(PCOL)])  24.5 us
    all_to_all x3, starting transfers between devices, along(): return lax.all_to_all(value, 'prow', 0, 0, axis_index_groups=groups)  21.3 us
    pallas_call x7, Pallas kernels, call(): pl.pallas_call(body, in_specs=[VMEM] * len(args), out_specs=out or [VMEM]...  11.5 us
    ppermute x2, waiting for transfers between devices, spread_rest(): left = lax.ppermute(near[:half], 'pcol', [(q + 4, q + 8) for q in range(4)])  11.1 us
    all_to_all x1, blocking collectives, along(): return lax.all_to_all(value, 'prow', 0, 0, axis_index_groups=groups)  8.38 us
    ppermute x6, waiting for transfers between devices, spread_rest(): lax.ppermute(near, 'pcol', [(q, q ^ n) for q in range(PCOL)])  7.45 us
    pallas_call x1, Pallas kernels, factor(): pl.pallas_call(factor_kernel, in_specs=[VMEM, HBM, VMEM, VMEM] + [HBM] *...  5.94 us
    ppermute x2, waiting for transfers between devices, spread_rest(): lax.ppermute(near[half:], 'pcol', [(q + 12, q + 8) for q in range(4)])  5.12 us
  transfers between devices with their start and end apart: 20, of which 9 were waited for; matrix products, arithmetic and copies ran while one was open for 0% of the time, Pallas kernels for 4%

profile of v11, /device:TPU:43, one launch (start us, length us, event | category | flops | bytes accessed | tf_op | source)
XLA Modules:
  0.0 113.6 jit_solution(1704400896986203702)
XLA Ops:
  0.0 3.4 %shard_map.48 = (f32[64,768]{1,0:T(8,128)}, f32[48,768]{1,0:T(8,128)}, f32[48,768]{1,0:T(8,128)}, f32[48,768]{1,0:T(8,128)}, f32[48,768]{1,0:T(8,128)}, /*index=...) custom-call(s32[4,128]{1,0:T(4,128)} %bitcast.32, f32[256,768]{1,0:T(8,128)} %a_ref.1), custom_call_target="tpu_custom_call" | custom-call | tf_op jit(solution)/shard_map/pallas_call | solution.py:437
  4.6 108.1 %conditional.1 = (f32[256,768]{1,0:T(8,128)S(1)}) conditional(s32[]{:T(128)} %bitcast.18, (s32[512]{0:T(512)}, f32[256,768]{1,0:T(8,128)}, f32[4,128,128]{2,1,0:T(8,128)}, f32[4,128,128]{2,1,0:T(8,128)}) %tuple.11, (f32[64,768]{1,0:T(8,128)}, s32[544,128]{1,0:T(8,128)}, f32[48,768]{1,0:T(8,128)}, f32[48,768]{1,0:T(8,128)}, f32[48,768]{1,0:T(8,128)}, ...), branch_computations={%region_0.4_spmd, %region_4.5_spmd} | conditional | flops 1392652 | bytes 63624084 | solution.py:566
  4.6 8.4 %all_to_all.41 = f32[4,16,768]{2,1,0:T(8,128)S(1)} all-to-all(f32[4,16,768]{2,1,0:T(8,128)} %bitcast.30), channel_id=1, replica_groups={{0,128,256,384},{16,144,272,400},{32,160,288,416},{48,176,304,432},{64,..., dimensions={0} | all-to-all | bytes 393216 | tf_op jit(solution)/shard_map/cond/branch_1_fun/all_to_all | solution.py:474
  13.0 1.9 %branch_1_fun.7 = (f32[8,32,128]{2,1,0:T(8,128)}, f32[32,640]{1,0:T(8,128)S(1)}) custom-call(s32[544,128]{1,0:T(8,128)} %get-tuple-element.45.plan_ref, f32[64,768]{1,0:T(8,128)S(1)} %bitcast.22), custom_call_target="tpu_custom_call" | custom-call | tf_op jit(solution)/shard_map/cond/branch_1_fun/pallas_call | solution.py:437
  14.8 10.0 %all-to-all-start.7 = ((f32[8,32,128]{2,1,0:T(8,128)}), f32[8,32,128]{2,1,0:T(8,128)S(1)}, u32[]{:S(2)}, u32[]{:S(2)}) async-start(f32[8,32,128]{2,1,0:T(8,128)} %get-tuple-element.47), calls=%async_computation.7 | async-start | bytes 262144 | tf_op jit(solution)/shard_map/cond/branch_1_fun/all_to_all | solution.py:474
  27.7 3.3 %collective-permute-done.7.leave1_ref = f32[48,768]{1,0:T(8,128)S(1)} collective-permute-done((f32[48,768]{1,0:T(8,128)}, f32[48,768]{1,0:T(8,128)S(1)}, u32[]{:S(2)}, u32[]{:S(2)}) %collective-permute-start.7) | collective-permute-done | bytes 147488 | tf_op jit(solution)/shard_map/cond/branch_1_fun/ppermute | solution.py:483
  31.0 2.4 %branch_1_fun.9 = f32[8,256,128]{2,1,0:T(8,128)} custom-call(s32[544,128]{1,0:T(8,128)} %get-tuple-element.45.plan_ref, f32[32,640]{1,0:T(8,128)S(1)} %get-tuple-element.48.rows_ref, f32[48,768]{1,0:T(8,128)} %get-tuple-element.49.leave0_ref, f32[48,768]{1,0:T(8,128)S(1)} %collective-permute-done.7.leave1_ref, ...), custom_call_target="tpu_custom_call" | custom-call | tf_op jit(solution)/shard_map/cond/branch_1_fun/pallas_call | solution.py:437
  33.4 4.8 %all-to-all-start.8 = ((f32[8,256,128]{2,1,0:T(8,128)}), f32[8,256,128]{2,1,0:T(8,128)S(1)}, u32[]{:S(2)}, u32[]{:S(2)}) async-start(f32[8,256,128]{2,1,0:T(8,128)} %branch_1_fun.9), calls=%async_computation.8 | async-start | bytes 2097152 | tf_op jit(solution)/shard_map/cond/branch_1_fun/all_to_all | solution.py:474
  42.5 6.0 %collective-permute-done.12 = f32[64,128]{1,0:T(8,128)S(1)} collective-permute-done((f32[64,128]{1,0:T(8,128)S(1)}, f32[64,128]{1,0:T(8,128)S(1)}, u32[]{:S(2)}, u32[]{:S(2)}) %collective-permute-start.12) | collective-permute-done | bytes 32800 | tf_op jit(solution)/shard_map/cond/branch_1_fun/ppermute | solution.py:136
  48.6 2.1 %collective-permute-done.13 = f32[64,128]{1,0:T(8,128)S(1)} collective-permute-done((f32[64,128]{1,0:T(8,128)S(1)}, f32[64,128]{1,0:T(8,128)S(1)}, u32[]{:S(2)}, u32[]{:S(2)}) %collective-permute-start.13) | collective-permute-done | bytes 32800 | tf_op jit(solution)/shard_map/cond/branch_1_fun/ppermute | solution.py:137
  50.7 7.3 %collective-permute-start.14 = (f32[128,128]{1,0:T(8,128)S(1)}, f32[128,128]{1,0:T(8,128)S(1)}, u32[]{:S(2)}, u32[]{:S(2)}) collective-permute-start(f32[128,128]{1,0:T(8,128)S(1)} %maximum_select_fusion.2.refs_0_), channel_id=1, source_target_pairs={{0,1},{1,0},{2,3},{3,2},{4,5},{5,4},{6,7},{7,6},{8,9},{9,8},{10,11... | collective-permute-start | bytes 196616 | tf_op jit(solution)/shard_map/cond/branch_1_fun/ppermute | solution.py:140
  58.0 3.6 %collective-permute-start.15 = (f32[128,128]{1,0:T(8,128)S(1)}, f32[128,128]{1,0:T(8,128)S(1)}, u32[]{:S(2)}, u32[]{:S(2)}) collective-permute-start(f32[128,128]{1,0:T(8,128)S(1)} %maximum_select_fusion.2.refs_0_), channel_id=1, source_target_pairs={{0,2},{1,3},{2,0},{3,1},{4,6},{5,7},{6,4},{7,5},{8,10},{9,11},{10,... | collective-permute-start | bytes 196616 | tf_op jit(solution)/shard_map/cond/branch_1_fun/ppermute | solution.py:140
  61.6 1.9 %collective-permute-start.16 = (f32[128,128]{1,0:T(8,128)S(1)}, f32[128,128]{1,0:T(8,128)S(1)}, u32[]{:S(2)}, u32[]{:S(2)}) collective-permute-start(f32[128,128]{1,0:T(8,128)S(1)} %maximum_select_fusion.2.refs_0_), channel_id=1, source_target_pairs={{0,3},{1,2},{2,1},{3,0},{4,7},{5,6},{6,5},{7,4},{8,11},{9,10},{10,... | collective-permute-start | bytes 196616 | tf_op jit(solution)/shard_map/cond/branch_1_fun/ppermute | solution.py:140
  63.9 3.6 %collective-permute-done.16.refs_3_ = f32[128,128]{1,0:T(8,128)S(1)} collective-permute-done((f32[128,128]{1,0:T(8,128)S(1)}, f32[128,128]{1,0:T(8,128)S(1)}, u32[]{:S(2)}, u32[]{:S(2)}) %collective-permute-start.16) | collective-permute-done | bytes 65568 | tf_op jit(solution)/shard_map/cond/branch_1_fun/ppermute | solution.py:140
  67.6 1.8 %branch_1_fun.10 = f32[4,128,1152]{2,1,0:T(8,128)} custom-call(s32[544,128]{1,0:T(8,128)S(1)} %copy-done.11, f32[128,128]{1,0:T(8,128)S(1)} %branch_1_fun.8.lead_ref, f32[8,256,128]{2,1,0:T(8,128)S(1)} %all-to-all-done.8.got_ref, f32[128,128]{1,0:T(8,128)S(1)} %maximum_select_fusion.2.refs_0_, f32[128,128]{1,0:T(8,128)S(1)} %collective-permute-done.14.refs_1_, ...), custom_call_target="tpu_custom_call" | custom-call | tf_op jit(solution)/shard_map/cond/branch_1_fun/pallas_call | solution.py:437
  69.4 6.4 %all-to-all-start.9 = ((f32[4,128,1152]{2,1,0:T(8,128)}), f32[4,128,1152]{2,1,0:T(8,128)S(1)}, u32[]{:S(2)}, u32[]{:S(2)}) async-start(f32[4,128,1152]{2,1,0:T(8,128)} %branch_1_fun.10), calls=%async_computation.9 | async-start | bytes 4718592 | tf_op jit(solution)/shard_map/cond/branch_1_fun/all_to_all | solution.py:474
  75.9 1.3 %branch_1_fun.11.rows_ref = f32[256,128]{1,0:T(8,128)S(1)} custom-call(s32[544,128]{1,0:T(8,128)} %get-tuple-element.45.plan_ref, f32[8,256,128]{2,1,0:T(8,128)S(1)} %all-to-all-done.8.got_ref, f32[256,128]{1,0:T(8,128)S(1)} %copy-done.19), custom_call_target="tpu_custom_call" | custom-call | tf_op jit(solution)/shard_map/cond/branch_1_fun/pallas_call | solution.py:437
  81.2 5.1 %collective-permute-done.19 = f32[128,128]{1,0:T(8,128)S(1)} collective-permute-done((f32[128,128]{1,0:T(8,128)S(1)}, f32[128,128]{1,0:T(8,128)S(1)}, u32[]{:S(2)}, u32[]{:S(2)}) %collective-permute-start.19) | collective-permute-done | bytes 65568 | tf_op jit(solution)/shard_map/cond/branch_1_fun/ppermute | solution.py:136
  86.3 3.0 %collective-permute-done.20 = f32[128,128]{1,0:T(8,128)S(1)} collective-permute-done((f32[128,128]{1,0:T(8,128)S(1)}, f32[128,128]{1,0:T(8,128)S(1)}, u32[]{:S(2)}, u32[]{:S(2)}) %collective-permute-start.20) | collective-permute-done | bytes 65568 | tf_op jit(solution)/shard_map/cond/branch_1_fun/ppermute | solution.py:137
  89.3 5.4 %collective-permute-start.21 = (f32[256,128]{1,0:T(8,128)S(1)}, f32[256,128]{1,0:T(8,128)S(1)}, u32[]{:S(2)}, u32[]{:S(2)}) collective-permute-start(f32[256,128]{1,0:T(8,128)S(1)} %maximum_select_fusion.1.left0_ref), channel_id=1, source_target_pairs={{0,1},{1,0},{2,3},{3,2},{4,5},{5,4},{6,7},{7,6},{8,9},{9,8},{10,11... | collective-permute-start | bytes 393224 | tf_op jit(solution)/shard_map/cond/branch_1_fun/ppermute | solution.py:140
  94.7 4.4 %collective-permute-start.22 = (f32[256,128]{1,0:T(8,128)S(1)}, f32[256,128]{1,0:T(8,128)S(1)}, u32[]{:S(2)}, u32[]{:S(2)}) collective-permute-start(f32[256,128]{1,0:T(8,128)S(1)} %maximum_select_fusion.1.left0_ref), channel_id=1, source_target_pairs={{0,2},{1,3},{2,0},{3,1},{4,6},{5,7},{6,4},{7,5},{8,10},{9,11},{10,... | collective-permute-start | bytes 393224 | tf_op jit(solution)/shard_map/cond/branch_1_fun/ppermute | solution.py:140
  99.1 1.9 %collective-permute-start.23 = (f32[256,128]{1,0:T(8,128)S(1)}, f32[256,128]{1,0:T(8,128)}, u32[]{:S(2)}, u32[]{:S(2)}) collective-permute-start(f32[256,128]{1,0:T(8,128)S(1)} %maximum_select_fusion.1.left0_ref), channel_id=1, source_target_pairs={{0,3},{1,2},{2,1},{3,0},{4,7},{5,6},{6,5},{7,4},{8,11},{9,10},{10,... | collective-permute-start | bytes 393224 | tf_op jit(solution)/shard_map/cond/branch_1_fun/ppermute | solution.py:140
  103.7 2.8 %collective-permute-done.23.left3_ref = f32[256,128]{1,0:T(8,128)} collective-permute-done((f32[256,128]{1,0:T(8,128)S(1)}, f32[256,128]{1,0:T(8,128)}, u32[]{:S(2)}, u32[]{:S(2)}) %collective-permute-start.23) | collective-permute-done | bytes 131104 | tf_op jit(solution)/shard_map/cond/branch_1_fun/ppermute | solution.py:140
  106.5 5.9 %branch_1_fun.13 = f32[256,768]{1,0:T(8,128)S(1)} custom-call(f32[512,1152]{1,0:T(8,128)S(1)} %bitcast.20, f32[256,768]{1,0:T(8,128)} %copy-done, f32[4,128,128]{2,1,0:T(8,128)} %get-tuple-element.55.lower_ref, f32[4,128,128]{2,1,0:T(8,128)} %get-tuple-element.56.upper_ref, f32[256,128]{1,0:T(8,128)} %copy-done.17, f32[256,128]{1,0:T(8,128)} %copy-done.20, ...), custom_call_target="tpu_custom_call" | custom-call | tf_op jit(solution)/shard_map/cond/branch_1_fun/pallas_call | solution.py:454
  (51 shorter events, 15.4 us)
Async XLA Ops:
  14.8 18.6 %all-to-all-start.7 = ((f32[8,32,128]{2,1,0:T(8,128)}), f32[8,32,128]{2,1,0:T(8,128)S(1)}, u32[]{:S(2)}, u32[]{:S(2)}) async-start(f32[8,32,128]{2,1,0:T(8,128)} %get-tuple-element.47), calls=%async_computation.7 | async-start | bytes 262144 | tf_op jit(solution)/shard_map/cond/branch_1_fun/all_to_all | solution.py:474
  24.9 6.1 %collective-permute-start.7 = (f32[48,768]{1,0:T(8,128)}, f32[48,768]{1,0:T(8,128)S(1)}, u32[]{:S(2)}, u32[]{:S(2)}) collective-permute-start(f32[48,768]{1,0:T(8,128)} %get-tuple-element.50), channel_id=1, source_target_pairs={{0,128},{16,144},{32,160},{48,176},{1,129},{17,145},{33,161},{49,1... | collective-permute-start | bytes 442376 | tf_op jit(solution)/shard_map/cond/branch_1_fun/ppermute | solution.py:483
  26.2 4.8 %collective-permute-start.8 = (f32[48,768]{1,0:T(8,128)}, f32[48,768]{1,0:T(8,128)S(1)}, u32[]{:S(2)}, u32[]{:S(2)}) collective-permute-start(f32[48,768]{1,0:T(8,128)} %get-tuple-element.51), channel_id=1, source_target_pairs={{0,256},{16,272},{32,288},{48,304},{1,257},{17,273},{33,289},{49,3... | collective-permute-start | bytes 442376 | tf_op jit(solution)/shard_map/cond/branch_1_fun/ppermute | solution.py:483
  26.8 4.1 %collective-permute-start.9 = (f32[48,768]{1,0:T(8,128)}, f32[48,768]{1,0:T(8,128)S(1)}, u32[]{:S(2)}, u32[]{:S(2)}) collective-permute-start(f32[48,768]{1,0:T(8,128)} %get-tuple-element.52), channel_id=1, source_target_pairs={{0,384},{16,400},{32,416},{48,432},{1,385},{17,401},{33,417},{49,4... | collective-permute-start | bytes 442376 | tf_op jit(solution)/shard_map/cond/branch_1_fun/ppermute | solution.py:483
  31.0 7.3 %copy-start.11 = (s32[544,128]{1,0:T(8,128)S(1)}, s32[544,128]{1,0:T(8,128)}, u32[]{:S(2)}) copy-start(s32[544,128]{1,0:T(8,128)} %get-tuple-element.45.plan_ref) | copy-start | bytes 835588 | tf_op jit(solution)/shard_map/cond
  33.4 34.2 %all-to-all-start.8 = ((f32[8,256,128]{2,1,0:T(8,128)}), f32[8,256,128]{2,1,0:T(8,128)S(1)}, u32[]{:S(2)}, u32[]{:S(2)}) async-start(f32[8,256,128]{2,1,0:T(8,128)} %branch_1_fun.9), calls=%async_computation.8 | async-start | bytes 2097152 | tf_op jit(solution)/shard_map/cond/branch_1_fun/all_to_all | solution.py:474
  38.5 1.4 %collective-permute-start.10 = (f32[128,128]{1,0:T(8,128)S(1)}, f32[128,128]{1,0:T(8,128)S(1)}, u32[]{:S(2)}, u32[]{:S(2)}) collective-permute-start(f32[128,128]{1,0:T(8,128)S(1)} %branch_1_fun.8.lead_ref), channel_id=1, source_target_pairs={{0,4},{1,5},{2,6},{3,7},{16,20},{17,21},{18,22},{19,23},{32,36},{3... | collective-permute-start | bytes 196616 | tf_op jit(solution)/shard_map/cond/branch_1_fun/ppermute | solution.py:124
  39.2 0.7 collective-permute-start.11
  39.9 8.7 %collective-permute-start.12 = (f32[64,128]{1,0:T(8,128)S(1)}, f32[64,128]{1,0:T(8,128)S(1)}, u32[]{:S(2)}, u32[]{:S(2)}) collective-permute-start(f32[64,128]{1,0:T(8,128)S(1)} %get-tuple-element.78), channel_id=1, source_target_pairs={{4,8},{5,9},{6,10},{7,11},{20,24},{21,25},{22,26},{23,27},{36,40},... | collective-permute-start | bytes 98312 | tf_op jit(solution)/shard_map/cond/branch_1_fun/ppermute | solution.py:136
  41.2 9.5 %collective-permute-start.13 = (f32[64,128]{1,0:T(8,128)S(1)}, f32[64,128]{1,0:T(8,128)S(1)}, u32[]{:S(2)}, u32[]{:S(2)}) collective-permute-start(f32[64,128]{1,0:T(8,128)S(1)} %get-tuple-element.79), channel_id=1, source_target_pairs={{12,8},{13,9},{14,10},{15,11},{28,24},{29,25},{30,26},{31,27},{44,... | collective-permute-start | bytes 98312 | tf_op jit(solution)/shard_map/cond/branch_1_fun/ppermute | solution.py:137
  50.7 12.8 %collective-permute-start.14 = (f32[128,128]{1,0:T(8,128)S(1)}, f32[128,128]{1,0:T(8,128)S(1)}, u32[]{:S(2)}, u32[]{:S(2)}) collective-permute-start(f32[128,128]{1,0:T(8,128)S(1)} %maximum_select_fusion.2.refs_0_), channel_id=1, source_target_pairs={{0,1},{1,0},{2,3},{3,2},{4,5},{5,4},{6,7},{7,6},{8,9},{9,8},{10,11... | collective-permute-start | bytes 196616 | tf_op jit(solution)/shard_map/cond/branch_1_fun/ppermute | solution.py:140
  58.0 6.0 %collective-permute-start.15 = (f32[128,128]{1,0:T(8,128)S(1)}, f32[128,128]{1,0:T(8,128)S(1)}, u32[]{:S(2)}, u32[]{:S(2)}) collective-permute-start(f32[128,128]{1,0:T(8,128)S(1)} %maximum_select_fusion.2.refs_0_), channel_id=1, source_target_pairs={{0,2},{1,3},{2,0},{3,1},{4,6},{5,7},{6,4},{7,5},{8,10},{9,11},{10,... | collective-permute-start | bytes 196616 | tf_op jit(solution)/shard_map/cond/branch_1_fun/ppermute | solution.py:140
  61.6 6.0 %collective-permute-start.16 = (f32[128,128]{1,0:T(8,128)S(1)}, f32[128,128]{1,0:T(8,128)S(1)}, u32[]{:S(2)}, u32[]{:S(2)}) collective-permute-start(f32[128,128]{1,0:T(8,128)S(1)} %maximum_select_fusion.2.refs_0_), channel_id=1, source_target_pairs={{0,3},{1,2},{2,1},{3,0},{4,7},{5,6},{6,5},{7,4},{8,11},{9,10},{10,... | collective-permute-start | bytes 196616 | tf_op jit(solution)/shard_map/cond/branch_1_fun/ppermute | solution.py:140
  69.4 37.1 %all-to-all-start.9 = ((f32[4,128,1152]{2,1,0:T(8,128)}), f32[4,128,1152]{2,1,0:T(8,128)S(1)}, u32[]{:S(2)}, u32[]{:S(2)}) async-start(f32[4,128,1152]{2,1,0:T(8,128)} %branch_1_fun.10), calls=%async_computation.9 | async-start | bytes 4718592 | tf_op jit(solution)/shard_map/cond/branch_1_fun/all_to_all | solution.py:474
  75.8 25.2 %copy-start.10 = (f32[256,768]{1,0:T(8,128)S(1)}, f32[256,768]{1,0:T(8,128)}, u32[]{:S(2)}) copy-start(f32[256,768]{1,0:T(8,128)} %get-tuple-element.54.a_ref) | copy-start | bytes 2359300 | tf_op jit(solution)/shard_map/cond
  75.9 25.2 %copy-start.12 = (s32[544,128]{1,0:T(8,128)S(1)}, s32[544,128]{1,0:T(8,128)}, u32[]{:S(2)}) copy-start(s32[544,128]{1,0:T(8,128)} %get-tuple-element.45.plan_ref) | copy-start | bytes 835588 | tf_op jit(solution)/shard_map/cond
  77.2 1.4 %collective-permute-start.17 = (f32[256,128]{1,0:T(8,128)S(1)}, f32[256,128]{1,0:T(8,128)S(1)}, u32[]{:S(2)}, u32[]{:S(2)}) collective-permute-start(f32[256,128]{1,0:T(8,128)S(1)} %branch_1_fun.11.rows_ref), channel_id=1, source_target_pairs={{0,4},{1,5},{2,6},{3,7},{16,20},{17,21},{18,22},{19,23},{32,36},{3... | collective-permute-start | bytes 393224 | tf_op jit(solution)/shard_map/cond/branch_1_fun/ppermute | solution.py:124
  77.8 0.7 collective-permute-start.18
  78.6 7.7 %collective-permute-start.19 = (f32[128,128]{1,0:T(8,128)S(1)}, f32[128,128]{1,0:T(8,128)S(1)}, u32[]{:S(2)}, u32[]{:S(2)}) collective-permute-start(f32[128,128]{1,0:T(8,128)S(1)} %get-tuple-element.76), channel_id=1, source_target_pairs={{4,8},{5,9},{6,10},{7,11},{20,24},{21,25},{22,26},{23,27},{36,40},... | collective-permute-start | bytes 196616 | tf_op jit(solution)/shard_map/cond/branch_1_fun/ppermute | solution.py:136
  79.9 9.4 %collective-permute-start.20 = (f32[128,128]{1,0:T(8,128)S(1)}, f32[128,128]{1,0:T(8,128)S(1)}, u32[]{:S(2)}, u32[]{:S(2)}) collective-permute-start(f32[128,128]{1,0:T(8,128)S(1)} %get-tuple-element.77), channel_id=1, source_target_pairs={{12,8},{13,9},{14,10},{15,11},{28,24},{29,25},{30,26},{31,27},{44,... | collective-permute-start | bytes 196616 | tf_op jit(solution)/shard_map/cond/branch_1_fun/ppermute | solution.py:137
  89.3 17.2 %copy-start.17 = (f32[256,128]{1,0:T(8,128)}, f32[256,128]{1,0:T(8,128)S(1)}, u32[]{:S(2)}) copy-start(f32[256,128]{1,0:T(8,128)S(1)} %maximum_select_fusion.1.left0_ref) | copy-start | bytes 393220 | tf_op jit(solution)/shard_map/cond
  89.3 13.1 %collective-permute-start.21 = (f32[256,128]{1,0:T(8,128)S(1)}, f32[256,128]{1,0:T(8,128)S(1)}, u32[]{:S(2)}, u32[]{:S(2)}) collective-permute-start(f32[256,128]{1,0:T(8,128)S(1)} %maximum_select_fusion.1.left0_ref), channel_id=1, source_target_pairs={{0,1},{1,0},{2,3},{3,2},{4,5},{5,4},{6,7},{7,6},{8,9},{9,8},{10,11... | collective-permute-start | bytes 393224 | tf_op jit(solution)/shard_map/cond/branch_1_fun/ppermute | solution.py:140
  94.7 8.2 %collective-permute-start.22 = (f32[256,128]{1,0:T(8,128)S(1)}, f32[256,128]{1,0:T(8,128)S(1)}, u32[]{:S(2)}, u32[]{:S(2)}) collective-permute-start(f32[256,128]{1,0:T(8,128)S(1)} %maximum_select_fusion.1.left0_ref), channel_id=1, source_target_pairs={{0,2},{1,3},{2,0},{3,1},{4,6},{5,7},{6,4},{7,5},{8,10},{9,11},{10,... | collective-permute-start | bytes 393224 | tf_op jit(solution)/shard_map/cond/branch_1_fun/ppermute | solution.py:140
  99.1 7.4 %collective-permute-start.23 = (f32[256,128]{1,0:T(8,128)S(1)}, f32[256,128]{1,0:T(8,128)}, u32[]{:S(2)}, u32[]{:S(2)}) collective-permute-start(f32[256,128]{1,0:T(8,128)S(1)} %maximum_select_fusion.1.left0_ref), channel_id=1, source_target_pairs={{0,3},{1,2},{2,1},{3,0},{4,7},{5,6},{6,5},{7,4},{8,11},{9,10},{10,... | collective-permute-start | bytes 393224 | tf_op jit(solution)/shard_map/cond/branch_1_fun/ppermute | solution.py:140
  (5 other events, 9.5 us)

commit v12 on v10

--- a/solution.py
+++ b/solution.py
@@ -429,7 +429,7 @@
     copy.wait()
 
 
-def kernel_call(body, shapes, scratch=(), out=None):
+def kernel_call(body, shapes, scratch=(), out=None, limit=None):
     def call(*args):
         return pl.pallas_call(
             body,
@@ -437,7 +437,7 @@
             out_specs=out or [VMEM] * len(shapes),
             out_shape=[jax.ShapeDtypeStruct(shape, kind) for shape, kind in shapes],
             scratch_shapes=list(scratch),
-            compiler_params=pltpu.CompilerParams(vmem_limit_bytes=KERNEL_VMEM),
+            compiler_params=pltpu.CompilerParams(vmem_limit_bytes=limit or KERNEL_VMEM),
         )(*args)
 
     return call
@@ -492,6 +492,7 @@
         [((4, NB, WIDE - NB), F32), ((ROWS, NB), F32)],
         [pltpu.VMEM((NB, WIDE - NB), F32), pltpu.SemaphoreType.DMA((4,))],
         [HBM, VMEM],
+        60 << 20,
     )(plan, lead, rest, block, *late)
     top = along(send, X_GROUPS).reshape(TOP, WIDE - NB)
     ends = spread_start(rows)

time: 114 us -> 116 us (1.018)
  Pallas kernels: 16.6 us -> 18.2 us
  waiting for transfers between devices: 25.5 us -> 26.9 us
    pallas_call x6, Pallas kernels: 10.6 us -> 12.2 us  [call(): pl.pallas_call(body, in_specs=[VMEM] * len(args), out_specs=out or [VMEM]...]
    ppermute x6, waiting for transfers between devices: 5.92 us -> 7.42 us  [spread_rest(): lax.ppermute(near, 'pcol', [(q, q ^ n) for q in range(PCOL)])]
    cond x16 -> x30, local copies, waits for them, and re-layouts: 3.6 us -> 2.6 us
  transfers between devices with their start and end apart: 20 -> 20, of which waited for: 8 -> 9; matrix products, arithmetic and copies ran while one was open for 0% -> 0% of each run, Pallas kernels for 4% -> 3%
where the time goes in v12:
time: 116 us; the launch traced here: 115 us
  starting transfers between devices  56.7 us (49%)
  waiting for transfers between devices  26.9 us (23%)
  Pallas kernels  18.2 us (16%)
  blocking collectives  8.38 us (7%)
  local copies, waits for them, and re-layouts  4 us (3%)
    ppermute x6, starting transfers between devices, spread_rest(): lax.ppermute(near, 'pcol', [(q, q ^ n) for q in range(PCOL)])  24.5 us
    all_to_all x3, starting transfers between devices, along(): return lax.all_to_all(value, 'prow', 0, 0, axis_index_groups=groups)  21.4 us
    pallas_call x6, Pallas kernels, call(): pl.pallas_call(body, in_specs=[VMEM] * len(args), out_specs=out or [VMEM]...  12.2 us
    ppermute x2, waiting for transfers between devices, spread_rest(): left = lax.ppermute(near[:half], 'pcol', [(q + 4, q + 8) for q in range(4)])  11.1 us
    all_to_all x1, blocking collectives, along(): return lax.all_to_all(value, 'prow', 0, 0, axis_index_groups=groups)  8.38 us
    ppermute x6, waiting for transfers between devices, spread_rest(): lax.ppermute(near, 'pcol', [(q, q ^ n) for q in range(PCOL)])  7.42 us
    pallas_call x1, Pallas kernels, factor(): pl.pallas_call(factor_kernel, in_specs=[VMEM, HBM, VMEM, VMEM] + [HBM] *...  5.94 us
    ppermute x2, waiting for transfers between devices, spread_rest(): lax.ppermute(near[half:], 'pcol', [(q + 12, q + 8) for q in range(4)])  5.07 us
  transfers between devices with their start and end apart: 20, of which 9 were waited for; matrix products, arithmetic and copies ran while one was open for 0% of the time, Pallas kernels for 3%

profile of v12, /device:TPU:43, one launch (start us, length us, event | category | flops | bytes accessed | tf_op | source)
XLA Modules:
  0.0 115.5 jit_solution(4659399031206033942)
XLA Ops:
  0.0 3.4 %shard_map.48 = (f32[64,768]{1,0:T(8,128)}, f32[48,768]{1,0:T(8,128)}, f32[48,768]{1,0:T(8,128)}, f32[48,768]{1,0:T(8,128)}, f32[48,768]{1,0:T(8,128)}, /*index=...) custom-call(s32[4,128]{1,0:T(4,128)} %bitcast.32, f32[256,768]{1,0:T(8,128)} %a_ref.1), custom_call_target="tpu_custom_call" | custom-call | tf_op jit(solution)/shard_map/pallas_call | solution.py:434
  4.6 110.0 %conditional.1 = (f32[256,768]{1,0:T(8,128)S(1)}) conditional(s32[]{:T(128)} %bitcast.18, (s32[512]{0:T(512)}, f32[256,768]{1,0:T(8,128)}, f32[4,128,128]{2,1,0:T(8,128)}, f32[4,128,128]{2,1,0:T(8,128)}) %tuple.11, (f32[64,768]{1,0:T(8,128)}, s32[544,128]{1,0:T(8,128)}, f32[48,768]{1,0:T(8,128)}, f32[48,768]{1,0:T(8,128)}, f32[48,768]{1,0:T(8,128)}, ...), branch_computations={%region_0.4_spmd, %region_4.5_spmd} | conditional | flops 1392652 | bytes 63624084 | solution.py:563
  4.6 8.4 %all_to_all.41 = f32[4,16,768]{2,1,0:T(8,128)S(1)} all-to-all(f32[4,16,768]{2,1,0:T(8,128)} %bitcast.30), channel_id=1, replica_groups={{0,128,256,384},{16,144,272,400},{32,160,288,416},{48,176,304,432},{64,..., dimensions={0} | all-to-all | bytes 393216 | tf_op jit(solution)/shard_map/cond/branch_1_fun/all_to_all | solution.py:471
  13.0 1.9 %branch_1_fun.6 = (f32[8,32,128]{2,1,0:T(8,128)}, f32[32,640]{1,0:T(8,128)S(1)}) custom-call(s32[544,128]{1,0:T(8,128)} %get-tuple-element.45.plan_ref, f32[64,768]{1,0:T(8,128)S(1)} %bitcast.22), custom_call_target="tpu_custom_call" | custom-call | tf_op jit(solution)/shard_map/cond/branch_1_fun/pallas_call | solution.py:434
  14.9 10.0 %all-to-all-start.7 = ((f32[8,32,128]{2,1,0:T(8,128)}), f32[8,32,128]{2,1,0:T(8,128)S(1)}, u32[]{:S(2)}, u32[]{:S(2)}) async-start(f32[8,32,128]{2,1,0:T(8,128)} %get-tuple-element.47), calls=%async_computation.7 | async-start | bytes 262144 | tf_op jit(solution)/shard_map/cond/branch_1_fun/all_to_all | solution.py:471
  27.7 3.3 %collective-permute-done.7.leave1_ref = f32[48,768]{1,0:T(8,128)S(1)} collective-permute-done((f32[48,768]{1,0:T(8,128)}, f32[48,768]{1,0:T(8,128)S(1)}, u32[]{:S(2)}, u32[]{:S(2)}) %collective-permute-start.7) | collective-permute-done | bytes 147488 | tf_op jit(solution)/shard_map/cond/branch_1_fun/ppermute | solution.py:480
  31.0 2.4 %branch_1_fun.8 = f32[8,256,128]{2,1,0:T(8,128)} custom-call(s32[544,128]{1,0:T(8,128)} %get-tuple-element.45.plan_ref, f32[32,640]{1,0:T(8,128)S(1)} %get-tuple-element.48.rows_ref, f32[48,768]{1,0:T(8,128)} %get-tuple-element.49.leave0_ref, f32[48,768]{1,0:T(8,128)S(1)} %collective-permute-done.7.leave1_ref, ...), custom_call_target="tpu_custom_call" | custom-call | tf_op jit(solution)/shard_map/cond/branch_1_fun/pallas_call | solution.py:434
  33.4 5.0 %all-to-all-start.8 = ((f32[8,256,128]{2,1,0:T(8,128)}), f32[8,256,128]{2,1,0:T(8,128)S(1)}, u32[]{:S(2)}, u32[]{:S(2)}) async-start(f32[8,256,128]{2,1,0:T(8,128)} %branch_1_fun.8), calls=%async_computation.8 | async-start | bytes 2097152 | tf_op jit(solution)/shard_map/cond/branch_1_fun/all_to_all | solution.py:471
  40.1 1.3 %collective-permute-start.12 = (f32[64,128]{1,0:T(8,128)S(1)}, f32[64,128]{1,0:T(8,128)S(1)}, u32[]{:S(2)}, u32[]{:S(2)}) collective-permute-start(f32[64,128]{1,0:T(8,128)S(1)} %get-tuple-element.80), channel_id=1, source_target_pairs={{4,8},{5,9},{6,10},{7,11},{20,24},{21,25},{22,26},{23,27},{36,40},... | collective-permute-start | bytes 98312 | tf_op jit(solution)/shard_map/cond/branch_1_fun/ppermute | solution.py:136
  42.7 6.0 %collective-permute-done.12 = f32[64,128]{1,0:T(8,128)S(1)} collective-permute-done((f32[64,128]{1,0:T(8,128)S(1)}, f32[64,128]{1,0:T(8,128)S(1)}, u32[]{:S(2)}, u32[]{:S(2)}) %collective-permute-start.12) | collective-permute-done | bytes 32800 | tf_op jit(solution)/shard_map/cond/branch_1_fun/ppermute | solution.py:136
  48.7 2.1 %collective-permute-done.13 = f32[64,128]{1,0:T(8,128)S(1)} collective-permute-done((f32[64,128]{1,0:T(8,128)S(1)}, f32[64,128]{1,0:T(8,128)S(1)}, u32[]{:S(2)}, u32[]{:S(2)}) %collective-permute-start.13) | collective-permute-done | bytes 32800 | tf_op jit(solution)/shard_map/cond/branch_1_fun/ppermute | solution.py:137
  50.9 7.3 %collective-permute-start.14 = (f32[128,128]{1,0:T(8,128)S(1)}, f32[128,128]{1,0:T(8,128)S(1)}, u32[]{:S(2)}, u32[]{:S(2)}) collective-permute-start(f32[128,128]{1,0:T(8,128)S(1)} %maximum_select_fusion.2.refs_0_), channel_id=1, source_target_pairs={{0,1},{1,0},{2,3},{3,2},{4,5},{5,4},{6,7},{7,6},{8,9},{9,8},{10,11... | collective-permute-start | bytes 196616 | tf_op jit(solution)/shard_map/cond/branch_1_fun/ppermute | solution.py:140
  58.1 3.6 %collective-permute-start.15 = (f32[128,128]{1,0:T(8,128)S(1)}, f32[128,128]{1,0:T(8,128)S(1)}, u32[]{:S(2)}, u32[]{:S(2)}) collective-permute-start(f32[128,128]{1,0:T(8,128)S(1)} %maximum_select_fusion.2.refs_0_), channel_id=1, source_target_pairs={{0,2},{1,3},{2,0},{3,1},{4,6},{5,7},{6,4},{7,5},{8,10},{9,11},{10,... | collective-permute-start | bytes 196616 | tf_op jit(solution)/shard_map/cond/branch_1_fun/ppermute | solution.py:140
  61.7 1.9 %collective-permute-start.16 = (f32[128,128]{1,0:T(8,128)S(1)}, f32[128,128]{1,0:T(8,128)S(1)}, u32[]{:S(2)}, u32[]{:S(2)}) collective-permute-start(f32[128,128]{1,0:T(8,128)S(1)} %maximum_select_fusion.2.refs_0_), channel_id=1, source_target_pairs={{0,3},{1,2},{2,1},{3,0},{4,7},{5,6},{6,5},{7,4},{8,11},{9,10},{10,... | collective-permute-start | bytes 196616 | tf_op jit(solution)/shard_map/cond/branch_1_fun/ppermute | solution.py:140
  64.1 3.6 %collective-permute-done.16.refs_3_ = f32[128,128]{1,0:T(8,128)S(1)} collective-permute-done((f32[128,128]{1,0:T(8,128)S(1)}, f32[128,128]{1,0:T(8,128)S(1)}, u32[]{:S(2)}, u32[]{:S(2)}) %collective-permute-start.16) | collective-permute-done | bytes 65568 | tf_op jit(solution)/shard_map/cond/branch_1_fun/ppermute | solution.py:140
  68.7 3.8 %branch_1_fun.9 = (f32[4,128,1152]{2,1,0:T(8,128)}, f32[256,128]{1,0:T(8,128)}) custom-call(s32[544,128]{1,0:T(8,128)S(1)} %copy-done.15, f32[128,128]{1,0:T(8,128)} %copy-done.10, f32[8,256,128]{2,1,0:T(8,128)} %copy-done, f32[256,128]{1,0:T(8,128)S(1)} %copy-done.23, f32[128,128]{1,0:T(8,128)} %copy-done.21, f32[128,128]{1,0:T(8,128)} %copy-done.26, ...), custom_call_target="tpu_custom_call" | custom-call | tf_op jit(solution)/shard_map/cond/branch_1_fun/pallas_call | solution.py:434
  72.5 6.4 %all-to-all-start.9 = ((f32[4,128,1152]{2,1,0:T(8,128)}), f32[4,128,1152]{2,1,0:T(8,128)S(1)}, u32[]{:S(2)}, u32[]{:S(2)}) async-start(f32[4,128,1152]{2,1,0:T(8,128)} %get-tuple-element.54), calls=%async_computation.9 | async-start | bytes 4718592 | tf_op jit(solution)/shard_map/cond/branch_1_fun/all_to_all | solution.py:471
  83.1 5.1 %collective-permute-done.19 = f32[128,128]{1,0:T(8,128)S(1)} collective-permute-done((f32[128,128]{1,0:T(8,128)S(1)}, f32[128,128]{1,0:T(8,128)S(1)}, u32[]{:S(2)}, u32[]{:S(2)}) %collective-permute-start.19) | collective-permute-done | bytes 65568 | tf_op jit(solution)/shard_map/cond/branch_1_fun/ppermute | solution.py:136
  88.2 2.9 %collective-permute-done.20 = f32[128,128]{1,0:T(8,128)S(1)} collective-permute-done((f32[128,128]{1,0:T(8,128)S(1)}, f32[128,128]{1,0:T(8,128)S(1)}, u32[]{:S(2)}, u32[]{:S(2)}) %collective-permute-start.20) | collective-permute-done | bytes 65568 | tf_op jit(solution)/shard_map/cond/branch_1_fun/ppermute | solution.py:137
  91.2 5.4 %collective-permute-start.21 = (f32[256,128]{1,0:T(8,128)S(1)}, f32[256,128]{1,0:T(8,128)S(1)}, u32[]{:S(2)}, u32[]{:S(2)}) collective-permute-start(f32[256,128]{1,0:T(8,128)S(1)} %maximum_select_fusion.1.left0_ref), channel_id=1, source_target_pairs={{0,1},{1,0},{2,3},{3,2},{4,5},{5,4},{6,7},{7,6},{8,9},{9,8},{10,11... | collective-permute-start | bytes 393224 | tf_op jit(solution)/shard_map/cond/branch_1_fun/ppermute | solution.py:140
  96.6 4.4 %collective-permute-start.22 = (f32[256,128]{1,0:T(8,128)S(1)}, f32[256,128]{1,0:T(8,128)S(1)}, u32[]{:S(2)}, u32[]{:S(2)}) collective-permute-start(f32[256,128]{1,0:T(8,128)S(1)} %maximum_select_fusion.1.left0_ref), channel_id=1, source_target_pairs={{0,2},{1,3},{2,0},{3,1},{4,6},{5,7},{6,4},{7,5},{8,10},{9,11},{10,... | collective-permute-start | bytes 393224 | tf_op jit(solution)/shard_map/cond/branch_1_fun/ppermute | solution.py:140
  101.0 1.9 %collective-permute-start.23 = (f32[256,128]{1,0:T(8,128)S(1)}, f32[256,128]{1,0:T(8,128)}, u32[]{:S(2)}, u32[]{:S(2)}) collective-permute-start(f32[256,128]{1,0:T(8,128)S(1)} %maximum_select_fusion.1.left0_ref), channel_id=1, source_target_pairs={{0,3},{1,2},{2,1},{3,0},{4,7},{5,6},{6,5},{7,4},{8,11},{9,10},{10,... | collective-permute-start | bytes 393224 | tf_op jit(solution)/shard_map/cond/branch_1_fun/ppermute | solution.py:140
  105.6 2.8 %collective-permute-done.23.left3_ref = f32[256,128]{1,0:T(8,128)} collective-permute-done((f32[256,128]{1,0:T(8,128)S(1)}, f32[256,128]{1,0:T(8,128)}, u32[]{:S(2)}, u32[]{:S(2)}) %collective-permute-start.23) | collective-permute-done | bytes 131104 | tf_op jit(solution)/shard_map/cond/branch_1_fun/ppermute | solution.py:140
  108.4 5.9 %branch_1_fun.11 = f32[256,768]{1,0:T(8,128)S(1)} custom-call(f32[512,1152]{1,0:T(8,128)S(1)} %bitcast.20, f32[256,768]{1,0:T(8,128)} %copy-done.2, f32[4,128,128]{2,1,0:T(8,128)} %get-tuple-element.57.lower_ref, f32[4,128,128]{2,1,0:T(8,128)} %get-tuple-element.58.upper_ref, f32[256,128]{1,0:T(8,128)} %copy-done.20, f32[256,128]{1,0:T(8,128)} %copy-done.24, ...), custom_call_target="tpu_custom_call" | custom-call | tf_op jit(solution)/shard_map/cond/branch_1_fun/pallas_call | solution.py:451
  (64 shorter events, 15.2 us)
Async XLA Ops:
  14.9 18.6 %all-to-all-start.7 = ((f32[8,32,128]{2,1,0:T(8,128)}), f32[8,32,128]{2,1,0:T(8,128)S(1)}, u32[]{:S(2)}, u32[]{:S(2)}) async-start(f32[8,32,128]{2,1,0:T(8,128)} %get-tuple-element.47), calls=%async_computation.7 | async-start | bytes 262144 | tf_op jit(solution)/shard_map/cond/branch_1_fun/all_to_all | solution.py:471
  24.9 6.1 %collective-permute-start.7 = (f32[48,768]{1,0:T(8,128)}, f32[48,768]{1,0:T(8,128)S(1)}, u32[]{:S(2)}, u32[]{:S(2)}) collective-permute-start(f32[48,768]{1,0:T(8,128)} %get-tuple-element.50), channel_id=1, source_target_pairs={{0,128},{16,144},{32,160},{48,176},{1,129},{17,145},{33,161},{49,1... | collective-permute-start | bytes 442376 | tf_op jit(solution)/shard_map/cond/branch_1_fun/ppermute | solution.py:480
  26.2 4.8 %collective-permute-start.8 = (f32[48,768]{1,0:T(8,128)}, f32[48,768]{1,0:T(8,128)S(1)}, u32[]{:S(2)}, u32[]{:S(2)}) collective-permute-start(f32[48,768]{1,0:T(8,128)} %get-tuple-element.51), channel_id=1, source_target_pairs={{0,256},{16,272},{32,288},{48,304},{1,257},{17,273},{33,289},{49,3... | collective-permute-start | bytes 442376 | tf_op jit(solution)/shard_map/cond/branch_1_fun/ppermute | solution.py:480
  26.9 4.1 %collective-permute-start.9 = (f32[48,768]{1,0:T(8,128)}, f32[48,768]{1,0:T(8,128)S(1)}, u32[]{:S(2)}, u32[]{:S(2)}) collective-permute-start(f32[48,768]{1,0:T(8,128)} %get-tuple-element.52), channel_id=1, source_target_pairs={{0,384},{16,400},{32,416},{48,432},{1,385},{17,401},{33,417},{49,4... | collective-permute-start | bytes 442376 | tf_op jit(solution)/shard_map/cond/branch_1_fun/ppermute | solution.py:480
  33.4 35.3 %copy-start.23 = (f32[256,128]{1,0:T(8,128)S(1)}, f32[256,128]{1,0:T(8,128)}, u32[]{:S(2)}) copy-start(f32[256,128]{1,0:T(8,128)} %get-tuple-element.53.block_ref) | copy-start | bytes 393220 | tf_op jit(solution)/shard_map/cond
  33.4 34.3 %all-to-all-start.8 = ((f32[8,256,128]{2,1,0:T(8,128)}), f32[8,256,128]{2,1,0:T(8,128)S(1)}, u32[]{:S(2)}, u32[]{:S(2)}) async-start(f32[8,256,128]{2,1,0:T(8,128)} %branch_1_fun.8), calls=%async_computation.8 | async-start | bytes 2097152 | tf_op jit(solution)/shard_map/cond/branch_1_fun/all_to_all | solution.py:471
  38.7 29.1 %copy-start.10 = (f32[128,128]{1,0:T(8,128)}, f32[128,128]{1,0:T(8,128)S(1)}, u32[]{:S(2)}) copy-start(f32[128,128]{1,0:T(8,128)S(1)} %branch_1_fun.7.lead_ref) | copy-start | bytes 196612 | tf_op jit(solution)/shard_map/cond
  38.7 1.4 %collective-permute-start.10 = (f32[128,128]{1,0:T(8,128)S(1)}, f32[128,128]{1,0:T(8,128)S(1)}, u32[]{:S(2)}, u32[]{:S(2)}) collective-permute-start(f32[128,128]{1,0:T(8,128)S(1)} %branch_1_fun.7.lead_ref), channel_id=1, source_target_pairs={{0,4},{1,5},{2,6},{3,7},{16,20},{17,21},{18,22},{19,23},{32,36},{3... | collective-permute-start | bytes 196616 | tf_op jit(solution)/shard_map/cond/branch_1_fun/ppermute | solution.py:124
  39.3 0.7 collective-permute-start.11
  40.1 8.7 %collective-permute-start.12 = (f32[64,128]{1,0:T(8,128)S(1)}, f32[64,128]{1,0:T(8,128)S(1)}, u32[]{:S(2)}, u32[]{:S(2)}) collective-permute-start(f32[64,128]{1,0:T(8,128)S(1)} %get-tuple-element.80), channel_id=1, source_target_pairs={{4,8},{5,9},{6,10},{7,11},{20,24},{21,25},{22,26},{23,27},{36,40},... | collective-permute-start | bytes 98312 | tf_op jit(solution)/shard_map/cond/branch_1_fun/ppermute | solution.py:136
  41.4 9.5 %collective-permute-start.13 = (f32[64,128]{1,0:T(8,128)S(1)}, f32[64,128]{1,0:T(8,128)S(1)}, u32[]{:S(2)}, u32[]{:S(2)}) collective-permute-start(f32[64,128]{1,0:T(8,128)S(1)} %get-tuple-element.81), channel_id=1, source_target_pairs={{12,8},{13,9},{14,10},{15,11},{28,24},{29,25},{30,26},{31,27},{44,... | collective-permute-start | bytes 98312 | tf_op jit(solution)/shard_map/cond/branch_1_fun/ppermute | solution.py:137
  50.9 12.8 %collective-permute-start.14 = (f32[128,128]{1,0:T(8,128)S(1)}, f32[128,128]{1,0:T(8,128)S(1)}, u32[]{:S(2)}, u32[]{:S(2)}) collective-permute-start(f32[128,128]{1,0:T(8,128)S(1)} %maximum_select_fusion.2.refs_0_), channel_id=1, source_target_pairs={{0,1},{1,0},{2,3},{3,2},{4,5},{5,4},{6,7},{7,6},{8,9},{9,8},{10,11... | collective-permute-start | bytes 196616 | tf_op jit(solution)/shard_map/cond/branch_1_fun/ppermute | solution.py:140
  58.1 6.0 %collective-permute-start.15 = (f32[128,128]{1,0:T(8,128)S(1)}, f32[128,128]{1,0:T(8,128)S(1)}, u32[]{:S(2)}, u32[]{:S(2)}) collective-permute-start(f32[128,128]{1,0:T(8,128)S(1)} %maximum_select_fusion.2.refs_0_), channel_id=1, source_target_pairs={{0,2},{1,3},{2,0},{3,1},{4,6},{5,7},{6,4},{7,5},{8,10},{9,11},{10,... | collective-permute-start | bytes 196616 | tf_op jit(solution)/shard_map/cond/branch_1_fun/ppermute | solution.py:140
  61.7 6.0 %collective-permute-start.16 = (f32[128,128]{1,0:T(8,128)S(1)}, f32[128,128]{1,0:T(8,128)S(1)}, u32[]{:S(2)}, u32[]{:S(2)}) collective-permute-start(f32[128,128]{1,0:T(8,128)S(1)} %maximum_select_fusion.2.refs_0_), channel_id=1, source_target_pairs={{0,3},{1,2},{2,1},{3,0},{4,7},{5,6},{6,5},{7,4},{8,11},{9,10},{10,... | collective-permute-start | bytes 196616 | tf_op jit(solution)/shard_map/cond/branch_1_fun/ppermute | solution.py:140
  72.5 30.4 %copy-start.14 = (f32[256,768]{1,0:T(8,128)S(1)}, f32[256,768]{1,0:T(8,128)}, u32[]{:S(2)}) copy-start(f32[256,768]{1,0:T(8,128)} %get-tuple-element.56.a_ref) | copy-start | bytes 2359300 | tf_op jit(solution)/shard_map/cond
  72.5 35.9 %all-to-all-start.9 = ((f32[4,128,1152]{2,1,0:T(8,128)}), f32[4,128,1152]{2,1,0:T(8,128)S(1)}, u32[]{:S(2)}, u32[]{:S(2)}) async-start(f32[4,128,1152]{2,1,0:T(8,128)} %get-tuple-element.54), calls=%async_computation.9 | async-start | bytes 4718592 | tf_op jit(solution)/shard_map/cond/branch_1_fun/all_to_all | solution.py:471
  79.0 24.0 %copy-start.1 = (f32[8,256,128]{2,1,0:T(8,128)S(1)}, f32[8,256,128]{2,1,0:T(8,128)}, u32[]{:S(2)}) copy-start(f32[8,256,128]{2,1,0:T(8,128)} %copy-done) | copy-start | bytes 3145732 | tf_op jit(solution)/shard_map/cond
  79.0 1.5 %collective-permute-start.17 = (f32[256,128]{1,0:T(8,128)S(1)}, f32[256,128]{1,0:T(8,128)S(1)}, u32[]{:S(2)}, u32[]{:S(2)}) collective-permute-start(f32[256,128]{1,0:T(8,128)S(1)} %copy-done.13), channel_id=1, source_target_pairs={{0,4},{1,5},{2,6},{3,7},{16,20},{17,21},{18,22},{19,23},{32,36},{3... | collective-permute-start | bytes 393224 | tf_op jit(solution)/shard_map/cond/branch_1_fun/ppermute | solution.py:124
  79.8 0.7 collective-permute-start.18
  80.5 7.7 %collective-permute-start.19 = (f32[128,128]{1,0:T(8,128)S(1)}, f32[128,128]{1,0:T(8,128)S(1)}, u32[]{:S(2)}, u32[]{:S(2)}) collective-permute-start(f32[128,128]{1,0:T(8,128)S(1)} %get-tuple-element.78), channel_id=1, source_target_pairs={{4,8},{5,9},{6,10},{7,11},{20,24},{21,25},{22,26},{23,27},{36,40},... | collective-permute-start | bytes 196616 | tf_op jit(solution)/shard_map/cond/branch_1_fun/ppermute | solution.py:136
  81.8 9.3 %collective-permute-start.20 = (f32[128,128]{1,0:T(8,128)S(1)}, f32[128,128]{1,0:T(8,128)S(1)}, u32[]{:S(2)}, u32[]{:S(2)}) collective-permute-start(f32[128,128]{1,0:T(8,128)S(1)} %get-tuple-element.79), channel_id=1, source_target_pairs={{12,8},{13,9},{14,10},{15,11},{28,24},{29,25},{30,26},{31,27},{44,... | collective-permute-start | bytes 196616 | tf_op jit(solution)/shard_map/cond/branch_1_fun/ppermute | solution.py:137
  91.2 13.1 %collective-permute-start.21 = (f32[256,128]{1,0:T(8,128)S(1)}, f32[256,128]{1,0:T(8,128)S(1)}, u32[]{:S(2)}, u32[]{:S(2)}) collective-permute-start(f32[256,128]{1,0:T(8,128)S(1)} %maximum_select_fusion.1.left0_ref), channel_id=1, source_target_pairs={{0,1},{1,0},{2,3},{3,2},{4,5},{5,4},{6,7},{7,6},{8,9},{9,8},{10,11... | collective-permute-start | bytes 393224 | tf_op jit(solution)/shard_map/cond/branch_1_fun/ppermute | solution.py:140
  96.6 8.2 %collective-permute-start.22 = (f32[256,128]{1,0:T(8,128)S(1)}, f32[256,128]{1,0:T(8,128)S(1)}, u32[]{:S(2)}, u32[]{:S(2)}) collective-permute-start(f32[256,128]{1,0:T(8,128)S(1)} %maximum_select_fusion.1.left0_ref), channel_id=1, source_target_pairs={{0,2},{1,3},{2,0},{3,1},{4,6},{5,7},{6,4},{7,5},{8,10},{9,11},{10,... | collective-permute-start | bytes 393224 | tf_op jit(solution)/shard_map/cond/branch_1_fun/ppermute | solution.py:140
  101.0 7.4 %collective-permute-start.23 = (f32[256,128]{1,0:T(8,128)S(1)}, f32[256,128]{1,0:T(8,128)}, u32[]{:S(2)}, u32[]{:S(2)}) collective-permute-start(f32[256,128]{1,0:T(8,128)S(1)} %maximum_select_fusion.1.left0_ref), channel_id=1, source_target_pairs={{0,3},{1,2},{2,1},{3,0},{4,7},{5,6},{6,5},{7,4},{8,11},{9,10},{10,... | collective-permute-start | bytes 393224 | tf_op jit(solution)/shard_map/cond/branch_1_fun/ppermute | solution.py:140
  (12 other events, 56.8 us)
